TPU v7x, 512 devices: a whole 4x4x16 slice. The times are simulated.
512 devices in a mesh: dp: 4 (over x), context: 16 (over z_lo, core), head: 8 (over y, z_hi).
Axes of the slice: x: 4, y: 4, z: 16 (z_hi: 2, z_lo: 8; z = z_hi * 8 + z_lo), core: 2. Of those that a mesh axis runs over, the one named last changes fastest.
Arguments:
- hidden: bfloat16 [4, 3072, 4096], P('dp', 'context'), may hold values from -6 to 6
- queries: bfloat16 [4, 3072, 4096], P('dp', 'context', 'head'), may hold values from -216 to 216
- grad_out: bfloat16 [4, 3072, 4096], P('dp', 'context', 'head'), may hold values from -6 to 6
- segment: int32 [4, 3072], P('dp', 'context'), may hold values from 0 to 3, never falling along the last dimension, each value on 1 to 1920 neighbouring positions
- key_proj: bfloat16 [4096, 1024], P(('dp', 'context'), 'head'), may hold values from -0.09375 to 0.09375
- value_proj: bfloat16 [4096, 1024], P(('dp', 'context'), 'head'), may hold values from -0.09375 to 0.09375
Outputs:
- grad_queries: bfloat16 [4, 3072, 4096], P('dp', 'context', 'head')
- grad_key_proj: float32 [4096, 1024], P(('dp', 'context'), 'head')
- grad_value_proj: float32 [4096, 1024], P(('dp', 'context'), 'head')
Inputs may be any that keep to these rules, and one draw needn't show every extreme that they name: segment ids never fall along a trace; each trace has 4 segments, one of exactly 1920 tokens.
All inputs are finite; a program needn't handle non-finite values.
Results may differ from a plain program's by a relative error of at most 0.04.
The roundings to bfloat16 on the way count: a program that leaves them out, or rounds other values in their place, can miss the bound.
Values may be sent and summed in bfloat16 or wider, within the bound.
A program may use at most 64 MiB of HBM per device.

v0:
```python
import jax
import jax.numpy as jnp
from jax import lax
from jax.sharding import PartitionSpec as P

HEADS = 32
KV_HEADS = 8
HEAD_DIM = 128


far_below = -1e30


def passed_along(block, axis, distance):
    devices = range(lax.axis_size(axis))
    route = [((i - distance) % len(devices), i) for i in devices]
    return lax.ppermute(block, axis, route)


def body(hidden, queries, grad_out, segment, key_proj, value_proj):
    tok_rows = hidden.shape[1]
    local_rows = hidden[0]
    kv_local = key_proj.shape[1] // HEAD_DIM
    group = HEADS // KV_HEADS
    scale = HEAD_DIM ** (-0.5)
    steps = lax.axis_size("context")
    pieces = (
        lax.all_gather(key_proj, ("dp", "context"), axis=0, tiled=True),
        lax.all_gather(value_proj, ("dp", "context"), axis=0, tiled=True),
    )
    columns = local_rows
    key_sum = jnp.dot(columns, pieces[0], preferred_element_type=jnp.float32)
    value_sum = jnp.dot(columns, pieces[1], preferred_element_type=jnp.float32)
    keys = key_sum.astype(jnp.bfloat16).reshape(tok_rows, kv_local, HEAD_DIM)
    values = value_sum.astype(jnp.bfloat16).reshape(tok_rows, kv_local, HEAD_DIM)
    marks = segment[0].astype(jnp.bfloat16)
    query_heads = queries[0].reshape(tok_rows, kv_local, group, HEAD_DIM)
    cot_heads = grad_out[0].reshape(tok_rows, kv_local, group, HEAD_DIM)

    def masked_scores(key_part, mark_part):
        raw = (
            jnp.einsum("qhgd,khd->qhgk", query_heads, key_part, preferred_element_type=jnp.float32)
            * scale
        )
        same = (marks[:, None] == mark_part[None, :])[:, None, None, :]
        return (jnp.where(same, raw, far_below), same)

    buffers = ()
    stat_shape = (tok_rows, kv_local, group)
    pieces = (
        lax.all_gather(keys, "context", axis=0, tiled=True),
        lax.all_gather(values, "context", axis=0, tiled=True),
        lax.all_gather(marks, "context", axis=0, tiled=True),
    )
    top = jnp.full(stat_shape, far_below, jnp.float32)
    stored = buffers
    raw, same = masked_scores(pieces[0], pieces[2])
    new_top = jnp.maximum(top, jnp.max(raw, axis=-1))
    weights = jnp.where(same, jnp.exp(raw - new_top[..., None]), 0.0)
    total = jnp.sum(weights, axis=-1)
    acc = jnp.einsum(
        "qhgk,khd->qhgd",
        weights.astype(jnp.bfloat16),
        pieces[1],
        preferred_element_type=jnp.float32,
    )
    top, total, acc, stored = (new_top, total, acc, stored)
    output = (acc / total[..., None]).astype(jnp.bfloat16)
    log_total = top + jnp.log(total)
    delta = jnp.sum(cot_heads.astype(jnp.float32) * output.astype(jnp.float32), axis=-1)

    def visit(key_part, value_part, mark_part, query_acc):
        raw, same = masked_scores(key_part, mark_part)
        probs = jnp.where(same, jnp.exp(raw - log_total[..., None]), 0.0)
        probs_b = probs.astype(jnp.bfloat16)
        value_part_grad = jnp.einsum(
            "qhgk,qhgd->khd", probs_b, cot_heads, preferred_element_type=jnp.float32
        )
        prob_grad = jnp.einsum(
            "qhgd,khd->qhgk", cot_heads, value_part, preferred_element_type=jnp.float32
        )
        dscores = (probs * (prob_grad - delta[..., None])).astype(jnp.bfloat16)
        query_acc = (
            query_acc
            + jnp.einsum("qhgk,khd->qhgd", dscores, key_part, preferred_element_type=jnp.float32)
            * scale
        )
        key_part_grad = (
            jnp.einsum("qhgk,qhgd->khd", dscores, query_heads, preferred_element_type=jnp.float32)
            * scale
        )
        return (query_acc, key_part_grad, value_part_grad)

    zero_grads = jnp.zeros((tok_rows, kv_local, HEAD_DIM), jnp.float32)
    query_zero = jnp.zeros((tok_rows, kv_local, group, HEAD_DIM), jnp.float32)

    def turn(index, state):
        key_part, value_part, mark_part, key_grad, value_grad, query_acc = state
        query_acc, key_more, value_more = visit(key_part, value_part, mark_part, query_acc)
        key_part, value_part, mark_part = passed_along(
            (key_part, value_part, mark_part), "context", 1
        )
        key_grad, value_grad = passed_along(
            (key_grad + key_more, value_grad + value_more), "context", 1
        )
        return (key_part, value_part, mark_part, key_grad, value_grad, query_acc)

    state = lax.fori_loop(0, steps, turn, (keys, values, marks, zero_grads, zero_grads, query_zero))
    key_grad, value_grad, query_acc = (state[3], state[4], state[5])
    grad_queries = query_acc.astype(jnp.bfloat16).reshape(1, tok_rows, kv_local * group * HEAD_DIM)
    both_grads = jnp.concatenate(
        [
            key_grad.astype(jnp.bfloat16).reshape(tok_rows, kv_local * HEAD_DIM),
            value_grad.astype(jnp.bfloat16).reshape(tok_rows, kv_local * HEAD_DIM),
        ],
        1,
    )
    columns = local_rows
    summed = lax.psum_scatter(
        jnp.einsum("td,tc->dc", columns, both_grads, preferred_element_type=jnp.float32),
        ("dp", "context"),
        scatter_dimension=0,
        tiled=True,
    )
    width_kv = key_proj.shape[1]
    return (grad_queries, summed[:, :width_kv], summed[:, width_kv:])


def solution(mesh):
    placed = (
        P("dp", "context", None),
        P("dp", "context", "head"),
        P("dp", "context", "head"),
        P("dp", "context"),
        P(("dp", "context"), "head"),
        P(("dp", "context"), "head"),
    )
    return jax.shard_map(
        body,
        mesh=mesh,
        in_specs=placed,
        out_specs=(
            P("dp", "context", "head"),
            P(("dp", "context"), "head"),
            P(("dp", "context"), "head"),
        ),
        check_vma=False,
    )
```

profile of v0, /device:TPU:24, one launch (start us, length us, event | category | flops | bytes accessed | tf_op | source)
XLA Modules:
  0.0 1097.1 jit_solution(6544349401803940098)
XLA Ops:
  13.6 56.4 %all-reduce = bf16[3072]{0:T(1024)(128)(2,1)S(1)} all-reduce(bf16[3072]{0:T(1024)(128)(2,1)S(1)} %dynamic-update-slice), channel_id=2, replica_groups=mesh['dp'=4,'context'=16,'head'=8] {'context'}, use_global_device_ids=true, to_apply=%add | all-reduce | flops 3072 | bytes 12288
  71.4 62.2 %all-gather.6.cloned.1.call-done = bf16[4096,128]{1,0:T(8,128)(2,1)} async-done(((bf16[64,128]{1,0:T(8,128)(2,1)}), bf16[4096,128]{1,0:T(8,128)(2,1)}) %all-gather.6.cloned.1.call-update) | async-done | bytes 1048592 | tf_op jit(solution)/shard_map/all_gather | solution.py:28
  135.4 33.4 %all-gather.1 = bf16[3072,128]{1,0:T(8,128)(2,1)S(1)} all-gather(bf16[192,128]{1,0:T(8,128)(2,1)S(1)} %fusion.40), channel_id=3, replica_groups=mesh['dp'=4,'context'=16,'head'=8] {'context'}, dimensions={0}, use_global_device_ids=true | all-gather | bytes 835584 | tf_op jit(solution)/shard_map/all_gather | solution.py:51
  168.8 5.6 fusion.25
  174.4 76.5 %all-gather.8.cloned.1.call-done = bf16[4096,128]{1,0:T(8,128)(2,1)} async-done(((bf16[64,128]{1,0:T(8,128)(2,1)}), bf16[4096,128]{1,0:T(8,128)(2,1)}) %all-gather.8.cloned.1.call-update) | async-done | bytes 1048592 | tf_op jit(solution)/shard_map/all_gather | solution.py:29
  250.9 1.9 fusion.43
  252.8 33.5 %all-gather.2 = bf16[3072,128]{1,0:T(8,128)(2,1)S(1)} all-gather(bf16[192,128]{1,0:T(8,128)(2,1)S(1)} %fusion.43), channel_id=4, replica_groups=mesh['dp'=4,'context'=16,'head'=8] {'context'}, dimensions={0}, use_global_device_ids=true | all-gather | bytes 835584 | tf_op jit(solution)/shard_map/all_gather | solution.py:52
  286.3 6.5 fusion.27
  292.9 2.7 fusion.61
  295.6 346.3 %while.21 = (s32[]{:T(128)}, bf16[192,1,128]{2,0,1:T(8,128)(2,1)S(1)}, bf16[192,1,128]{2,0,1:T(8,128)(2,1)S(1)}, bf16[192]{0:T(256)(128)(2,1)S(1)}, f32[192,1,12...) while((s32[]{:T(128)}, ...), condition=%wide.region_4.5_spmd.clone, body=%wide.region_3.4_spmd.clone.sunk | while | flops 190328832 | bytes 6227287 | solution.py:108
  295.6 2.3 collective-permute-start
  299.8 1.9 collective-permute-start.2
  307.4 3.9 collective-permute-done.2
  311.3 4.1 collective-permute-done.3
  315.4 2.2 collective-permute-done.4
  321.5 1.9 collective-permute-start.2
  329.0 3.9 collective-permute-done.2
  332.9 4.1 collective-permute-done.3
  337.0 2.2 collective-permute-done.4
  350.6 3.9 collective-permute-done.2
  354.6 4.1 collective-permute-done.3
  358.6 2.2 collective-permute-done.4
  372.2 3.9 collective-permute-done.2
  376.2 4.1 collective-permute-done.3
  380.2 2.2 collective-permute-done.4
  393.9 3.9 collective-permute-done.2
  397.8 4.1 collective-permute-done.3
  401.8 2.2 collective-permute-done.4
  415.5 3.9 collective-permute-done.2
  419.4 4.1 collective-permute-done.3
  423.5 2.2 collective-permute-done.4
  437.1 3.9 collective-permute-done.2
  441.0 4.1 collective-permute-done.3
  445.1 2.2 collective-permute-done.4
  458.7 3.9 collective-permute-done.2
  462.6 4.1 collective-permute-done.3
  466.7 2.2 collective-permute-done.4
  480.3 3.9 collective-permute-done.2
  484.3 4.1 collective-permute-done.3
  488.3 2.2 collective-permute-done.4
  501.9 3.9 collective-permute-done.2
  505.9 4.1 collective-permute-done.3
  509.9 2.2 collective-permute-done.4
  523.6 3.9 collective-permute-done.2
  527.5 4.1 collective-permute-done.3
  531.6 2.2 collective-permute-done.4
  545.2 3.9 collective-permute-done.2
  549.1 4.1 collective-permute-done.3
  553.2 2.2 collective-permute-done.4
  566.8 3.9 collective-permute-done.2
  570.7 4.1 collective-permute-done.3
  574.8 2.2 collective-permute-done.4
  588.4 3.9 collective-permute-done.2
  592.4 4.1 collective-permute-done.3
  596.4 2.2 collective-permute-done.4
  610.0 3.9 collective-permute-done.2
  614.0 4.1 collective-permute-done.3
  618.0 2.2 collective-permute-done.4
  631.7 3.9 collective-permute-done.2
  635.6 4.1 collective-permute-done.3
  639.6 2.2 collective-permute-done.4
  641.9 2.7 convolution_bitcast_fusion.3
  644.6 5.6 copy.31
  651.2 438.0 %reduce-scatter.4.cloned.1.call-done = f32[64,256]{1,0:T(8,128)} async-done(((f32[4096,256]{1,0:T(8,128)}), f32[64,256]{1,0:T(8,128)}) %reduce-scatter.4.cloned.1.call-update) | async-done | bytes 65552
  (285 shorter events, 186.5 us)
Async XLA Ops:
  7.2 126.5 %all-gather.6.cloned.1.call-start = ((), (), s32[]{:S(2)}) async-start(), calls=%async_computation.1 | async-start | bytes 1064960 | tf_op jit(solution)/shard_map/all_gather | solution.py:28
  7.9 243.0 %all-gather.8.cloned.1.call-start = ((), (), s32[]{:S(2)}) async-start(), calls=%async_computation.2 | async-start | bytes 1064960 | tf_op jit(solution)/shard_map/all_gather | solution.py:29
  8.7 1080.6 %reduce-scatter.4.cloned.1.call-start = ((), (), s32[]{:S(2)}) async-start(), calls=%async_computation.3 | async-start | bytes 4259840
  295.6 15.7 %collective-permute-start = (bf16[192,1,128]{2,0,1:T(8,128)(2,1)S(1)}, bf16[192,1,128]{2,0,1:T(8,128)(2,1)S(1)}, u32[]{:S(2)}, u32[]{:S(2)}) collective-permute-start(bf16[192,1,128]{2,0,1:T(8,128)(2,1)S(1)} %copy.49), channel_id=1, source_target_pairs={{120,0},{0,8},{8,16},{16,24},{24,32},{32,40},{40,48},{48,56},{56,6... | collective-permute-start | bytes 147464 | tf_op jit(solution)/shard_map/while/body/eval_jaxpr/ppermute | solution.py:17
  297.9 13.4 %collective-permute-start.1 = (bf16[192,1,128]{2,0,1:T(8,128)(2,1)S(1)}, bf16[192,1,128]{2,0,1:T(8,128)(2,1)S(1)}, u32[]{:S(2)}, u32[]{:S(2)}) collective-permute-start(bf16[192,1,128]{2,0,1:T(8,128)(2,1)S(1)} %copy.50), channel_id=1, source_target_pairs={{120,0},{0,8},{8,16},{16,24},{24,32},{32,40},{40,48},{48,56},{56,6... | collective-permute-start | bytes 147464 | tf_op jit(solution)/shard_map/while/body/eval_jaxpr/ppermute | solution.py:17
  302.8 12.5 %collective-permute-start.3 = (f32[192,1,128]{2,0,1:T(8,128)S(1)}, f32[192,1,128]{2,0,1:T(8,128)S(1)}, u32[]{:S(2)}, u32[]{:S(2)}) collective-permute-start(f32[192,1,128]{2,0,1:T(8,128)S(1)} %fusion.107), channel_id=1, source_target_pairs={{120,0},{0,8},{8,16},{16,24},{24,32},{32,40},{40,48},{48,56},{56,6... | collective-permute-start | bytes 294920 | tf_op jit(solution)/shard_map/while/body/eval_jaxpr/ppermute | solution.py:17
  305.0 12.5 %collective-permute-start.4 = (f32[192,1,128]{2,0,1:T(8,128)S(1)}, f32[192,1,128]{2,0,1:T(8,128)S(1)}, u32[]{:S(2)}, u32[]{:S(2)}) collective-permute-start(f32[192,1,128]{2,0,1:T(8,128)S(1)} %fusion.108), channel_id=1, source_target_pairs={{120,0},{0,8},{8,16},{16,24},{24,32},{32,40},{40,48},{48,56},{56,6... | collective-permute-start | bytes 294920 | tf_op jit(solution)/shard_map/while/body/eval_jaxpr/ppermute | solution.py:17
  317.6 15.3 %collective-permute-start = (bf16[192,1,128]{2,0,1:T(8,128)(2,1)S(1)}, bf16[192,1,128]{2,0,1:T(8,128)(2,1)S(1)}, u32[]{:S(2)}, u32[]{:S(2)}) collective-permute-start(bf16[192,1,128]{2,0,1:T(8,128)(2,1)S(1)} %copy.49), channel_id=1, source_target_pairs={{120,0},{0,8},{8,16},{16,24},{24,32},{32,40},{40,48},{48,56},{56,6... | collective-permute-start | bytes 147464 | tf_op jit(solution)/shard_map/while/body/eval_jaxpr/ppermute | solution.py:17
  319.5 13.4 %collective-permute-start.1 = (bf16[192,1,128]{2,0,1:T(8,128)(2,1)S(1)}, bf16[192,1,128]{2,0,1:T(8,128)(2,1)S(1)}, u32[]{:S(2)}, u32[]{:S(2)}) collective-permute-start(bf16[192,1,128]{2,0,1:T(8,128)(2,1)S(1)} %copy.50), channel_id=1, source_target_pairs={{120,0},{0,8},{8,16},{16,24},{24,32},{32,40},{40,48},{48,56},{56,6... | collective-permute-start | bytes 147464 | tf_op jit(solution)/shard_map/while/body/eval_jaxpr/ppermute | solution.py:17
  324.4 12.5 %collective-permute-start.3 = (f32[192,1,128]{2,0,1:T(8,128)S(1)}, f32[192,1,128]{2,0,1:T(8,128)S(1)}, u32[]{:S(2)}, u32[]{:S(2)}) collective-permute-start(f32[192,1,128]{2,0,1:T(8,128)S(1)} %fusion.107), channel_id=1, source_target_pairs={{120,0},{0,8},{8,16},{16,24},{24,32},{32,40},{40,48},{48,56},{56,6... | collective-permute-start | bytes 294920 | tf_op jit(solution)/shard_map/while/body/eval_jaxpr/ppermute | solution.py:17
  326.7 12.5 %collective-permute-start.4 = (f32[192,1,128]{2,0,1:T(8,128)S(1)}, f32[192,1,128]{2,0,1:T(8,128)S(1)}, u32[]{:S(2)}, u32[]{:S(2)}) collective-permute-start(f32[192,1,128]{2,0,1:T(8,128)S(1)} %fusion.108), channel_id=1, source_target_pairs={{120,0},{0,8},{8,16},{16,24},{24,32},{32,40},{40,48},{48,56},{56,6... | collective-permute-start | bytes 294920 | tf_op jit(solution)/shard_map/while/body/eval_jaxpr/ppermute | solution.py:17
  339.2 15.3 %collective-permute-start = (bf16[192,1,128]{2,0,1:T(8,128)(2,1)S(1)}, bf16[192,1,128]{2,0,1:T(8,128)(2,1)S(1)}, u32[]{:S(2)}, u32[]{:S(2)}) collective-permute-start(bf16[192,1,128]{2,0,1:T(8,128)(2,1)S(1)} %copy.49), channel_id=1, source_target_pairs={{120,0},{0,8},{8,16},{16,24},{24,32},{32,40},{40,48},{48,56},{56,6... | collective-permute-start | bytes 147464 | tf_op jit(solution)/shard_map/while/body/eval_jaxpr/ppermute | solution.py:17
  341.1 13.4 %collective-permute-start.1 = (bf16[192,1,128]{2,0,1:T(8,128)(2,1)S(1)}, bf16[192,1,128]{2,0,1:T(8,128)(2,1)S(1)}, u32[]{:S(2)}, u32[]{:S(2)}) collective-permute-start(bf16[192,1,128]{2,0,1:T(8,128)(2,1)S(1)} %copy.50), channel_id=1, source_target_pairs={{120,0},{0,8},{8,16},{16,24},{24,32},{32,40},{40,48},{48,56},{56,6... | collective-permute-start | bytes 147464 | tf_op jit(solution)/shard_map/while/body/eval_jaxpr/ppermute | solution.py:17
  346.1 12.5 %collective-permute-start.3 = (f32[192,1,128]{2,0,1:T(8,128)S(1)}, f32[192,1,128]{2,0,1:T(8,128)S(1)}, u32[]{:S(2)}, u32[]{:S(2)}) collective-permute-start(f32[192,1,128]{2,0,1:T(8,128)S(1)} %fusion.107), channel_id=1, source_target_pairs={{120,0},{0,8},{8,16},{16,24},{24,32},{32,40},{40,48},{48,56},{56,6... | collective-permute-start | bytes 294920 | tf_op jit(solution)/shard_map/while/body/eval_jaxpr/ppermute | solution.py:17
  348.3 12.5 %collective-permute-start.4 = (f32[192,1,128]{2,0,1:T(8,128)S(1)}, f32[192,1,128]{2,0,1:T(8,128)S(1)}, u32[]{:S(2)}, u32[]{:S(2)}) collective-permute-start(f32[192,1,128]{2,0,1:T(8,128)S(1)} %fusion.108), channel_id=1, source_target_pairs={{120,0},{0,8},{8,16},{16,24},{24,32},{32,40},{40,48},{48,56},{56,6... | collective-permute-start | bytes 294920 | tf_op jit(solution)/shard_map/while/body/eval_jaxpr/ppermute | solution.py:17
  360.8 15.3 %collective-permute-start = (bf16[192,1,128]{2,0,1:T(8,128)(2,1)S(1)}, bf16[192,1,128]{2,0,1:T(8,128)(2,1)S(1)}, u32[]{:S(2)}, u32[]{:S(2)}) collective-permute-start(bf16[192,1,128]{2,0,1:T(8,128)(2,1)S(1)} %copy.49), channel_id=1, source_target_pairs={{120,0},{0,8},{8,16},{16,24},{24,32},{32,40},{40,48},{48,56},{56,6... | collective-permute-start | bytes 147464 | tf_op jit(solution)/shard_map/while/body/eval_jaxpr/ppermute | solution.py:17
  362.8 13.4 %collective-permute-start.1 = (bf16[192,1,128]{2,0,1:T(8,128)(2,1)S(1)}, bf16[192,1,128]{2,0,1:T(8,128)(2,1)S(1)}, u32[]{:S(2)}, u32[]{:S(2)}) collective-permute-start(bf16[192,1,128]{2,0,1:T(8,128)(2,1)S(1)} %copy.50), channel_id=1, source_target_pairs={{120,0},{0,8},{8,16},{16,24},{24,32},{32,40},{40,48},{48,56},{56,6... | collective-permute-start | bytes 147464 | tf_op jit(solution)/shard_map/while/body/eval_jaxpr/ppermute | solution.py:17
  367.7 12.5 %collective-permute-start.3 = (f32[192,1,128]{2,0,1:T(8,128)S(1)}, f32[192,1,128]{2,0,1:T(8,128)S(1)}, u32[]{:S(2)}, u32[]{:S(2)}) collective-permute-start(f32[192,1,128]{2,0,1:T(8,128)S(1)} %fusion.107), channel_id=1, source_target_pairs={{120,0},{0,8},{8,16},{16,24},{24,32},{32,40},{40,48},{48,56},{56,6... | collective-permute-start | bytes 294920 | tf_op jit(solution)/shard_map/while/body/eval_jaxpr/ppermute | solution.py:17
  369.9 12.5 %collective-permute-start.4 = (f32[192,1,128]{2,0,1:T(8,128)S(1)}, f32[192,1,128]{2,0,1:T(8,128)S(1)}, u32[]{:S(2)}, u32[]{:S(2)}) collective-permute-start(f32[192,1,128]{2,0,1:T(8,128)S(1)} %fusion.108), channel_id=1, source_target_pairs={{120,0},{0,8},{8,16},{16,24},{24,32},{32,40},{40,48},{48,56},{56,6... | collective-permute-start | bytes 294920 | tf_op jit(solution)/shard_map/while/body/eval_jaxpr/ppermute | solution.py:17
  382.4 15.3 %collective-permute-start = (bf16[192,1,128]{2,0,1:T(8,128)(2,1)S(1)}, bf16[192,1,128]{2,0,1:T(8,128)(2,1)S(1)}, u32[]{:S(2)}, u32[]{:S(2)}) collective-permute-start(bf16[192,1,128]{2,0,1:T(8,128)(2,1)S(1)} %copy.49), channel_id=1, source_target_pairs={{120,0},{0,8},{8,16},{16,24},{24,32},{32,40},{40,48},{48,56},{56,6... | collective-permute-start | bytes 147464 | tf_op jit(solution)/shard_map/while/body/eval_jaxpr/ppermute | solution.py:17
  384.4 13.4 %collective-permute-start.1 = (bf16[192,1,128]{2,0,1:T(8,128)(2,1)S(1)}, bf16[192,1,128]{2,0,1:T(8,128)(2,1)S(1)}, u32[]{:S(2)}, u32[]{:S(2)}) collective-permute-start(bf16[192,1,128]{2,0,1:T(8,128)(2,1)S(1)} %copy.50), channel_id=1, source_target_pairs={{120,0},{0,8},{8,16},{16,24},{24,32},{32,40},{40,48},{48,56},{56,6... | collective-permute-start | bytes 147464 | tf_op jit(solution)/shard_map/while/body/eval_jaxpr/ppermute | solution.py:17
  389.3 12.5 %collective-permute-start.3 = (f32[192,1,128]{2,0,1:T(8,128)S(1)}, f32[192,1,128]{2,0,1:T(8,128)S(1)}, u32[]{:S(2)}, u32[]{:S(2)}) collective-permute-start(f32[192,1,128]{2,0,1:T(8,128)S(1)} %fusion.107), channel_id=1, source_target_pairs={{120,0},{0,8},{8,16},{16,24},{24,32},{32,40},{40,48},{48,56},{56,6... | collective-permute-start | bytes 294920 | tf_op jit(solution)/shard_map/while/body/eval_jaxpr/ppermute | solution.py:17
  391.5 12.5 %collective-permute-start.4 = (f32[192,1,128]{2,0,1:T(8,128)S(1)}, f32[192,1,128]{2,0,1:T(8,128)S(1)}, u32[]{:S(2)}, u32[]{:S(2)}) collective-permute-start(f32[192,1,128]{2,0,1:T(8,128)S(1)} %fusion.108), channel_id=1, source_target_pairs={{120,0},{0,8},{8,16},{16,24},{24,32},{32,40},{40,48},{48,56},{56,6... | collective-permute-start | bytes 294920 | tf_op jit(solution)/shard_map/while/body/eval_jaxpr/ppermute | solution.py:17
  404.1 15.3 %collective-permute-start = (bf16[192,1,128]{2,0,1:T(8,128)(2,1)S(1)}, bf16[192,1,128]{2,0,1:T(8,128)(2,1)S(1)}, u32[]{:S(2)}, u32[]{:S(2)}) collective-permute-start(bf16[192,1,128]{2,0,1:T(8,128)(2,1)S(1)} %copy.49), channel_id=1, source_target_pairs={{120,0},{0,8},{8,16},{16,24},{24,32},{32,40},{40,48},{48,56},{56,6... | collective-permute-start | bytes 147464 | tf_op jit(solution)/shard_map/while/body/eval_jaxpr/ppermute | solution.py:17
  406.0 13.4 %collective-permute-start.1 = (bf16[192,1,128]{2,0,1:T(8,128)(2,1)S(1)}, bf16[192,1,128]{2,0,1:T(8,128)(2,1)S(1)}, u32[]{:S(2)}, u32[]{:S(2)}) collective-permute-start(bf16[192,1,128]{2,0,1:T(8,128)(2,1)S(1)} %copy.50), channel_id=1, source_target_pairs={{120,0},{0,8},{8,16},{16,24},{24,32},{32,40},{40,48},{48,56},{56,6... | collective-permute-start | bytes 147464 | tf_op jit(solution)/shard_map/while/body/eval_jaxpr/ppermute | solution.py:17
  410.9 12.5 %collective-permute-start.3 = (f32[192,1,128]{2,0,1:T(8,128)S(1)}, f32[192,1,128]{2,0,1:T(8,128)S(1)}, u32[]{:S(2)}, u32[]{:S(2)}) collective-permute-start(f32[192,1,128]{2,0,1:T(8,128)S(1)} %fusion.107), channel_id=1, source_target_pairs={{120,0},{0,8},{8,16},{16,24},{24,32},{32,40},{40,48},{48,56},{56,6... | collective-permute-start | bytes 294920 | tf_op jit(solution)/shard_map/while/body/eval_jaxpr/ppermute | solution.py:17
  413.1 12.5 %collective-permute-start.4 = (f32[192,1,128]{2,0,1:T(8,128)S(1)}, f32[192,1,128]{2,0,1:T(8,128)S(1)}, u32[]{:S(2)}, u32[]{:S(2)}) collective-permute-start(f32[192,1,128]{2,0,1:T(8,128)S(1)} %fusion.108), channel_id=1, source_target_pairs={{120,0},{0,8},{8,16},{16,24},{24,32},{32,40},{40,48},{48,56},{56,6... | collective-permute-start | bytes 294920 | tf_op jit(solution)/shard_map/while/body/eval_jaxpr/ppermute | solution.py:17
  425.7 15.3 %collective-permute-start = (bf16[192,1,128]{2,0,1:T(8,128)(2,1)S(1)}, bf16[192,1,128]{2,0,1:T(8,128)(2,1)S(1)}, u32[]{:S(2)}, u32[]{:S(2)}) collective-permute-start(bf16[192,1,128]{2,0,1:T(8,128)(2,1)S(1)} %copy.49), channel_id=1, source_target_pairs={{120,0},{0,8},{8,16},{16,24},{24,32},{32,40},{40,48},{48,56},{56,6... | collective-permute-start | bytes 147464 | tf_op jit(solution)/shard_map/while/body/eval_jaxpr/ppermute | solution.py:17
  427.6 13.4 %collective-permute-start.1 = (bf16[192,1,128]{2,0,1:T(8,128)(2,1)S(1)}, bf16[192,1,128]{2,0,1:T(8,128)(2,1)S(1)}, u32[]{:S(2)}, u32[]{:S(2)}) collective-permute-start(bf16[192,1,128]{2,0,1:T(8,128)(2,1)S(1)} %copy.50), channel_id=1, source_target_pairs={{120,0},{0,8},{8,16},{16,24},{24,32},{32,40},{40,48},{48,56},{56,6... | collective-permute-start | bytes 147464 | tf_op jit(solution)/shard_map/while/body/eval_jaxpr/ppermute | solution.py:17
  432.5 12.5 %collective-permute-start.3 = (f32[192,1,128]{2,0,1:T(8,128)S(1)}, f32[192,1,128]{2,0,1:T(8,128)S(1)}, u32[]{:S(2)}, u32[]{:S(2)}) collective-permute-start(f32[192,1,128]{2,0,1:T(8,128)S(1)} %fusion.107), channel_id=1, source_target_pairs={{120,0},{0,8},{8,16},{16,24},{24,32},{32,40},{40,48},{48,56},{56,6... | collective-permute-start | bytes 294920 | tf_op jit(solution)/shard_map/while/body/eval_jaxpr/ppermute | solution.py:17
  434.8 12.5 %collective-permute-start.4 = (f32[192,1,128]{2,0,1:T(8,128)S(1)}, f32[192,1,128]{2,0,1:T(8,128)S(1)}, u32[]{:S(2)}, u32[]{:S(2)}) collective-permute-start(f32[192,1,128]{2,0,1:T(8,128)S(1)} %fusion.108), channel_id=1, source_target_pairs={{120,0},{0,8},{8,16},{16,24},{24,32},{32,40},{40,48},{48,56},{56,6... | collective-permute-start | bytes 294920 | tf_op jit(solution)/shard_map/while/body/eval_jaxpr/ppermute | solution.py:17
  447.3 15.3 %collective-permute-start = (bf16[192,1,128]{2,0,1:T(8,128)(2,1)S(1)}, bf16[192,1,128]{2,0,1:T(8,128)(2,1)S(1)}, u32[]{:S(2)}, u32[]{:S(2)}) collective-permute-start(bf16[192,1,128]{2,0,1:T(8,128)(2,1)S(1)} %copy.49), channel_id=1, source_target_pairs={{120,0},{0,8},{8,16},{16,24},{24,32},{32,40},{40,48},{48,56},{56,6... | collective-permute-start | bytes 147464 | tf_op jit(solution)/shard_map/while/body/eval_jaxpr/ppermute | solution.py:17
  449.2 13.4 %collective-permute-start.1 = (bf16[192,1,128]{2,0,1:T(8,128)(2,1)S(1)}, bf16[192,1,128]{2,0,1:T(8,128)(2,1)S(1)}, u32[]{:S(2)}, u32[]{:S(2)}) collective-permute-start(bf16[192,1,128]{2,0,1:T(8,128)(2,1)S(1)} %copy.50), channel_id=1, source_target_pairs={{120,0},{0,8},{8,16},{16,24},{24,32},{32,40},{40,48},{48,56},{56,6... | collective-permute-start | bytes 147464 | tf_op jit(solution)/shard_map/while/body/eval_jaxpr/ppermute | solution.py:17
  454.2 12.5 %collective-permute-start.3 = (f32[192,1,128]{2,0,1:T(8,128)S(1)}, f32[192,1,128]{2,0,1:T(8,128)S(1)}, u32[]{:S(2)}, u32[]{:S(2)}) collective-permute-start(f32[192,1,128]{2,0,1:T(8,128)S(1)} %fusion.107), channel_id=1, source_target_pairs={{120,0},{0,8},{8,16},{16,24},{24,32},{32,40},{40,48},{48,56},{56,6... | collective-permute-start | bytes 294920 | tf_op jit(solution)/shard_map/while/body/eval_jaxpr/ppermute | solution.py:17
  456.4 12.5 %collective-permute-start.4 = (f32[192,1,128]{2,0,1:T(8,128)S(1)}, f32[192,1,128]{2,0,1:T(8,128)S(1)}, u32[]{:S(2)}, u32[]{:S(2)}) collective-permute-start(f32[192,1,128]{2,0,1:T(8,128)S(1)} %fusion.108), channel_id=1, source_target_pairs={{120,0},{0,8},{8,16},{16,24},{24,32},{32,40},{40,48},{48,56},{56,6... | collective-permute-start | bytes 294920 | tf_op jit(solution)/shard_map/while/body/eval_jaxpr/ppermute | solution.py:17
  468.9 15.3 %collective-permute-start = (bf16[192,1,128]{2,0,1:T(8,128)(2,1)S(1)}, bf16[192,1,128]{2,0,1:T(8,128)(2,1)S(1)}, u32[]{:S(2)}, u32[]{:S(2)}) collective-permute-start(bf16[192,1,128]{2,0,1:T(8,128)(2,1)S(1)} %copy.49), channel_id=1, source_target_pairs={{120,0},{0,8},{8,16},{16,24},{24,32},{32,40},{40,48},{48,56},{56,6... | collective-permute-start | bytes 147464 | tf_op jit(solution)/shard_map/while/body/eval_jaxpr/ppermute | solution.py:17
  470.9 13.4 %collective-permute-start.1 = (bf16[192,1,128]{2,0,1:T(8,128)(2,1)S(1)}, bf16[192,1,128]{2,0,1:T(8,128)(2,1)S(1)}, u32[]{:S(2)}, u32[]{:S(2)}) collective-permute-start(bf16[192,1,128]{2,0,1:T(8,128)(2,1)S(1)} %copy.50), channel_id=1, source_target_pairs={{120,0},{0,8},{8,16},{16,24},{24,32},{32,40},{40,48},{48,56},{56,6... | collective-permute-start | bytes 147464 | tf_op jit(solution)/shard_map/while/body/eval_jaxpr/ppermute | solution.py:17
  475.8 12.5 %collective-permute-start.3 = (f32[192,1,128]{2,0,1:T(8,128)S(1)}, f32[192,1,128]{2,0,1:T(8,128)S(1)}, u32[]{:S(2)}, u32[]{:S(2)}) collective-permute-start(f32[192,1,128]{2,0,1:T(8,128)S(1)} %fusion.107), channel_id=1, source_target_pairs={{120,0},{0,8},{8,16},{16,24},{24,32},{32,40},{40,48},{48,56},{56,6... | collective-permute-start | bytes 294920 | tf_op jit(solution)/shard_map/while/body/eval_jaxpr/ppermute | solution.py:17
  478.0 12.5 %collective-permute-start.4 = (f32[192,1,128]{2,0,1:T(8,128)S(1)}, f32[192,1,128]{2,0,1:T(8,128)S(1)}, u32[]{:S(2)}, u32[]{:S(2)}) collective-permute-start(f32[192,1,128]{2,0,1:T(8,128)S(1)} %fusion.108), channel_id=1, source_target_pairs={{120,0},{0,8},{8,16},{16,24},{24,32},{32,40},{40,48},{48,56},{56,6... | collective-permute-start | bytes 294920 | tf_op jit(solution)/shard_map/while/body/eval_jaxpr/ppermute | solution.py:17
  490.5 15.3 %collective-permute-start = (bf16[192,1,128]{2,0,1:T(8,128)(2,1)S(1)}, bf16[192,1,128]{2,0,1:T(8,128)(2,1)S(1)}, u32[]{:S(2)}, u32[]{:S(2)}) collective-permute-start(bf16[192,1,128]{2,0,1:T(8,128)(2,1)S(1)} %copy.49), channel_id=1, source_target_pairs={{120,0},{0,8},{8,16},{16,24},{24,32},{32,40},{40,48},{48,56},{56,6... | collective-permute-start | bytes 147464 | tf_op jit(solution)/shard_map/while/body/eval_jaxpr/ppermute | solution.py:17
  492.5 13.4 %collective-permute-start.1 = (bf16[192,1,128]{2,0,1:T(8,128)(2,1)S(1)}, bf16[192,1,128]{2,0,1:T(8,128)(2,1)S(1)}, u32[]{:S(2)}, u32[]{:S(2)}) collective-permute-start(bf16[192,1,128]{2,0,1:T(8,128)(2,1)S(1)} %copy.50), channel_id=1, source_target_pairs={{120,0},{0,8},{8,16},{16,24},{24,32},{32,40},{40,48},{48,56},{56,6... | collective-permute-start | bytes 147464 | tf_op jit(solution)/shard_map/while/body/eval_jaxpr/ppermute | solution.py:17
  497.4 12.5 %collective-permute-start.3 = (f32[192,1,128]{2,0,1:T(8,128)S(1)}, f32[192,1,128]{2,0,1:T(8,128)S(1)}, u32[]{:S(2)}, u32[]{:S(2)}) collective-permute-start(f32[192,1,128]{2,0,1:T(8,128)S(1)} %fusion.107), channel_id=1, source_target_pairs={{120,0},{0,8},{8,16},{16,24},{24,32},{32,40},{40,48},{48,56},{56,6... | collective-permute-start | bytes 294920 | tf_op jit(solution)/shard_map/while/body/eval_jaxpr/ppermute | solution.py:17
  499.6 12.5 %collective-permute-start.4 = (f32[192,1,128]{2,0,1:T(8,128)S(1)}, f32[192,1,128]{2,0,1:T(8,128)S(1)}, u32[]{:S(2)}, u32[]{:S(2)}) collective-permute-start(f32[192,1,128]{2,0,1:T(8,128)S(1)} %fusion.108), channel_id=1, source_target_pairs={{120,0},{0,8},{8,16},{16,24},{24,32},{32,40},{40,48},{48,56},{56,6... | collective-permute-start | bytes 294920 | tf_op jit(solution)/shard_map/while/body/eval_jaxpr/ppermute | solution.py:17
  512.2 15.3 %collective-permute-start = (bf16[192,1,128]{2,0,1:T(8,128)(2,1)S(1)}, bf16[192,1,128]{2,0,1:T(8,128)(2,1)S(1)}, u32[]{:S(2)}, u32[]{:S(2)}) collective-permute-start(bf16[192,1,128]{2,0,1:T(8,128)(2,1)S(1)} %copy.49), channel_id=1, source_target_pairs={{120,0},{0,8},{8,16},{16,24},{24,32},{32,40},{40,48},{48,56},{56,6... | collective-permute-start | bytes 147464 | tf_op jit(solution)/shard_map/while/body/eval_jaxpr/ppermute | solution.py:17
  514.1 13.4 %collective-permute-start.1 = (bf16[192,1,128]{2,0,1:T(8,128)(2,1)S(1)}, bf16[192,1,128]{2,0,1:T(8,128)(2,1)S(1)}, u32[]{:S(2)}, u32[]{:S(2)}) collective-permute-start(bf16[192,1,128]{2,0,1:T(8,128)(2,1)S(1)} %copy.50), channel_id=1, source_target_pairs={{120,0},{0,8},{8,16},{16,24},{24,32},{32,40},{40,48},{48,56},{56,6... | collective-permute-start | bytes 147464 | tf_op jit(solution)/shard_map/while/body/eval_jaxpr/ppermute | solution.py:17
  519.0 12.5 %collective-permute-start.3 = (f32[192,1,128]{2,0,1:T(8,128)S(1)}, f32[192,1,128]{2,0,1:T(8,128)S(1)}, u32[]{:S(2)}, u32[]{:S(2)}) collective-permute-start(f32[192,1,128]{2,0,1:T(8,128)S(1)} %fusion.107), channel_id=1, source_target_pairs={{120,0},{0,8},{8,16},{16,24},{24,32},{32,40},{40,48},{48,56},{56,6... | collective-permute-start | bytes 294920 | tf_op jit(solution)/shard_map/while/body/eval_jaxpr/ppermute | solution.py:17
  521.2 12.5 %collective-permute-start.4 = (f32[192,1,128]{2,0,1:T(8,128)S(1)}, f32[192,1,128]{2,0,1:T(8,128)S(1)}, u32[]{:S(2)}, u32[]{:S(2)}) collective-permute-start(f32[192,1,128]{2,0,1:T(8,128)S(1)} %fusion.108), channel_id=1, source_target_pairs={{120,0},{0,8},{8,16},{16,24},{24,32},{32,40},{40,48},{48,56},{56,6... | collective-permute-start | bytes 294920 | tf_op jit(solution)/shard_map/while/body/eval_jaxpr/ppermute | solution.py:17
  533.8 15.3 %collective-permute-start = (bf16[192,1,128]{2,0,1:T(8,128)(2,1)S(1)}, bf16[192,1,128]{2,0,1:T(8,128)(2,1)S(1)}, u32[]{:S(2)}, u32[]{:S(2)}) collective-permute-start(bf16[192,1,128]{2,0,1:T(8,128)(2,1)S(1)} %copy.49), channel_id=1, source_target_pairs={{120,0},{0,8},{8,16},{16,24},{24,32},{32,40},{40,48},{48,56},{56,6... | collective-permute-start | bytes 147464 | tf_op jit(solution)/shard_map/while/body/eval_jaxpr/ppermute | solution.py:17
  535.7 13.4 %collective-permute-start.1 = (bf16[192,1,128]{2,0,1:T(8,128)(2,1)S(1)}, bf16[192,1,128]{2,0,1:T(8,128)(2,1)S(1)}, u32[]{:S(2)}, u32[]{:S(2)}) collective-permute-start(bf16[192,1,128]{2,0,1:T(8,128)(2,1)S(1)} %copy.50), channel_id=1, source_target_pairs={{120,0},{0,8},{8,16},{16,24},{24,32},{32,40},{40,48},{48,56},{56,6... | collective-permute-start | bytes 147464 | tf_op jit(solution)/shard_map/while/body/eval_jaxpr/ppermute | solution.py:17
  540.6 12.5 %collective-permute-start.3 = (f32[192,1,128]{2,0,1:T(8,128)S(1)}, f32[192,1,128]{2,0,1:T(8,128)S(1)}, u32[]{:S(2)}, u32[]{:S(2)}) collective-permute-start(f32[192,1,128]{2,0,1:T(8,128)S(1)} %fusion.107), channel_id=1, source_target_pairs={{120,0},{0,8},{8,16},{16,24},{24,32},{32,40},{40,48},{48,56},{56,6... | collective-permute-start | bytes 294920 | tf_op jit(solution)/shard_map/while/body/eval_jaxpr/ppermute | solution.py:17
  542.9 12.5 %collective-permute-start.4 = (f32[192,1,128]{2,0,1:T(8,128)S(1)}, f32[192,1,128]{2,0,1:T(8,128)S(1)}, u32[]{:S(2)}, u32[]{:S(2)}) collective-permute-start(f32[192,1,128]{2,0,1:T(8,128)S(1)} %fusion.108), channel_id=1, source_target_pairs={{120,0},{0,8},{8,16},{16,24},{24,32},{32,40},{40,48},{48,56},{56,6... | collective-permute-start | bytes 294920 | tf_op jit(solution)/shard_map/while/body/eval_jaxpr/ppermute | solution.py:17
  555.4 15.3 %collective-permute-start = (bf16[192,1,128]{2,0,1:T(8,128)(2,1)S(1)}, bf16[192,1,128]{2,0,1:T(8,128)(2,1)S(1)}, u32[]{:S(2)}, u32[]{:S(2)}) collective-permute-start(bf16[192,1,128]{2,0,1:T(8,128)(2,1)S(1)} %copy.49), channel_id=1, source_target_pairs={{120,0},{0,8},{8,16},{16,24},{24,32},{32,40},{40,48},{48,56},{56,6... | collective-permute-start | bytes 147464 | tf_op jit(solution)/shard_map/while/body/eval_jaxpr/ppermute | solution.py:17
  557.3 13.4 %collective-permute-start.1 = (bf16[192,1,128]{2,0,1:T(8,128)(2,1)S(1)}, bf16[192,1,128]{2,0,1:T(8,128)(2,1)S(1)}, u32[]{:S(2)}, u32[]{:S(2)}) collective-permute-start(bf16[192,1,128]{2,0,1:T(8,128)(2,1)S(1)} %copy.50), channel_id=1, source_target_pairs={{120,0},{0,8},{8,16},{16,24},{24,32},{32,40},{40,48},{48,56},{56,6... | collective-permute-start | bytes 147464 | tf_op jit(solution)/shard_map/while/body/eval_jaxpr/ppermute | solution.py:17
  562.3 12.5 %collective-permute-start.3 = (f32[192,1,128]{2,0,1:T(8,128)S(1)}, f32[192,1,128]{2,0,1:T(8,128)S(1)}, u32[]{:S(2)}, u32[]{:S(2)}) collective-permute-start(f32[192,1,128]{2,0,1:T(8,128)S(1)} %fusion.107), channel_id=1, source_target_pairs={{120,0},{0,8},{8,16},{16,24},{24,32},{32,40},{40,48},{48,56},{56,6... | collective-permute-start | bytes 294920 | tf_op jit(solution)/shard_map/while/body/eval_jaxpr/ppermute | solution.py:17
  577.0 15.3 %collective-permute-start = (bf16[192,1,128]{2,0,1:T(8,128)(2,1)S(1)}, bf16[192,1,128]{2,0,1:T(8,128)(2,1)S(1)}, u32[]{:S(2)}, u32[]{:S(2)}) collective-permute-start(bf16[192,1,128]{2,0,1:T(8,128)(2,1)S(1)} %copy.49), channel_id=1, source_target_pairs={{120,0},{0,8},{8,16},{16,24},{24,32},{32,40},{40,48},{48,56},{56,6... | collective-permute-start | bytes 147464 | tf_op jit(solution)/shard_map/while/body/eval_jaxpr/ppermute | solution.py:17
  578.9 13.4 %collective-permute-start.1 = (bf16[192,1,128]{2,0,1:T(8,128)(2,1)S(1)}, bf16[192,1,128]{2,0,1:T(8,128)(2,1)S(1)}, u32[]{:S(2)}, u32[]{:S(2)}) collective-permute-start(bf16[192,1,128]{2,0,1:T(8,128)(2,1)S(1)} %copy.50), channel_id=1, source_target_pairs={{120,0},{0,8},{8,16},{16,24},{24,32},{32,40},{40,48},{48,56},{56,6... | collective-permute-start | bytes 147464 | tf_op jit(solution)/shard_map/while/body/eval_jaxpr/ppermute | solution.py:17
  598.6 15.3 %collective-permute-start = (bf16[192,1,128]{2,0,1:T(8,128)(2,1)S(1)}, bf16[192,1,128]{2,0,1:T(8,128)(2,1)S(1)}, u32[]{:S(2)}, u32[]{:S(2)}) collective-permute-start(bf16[192,1,128]{2,0,1:T(8,128)(2,1)S(1)} %copy.49), channel_id=1, source_target_pairs={{120,0},{0,8},{8,16},{16,24},{24,32},{32,40},{40,48},{48,56},{56,6... | collective-permute-start | bytes 147464 | tf_op jit(solution)/shard_map/while/body/eval_jaxpr/ppermute | solution.py:17
  600.6 13.4 %collective-permute-start.1 = (bf16[192,1,128]{2,0,1:T(8,128)(2,1)S(1)}, bf16[192,1,128]{2,0,1:T(8,128)(2,1)S(1)}, u32[]{:S(2)}, u32[]{:S(2)}) collective-permute-start(bf16[192,1,128]{2,0,1:T(8,128)(2,1)S(1)} %copy.50), channel_id=1, source_target_pairs={{120,0},{0,8},{8,16},{16,24},{24,32},{32,40},{40,48},{48,56},{56,6... | collective-permute-start | bytes 147464 | tf_op jit(solution)/shard_map/while/body/eval_jaxpr/ppermute | solution.py:17
  605.5 12.5 %collective-permute-start.3 = (f32[192,1,128]{2,0,1:T(8,128)S(1)}, f32[192,1,128]{2,0,1:T(8,128)S(1)}, u32[]{:S(2)}, u32[]{:S(2)}) collective-permute-start(f32[192,1,128]{2,0,1:T(8,128)S(1)} %fusion.107), channel_id=1, source_target_pairs={{120,0},{0,8},{8,16},{16,24},{24,32},{32,40},{40,48},{48,56},{56,6... | collective-permute-start | bytes 294920 | tf_op jit(solution)/shard_map/while/body/eval_jaxpr/ppermute | solution.py:17
  607.7 12.5 %collective-permute-start.4 = (f32[192,1,128]{2,0,1:T(8,128)S(1)}, f32[192,1,128]{2,0,1:T(8,128)S(1)}, u32[]{:S(2)}, u32[]{:S(2)}) collective-permute-start(f32[192,1,128]{2,0,1:T(8,128)S(1)} %fusion.108), channel_id=1, source_target_pairs={{120,0},{0,8},{8,16},{16,24},{24,32},{32,40},{40,48},{48,56},{56,6... | collective-permute-start | bytes 294920 | tf_op jit(solution)/shard_map/while/body/eval_jaxpr/ppermute | solution.py:17
  620.3 15.3 %collective-permute-start = (bf16[192,1,128]{2,0,1:T(8,128)(2,1)S(1)}, bf16[192,1,128]{2,0,1:T(8,128)(2,1)S(1)}, u32[]{:S(2)}, u32[]{:S(2)}) collective-permute-start(bf16[192,1,128]{2,0,1:T(8,128)(2,1)S(1)} %copy.49), channel_id=1, source_target_pairs={{120,0},{0,8},{8,16},{16,24},{24,32},{32,40},{40,48},{48,56},{56,6... | collective-permute-start | bytes 147464 | tf_op jit(solution)/shard_map/while/body/eval_jaxpr/ppermute | solution.py:17
  622.2 13.4 %collective-permute-start.1 = (bf16[192,1,128]{2,0,1:T(8,128)(2,1)S(1)}, bf16[192,1,128]{2,0,1:T(8,128)(2,1)S(1)}, u32[]{:S(2)}, u32[]{:S(2)}) collective-permute-start(bf16[192,1,128]{2,0,1:T(8,128)(2,1)S(1)} %copy.50), channel_id=1, source_target_pairs={{120,0},{0,8},{8,16},{16,24},{24,32},{32,40},{40,48},{48,56},{56,6... | collective-permute-start | bytes 147464 | tf_op jit(solution)/shard_map/while/body/eval_jaxpr/ppermute | solution.py:17
  627.1 12.5 %collective-permute-start.3 = (f32[192,1,128]{2,0,1:T(8,128)S(1)}, f32[192,1,128]{2,0,1:T(8,128)S(1)}, u32[]{:S(2)}, u32[]{:S(2)}) collective-permute-start(f32[192,1,128]{2,0,1:T(8,128)S(1)} %fusion.107), channel_id=1, source_target_pairs={{120,0},{0,8},{8,16},{16,24},{24,32},{32,40},{40,48},{48,56},{56,6... | collective-permute-start | bytes 294920 | tf_op jit(solution)/shard_map/while/body/eval_jaxpr/ppermute | solution.py:17
  629.3 12.5 %collective-permute-start.4 = (f32[192,1,128]{2,0,1:T(8,128)S(1)}, f32[192,1,128]{2,0,1:T(8,128)S(1)}, u32[]{:S(2)}, u32[]{:S(2)}) collective-permute-start(f32[192,1,128]{2,0,1:T(8,128)S(1)} %fusion.108), channel_id=1, source_target_pairs={{120,0},{0,8},{8,16},{16,24},{24,32},{32,40},{40,48},{48,56},{56,6... | collective-permute-start | bytes 294920 | tf_op jit(solution)/shard_map/while/body/eval_jaxpr/ppermute | solution.py:17
  (21 other events, 389.6 us)
Sparse Core Ops, SparseCore 0:
  10.2 123.4 all-gather.5
  135.8 115.0 all-gather.7
  650.3 438.8 reduce-scatter.3
where the time goes:
time: 1100 us
  waiting for transfers between devices  741 us (67%)
  starting transfers between devices  154 us (14%)
  blocking collectives  123 us (11%)
  matrix products  40.3 us (4%)
  between operations  14.5 us (1%)
  local copies, waits for them, and re-layouts  12.7 us (1%)
    unnamed x4, waiting for transfers between devices  439 us
    ppermute x80, waiting for transfers between devices, passed_along(): return lax.ppermute(block, axis, route)  163 us
    ppermute x80, starting transfers between devices, passed_along(): return lax.ppermute(block, axis, route)  154 us
    all_gather x1, waiting for transfers between devices, body(): lax.all_gather(value_proj, ('dp', 'context'), axis=0, tiled=True)  76.5 us
    all_gather x1, waiting for transfers between devices, body(): lax.all_gather(key_proj, ('dp', 'context'), axis=0, tiled=True)  62.2 us
    unnamed x1, blocking collectives  56.4 us
    all_gather x1, blocking collectives, body(): lax.all_gather(values, 'context', axis=0, tiled=True)  33.5 us
    all_gather x1, blocking collectives, body(): lax.all_gather(keys, 'context', axis=0, tiled=True)  33.4 us
  transfers between devices with their start and end apart: 83, of which 51 were waited for; matrix products, arithmetic and copies ran while one was open for 4% of the time, Pallas kernels for 0%

commit v1 on v0

v1 whole, which is shorter than its diff:
```python
import jax
import jax.numpy as jnp
from jax import lax
from jax.sharding import PartitionSpec as P

HEADS = 32
KV_HEADS = 8
HEAD_DIM = 128


far_below = -1e30


def _bits(n):
    return n.bit_length() - 1


def _exchange(x, axis, size, bit):
    perm = [(i, i ^ (1 << bit)) for i in range(size)]
    return lax.ppermute(x, axis, perm)


def _my_bit(axis, bit):
    return ((lax.axis_index(axis) >> bit) & 1) == 1


def gather_blocks(x, steps, canon):
    cur = x
    dims = []
    for axis, size, bit in steps:
        recv = _exchange(cur, axis, size, bit)
        mine = _my_bit(axis, bit)
        cur = jnp.where(mine, jnp.stack([recv, cur]), jnp.stack([cur, recv]))
        dims.insert(0, (axis, bit))
    order = [dims.index(c) for c in canon]
    cur = jnp.transpose(cur, order + list(range(len(dims), cur.ndim)))
    return cur.reshape((-1,) + x.shape[1:])


def scatter_sum(x, steps, canon):
    nb = len(canon)
    block = x.shape[0] >> nb
    cur = x.reshape((2,) * nb + (block,) + x.shape[1:])
    dims = list(canon)
    for axis, size, bit in steps:
        at = dims.index((axis, bit))
        lo = lax.index_in_dim(cur, 0, at, keepdims=False)
        hi = lax.index_in_dim(cur, 1, at, keepdims=False)
        mine = _my_bit(axis, bit)
        keep = jnp.where(mine, hi, lo)
        send = jnp.where(mine, lo, hi)
        cur = keep + _exchange(send, axis, size, bit)
        dims.pop(at)
    return cur


def body(hidden, queries, grad_out, segment, key_proj, value_proj):
    tok_rows = hidden.shape[1]
    n_dp = lax.axis_size("dp")
    n_ctx = lax.axis_size("context")
    group = HEADS // KV_HEADS
    scale = HEAD_DIM ** (-0.5)
    width_kv = key_proj.shape[1]
    local_rows = hidden[0]

    ctx_canon = [("context", b) for b in reversed(range(_bits(n_ctx)))]
    dp_canon = [("dp", b) for b in reversed(range(_bits(n_dp)))]
    both_canon = dp_canon + ctx_canon

    def step(axis, bit):
        return (axis, n_dp if axis == "dp" else n_ctx, bit)

    far_first = [step(a, b) for a, b in both_canon[::-1]]
    far_first = sorted(far_first, key=lambda s: (-(s[2] + (1 if s[0] == "dp" else 0))))
    near_first = far_first[::-1]

    proj = jnp.concatenate([key_proj, value_proj], axis=1)
    proj_all = gather_blocks(proj, far_first, both_canon)
    kv = jnp.dot(local_rows, proj_all, preferred_element_type=jnp.float32).astype(jnp.bfloat16)
    marks_col = jnp.broadcast_to(segment[0].astype(jnp.bfloat16)[:, None], (tok_rows, 128))
    kvm = jnp.concatenate([kv, marks_col], axis=1)
    ctx_far_first = [step("context", b) for b in reversed(range(_bits(n_ctx)))]
    kvm_all = gather_blocks(kvm, ctx_far_first, ctx_canon)
    keys = kvm_all[:, :HEAD_DIM]
    values = kvm_all[:, HEAD_DIM:2 * HEAD_DIM]
    marks_all = kvm_all[:, 2 * HEAD_DIM]
    marks = segment[0].astype(jnp.bfloat16)

    q = queries[0].reshape(tok_rows, group, HEAD_DIM)
    do = grad_out[0].reshape(tok_rows, group, HEAD_DIM)
    same = (marks[:, None] == marks_all[None, :])[:, None, :]
    raw = jnp.einsum("qgd,kd->qgk", q, keys, preferred_element_type=jnp.float32) * scale
    raw = jnp.where(same, raw, far_below)
    top = jnp.max(raw, axis=-1)
    total = jnp.sum(jnp.where(same, jnp.exp(raw - top[..., None]), 0.0), axis=-1)
    log_total = top + jnp.log(total)
    probs = jnp.where(same, jnp.exp(raw - log_total[..., None]), 0.0)
    probs_b = probs.astype(jnp.bfloat16)
    output = jnp.einsum("qgk,kd->qgd", probs_b, values, preferred_element_type=jnp.float32).astype(
        jnp.bfloat16
    )
    delta = jnp.sum(do.astype(jnp.float32) * output.astype(jnp.float32), axis=-1)
    value_part = jnp.einsum("qgk,qgd->kd", probs_b, do, preferred_element_type=jnp.float32)
    prob_grad = jnp.einsum("qgd,kd->qgk", do, values, preferred_element_type=jnp.float32)
    dscores = (probs * (prob_grad - delta[..., None])).astype(jnp.bfloat16)
    grad_q = (
        jnp.einsum("qgk,kd->qgd", dscores, keys, preferred_element_type=jnp.float32) * scale
    ).astype(jnp.bfloat16)
    key_part = jnp.einsum("qgk,qgd->kd", dscores, q, preferred_element_type=jnp.float32) * scale

    kv_part = jnp.concatenate([key_part, value_part], axis=1)
    ctx_near_first = ctx_far_first[::-1]
    kv_grad = scatter_sum(kv_part, ctx_near_first, ctx_canon).astype(jnp.bfloat16)

    proj_part = jnp.einsum("td,tc->dc", local_rows, kv_grad, preferred_element_type=jnp.float32)
    summed = scatter_sum(proj_part, near_first, both_canon)
    grad_queries = grad_q.reshape(1, tok_rows, group * HEAD_DIM)
    return (grad_queries, summed[:, :width_kv], summed[:, width_kv:])


def solution(mesh):
    placed = (
        P("dp", "context", None),
        P("dp", "context", "head"),
        P("dp", "context", "head"),
        P("dp", "context"),
        P(("dp", "context"), "head"),
        P(("dp", "context"), "head"),
    )
    return jax.shard_map(
        body,
        mesh=mesh,
        in_specs=placed,
        out_specs=(
            P("dp", "context", "head"),
            P(("dp", "context"), "head"),
            P(("dp", "context"), "head"),
        ),
        check_vma=False,
    )
```

time: 1100 us -> 315 us (0.29)
  waiting for transfers between devices: 741 us -> 190 us
  blocking collectives: 123 us -> 0 us
  starting transfers between devices: 154 us -> 69.3 us
  matrix products: 40.3 us -> 18.5 us
  between operations: 14.5 us -> 1.29 us
    unnamed x4 -> x0, waiting for transfers between devices: 439 us -> none
    all_gather x2 -> x0, waiting for transfers between devices: 139 us -> none  [the longest x1 76.5 us: body(): lax.all_gather(value_proj, ('dp', 'context'), axis=0, tiled=True)]
    ppermute x80 -> x20, starting transfers between devices: 154 us -> 69.3 us  [_exchange(): return lax.ppermute(x, axis, perm)]
    all_gather x2 -> x0, blocking collectives: 66.9 us -> none  [the longest x1 33.5 us: body(): lax.all_gather(values, 'context', axis=0, tiled=True)]
    unnamed x1 -> x0, blocking collectives: 56.4 us -> none
    ppermute x80 -> x20, waiting for transfers between devices: 163 us -> 190 us  [_exchange(): return lax.ppermute(x, axis, perm)]
    dot_general x85 -> x8, matrix products: 40.3 us -> 18.5 us  [the longest x1 3.87 us: body(): jnp.einsum('qgd,kd->qgk', do, values, preferred_element_type=jnp.float32)]
  transfers between devices with their start and end apart: 83 -> 20, of which waited for: 51 -> 20; matrix products, arithmetic and copies ran while one was open for 4% -> 1% of each run, Pallas kernels for 0% -> 0%
where the time goes in v1:
time: 315 us; the launch traced here: 313 us
  waiting for transfers between devices  190 us (60%)
  starting transfers between devices  69.3 us (22%)
  other arithmetic  18.8 us (6%)
  matrix products  18.5 us (6%)
  local copies, waits for them, and re-layouts  15.8 us (5%)
    ppermute x20, waiting for transfers between devices, _exchange(): return lax.ppermute(x, axis, perm)  190 us
    ppermute x20, starting transfers between devices, _exchange(): return lax.ppermute(x, axis, perm)  69.3 us
  transfers between devices with their start and end apart: 20, of which 20 were waited for; matrix products, arithmetic and copies ran while one was open for 1% of the time, Pallas kernels for 0%

profile of v1, /device:TPU:24, one launch (start us, length us, event | category | flops | bytes accessed | tf_op | source)
XLA Modules:
  0.0 313.3 jit_solution(2527266200159055053)
XLA Ops:
  0.6 0.8 constant_dynamic-update-slice_fusion.1
  1.5 0.7 constant_dynamic-update-slice_fusion
  2.2 9.1 %collective-permute-start = (bf16[64,256]{1,0:T(8,128)(2,1)S(1)}, bf16[64,256]{1,0:T(8,128)(2,1)S(1)}, u32[]{:S(2)}, u32[]{:S(2)}) collective-permute-start(bf16[64,256]{1,0:T(8,128)(2,1)S(1)} %constant_dynamic-update-slice_fusion), channel_id=1, source_target_pairs={{0,64},{8,72},{16,80},{24,88},{32,96},{40,104},{48,112},{56,120},{... | collective-permute-start | bytes 98312 | tf_op jit(solution)/shard_map/ppermute | solution.py:20
  11.3 1.9 collective-permute-done
  13.2 5.2 %collective-permute-start.1 = (bf16[2,64,256]{2,1,0:T(8,128)(2,1)S(1)}, bf16[2,64,256]{2,1,0:T(8,128)(2,1)S(1)}, u32[]{:S(2)}, u32[]{:S(2)}) collective-permute-start(bf16[2,64,256]{2,1,0:T(8,128)(2,1)S(1)} %maximum_select_fusion.13), channel_id=1, source_target_pairs={{0,32},{8,40},{16,48},{24,56},{32,0},{40,8},{48,16},{56,24},{64,96... | collective-permute-start | bytes 196616 | tf_op jit(solution)/shard_map/ppermute | solution.py:20
  18.4 3.6 %collective-permute-done.1 = bf16[2,64,256]{2,1,0:T(8,128)(2,1)S(1)} collective-permute-done((bf16[2,64,256]{2,1,0:T(8,128)(2,1)S(1)}, bf16[2,64,256]{2,1,0:T(8,128)(2,1)S(1)}, u32[]{:S(2)}, u32[]{:S(2)}) %collective-permute-start.1) | collective-permute-done | bytes 65568 | tf_op jit(solution)/shard_map/ppermute | solution.py:20
  22.0 4.9 %collective-permute-start.2 = (bf16[2,2,64,256]{3,2,0,1:T(8,128)(2,1)S(1)}, bf16[2,2,64,256]{3,2,0,1:T(8,128)(2,1)S(1)}, u32[]{:S(2)}, u32[]{:S(2)}) collective-permute-start(bf16[2,2,64,256]{3,2,0,1:T(8,128)(2,1)S(1)} %maximum_select_fusion.12), channel_id=1, source_target_pairs={{0,256},{128,384},{256,0},{384,128},{1,257},{129,385},{257,1},{385... | collective-permute-start | bytes 393224 | tf_op jit(solution)/shard_map/ppermute | solution.py:20
  27.0 3.4 %collective-permute-done.2 = bf16[2,2,64,256]{3,2,0,1:T(8,128)(2,1)S(1)} collective-permute-done((bf16[2,2,64,256]{3,2,0,1:T(8,128)(2,1)S(1)}, bf16[2,2,64,256]{3,2,0,1:T(8,128)(2,1)S(1)}, u32[]{:S(2)}, u32[]{:S(2)}) %collective-permute-start.2) | collective-permute-done | bytes 131104 | tf_op jit(solution)/shard_map/ppermute | solution.py:20
  30.4 2.4 collective-permute-start.3
  32.9 5.8 %collective-permute-done.3 = bf16[2,2,2,64,256]{4,3,1,2,0:T(8,128)(2,1)S(1)} collective-permute-done((bf16[2,2,2,64,256]{4,3,1,2,0:T(8,128)(2,1)S(1)}, bf16[2,2,2,64,256]{4,3,1,2,0:T(8,128)(2,1)S(1)}, u32[]{:S(2)}, u32[]{:S(2)}) %collective-permute-start.3) | collective-permute-done | bytes 262176 | tf_op jit(solution)/shard_map/ppermute | solution.py:20
  38.8 3.4 %collective-permute-start.4 = (bf16[2,2,2,2,64,256]{5,4,0,2,3,1:T(8,128)(2,1)S(1)}, bf16[2,2,2,2,64,256]{5,4,0,2,3,1:T(8,128)(2,1)S(1)}, u32[]{:S(2)}, u32[]{:S(2)}) collective-permute-start(bf16[2,2,2,2,64,256]{5,4,0,2,3,1:T(8,128)(2,1)S(1)} %maximum_select_fusion.8), channel_id=1, source_target_pairs={{0,128},{128,0},{256,384},{384,256},{1,129},{129,1},{257,385},{385... | collective-permute-start | bytes 1572872 | tf_op jit(solution)/shard_map/ppermute | solution.py:20
  42.4 7.5 %collective-permute-done.4 = bf16[2,2,2,2,64,256]{5,4,0,2,3,1:T(8,128)(2,1)S(1)} collective-permute-done((bf16[2,2,2,2,64,256]{5,4,0,2,3,1:T(8,128)(2,1)S(1)}, bf16[2,2,2,2,64,256]{5,4,0,2,3,1:T(8,128)(2,1)S(1)}, u32[]{:S(2)}, u32[]{:S(2)}) %collective-permute-start.4) | collective-permute-done | bytes 524320 | tf_op jit(solution)/shard_map/ppermute | solution.py:20
  49.8 1.2 maximum_select_fusion.4
  51.0 1.9 collective-permute-start.5
  53.1 2.8 collective-permute-done.5
  55.9 1.3 copy.83
  57.4 0.6 fusion.17
  58.1 8.2 %collective-permute-start.6 = (bf16[192,384]{1,0:T(8,128)(2,1)S(1)}, bf16[192,384]{1,0:T(8,128)(2,1)S(1)}, u32[]{:S(2)}, u32[]{:S(2)}) collective-permute-start(bf16[192,384]{1,0:T(8,128)(2,1)S(1)} %get-tuple-element.7), channel_id=1, source_target_pairs={{0,64},{8,72},{16,80},{24,88},{32,96},{40,104},{48,112},{56,120},{... | collective-permute-start | bytes 442376 | tf_op jit(solution)/shard_map/ppermute | solution.py:20
  66.3 13.6 %collective-permute-done.6 = bf16[192,384]{1,0:T(8,128)(2,1)S(1)} collective-permute-done((bf16[192,384]{1,0:T(8,128)(2,1)S(1)}, bf16[192,384]{1,0:T(8,128)(2,1)S(1)}, u32[]{:S(2)}, u32[]{:S(2)}) %collective-permute-start.6) | collective-permute-done | bytes 147488 | tf_op jit(solution)/shard_map/ppermute | solution.py:20
  80.0 1.9 collective-permute-start.7
  82.0 15.7 %collective-permute-done.7 = bf16[2,192,384]{2,1,0:T(8,128)(2,1)S(1)} collective-permute-done((bf16[2,192,384]{2,1,0:T(8,128)(2,1)S(1)}, bf16[2,192,384]{2,1,0:T(8,128)(2,1)S(1)}, u32[]{:S(2)}, u32[]{:S(2)}) %collective-permute-start.7) | collective-permute-done | bytes 294944 | tf_op jit(solution)/shard_map/ppermute | solution.py:20
  97.8 2.1 collective-permute-start.8
  100.0 14.7 %collective-permute-done.8 = bf16[2,2,192,384]{3,2,1,0:T(8,128)(2,1)S(1)} collective-permute-done((bf16[2,2,192,384]{3,2,1,0:T(8,128)(2,1)S(1)}, bf16[2,2,192,384]{3,2,1,0:T(8,128)(2,1)S(1)}, u32[]{:S(2)}, u32[]{:S(2)}) %collective-permute-start.8) | collective-permute-done | bytes 589856 | tf_op jit(solution)/shard_map/ppermute | solution.py:20
  114.7 1.3 maximum_select_fusion.2
  116.0 1.9 collective-permute-start.9
  118.4 2.7 collective-permute-done.9
  121.0 2.1 fusion.4
  124.1 2.1 fusion.2
  126.1 3.4 %select_reduce_fusion = f32[192,4]{0,1:T(4,128)S(1)} fusion(f32[3072,192,4]{0,1,2:T(8,128)S(1)} %get-tuple-element.13, f32[192,4]{0,1:T(4,128)S(1)} %get-tuple-element.12, pred[192,3072]{1,0:T(8,128)(4,1)S(1)} %broadcast_compare_fusion), kind=kLoop, calls=%fused_computation.4 | loop fusion | flops 11795712 | bytes 10033152 | tf_op jit(solution)/shard_map/reduce_sum | solution.py:95
  129.5 3.0 fusion.13
  132.5 2.9 convolution_bitcast_fusion.1
  135.4 3.9 %fusion = bf16[192,4,3072]{2,0,1:T(8,128)(2,1)S(1)} fusion(f32[3072,192,4]{0,1,2:T(8,128)S(1)} %get-tuple-element.13, f32[192,4]{0,1:T(4,128)S(1)} %fusion.13, f32[192,4]{0,1:T(4,128)S(1)} %log_add_fusion, pred[192,3072]{1,0:T(8,128)(4,1)S(1)} %broadcast_compare_fusion, bf16[3072,384]{1,0:T(8,128)(2,1)S(1)} %bitcast.226, ...), kind=kOutput, calls=%fused_computation.1 | convolution fusion | flops 620494848 | bytes 15736832 | tf_op jit(solution)/shard_map/qgd,kd->qgk/dot_general | solution.py:104
  139.3 0.9 fusion.3
  140.2 1.3 copy-done.3
  141.4 2.0 pad_maximum_fusion
  143.4 3.6 %copy.45 = f32[3072,256]{1,0:T(8,128)} copy(f32[3072,256]{0,1:T(8,128)} %pad_maximum_fusion) | data formatting | bytes 6291456 | tf_op jit(solution)/shard_map/concatenate | solution.py:111
  147.1 2.2 select_bitcast_fusion.1
  149.3 2.0 collective-permute-start.10
  151.4 3.2 %collective-permute-done.10 = f32[2,2,2,192,256]{4,3,2,1,0:T(8,128)S(1)} collective-permute-done((f32[2,2,2,192,256]{4,3,2,1,0:T(8,128)S(1)}, f32[2,2,2,192,256]{4,3,2,1,0:T(8,128)S(1)}, u32[]{:S(2)}, u32[]{:S(2)}) %collective-permute-start.10) | collective-permute-done | bytes 1572896 | tf_op jit(solution)/shard_map/ppermute | solution.py:20
  155.0 2.2 collective-permute-start.11
  157.3 19.3 %collective-permute-done.11 = f32[2,2,192,256]{3,2,1,0:T(8,128)S(1)} collective-permute-done((f32[2,2,192,256]{3,2,1,0:T(8,128)S(1)}, f32[2,2,192,256]{3,2,1,0:T(8,128)S(1)}, u32[]{:S(2)}, u32[]{:S(2)}) %collective-permute-start.11) | collective-permute-done | bytes 786464 | tf_op jit(solution)/shard_map/ppermute | solution.py:20
  176.8 2.3 collective-permute-start.12
  179.1 19.0 %collective-permute-done.12 = f32[2,192,256]{2,1,0:T(8,128)S(1)} collective-permute-done((f32[2,192,256]{2,1,0:T(8,128)S(1)}, f32[2,192,256]{2,1,0:T(8,128)S(1)}, u32[]{:S(2)}, u32[]{:S(2)}) %collective-permute-start.12) | collective-permute-done | bytes 393248 | tf_op jit(solution)/shard_map/ppermute | solution.py:20
  198.2 5.1 %collective-permute-start.13 = (f32[192,256]{1,0:T(8,128)S(1)}, f32[192,256]{1,0:T(8,128)S(1)}, u32[]{:S(2)}, u32[]{:S(2)}) collective-permute-start(f32[192,256]{1,0:T(8,128)S(1)} %select_bitcast_fusion.7), channel_id=1, source_target_pairs={{0,64},{8,72},{16,80},{24,88},{32,96},{40,104},{48,112},{56,120},{... | collective-permute-start | bytes 589832 | tf_op jit(solution)/shard_map/ppermute | solution.py:20
  203.3 18.3 %collective-permute-done.13 = f32[192,256]{1,0:T(8,128)S(1)} collective-permute-done((f32[192,256]{1,0:T(8,128)S(1)}, f32[192,256]{1,0:T(8,128)S(1)}, u32[]{:S(2)}, u32[]{:S(2)}) %collective-permute-start.13) | collective-permute-done | bytes 196640 | tf_op jit(solution)/shard_map/ppermute | solution.py:20
  221.6 2.8 convolution_bitcast_fusion
  224.4 5.7 %copy.46 = f32[4096,256]{1,0:T(8,128)} copy(f32[4096,256]{0,1:T(8,128)} %convolution_bitcast_fusion) | data formatting | bytes 8388608 | tf_op jit(solution)/shard_map/td,tc->dc/dot_general | solution.py:115
  230.0 2.8 select_bitcast_fusion
  232.8 1.9 collective-permute-start.14
  234.7 4.1 %collective-permute-done.14 = f32[2,2,2,2,2,64,256]{6,5,4,3,2,1,0:T(8,128)S(1)} collective-permute-done((f32[2,2,2,2,2,64,256]{6,5,4,3,2,1,0:T(8,128)S(1)}, f32[2,2,2,2,2,64,256]{6,5,4,3,2,1,0:T(8,128)S(1)}, u32[]{:S(2)}, u32[]{:S(2)}) %collective-permute-start.14) | collective-permute-done | bytes 2097184 | tf_op jit(solution)/shard_map/ppermute | solution.py:20
  238.9 0.6 fusion.6
  239.7 3.7 %collective-permute-start.15 = (f32[2,2,2,2,64,256]{5,4,3,2,1,0:T(8,128)S(1)}, f32[2,2,2,2,64,256]{5,4,3,2,1,0:T(8,128)S(1)}, u32[]{:S(2)}, u32[]{:S(2)}) collective-permute-start(f32[2,2,2,2,64,256]{5,4,3,2,1,0:T(8,128)S(1)} %select_bitcast_fusion.2), channel_id=1, source_target_pairs={{0,128},{128,0},{256,384},{384,256},{1,129},{129,1},{257,385},{385... | collective-permute-start | bytes 3145736 | tf_op jit(solution)/shard_map/ppermute | solution.py:20
  243.3 23.7 %collective-permute-done.15 = f32[2,2,2,2,64,256]{5,4,3,2,1,0:T(8,128)S(1)} collective-permute-done((f32[2,2,2,2,64,256]{5,4,3,2,1,0:T(8,128)S(1)}, f32[2,2,2,2,64,256]{5,4,3,2,1,0:T(8,128)S(1)}, u32[]{:S(2)}, u32[]{:S(2)}) %collective-permute-start.15) | collective-permute-done | bytes 1048608 | tf_op jit(solution)/shard_map/ppermute | solution.py:20
  267.3 1.9 collective-permute-start.16
  269.3 13.1 %collective-permute-done.16 = f32[2,2,2,64,256]{4,3,2,1,0:T(8,128)S(1)} collective-permute-done((f32[2,2,2,64,256]{4,3,2,1,0:T(8,128)S(1)}, f32[2,2,2,64,256]{4,3,2,1,0:T(8,128)S(1)}, u32[]{:S(2)}, u32[]{:S(2)}) %collective-permute-start.16) | collective-permute-done | bytes 524320 | tf_op jit(solution)/shard_map/ppermute | solution.py:20
  282.5 4.9 %collective-permute-start.17 = (f32[2,2,64,256]{3,2,1,0:T(8,128)S(1)}, f32[2,2,64,256]{3,2,1,0:T(8,128)S(1)}, u32[]{:S(2)}, u32[]{:S(2)}) collective-permute-start(f32[2,2,64,256]{3,2,1,0:T(8,128)S(1)} %select_bitcast_fusion.6), channel_id=1, source_target_pairs={{0,256},{128,384},{256,0},{384,128},{1,257},{129,385},{257,1},{385... | collective-permute-start | bytes 786440 | tf_op jit(solution)/shard_map/ppermute | solution.py:20
  287.4 5.1 %collective-permute-done.17 = f32[2,2,64,256]{3,2,1,0:T(8,128)S(1)} collective-permute-done((f32[2,2,64,256]{3,2,1,0:T(8,128)S(1)}, f32[2,2,64,256]{3,2,1,0:T(8,128)S(1)}, u32[]{:S(2)}, u32[]{:S(2)}) %collective-permute-start.17) | collective-permute-done | bytes 262176 | tf_op jit(solution)/shard_map/ppermute | solution.py:20
  292.6 1.9 collective-permute-start.18
  294.5 7.2 %collective-permute-done.18 = f32[2,64,256]{2,1,0:T(8,128)S(1)} collective-permute-done((f32[2,64,256]{2,1,0:T(8,128)S(1)}, f32[2,64,256]{2,1,0:T(8,128)S(1)}, u32[]{:S(2)}, u32[]{:S(2)}) %collective-permute-start.18) | collective-permute-done | bytes 131104 | tf_op jit(solution)/shard_map/ppermute | solution.py:20
  301.8 2.3 collective-permute-start.19
  304.1 2.5 fusion.10
  306.8 0.8 reshape.923
  307.5 5.2 %collective-permute-done.19 = f32[64,256]{1,0:T(8,128)S(1)} collective-permute-done((f32[64,256]{1,0:T(8,128)S(1)}, f32[64,256]{1,0:T(8,128)S(1)}, u32[]{:S(2)}, u32[]{:S(2)}) %collective-permute-start.19) | collective-permute-done | bytes 65568 | tf_op jit(solution)/shard_map/ppermute | solution.py:20
  312.7 0.6 fusion.40
  (67 shorter events, 4.2 us)
Async XLA Ops:
  0.6 56.7 %copy-start = (bf16[1,192,4096]{2,1,0:T(8,128)(2,1)S(1)}, bf16[1,192,4096]{2,1,0:T(8,128)(2,1)}, u32[]{:S(2)}) copy-start(bf16[1,192,4096]{2,1,0:T(8,128)(2,1)} %param.6) | copy-start | bytes 4718596
  2.2 11.0 %collective-permute-start = (bf16[64,256]{1,0:T(8,128)(2,1)S(1)}, bf16[64,256]{1,0:T(8,128)(2,1)S(1)}, u32[]{:S(2)}, u32[]{:S(2)}) collective-permute-start(bf16[64,256]{1,0:T(8,128)(2,1)S(1)} %constant_dynamic-update-slice_fusion), channel_id=1, source_target_pairs={{0,64},{8,72},{16,80},{24,88},{32,96},{40,104},{48,112},{56,120},{... | collective-permute-start | bytes 98312 | tf_op jit(solution)/shard_map/ppermute | solution.py:20
  13.2 8.8 %collective-permute-start.1 = (bf16[2,64,256]{2,1,0:T(8,128)(2,1)S(1)}, bf16[2,64,256]{2,1,0:T(8,128)(2,1)S(1)}, u32[]{:S(2)}, u32[]{:S(2)}) collective-permute-start(bf16[2,64,256]{2,1,0:T(8,128)(2,1)S(1)} %maximum_select_fusion.13), channel_id=1, source_target_pairs={{0,32},{8,40},{16,48},{24,56},{32,0},{40,8},{48,16},{56,24},{64,96... | collective-permute-start | bytes 196616 | tf_op jit(solution)/shard_map/ppermute | solution.py:20
  22.0 8.4 %collective-permute-start.2 = (bf16[2,2,64,256]{3,2,0,1:T(8,128)(2,1)S(1)}, bf16[2,2,64,256]{3,2,0,1:T(8,128)(2,1)S(1)}, u32[]{:S(2)}, u32[]{:S(2)}) collective-permute-start(bf16[2,2,64,256]{3,2,0,1:T(8,128)(2,1)S(1)} %maximum_select_fusion.12), channel_id=1, source_target_pairs={{0,256},{128,384},{256,0},{384,128},{1,257},{129,385},{257,1},{385... | collective-permute-start | bytes 393224 | tf_op jit(solution)/shard_map/ppermute | solution.py:20
  30.4 8.3 %collective-permute-start.3 = (bf16[2,2,2,64,256]{4,3,1,2,0:T(8,128)(2,1)S(1)}, bf16[2,2,2,64,256]{4,3,1,2,0:T(8,128)(2,1)S(1)}, u32[]{:S(2)}, u32[]{:S(2)}) collective-permute-start(bf16[2,2,2,64,256]{4,3,1,2,0:T(8,128)(2,1)S(1)} %maximum_select_fusion.11), channel_id=1, source_target_pairs={{0,16},{8,24},{16,0},{24,8},{32,48},{40,56},{48,32},{56,40},{64,80... | collective-permute-start | bytes 786440 | tf_op jit(solution)/shard_map/ppermute | solution.py:20
  38.8 11.1 %collective-permute-start.4 = (bf16[2,2,2,2,64,256]{5,4,0,2,3,1:T(8,128)(2,1)S(1)}, bf16[2,2,2,2,64,256]{5,4,0,2,3,1:T(8,128)(2,1)S(1)}, u32[]{:S(2)}, u32[]{:S(2)}) collective-permute-start(bf16[2,2,2,2,64,256]{5,4,0,2,3,1:T(8,128)(2,1)S(1)} %maximum_select_fusion.8), channel_id=1, source_target_pairs={{0,128},{128,0},{256,384},{384,256},{1,129},{129,1},{257,385},{385... | collective-permute-start | bytes 1572872 | tf_op jit(solution)/shard_map/ppermute | solution.py:20
  42.2 10.7 %copy-start.7 = (s32[1,192]{1,0:T(1,128)S(1)}, s32[1,192]{1,0:T(1,128)}, u32[]{:S(2)}) copy-start(s32[1,192]{1,0:T(1,128)} %param.9) | copy-start | bytes 2308
  51.0 4.9 %collective-permute-start.5 = (bf16[2,2,2,2,2,64,256]{6,5,1,3,4,2,0:T(8,128)(2,1)}, bf16[2,2,2,2,2,64,256]{6,5,1,3,4,2,0:T(8,128)(2,1)}, u32[]{:S(2)}, u32[]{:S(2)}) collective-permute-start(bf16[2,2,2,2,2,64,256]{6,5,1,3,4,2,0:T(8,128)(2,1)} %maximum_select_fusion.4), channel_id=1, source_target_pairs={{0,8},{8,0},{16,24},{24,16},{32,40},{40,32},{48,56},{56,48},{64,72... | collective-permute-start | bytes 3145736 | tf_op jit(solution)/shard_map/ppermute | solution.py:20
  58.1 21.8 %collective-permute-start.6 = (bf16[192,384]{1,0:T(8,128)(2,1)S(1)}, bf16[192,384]{1,0:T(8,128)(2,1)S(1)}, u32[]{:S(2)}, u32[]{:S(2)}) collective-permute-start(bf16[192,384]{1,0:T(8,128)(2,1)S(1)} %get-tuple-element.7), channel_id=1, source_target_pairs={{0,64},{8,72},{16,80},{24,88},{32,96},{40,104},{48,112},{56,120},{... | collective-permute-start | bytes 442376 | tf_op jit(solution)/shard_map/ppermute | solution.py:20
  80.0 17.7 %collective-permute-start.7 = (bf16[2,192,384]{2,1,0:T(8,128)(2,1)S(1)}, bf16[2,192,384]{2,1,0:T(8,128)(2,1)S(1)}, u32[]{:S(2)}, u32[]{:S(2)}) collective-permute-start(bf16[2,192,384]{2,1,0:T(8,128)(2,1)S(1)} %maximum_select_fusion.9), channel_id=1, source_target_pairs={{0,32},{8,40},{16,48},{24,56},{32,0},{40,8},{48,16},{56,24},{64,96... | collective-permute-start | bytes 884744 | tf_op jit(solution)/shard_map/ppermute | solution.py:20
  97.7 20.2 %copy-start.5 = (bf16[1,192,512]{2,1,0:T(8,128)(2,1)S(1)}, bf16[1,192,512]{2,1,0:T(8,128)(2,1)}, u32[]{:S(2)}) copy-start(bf16[1,192,512]{2,1,0:T(8,128)(2,1)} %param.7) | copy-start | bytes 589828
  97.7 20.2 %copy-start.6 = (bf16[1,192,512]{2,1,0:T(8,128)(2,1)S(1)}, bf16[1,192,512]{2,1,0:T(8,128)(2,1)}, u32[]{:S(2)}) copy-start(bf16[1,192,512]{2,1,0:T(8,128)(2,1)} %param.8) | copy-start | bytes 589828
  97.8 16.9 %collective-permute-start.8 = (bf16[2,2,192,384]{3,2,1,0:T(8,128)(2,1)S(1)}, bf16[2,2,192,384]{3,2,1,0:T(8,128)(2,1)S(1)}, u32[]{:S(2)}, u32[]{:S(2)}) collective-permute-start(bf16[2,2,192,384]{3,2,1,0:T(8,128)(2,1)S(1)} %maximum_select_fusion.6), channel_id=1, source_target_pairs={{0,16},{8,24},{16,0},{24,8},{32,48},{40,56},{48,32},{56,40},{64,80... | collective-permute-start | bytes 1769480 | tf_op jit(solution)/shard_map/ppermute | solution.py:20
  116.0 5.1 %collective-permute-start.9 = (bf16[2,2,2,192,384]{4,3,2,1,0:T(8,128)(2,1)}, bf16[2,2,2,192,384]{4,3,2,1,0:T(8,128)(2,1)}, u32[]{:S(2)}, u32[]{:S(2)}) collective-permute-start(bf16[2,2,2,192,384]{4,3,2,1,0:T(8,128)(2,1)} %maximum_select_fusion.2), channel_id=1, source_target_pairs={{0,8},{8,0},{16,24},{24,16},{32,40},{40,32},{48,56},{56,48},{64,72... | collective-permute-start | bytes 3538952 | tf_op jit(solution)/shard_map/ppermute | solution.py:20
  123.4 12.1 %copy-start.4 = (bf16[2,2,2,2,192,384]{5,4,3,2,1,0:T(8,128)(2,1)}, bf16[2,2,2,2,192,384]{5,4,3,2,1,0:T(8,128)(2,1)S(1)}, u32[]{:S(2)}) copy-start(bf16[2,2,2,2,192,384]{5,4,3,2,1,0:T(8,128)(2,1)S(1)} %copy.38) | copy-start | bytes 7077892
  139.3 2.1 copy-start.3
  147.1 7.6 %copy-start.2 = (f32[3072,256]{1,0:T(8,128)S(1)}, f32[3072,256]{1,0:T(8,128)}, u32[]{:S(2)}) copy-start(f32[3072,256]{1,0:T(8,128)} %copy.45) | copy-start | bytes 9437188
  149.3 5.3 %collective-permute-start.10 = (f32[2,2,2,192,256]{4,3,2,1,0:T(8,128)S(1)}, f32[2,2,2,192,256]{4,3,2,1,0:T(8,128)S(1)}, u32[]{:S(2)}, u32[]{:S(2)}) collective-permute-start(f32[2,2,2,192,256]{4,3,2,1,0:T(8,128)S(1)} %select_bitcast_fusion.1), channel_id=1, source_target_pairs={{0,8},{8,0},{16,24},{24,16},{32,40},{40,32},{48,56},{56,48},{64,72... | collective-permute-start | bytes 4718600 | tf_op jit(solution)/shard_map/ppermute | solution.py:20
  155.0 21.5 %collective-permute-start.11 = (f32[2,2,192,256]{3,2,1,0:T(8,128)S(1)}, f32[2,2,192,256]{3,2,1,0:T(8,128)S(1)}, u32[]{:S(2)}, u32[]{:S(2)}) collective-permute-start(f32[2,2,192,256]{3,2,1,0:T(8,128)S(1)} %select_bitcast_fusion.3), channel_id=1, source_target_pairs={{0,16},{8,24},{16,0},{24,8},{32,48},{40,56},{48,32},{56,40},{64,80... | collective-permute-start | bytes 2359304 | tf_op jit(solution)/shard_map/ppermute | solution.py:20
  176.8 21.3 %collective-permute-start.12 = (f32[2,192,256]{2,1,0:T(8,128)S(1)}, f32[2,192,256]{2,1,0:T(8,128)S(1)}, u32[]{:S(2)}, u32[]{:S(2)}) collective-permute-start(f32[2,192,256]{2,1,0:T(8,128)S(1)} %select_bitcast_fusion.5), channel_id=1, source_target_pairs={{0,32},{8,40},{16,48},{24,56},{32,0},{40,8},{48,16},{56,24},{64,96... | collective-permute-start | bytes 1179656 | tf_op jit(solution)/shard_map/ppermute | solution.py:20
  198.2 23.4 %collective-permute-start.13 = (f32[192,256]{1,0:T(8,128)S(1)}, f32[192,256]{1,0:T(8,128)S(1)}, u32[]{:S(2)}, u32[]{:S(2)}) collective-permute-start(f32[192,256]{1,0:T(8,128)S(1)} %select_bitcast_fusion.7), channel_id=1, source_target_pairs={{0,64},{8,72},{16,80},{24,88},{32,96},{40,104},{48,112},{56,120},{... | collective-permute-start | bytes 589832 | tf_op jit(solution)/shard_map/ppermute | solution.py:20
  230.0 8.8 %copy-start.1 = (f32[4096,256]{1,0:T(8,128)S(1)}, f32[4096,256]{1,0:T(8,128)}, u32[]{:S(2)}) copy-start(f32[4096,256]{1,0:T(8,128)} %copy.46) | copy-start | bytes 12582916
  232.8 6.1 %collective-permute-start.14 = (f32[2,2,2,2,2,64,256]{6,5,4,3,2,1,0:T(8,128)S(1)}, f32[2,2,2,2,2,64,256]{6,5,4,3,2,1,0:T(8,128)S(1)}, u32[]{:S(2)}, u32[]{:S(2)}) collective-permute-start(f32[2,2,2,2,2,64,256]{6,5,4,3,2,1,0:T(8,128)S(1)} %select_bitcast_fusion), channel_id=1, source_target_pairs={{0,8},{8,0},{16,24},{24,16},{32,40},{40,32},{48,56},{56,48},{64,72... | collective-permute-start | bytes 6291464 | tf_op jit(solution)/shard_map/ppermute | solution.py:20
  239.5 64.6 %slice-start = ((s8[4718592]{0:T(1024)(128)(4,1)}), s8[4194304]{0:T(1024)(128)(4,1)S(1)}, s32[]{:S(2)}) async-start(s8[4718592]{0:T(1024)(128)(4,1)} %bitcast.219), calls=%async_computation | async-start | bytes 8388608
  239.7 64.4 %slice-start.1 = ((s8[4718592]{0:T(1024)(128)(4,1)}), s8[524288]{0:T(1024)(128)(4,1)S(1)}, s32[]{:S(2)}) async-start(s8[4718592]{0:T(1024)(128)(4,1)} %bitcast.219), calls=%async_computation.1 | async-start | bytes 1048576
  239.7 27.4 %collective-permute-start.15 = (f32[2,2,2,2,64,256]{5,4,3,2,1,0:T(8,128)S(1)}, f32[2,2,2,2,64,256]{5,4,3,2,1,0:T(8,128)S(1)}, u32[]{:S(2)}, u32[]{:S(2)}) collective-permute-start(f32[2,2,2,2,64,256]{5,4,3,2,1,0:T(8,128)S(1)} %select_bitcast_fusion.2), channel_id=1, source_target_pairs={{0,128},{128,0},{256,384},{384,256},{1,129},{129,1},{257,385},{385... | collective-permute-start | bytes 3145736 | tf_op jit(solution)/shard_map/ppermute | solution.py:20
  267.3 15.0 %collective-permute-start.16 = (f32[2,2,2,64,256]{4,3,2,1,0:T(8,128)S(1)}, f32[2,2,2,64,256]{4,3,2,1,0:T(8,128)S(1)}, u32[]{:S(2)}, u32[]{:S(2)}) collective-permute-start(f32[2,2,2,64,256]{4,3,2,1,0:T(8,128)S(1)} %select_bitcast_fusion.4), channel_id=1, source_target_pairs={{0,16},{8,24},{16,0},{24,8},{32,48},{40,56},{48,32},{56,40},{64,80... | collective-permute-start | bytes 1572872 | tf_op jit(solution)/shard_map/ppermute | solution.py:20
  282.5 10.0 %collective-permute-start.17 = (f32[2,2,64,256]{3,2,1,0:T(8,128)S(1)}, f32[2,2,64,256]{3,2,1,0:T(8,128)S(1)}, u32[]{:S(2)}, u32[]{:S(2)}) collective-permute-start(f32[2,2,64,256]{3,2,1,0:T(8,128)S(1)} %select_bitcast_fusion.6), channel_id=1, source_target_pairs={{0,256},{128,384},{256,0},{384,128},{1,257},{129,385},{257,1},{385... | collective-permute-start | bytes 786440 | tf_op jit(solution)/shard_map/ppermute | solution.py:20
  292.6 9.2 %collective-permute-start.18 = (f32[2,64,256]{2,1,0:T(8,128)S(1)}, f32[2,64,256]{2,1,0:T(8,128)S(1)}, u32[]{:S(2)}, u32[]{:S(2)}) collective-permute-start(f32[2,64,256]{2,1,0:T(8,128)S(1)} %select_bitcast_fusion.8), channel_id=1, source_target_pairs={{0,32},{8,40},{16,48},{24,56},{32,0},{40,8},{48,16},{56,24},{64,96... | collective-permute-start | bytes 393224 | tf_op jit(solution)/shard_map/ppermute | solution.py:20
  301.8 10.9 %collective-permute-start.19 = (f32[64,256]{1,0:T(8,128)S(1)}, f32[64,256]{1,0:T(8,128)S(1)}, u32[]{:S(2)}, u32[]{:S(2)}) collective-permute-start(f32[64,256]{1,0:T(8,128)S(1)} %select_bitcast_fusion.9), channel_id=1, source_target_pairs={{0,64},{8,72},{16,80},{24,88},{32,96},{40,104},{48,112},{56,120},{... | collective-permute-start | bytes 196616 | tf_op jit(solution)/shard_map/ppermute | solution.py:20

commit v2 on v1

--- a/solution.py
+++ b/solution.py
@@ -37,8 +37,9 @@
     return cur.reshape((-1,) + x.shape[1:])
 
 
-def scatter_sum(x, steps, canon):
+def scatter_sum(x, steps, canon, acc=None):
     nb = len(canon)
+    acc = acc or x.dtype
     block = x.shape[0] >> nb
     cur = x.reshape((2,) * nb + (block,) + x.shape[1:])
     dims = list(canon)
@@ -49,7 +50,8 @@
         mine = _my_bit(axis, bit)
         keep = jnp.where(mine, hi, lo)
         send = jnp.where(mine, lo, hi)
-        cur = keep + _exchange(send, axis, size, bit)
+        total = keep.astype(acc) + _exchange(send, axis, size, bit).astype(acc)
+        cur = total if len(dims) == 1 else total.astype(x.dtype)
         dims.pop(at)
     return cur
 
@@ -77,14 +79,14 @@
     proj = jnp.concatenate([key_proj, value_proj], axis=1)
     proj_all = gather_blocks(proj, far_first, both_canon)
     kv = jnp.dot(local_rows, proj_all, preferred_element_type=jnp.float32).astype(jnp.bfloat16)
-    marks_col = jnp.broadcast_to(segment[0].astype(jnp.bfloat16)[:, None], (tok_rows, 128))
-    kvm = jnp.concatenate([kv, marks_col], axis=1)
+    marks = segment[0].astype(jnp.bfloat16)
+    marks_row = jnp.pad(marks, (0, 2 * HEAD_DIM - tok_rows))[None, :]
+    kvm = jnp.concatenate([kv, marks_row], axis=0)[None]
     ctx_far_first = [step("context", b) for b in reversed(range(_bits(n_ctx)))]
     kvm_all = gather_blocks(kvm, ctx_far_first, ctx_canon)
-    keys = kvm_all[:, :HEAD_DIM]
-    values = kvm_all[:, HEAD_DIM:2 * HEAD_DIM]
-    marks_all = kvm_all[:, 2 * HEAD_DIM]
-    marks = segment[0].astype(jnp.bfloat16)
+    keys = kvm_all[:, :tok_rows, :HEAD_DIM].reshape(-1, HEAD_DIM)
+    values = kvm_all[:, :tok_rows, HEAD_DIM:].reshape(-1, HEAD_DIM)
+    marks_all = kvm_all[:, tok_rows, :tok_rows].reshape(-1)
 
     q = queries[0].reshape(tok_rows, group, HEAD_DIM)
     do = grad_out[0].reshape(tok_rows, group, HEAD_DIM)
@@ -108,9 +110,9 @@
     ).astype(jnp.bfloat16)
     key_part = jnp.einsum("qgk,qgd->kd", dscores, q, preferred_element_type=jnp.float32) * scale
 
-    kv_part = jnp.concatenate([key_part, value_part], axis=1)
+    kv_part = jnp.concatenate([key_part, value_part], axis=1).astype(jnp.bfloat16)
     ctx_near_first = ctx_far_first[::-1]
-    kv_grad = scatter_sum(kv_part, ctx_near_first, ctx_canon).astype(jnp.bfloat16)
+    kv_grad = scatter_sum(kv_part, ctx_near_first, ctx_canon, jnp.float32).astype(jnp.bfloat16)
 
     proj_part = jnp.einsum("td,tc->dc", local_rows, kv_grad, preferred_element_type=jnp.float32)
     summed = scatter_sum(proj_part, near_first, both_canon)

time: 315 us -> 293 us (0.930)
  waiting for transfers between devices: 190 us -> 136 us
  local copies, waits for them, and re-layouts: 15.8 us -> 31.4 us
  starting transfers between devices: 69.3 us -> 81.9 us
  matrix products: 18.5 us -> 23 us
    ppermute x20, waiting for transfers between devices: 190 us -> 136 us  [_exchange(): return lax.ppermute(x, axis, perm)]
    dot_general x0 -> x1, local copies, waits for them, and re-layouts: none -> 16.2 us  [body(): jnp.einsum('qgk,qgd->kd', probs_b, do, preferred_element_type=jnp.float32)]
    ppermute x20, starting transfers between devices: 69.3 us -> 81.9 us  [_exchange(): return lax.ppermute(x, axis, perm)]
    convert_element_type x0 -> x4, other arithmetic: none -> 4.57 us  [the longest x1 3.99 us: body(): probs_b = probs.astype(jnp.bfloat16)]
    concatenate x1 -> x0, local copies, waits for them, and re-layouts: 3.65 us -> none  [body(): kv_part = jnp.concatenate([key_part, value_part], axis=1)]
  transfers between devices with their start and end apart: 20 -> 20, of which waited for: 20 -> 19; matrix products, arithmetic and copies ran while one was open for 1% -> 2% of each run, Pallas kernels for 0% -> 0%
where the time goes in v2:
time: 293 us; the launch traced here: 289 us
  waiting for transfers between devices  136 us (46%)
  starting transfers between devices  81.9 us (28%)
  local copies, waits for them, and re-layouts  31.4 us (11%)
  matrix products  23 us (8%)
  other arithmetic  15.8 us (5%)
    ppermute x20, waiting for transfers between devices, _exchange(): return lax.ppermute(x, axis, perm)  136 us
    ppermute x20, starting transfers between devices, _exchange(): return lax.ppermute(x, axis, perm)  81.9 us
    dot_general x1, local copies, waits for them, and re-layouts, body(): jnp.einsum('qgk,qgd->kd', probs_b, do, preferred_element_type=jnp.float32)  16.2 us
  transfers between devices with their start and end apart: 20, of which 19 were waited for; matrix products, arithmetic and copies ran while one was open for 2% of the time, Pallas kernels for 0%

profile of v2, /device:TPU:24, one launch (start us, length us, event | category | flops | bytes accessed | tf_op | source)
XLA Modules:
  0.0 289.0 jit_solution(4931189340277567995)
XLA Ops:
  0.6 0.8 constant_dynamic-update-slice_fusion.1
  1.5 0.7 constant_dynamic-update-slice_fusion
  2.2 9.1 %collective-permute-start = (bf16[64,256]{1,0:T(8,128)(2,1)S(1)}, bf16[64,256]{1,0:T(8,128)(2,1)S(1)}, u32[]{:S(2)}, u32[]{:S(2)}) collective-permute-start(bf16[64,256]{1,0:T(8,128)(2,1)S(1)} %constant_dynamic-update-slice_fusion), channel_id=1, source_target_pairs={{0,64},{8,72},{16,80},{24,88},{32,96},{40,104},{48,112},{56,120},{... | collective-permute-start | bytes 98312 | tf_op jit(solution)/shard_map/ppermute | solution.py:20
  11.3 1.9 collective-permute-done
  13.2 5.2 %collective-permute-start.1 = (bf16[2,64,256]{2,1,0:T(8,128)(2,1)S(1)}, bf16[2,64,256]{2,1,0:T(8,128)(2,1)S(1)}, u32[]{:S(2)}, u32[]{:S(2)}) collective-permute-start(bf16[2,64,256]{2,1,0:T(8,128)(2,1)S(1)} %maximum_select_fusion.12), channel_id=1, source_target_pairs={{0,32},{8,40},{16,48},{24,56},{32,0},{40,8},{48,16},{56,24},{64,96... | collective-permute-start | bytes 196616 | tf_op jit(solution)/shard_map/ppermute | solution.py:20
  18.4 3.6 %collective-permute-done.1 = bf16[2,64,256]{2,1,0:T(8,128)(2,1)S(1)} collective-permute-done((bf16[2,64,256]{2,1,0:T(8,128)(2,1)S(1)}, bf16[2,64,256]{2,1,0:T(8,128)(2,1)S(1)}, u32[]{:S(2)}, u32[]{:S(2)}) %collective-permute-start.1) | collective-permute-done | bytes 65568 | tf_op jit(solution)/shard_map/ppermute | solution.py:20
  22.0 4.9 %collective-permute-start.2 = (bf16[2,2,64,256]{3,2,0,1:T(8,128)(2,1)S(1)}, bf16[2,2,64,256]{3,2,0,1:T(8,128)(2,1)S(1)}, u32[]{:S(2)}, u32[]{:S(2)}) collective-permute-start(bf16[2,2,64,256]{3,2,0,1:T(8,128)(2,1)S(1)} %maximum_select_fusion.11), channel_id=1, source_target_pairs={{0,256},{128,384},{256,0},{384,128},{1,257},{129,385},{257,1},{385... | collective-permute-start | bytes 393224 | tf_op jit(solution)/shard_map/ppermute | solution.py:20
  27.0 3.4 %collective-permute-done.2 = bf16[2,2,64,256]{3,2,0,1:T(8,128)(2,1)S(1)} collective-permute-done((bf16[2,2,64,256]{3,2,0,1:T(8,128)(2,1)S(1)}, bf16[2,2,64,256]{3,2,0,1:T(8,128)(2,1)S(1)}, u32[]{:S(2)}, u32[]{:S(2)}) %collective-permute-start.2) | collective-permute-done | bytes 131104 | tf_op jit(solution)/shard_map/ppermute | solution.py:20
  30.4 2.4 collective-permute-start.3
  32.9 5.8 %collective-permute-done.3 = bf16[2,2,2,64,256]{4,3,1,2,0:T(8,128)(2,1)S(1)} collective-permute-done((bf16[2,2,2,64,256]{4,3,1,2,0:T(8,128)(2,1)S(1)}, bf16[2,2,2,64,256]{4,3,1,2,0:T(8,128)(2,1)S(1)}, u32[]{:S(2)}, u32[]{:S(2)}) %collective-permute-start.3) | collective-permute-done | bytes 262176 | tf_op jit(solution)/shard_map/ppermute | solution.py:20
  38.8 3.4 %collective-permute-start.4 = (bf16[2,2,2,2,64,256]{5,4,0,2,3,1:T(8,128)(2,1)S(1)}, bf16[2,2,2,2,64,256]{5,4,0,2,3,1:T(8,128)(2,1)S(1)}, u32[]{:S(2)}, u32[]{:S(2)}) collective-permute-start(bf16[2,2,2,2,64,256]{5,4,0,2,3,1:T(8,128)(2,1)S(1)} %maximum_select_fusion.6), channel_id=1, source_target_pairs={{0,128},{128,0},{256,384},{384,256},{1,129},{129,1},{257,385},{385... | collective-permute-start | bytes 1572872 | tf_op jit(solution)/shard_map/ppermute | solution.py:20
  42.4 7.5 %collective-permute-done.4 = bf16[2,2,2,2,64,256]{5,4,0,2,3,1:T(8,128)(2,1)S(1)} collective-permute-done((bf16[2,2,2,2,64,256]{5,4,0,2,3,1:T(8,128)(2,1)S(1)}, bf16[2,2,2,2,64,256]{5,4,0,2,3,1:T(8,128)(2,1)S(1)}, u32[]{:S(2)}, u32[]{:S(2)}) %collective-permute-start.4) | collective-permute-done | bytes 524320 | tf_op jit(solution)/shard_map/ppermute | solution.py:20
  49.8 1.2 maximum_select_fusion.2
  51.0 1.9 collective-permute-start.5
  53.1 2.8 collective-permute-done.5
  55.9 1.3 copy.167
  57.4 0.6 fusion.38
  58.0 8.2 %collective-permute-start.6 = (bf16[1,193,256]{2,1,0:T(8,128)(2,1)S(1)}, bf16[1,193,256]{2,1,0:T(8,128)(2,1)S(1)}, u32[]{:S(2)}, u32[]{:S(2)}) collective-permute-start(bf16[1,193,256]{2,1,0:T(8,128)(2,1)S(1)} %get-tuple-element.15), channel_id=1, source_target_pairs={{0,64},{8,72},{16,80},{24,88},{32,96},{40,104},{48,112},{56,120},{... | collective-permute-start | bytes 296456 | tf_op jit(solution)/shard_map/ppermute | solution.py:20
  66.2 9.8 %collective-permute-done.6 = bf16[1,193,256]{2,1,0:T(8,128)(2,1)S(1)} collective-permute-done((bf16[1,193,256]{2,1,0:T(8,128)(2,1)S(1)}, bf16[1,193,256]{2,1,0:T(8,128)(2,1)S(1)}, u32[]{:S(2)}, u32[]{:S(2)}) %collective-permute-start.6) | collective-permute-done | bytes 98848 | tf_op jit(solution)/shard_map/ppermute | solution.py:20
  76.0 2.1 collective-permute-start.7
  78.1 9.8 %collective-permute-done.7 = bf16[2,1,193,256]{3,2,0,1:T(8,128)(2,1)S(1)} collective-permute-done((bf16[2,1,193,256]{3,2,0,1:T(8,128)(2,1)S(1)}, bf16[2,1,193,256]{3,2,0,1:T(8,128)(2,1)S(1)}, u32[]{:S(2)}, u32[]{:S(2)}) %collective-permute-start.7) | collective-permute-done | bytes 197664 | tf_op jit(solution)/shard_map/ppermute | solution.py:20
  87.9 2.2 collective-permute-start.8
  90.2 9.6 %collective-permute-done.8 = bf16[2,2,1,193,256]{4,3,1,0,2:T(8,128)(2,1)S(1)} collective-permute-done((bf16[2,2,1,193,256]{4,3,1,0,2:T(8,128)(2,1)S(1)}, bf16[2,2,1,193,256]{4,3,1,0,2:T(8,128)(2,1)S(1)}, u32[]{:S(2)}, u32[]{:S(2)}) %collective-permute-start.8) | collective-permute-done | bytes 395296 | tf_op jit(solution)/shard_map/ppermute | solution.py:20
  99.9 0.6 copy.96
  100.5 1.9 collective-permute-start.9
  102.4 0.7 reshape_squeeze.6
  103.2 1.6 reshape_squeeze.7
  105.0 1.2 copy.168
  106.7 0.4 fusion.82
  108.0 2.0 fusion.7
  110.0 3.4 %select_reduce_fusion = f32[192,4]{0,1:T(4,128)S(1)} fusion(f32[3072,192,4]{0,1,2:T(8,128)S(1)} %get-tuple-element.19, f32[192,4]{0,1:T(4,128)S(1)} %get-tuple-element.18, pred[192,3072]{1,0:T(8,128)(4,1)S(1)} %broadcast_compare_fusion.1), kind=kLoop, calls=%fused_computation.8 | loop fusion | flops 11795712 | bytes 10033152 | tf_op jit(solution)/shard_map/reduce_sum | solution.py:97
  113.4 2.9 fusion.32
  116.3 5.3 %fusion.3 = bf16[192,4,3072]{2,0,1:T(8,128)(2,1)} fusion(f32[3072,192,4]{0,1,2:T(8,128)S(1)} %get-tuple-element.19, bf16[3072,128,1]{1,0,2:T(8,128)(2,1)S(1)} %bitcast.340, f32[192,4]{0,1:T(4,128)S(1)} %fusion.32, f32[192,4]{0,1:T(4,128)S(1)} %log_add_fusion, pred[192,3072]{1,0:T(8,128)(4,1)S(1)} %broadcast_compare_fusion.1, ...), kind=kOutput, calls=%fused_computation.5 | convolution fusion | flops 620494848 | bytes 15734784 | tf_op jit(solution)/shard_map/qgd,kd->qgk/dot_general | solution.py:106
  121.6 4.0 %fusion.2 = bf16[3072,4,192]{0,2,1:T(8,128)(2,1)} fusion(f32[3072,192,4]{0,1,2:T(8,128)S(1)} %get-tuple-element.19, f32[4,192]{1,0:T(4,128)S(1)} %bitcast.350, pred[3072,192]{0,1:T(8,128)(4,1)S(1)} %broadcast_compare_fusion), kind=kLoop, calls=%fused_computation.3 | loop fusion | flops 11796480 | bytes 14748672 | tf_op jit(solution)/shard_map/convert_element_type | solution.py:100
  125.6 16.2 %dot_general.34 = bf16[2,2,2,2,192,4,192]{4,3,2,1,0,6,5:T(2,128)(2,1)} reshape(bf16[3072,4,192]{0,2,1:T(8,128)(2,1)} %fusion.2) | data formatting | bytes 9437184 | tf_op jit(solution)/shard_map/qgk,qgd->kd/dot_general | solution.py:105
  141.8 3.9 %fusion.12 = bf16[3072,128]{1,0:T(8,128)(2,1)S(1)} fusion(bf16[192,4,3072]{2,0,1:T(8,128)(2,1)} %fusion.3, bf16[192,4,128]{2,1,0:T(4,128)(2,1)S(1)} %copy-done.5), kind=kOutput, calls=%fused_computation.18 | convolution fusion | flops 604766208 | bytes 5701632 | tf_op jit(solution)/shard_map/qgk,qgd->kd/dot_general | solution.py:111
  146.0 4.2 %bitcast_convert_fusion = bf16[2,2,2,2,192,128]{5,4,3,2,1,0:T(8,128)(2,1)S(1)} fusion(bf16[2,2,2,2,192,4,192]{4,3,2,1,0,6,5:T(2,128)(2,1)S(1)} %copy-done.2, bf16[192,4,128,1,1,1,1]{2,1,0,6,5,4,3:T(4,128)(2,1)S(1)} %bitcast.349), kind=kOutput, calls=%fused_computation.30 | convolution fusion | flops 604372992 | bytes 5701632 | tf_op jit(solution)/shard_map/qgk,qgd->kd/dot_general | solution.py:105
  150.4 2.4 collective-permute-start.10
  152.9 1.9 collective-permute-done.10
  155.1 3.7 %collective-permute-start.11 = (bf16[2,2,192,256]{3,2,1,0:T(8,128)(2,1)S(1)}, bf16[2,2,192,256]{3,2,1,0:T(8,128)(2,1)S(1)}, u32[]{:S(2)}, u32[]{:S(2)}) collective-permute-start(bf16[2,2,192,256]{3,2,1,0:T(8,128)(2,1)S(1)} %fusion.50), channel_id=1, source_target_pairs={{0,16},{8,24},{16,0},{24,8},{32,48},{40,56},{48,32},{56,40},{64,80... | collective-permute-start | bytes 1179656 | tf_op jit(solution)/shard_map/ppermute | solution.py:20
  158.8 9.6 %collective-permute-done.11 = bf16[2,2,192,256]{3,2,1,0:T(8,128)(2,1)S(1)} collective-permute-done((bf16[2,2,192,256]{3,2,1,0:T(8,128)(2,1)S(1)}, bf16[2,2,192,256]{3,2,1,0:T(8,128)(2,1)S(1)}, u32[]{:S(2)}, u32[]{:S(2)}) %collective-permute-start.11) | collective-permute-done | bytes 393248 | tf_op jit(solution)/shard_map/ppermute | solution.py:20
  168.6 5.3 %collective-permute-start.12 = (bf16[2,192,256]{2,1,0:T(8,128)(2,1)S(1)}, bf16[2,192,256]{2,1,0:T(8,128)(2,1)S(1)}, u32[]{:S(2)}, u32[]{:S(2)}) collective-permute-start(bf16[2,192,256]{2,1,0:T(8,128)(2,1)S(1)} %fusion.55), channel_id=1, source_target_pairs={{0,32},{8,40},{16,48},{24,56},{32,0},{40,8},{48,16},{56,24},{64,96... | collective-permute-start | bytes 589832 | tf_op jit(solution)/shard_map/ppermute | solution.py:20
  173.9 8.8 %collective-permute-done.12 = bf16[2,192,256]{2,1,0:T(8,128)(2,1)S(1)} collective-permute-done((bf16[2,192,256]{2,1,0:T(8,128)(2,1)S(1)}, bf16[2,192,256]{2,1,0:T(8,128)(2,1)S(1)}, u32[]{:S(2)}, u32[]{:S(2)}) %collective-permute-start.12) | collective-permute-done | bytes 196640 | tf_op jit(solution)/shard_map/ppermute | solution.py:20
  182.9 8.0 %collective-permute-start.13 = (bf16[192,256]{1,0:T(8,128)(2,1)S(1)}, bf16[192,256]{1,0:T(8,128)(2,1)S(1)}, u32[]{:S(2)}, u32[]{:S(2)}) collective-permute-start(bf16[192,256]{1,0:T(8,128)(2,1)S(1)} %select_bitcast_fusion.5), channel_id=1, source_target_pairs={{0,64},{8,72},{16,80},{24,88},{32,96},{40,104},{48,112},{56,120},{... | collective-permute-start | bytes 294920 | tf_op jit(solution)/shard_map/ppermute | solution.py:20
  190.9 7.2 %collective-permute-done.13 = bf16[192,256]{1,0:T(8,128)(2,1)S(1)} collective-permute-done((bf16[192,256]{1,0:T(8,128)(2,1)S(1)}, bf16[192,256]{1,0:T(8,128)(2,1)S(1)}, u32[]{:S(2)}, u32[]{:S(2)}) %collective-permute-start.13) | collective-permute-done | bytes 98336 | tf_op jit(solution)/shard_map/ppermute | solution.py:20
  198.1 2.7 convolution_bitcast_fusion
  200.8 5.6 %copy.118 = f32[4096,256]{1,0:T(8,128)} copy(f32[4096,256]{0,1:T(8,128)} %convolution_bitcast_fusion) | data formatting | bytes 8388608 | tf_op jit(solution)/shard_map/td,tc->dc/dot_general | solution.py:117
  206.4 2.8 select_bitcast_fusion
  209.2 1.9 collective-permute-start.14
  211.1 4.1 %collective-permute-done.14 = f32[2,2,2,2,2,64,256]{6,5,4,3,2,1,0:T(8,128)S(1)} collective-permute-done((f32[2,2,2,2,2,64,256]{6,5,4,3,2,1,0:T(8,128)S(1)}, f32[2,2,2,2,2,64,256]{6,5,4,3,2,1,0:T(8,128)S(1)}, u32[]{:S(2)}, u32[]{:S(2)}) %collective-permute-start.14) | collective-permute-done | bytes 2097184 | tf_op jit(solution)/shard_map/ppermute | solution.py:20
  215.2 0.6 fusion.14
  216.1 3.6 %collective-permute-start.15 = (f32[2,2,2,2,64,256]{5,4,3,2,1,0:T(8,128)S(1)}, f32[2,2,2,2,64,256]{5,4,3,2,1,0:T(8,128)S(1)}, u32[]{:S(2)}, u32[]{:S(2)}) collective-permute-start(f32[2,2,2,2,64,256]{5,4,3,2,1,0:T(8,128)S(1)} %select_bitcast_fusion.1), channel_id=1, source_target_pairs={{0,128},{128,0},{256,384},{384,256},{1,129},{129,1},{257,385},{385... | collective-permute-start | bytes 3145736 | tf_op jit(solution)/shard_map/ppermute | solution.py:20
  219.7 23.7 %collective-permute-done.15 = f32[2,2,2,2,64,256]{5,4,3,2,1,0:T(8,128)S(1)} collective-permute-done((f32[2,2,2,2,64,256]{5,4,3,2,1,0:T(8,128)S(1)}, f32[2,2,2,2,64,256]{5,4,3,2,1,0:T(8,128)S(1)}, u32[]{:S(2)}, u32[]{:S(2)}) %collective-permute-start.15) | collective-permute-done | bytes 1048608 | tf_op jit(solution)/shard_map/ppermute | solution.py:20
  243.7 1.9 collective-permute-start.16
  245.6 13.1 %collective-permute-done.16 = f32[2,2,2,64,256]{4,3,2,1,0:T(8,128)S(1)} collective-permute-done((f32[2,2,2,64,256]{4,3,2,1,0:T(8,128)S(1)}, f32[2,2,2,64,256]{4,3,2,1,0:T(8,128)S(1)}, u32[]{:S(2)}, u32[]{:S(2)}) %collective-permute-start.16) | collective-permute-done | bytes 524320 | tf_op jit(solution)/shard_map/ppermute | solution.py:20
  258.9 4.9 %collective-permute-start.17 = (f32[2,2,64,256]{3,2,1,0:T(8,128)S(1)}, f32[2,2,64,256]{3,2,1,0:T(8,128)S(1)}, u32[]{:S(2)}, u32[]{:S(2)}) collective-permute-start(f32[2,2,64,256]{3,2,1,0:T(8,128)S(1)} %select_bitcast_fusion.3), channel_id=1, source_target_pairs={{0,256},{128,384},{256,0},{384,128},{1,257},{129,385},{257,1},{385... | collective-permute-start | bytes 786440 | tf_op jit(solution)/shard_map/ppermute | solution.py:20
  263.8 5.1 %collective-permute-done.17 = f32[2,2,64,256]{3,2,1,0:T(8,128)S(1)} collective-permute-done((f32[2,2,64,256]{3,2,1,0:T(8,128)S(1)}, f32[2,2,64,256]{3,2,1,0:T(8,128)S(1)}, u32[]{:S(2)}, u32[]{:S(2)}) %collective-permute-start.17) | collective-permute-done | bytes 262176 | tf_op jit(solution)/shard_map/ppermute | solution.py:20
  269.0 2.7 collective-permute-start.18
  271.7 6.5 %collective-permute-done.18 = f32[2,64,256]{2,1,0:T(8,128)S(1)} collective-permute-done((f32[2,64,256]{2,1,0:T(8,128)S(1)}, f32[2,64,256]{2,1,0:T(8,128)S(1)}, u32[]{:S(2)}, u32[]{:S(2)}) %collective-permute-start.18) | collective-permute-done | bytes 131104 | tf_op jit(solution)/shard_map/ppermute | solution.py:20
  278.2 6.2 %collective-permute-start.19 = (f32[64,256]{1,0:T(8,128)S(1)}, f32[64,256]{1,0:T(8,128)S(1)}, u32[]{:S(2)}, u32[]{:S(2)}) collective-permute-start(f32[64,256]{1,0:T(8,128)S(1)} %select_bitcast_fusion.6), channel_id=1, source_target_pairs={{0,64},{8,72},{16,80},{24,88},{32,96},{40,104},{48,112},{56,120},{... | collective-permute-start | bytes 196616 | tf_op jit(solution)/shard_map/ppermute | solution.py:20
  284.4 1.4 fusion.22
  285.9 0.8 reshape.1433
  286.7 1.7 collective-permute-done.19
  288.4 0.6 fusion.83
  (69 shorter events, 4.5 us)
Async XLA Ops:
  0.6 56.7 %copy-start = (bf16[1,192,4096]{2,1,0:T(8,128)(2,1)S(1)}, bf16[1,192,4096]{2,1,0:T(8,128)(2,1)}, u32[]{:S(2)}) copy-start(bf16[1,192,4096]{2,1,0:T(8,128)(2,1)} %param.6) | copy-start | bytes 4718596
  2.2 11.0 %collective-permute-start = (bf16[64,256]{1,0:T(8,128)(2,1)S(1)}, bf16[64,256]{1,0:T(8,128)(2,1)S(1)}, u32[]{:S(2)}, u32[]{:S(2)}) collective-permute-start(bf16[64,256]{1,0:T(8,128)(2,1)S(1)} %constant_dynamic-update-slice_fusion), channel_id=1, source_target_pairs={{0,64},{8,72},{16,80},{24,88},{32,96},{40,104},{48,112},{56,120},{... | collective-permute-start | bytes 98312 | tf_op jit(solution)/shard_map/ppermute | solution.py:20
  13.2 8.8 %collective-permute-start.1 = (bf16[2,64,256]{2,1,0:T(8,128)(2,1)S(1)}, bf16[2,64,256]{2,1,0:T(8,128)(2,1)S(1)}, u32[]{:S(2)}, u32[]{:S(2)}) collective-permute-start(bf16[2,64,256]{2,1,0:T(8,128)(2,1)S(1)} %maximum_select_fusion.12), channel_id=1, source_target_pairs={{0,32},{8,40},{16,48},{24,56},{32,0},{40,8},{48,16},{56,24},{64,96... | collective-permute-start | bytes 196616 | tf_op jit(solution)/shard_map/ppermute | solution.py:20
  22.0 8.4 %collective-permute-start.2 = (bf16[2,2,64,256]{3,2,0,1:T(8,128)(2,1)S(1)}, bf16[2,2,64,256]{3,2,0,1:T(8,128)(2,1)S(1)}, u32[]{:S(2)}, u32[]{:S(2)}) collective-permute-start(bf16[2,2,64,256]{3,2,0,1:T(8,128)(2,1)S(1)} %maximum_select_fusion.11), channel_id=1, source_target_pairs={{0,256},{128,384},{256,0},{384,128},{1,257},{129,385},{257,1},{385... | collective-permute-start | bytes 393224 | tf_op jit(solution)/shard_map/ppermute | solution.py:20
  30.4 8.3 %collective-permute-start.3 = (bf16[2,2,2,64,256]{4,3,1,2,0:T(8,128)(2,1)S(1)}, bf16[2,2,2,64,256]{4,3,1,2,0:T(8,128)(2,1)S(1)}, u32[]{:S(2)}, u32[]{:S(2)}) collective-permute-start(bf16[2,2,2,64,256]{4,3,1,2,0:T(8,128)(2,1)S(1)} %maximum_select_fusion.9), channel_id=1, source_target_pairs={{0,16},{8,24},{16,0},{24,8},{32,48},{40,56},{48,32},{56,40},{64,80... | collective-permute-start | bytes 786440 | tf_op jit(solution)/shard_map/ppermute | solution.py:20
  38.8 11.1 %collective-permute-start.4 = (bf16[2,2,2,2,64,256]{5,4,0,2,3,1:T(8,128)(2,1)S(1)}, bf16[2,2,2,2,64,256]{5,4,0,2,3,1:T(8,128)(2,1)S(1)}, u32[]{:S(2)}, u32[]{:S(2)}) collective-permute-start(bf16[2,2,2,2,64,256]{5,4,0,2,3,1:T(8,128)(2,1)S(1)} %maximum_select_fusion.6), channel_id=1, source_target_pairs={{0,128},{128,0},{256,384},{384,256},{1,129},{129,1},{257,385},{385... | collective-permute-start | bytes 1572872 | tf_op jit(solution)/shard_map/ppermute | solution.py:20
  42.2 10.7 %copy-start.6 = (s32[1,192]{1,0:T(1,128)S(1)}, s32[1,192]{1,0:T(1,128)}, u32[]{:S(2)}) copy-start(s32[1,192]{1,0:T(1,128)} %param.9) | copy-start | bytes 2308
  51.0 4.9 %collective-permute-start.5 = (bf16[2,2,2,2,2,64,256]{6,5,1,3,4,2,0:T(8,128)(2,1)}, bf16[2,2,2,2,2,64,256]{6,5,1,3,4,2,0:T(8,128)(2,1)}, u32[]{:S(2)}, u32[]{:S(2)}) collective-permute-start(bf16[2,2,2,2,2,64,256]{6,5,1,3,4,2,0:T(8,128)(2,1)} %maximum_select_fusion.2), channel_id=1, source_target_pairs={{0,8},{8,0},{16,24},{24,16},{32,40},{40,32},{48,56},{56,48},{64,72... | collective-permute-start | bytes 3145736 | tf_op jit(solution)/shard_map/ppermute | solution.py:20
  58.0 17.9 %collective-permute-start.6 = (bf16[1,193,256]{2,1,0:T(8,128)(2,1)S(1)}, bf16[1,193,256]{2,1,0:T(8,128)(2,1)S(1)}, u32[]{:S(2)}, u32[]{:S(2)}) collective-permute-start(bf16[1,193,256]{2,1,0:T(8,128)(2,1)S(1)} %get-tuple-element.15), channel_id=1, source_target_pairs={{0,64},{8,72},{16,80},{24,88},{32,96},{40,104},{48,112},{56,120},{... | collective-permute-start | bytes 296456 | tf_op jit(solution)/shard_map/ppermute | solution.py:20
  76.0 11.9 %collective-permute-start.7 = (bf16[2,1,193,256]{3,2,0,1:T(8,128)(2,1)S(1)}, bf16[2,1,193,256]{3,2,0,1:T(8,128)(2,1)S(1)}, u32[]{:S(2)}, u32[]{:S(2)}) collective-permute-start(bf16[2,1,193,256]{3,2,0,1:T(8,128)(2,1)S(1)} %maximum_select_fusion.10), channel_id=1, source_target_pairs={{0,32},{8,40},{16,48},{24,56},{32,0},{40,8},{48,16},{56,24},{64,96... | collective-permute-start | bytes 592904 | tf_op jit(solution)/shard_map/ppermute | solution.py:20
  87.9 14.5 %copy-start.3 = (bf16[1,192,512]{2,1,0:T(8,128)(2,1)S(1)}, bf16[1,192,512]{2,1,0:T(8,128)(2,1)}, u32[]{:S(2)}) copy-start(bf16[1,192,512]{2,1,0:T(8,128)(2,1)} %param.7) | copy-start | bytes 589828
  87.9 11.8 %collective-permute-start.8 = (bf16[2,2,1,193,256]{4,3,1,0,2:T(8,128)(2,1)S(1)}, bf16[2,2,1,193,256]{4,3,1,0,2:T(8,128)(2,1)S(1)}, u32[]{:S(2)}, u32[]{:S(2)}) collective-permute-start(bf16[2,2,1,193,256]{4,3,1,0,2:T(8,128)(2,1)S(1)} %maximum_select_fusion.7), channel_id=1, source_target_pairs={{0,16},{8,24},{16,0},{24,8},{32,48},{40,56},{48,32},{56,40},{64,80... | collective-permute-start | bytes 1185800 | tf_op jit(solution)/shard_map/ppermute | solution.py:20
  100.5 4.4 %collective-permute-start.9 = (bf16[2,2,2,1,193,256]{5,2,4,3,1,0:T(2,128)(2,1)S(1)}, bf16[2,2,2,1,193,256]{5,2,4,3,1,0:T(2,128)(2,1)}, u32[]{:S(2)}, u32[]{:S(2)}) collective-permute-start(bf16[2,2,2,1,193,256]{5,2,4,3,1,0:T(2,128)(2,1)S(1)} %copy.96), channel_id=1, source_target_pairs={{0,8},{8,0},{16,24},{24,16},{32,40},{40,32},{48,56},{56,48},{64,72... | collective-permute-start | bytes 2371592 | tf_op jit(solution)/shard_map/ppermute | solution.py:20
  106.6 1.4 copy-start.5
  110.0 3.4 %copy-start.4 = (bf16[192,4,128]{2,1,0:T(4,128)(2,1)S(1)}, bf16[192,4,128]{2,1,0:T(4,128)(2,1)}, u32[]{:S(2)}) copy-start(bf16[192,4,128]{2,1,0:T(4,128)(2,1)} %reshape_squeeze.7) | copy-start | bytes 589828
  141.8 4.2 %copy-start.2 = (bf16[2,2,2,2,192,4,192]{4,3,2,1,0,6,5:T(2,128)(2,1)S(1)}, bf16[2,2,2,2,192,4,192]{4,3,2,1,0,6,5:T(2,128)(2,1)}, u32[]{:S(2)}) copy-start(bf16[2,2,2,2,192,4,192]{4,3,2,1,0,6,5:T(2,128)(2,1)} %dot_general.34) | copy-start | bytes 14155780
  150.4 4.3 %collective-permute-start.10 = (bf16[2,2,2,192,256]{4,3,2,1,0:T(8,128)(2,1)S(1)}, bf16[2,2,2,192,256]{4,3,2,1,0:T(8,128)(2,1)S(1)}, u32[]{:S(2)}, u32[]{:S(2)}) collective-permute-start(bf16[2,2,2,192,256]{4,3,2,1,0:T(8,128)(2,1)S(1)} %fusion.44), channel_id=1, source_target_pairs={{0,8},{8,0},{16,24},{24,16},{32,40},{40,32},{48,56},{56,48},{64,72... | collective-permute-start | bytes 2359304 | tf_op jit(solution)/shard_map/ppermute | solution.py:20
  155.1 13.3 %collective-permute-start.11 = (bf16[2,2,192,256]{3,2,1,0:T(8,128)(2,1)S(1)}, bf16[2,2,192,256]{3,2,1,0:T(8,128)(2,1)S(1)}, u32[]{:S(2)}, u32[]{:S(2)}) collective-permute-start(bf16[2,2,192,256]{3,2,1,0:T(8,128)(2,1)S(1)} %fusion.50), channel_id=1, source_target_pairs={{0,16},{8,24},{16,0},{24,8},{32,48},{40,56},{48,32},{56,40},{64,80... | collective-permute-start | bytes 1179656 | tf_op jit(solution)/shard_map/ppermute | solution.py:20
  168.6 14.1 %collective-permute-start.12 = (bf16[2,192,256]{2,1,0:T(8,128)(2,1)S(1)}, bf16[2,192,256]{2,1,0:T(8,128)(2,1)S(1)}, u32[]{:S(2)}, u32[]{:S(2)}) collective-permute-start(bf16[2,192,256]{2,1,0:T(8,128)(2,1)S(1)} %fusion.55), channel_id=1, source_target_pairs={{0,32},{8,40},{16,48},{24,56},{32,0},{40,8},{48,16},{56,24},{64,96... | collective-permute-start | bytes 589832 | tf_op jit(solution)/shard_map/ppermute | solution.py:20
  182.9 15.3 %collective-permute-start.13 = (bf16[192,256]{1,0:T(8,128)(2,1)S(1)}, bf16[192,256]{1,0:T(8,128)(2,1)S(1)}, u32[]{:S(2)}, u32[]{:S(2)}) collective-permute-start(bf16[192,256]{1,0:T(8,128)(2,1)S(1)} %select_bitcast_fusion.5), channel_id=1, source_target_pairs={{0,64},{8,72},{16,80},{24,88},{32,96},{40,104},{48,112},{56,120},{... | collective-permute-start | bytes 294920 | tf_op jit(solution)/shard_map/ppermute | solution.py:20
  206.4 8.8 %copy-start.1 = (f32[4096,256]{1,0:T(8,128)S(1)}, f32[4096,256]{1,0:T(8,128)}, u32[]{:S(2)}) copy-start(f32[4096,256]{1,0:T(8,128)} %copy.118) | copy-start | bytes 12582916
  209.2 6.1 %collective-permute-start.14 = (f32[2,2,2,2,2,64,256]{6,5,4,3,2,1,0:T(8,128)S(1)}, f32[2,2,2,2,2,64,256]{6,5,4,3,2,1,0:T(8,128)S(1)}, u32[]{:S(2)}, u32[]{:S(2)}) collective-permute-start(f32[2,2,2,2,2,64,256]{6,5,4,3,2,1,0:T(8,128)S(1)} %select_bitcast_fusion), channel_id=1, source_target_pairs={{0,8},{8,0},{16,24},{24,16},{32,40},{40,32},{48,56},{56,48},{64,72... | collective-permute-start | bytes 6291464 | tf_op jit(solution)/shard_map/ppermute | solution.py:20
  215.9 68.5 %slice-start = ((s8[4718592]{0:T(1024)(128)(4,1)}), s8[4194304]{0:T(1024)(128)(4,1)S(1)}, s32[]{:S(2)}) async-start(s8[4718592]{0:T(1024)(128)(4,1)} %bitcast.351), calls=%async_computation | async-start | bytes 8388608
  216.0 68.3 %slice-start.1 = ((s8[4718592]{0:T(1024)(128)(4,1)}), s8[524288]{0:T(1024)(128)(4,1)S(1)}, s32[]{:S(2)}) async-start(s8[4718592]{0:T(1024)(128)(4,1)} %bitcast.351), calls=%async_computation.1 | async-start | bytes 1048576
  216.1 27.4 %collective-permute-start.15 = (f32[2,2,2,2,64,256]{5,4,3,2,1,0:T(8,128)S(1)}, f32[2,2,2,2,64,256]{5,4,3,2,1,0:T(8,128)S(1)}, u32[]{:S(2)}, u32[]{:S(2)}) collective-permute-start(f32[2,2,2,2,64,256]{5,4,3,2,1,0:T(8,128)S(1)} %select_bitcast_fusion.1), channel_id=1, source_target_pairs={{0,128},{128,0},{256,384},{384,256},{1,129},{129,1},{257,385},{385... | collective-permute-start | bytes 3145736 | tf_op jit(solution)/shard_map/ppermute | solution.py:20
  243.7 15.0 %collective-permute-start.16 = (f32[2,2,2,64,256]{4,3,2,1,0:T(8,128)S(1)}, f32[2,2,2,64,256]{4,3,2,1,0:T(8,128)S(1)}, u32[]{:S(2)}, u32[]{:S(2)}) collective-permute-start(f32[2,2,2,64,256]{4,3,2,1,0:T(8,128)S(1)} %select_bitcast_fusion.2), channel_id=1, source_target_pairs={{0,16},{8,24},{16,0},{24,8},{32,48},{40,56},{48,32},{56,40},{64,80... | collective-permute-start | bytes 1572872 | tf_op jit(solution)/shard_map/ppermute | solution.py:20
  258.9 10.0 %collective-permute-start.17 = (f32[2,2,64,256]{3,2,1,0:T(8,128)S(1)}, f32[2,2,64,256]{3,2,1,0:T(8,128)S(1)}, u32[]{:S(2)}, u32[]{:S(2)}) collective-permute-start(f32[2,2,64,256]{3,2,1,0:T(8,128)S(1)} %select_bitcast_fusion.3), channel_id=1, source_target_pairs={{0,256},{128,384},{256,0},{384,128},{1,257},{129,385},{257,1},{385... | collective-permute-start | bytes 786440 | tf_op jit(solution)/shard_map/ppermute | solution.py:20
  269.0 9.2 %collective-permute-start.18 = (f32[2,64,256]{2,1,0:T(8,128)S(1)}, f32[2,64,256]{2,1,0:T(8,128)S(1)}, u32[]{:S(2)}, u32[]{:S(2)}) collective-permute-start(f32[2,64,256]{2,1,0:T(8,128)S(1)} %select_bitcast_fusion.4), channel_id=1, source_target_pairs={{0,32},{8,40},{16,48},{24,56},{32,0},{40,8},{48,16},{56,24},{64,96... | collective-permute-start | bytes 393224 | tf_op jit(solution)/shard_map/ppermute | solution.py:20
  278.2 10.2 %collective-permute-start.19 = (f32[64,256]{1,0:T(8,128)S(1)}, f32[64,256]{1,0:T(8,128)S(1)}, u32[]{:S(2)}, u32[]{:S(2)}) collective-permute-start(f32[64,256]{1,0:T(8,128)S(1)} %select_bitcast_fusion.6), channel_id=1, source_target_pairs={{0,64},{8,72},{16,80},{24,88},{32,96},{40,104},{48,112},{56,120},{... | collective-permute-start | bytes 196616 | tf_op jit(solution)/shard_map/ppermute | solution.py:20

commit v3 on v2

--- a/solution.py
+++ b/solution.py
@@ -72,17 +72,25 @@
     def step(axis, bit):
         return (axis, n_dp if axis == "dp" else n_ctx, bit)
 
-    far_first = [step(a, b) for a, b in both_canon[::-1]]
-    far_first = sorted(far_first, key=lambda s: (-(s[2] + (1 if s[0] == "dp" else 0))))
-    near_first = far_first[::-1]
+    ctx_far = [step("context", b) for b in reversed(range(_bits(n_ctx)))]
+    dp_far = [step("dp", b) for b in reversed(range(_bits(n_dp)))]
+    def interleave(first, second):
+        out = []
+        for k in range(max(len(first), len(second))):
+            out += first[k:k + 1] + second[k:k + 1]
+        return out
 
-    proj = jnp.concatenate([key_proj, value_proj], axis=1)
-    proj_all = gather_blocks(proj, far_first, both_canon)
+    order_a = ctx_far[:1] + interleave(ctx_far[1:-1], dp_far) + ctx_far[-1:]
+    order_b = ctx_far[:1] + interleave(dp_far, ctx_far[1:-1]) + ctx_far[-1:]
+
+    key_all = gather_blocks(key_proj, order_a, both_canon)
+    value_all = gather_blocks(value_proj, order_b, both_canon)
+    proj_all = jnp.concatenate([key_all, value_all], axis=1)
     kv = jnp.dot(local_rows, proj_all, preferred_element_type=jnp.float32).astype(jnp.bfloat16)
     marks = segment[0].astype(jnp.bfloat16)
     marks_row = jnp.pad(marks, (0, 2 * HEAD_DIM - tok_rows))[None, :]
     kvm = jnp.concatenate([kv, marks_row], axis=0)[None]
-    ctx_far_first = [step("context", b) for b in reversed(range(_bits(n_ctx)))]
+    ctx_far_first = ctx_far
     kvm_all = gather_blocks(kvm, ctx_far_first, ctx_canon)
     keys = kvm_all[:, :tok_rows, :HEAD_DIM].reshape(-1, HEAD_DIM)
     values = kvm_all[:, :tok_rows, HEAD_DIM:].reshape(-1, HEAD_DIM)
@@ -115,9 +123,10 @@
     kv_grad = scatter_sum(kv_part, ctx_near_first, ctx_canon, jnp.float32).astype(jnp.bfloat16)
 
     proj_part = jnp.einsum("td,tc->dc", local_rows, kv_grad, preferred_element_type=jnp.float32)
-    summed = scatter_sum(proj_part, near_first, both_canon)
+    key_sum = scatter_sum(proj_part[:, :width_kv], order_a[::-1], both_canon)
+    value_sum = scatter_sum(proj_part[:, width_kv:], order_b[::-1], both_canon)
     grad_queries = grad_q.reshape(1, tok_rows, group * HEAD_DIM)
-    return (grad_queries, summed[:, :width_kv], summed[:, width_kv:])
+    return (grad_queries, key_sum, value_sum)
 
 
 def solution(mesh):

time: 293 us -> 290 us (0.990)
  waiting for transfers between devices: 136 us -> 105 us
  starting transfers between devices: 81.9 us -> 97.4 us
  other arithmetic: 15.8 us -> 25.1 us
  local copies, waits for them, and re-layouts: 31.4 us -> 37.2 us
    ppermute x20 -> x32, waiting for transfers between devices: 136 us -> 105 us  [_exchange(): return lax.ppermute(x, axis, perm)]
    ppermute x20 -> x32, starting transfers between devices: 81.9 us -> 97.4 us  [_exchange(): return lax.ppermute(x, axis, perm)]
    slice x1 -> x5, local copies, waits for them, and re-layouts: 0.63 us -> 11.6 us  [the longest x2 5.15 us: body(): value_sum = scatter_sum(proj_part[:, width_kv:], order_b[::-1], both_canon)]
    dot_general x1 -> x0, local copies, waits for them, and re-layouts: 5.6 us -> none  [body(): jnp.einsum('td,tc->dc', local_rows, kv_grad, preferred_element_type=jnp.f...]
    add x6 -> x12, other arithmetic: 1.04 us -> 5.86 us  [scatter_sum(): total = keep.astype(acc) + _exchange(send, axis, size, bit).astype(acc)]
    select_n x14 -> x24, other arithmetic: 1.93 us -> 5.63 us  [gather_blocks(): cur = jnp.where(mine, jnp.stack([recv, cur]), jnp.stack([cur, recv]))]
  transfers between devices with their start and end apart: 20 -> 32, of which waited for: 19 -> 23; matrix products, arithmetic and copies ran while one was open for 2% -> 8% of each run, Pallas kernels for 0% -> 0%
where the time goes in v3:
time: 290 us; the launch traced here: 288 us
  waiting for transfers between devices  105 us (36%)
  starting transfers between devices  97.4 us (34%)
  local copies, waits for them, and re-layouts  37.2 us (13%)
  other arithmetic  25.1 us (9%)
  matrix products  21.1 us (7%)
    ppermute x32, waiting for transfers between devices, _exchange(): return lax.ppermute(x, axis, perm)  105 us
    ppermute x32, starting transfers between devices, _exchange(): return lax.ppermute(x, axis, perm)  97.4 us
    dot_general x1, local copies, waits for them, and re-layouts, body(): jnp.einsum('qgk,qgd->kd', probs_b, do, preferred_element_type=jnp.float32)  16.2 us
    add x12, other arithmetic, scatter_sum(): total = keep.astype(acc) + _exchange(send, axis, size, bit).astype(acc)  5.86 us
  transfers between devices with their start and end apart: 32, of which 23 were waited for; matrix products, arithmetic and copies ran while one was open for 8% of the time, Pallas kernels for 0%

profile of v3, /device:TPU:24, one launch (start us, length us, event | category | flops | bytes accessed | tf_op | source)
XLA Modules:
  0.0 287.9 jit_solution(5313306917917509691)
XLA Ops:
  0.7 9.2 %collective-permute-start.6 = (bf16[64,128]{1,0:T(8,128)(2,1)}, bf16[64,128]{1,0:T(8,128)(2,1)S(1)}, u32[]{:S(2)}, u32[]{:S(2)}) collective-permute-start(bf16[64,128]{1,0:T(8,128)(2,1)} %param.11), channel_id=1, source_target_pairs={{0,64},{8,72},{16,80},{24,88},{32,96},{40,104},{48,112},{56,120},{... | collective-permute-start | bytes 49160 | tf_op jit(solution)/shard_map/ppermute | solution.py:20
  9.9 1.9 collective-permute-start
  13.5 6.3 %collective-permute-done = bf16[64,128]{1,0:T(8,128)(2,1)S(1)} collective-permute-done((bf16[64,128]{1,0:T(8,128)(2,1)}, bf16[64,128]{1,0:T(8,128)(2,1)S(1)}, u32[]{:S(2)}, u32[]{:S(2)}) %collective-permute-start) | collective-permute-done | bytes 16416 | tf_op jit(solution)/shard_map/ppermute | solution.py:20
  22.2 4.9 %collective-permute-start.7 = (bf16[2,64,128]{2,1,0:T(8,128)(2,1)S(1)}, bf16[2,64,128]{2,1,0:T(8,128)(2,1)S(1)}, u32[]{:S(2)}, u32[]{:S(2)}) collective-permute-start(bf16[2,64,128]{2,1,0:T(8,128)(2,1)S(1)} %maximum_select_fusion.22), channel_id=1, source_target_pairs={{0,256},{128,384},{256,0},{384,128},{1,257},{129,385},{257,1},{385... | collective-permute-start | bytes 98312 | tf_op jit(solution)/shard_map/ppermute | solution.py:20
  27.9 5.2 %collective-permute-start.1 = (bf16[2,64,128]{2,1,0:T(8,128)(2,1)S(1)}, bf16[2,64,128]{2,1,0:T(8,128)(2,1)S(1)}, u32[]{:S(2)}, u32[]{:S(2)}) collective-permute-start(bf16[2,64,128]{2,1,0:T(8,128)(2,1)S(1)} %maximum_select_fusion.21), channel_id=1, source_target_pairs={{0,32},{8,40},{16,48},{24,56},{32,0},{40,8},{48,16},{56,24},{64,96... | collective-permute-start | bytes 98312 | tf_op jit(solution)/shard_map/ppermute | solution.py:20
  33.1 1.9 collective-permute-start.8
  35.1 4.6 %collective-permute-start.2 = (bf16[2,2,64,128]{3,2,0,1:T(8,128)(2,1)S(1)}, bf16[2,2,64,128]{3,2,0,1:T(8,128)(2,1)S(1)}, u32[]{:S(2)}, u32[]{:S(2)}) collective-permute-start(bf16[2,2,64,128]{3,2,0,1:T(8,128)(2,1)S(1)} %maximum_select_fusion.18), channel_id=1, source_target_pairs={{0,256},{128,384},{256,0},{384,128},{1,257},{129,385},{257,1},{385... | collective-permute-start | bytes 196616 | tf_op jit(solution)/shard_map/ppermute | solution.py:20
  40.2 2.5 collective-permute-start.9
  43.4 3.7 %collective-permute-start.3 = (bf16[2,2,2,64,128]{4,3,1,2,0:T(8,128)(2,1)S(1)}, bf16[2,2,2,64,128]{4,3,1,2,0:T(8,128)(2,1)S(1)}, u32[]{:S(2)}, u32[]{:S(2)}) collective-permute-start(bf16[2,2,2,64,128]{4,3,1,2,0:T(8,128)(2,1)S(1)} %maximum_select_fusion.15), channel_id=1, source_target_pairs={{0,16},{8,24},{16,0},{24,8},{32,48},{40,56},{48,32},{56,40},{64,80... | collective-permute-start | bytes 393224 | tf_op jit(solution)/shard_map/ppermute | solution.py:20
  47.2 3.5 %collective-permute-start.10 = (bf16[2,2,2,2,64,128]{5,4,3,2,1,0:T(8,128)(2,1)S(1)}, bf16[2,2,2,2,64,128]{5,4,3,2,1,0:T(8,128)(2,1)S(1)}, u32[]{:S(2)}, u32[]{:S(2)}) collective-permute-start(bf16[2,2,2,2,64,128]{5,4,3,2,1,0:T(8,128)(2,1)S(1)} %maximum_select_fusion.12), channel_id=1, source_target_pairs={{0,16},{8,24},{16,0},{24,8},{32,48},{40,56},{48,32},{56,40},{64,80... | collective-permute-start | bytes 786440 | tf_op jit(solution)/shard_map/ppermute | solution.py:20
  51.7 2.7 collective-permute-start.4
  56.4 1.9 collective-permute-start.11
  58.3 1.7 collective-permute-done.4
  60.8 1.9 collective-permute-start.5
  63.3 1.7 collective-permute-done.5
  66.8 2.1 collective-permute-start.12
  68.9 15.4 %collective-permute-done.12 = bf16[1,193,256]{2,1,0:T(8,128)(2,1)S(1)} collective-permute-done((bf16[1,193,256]{2,1,0:T(8,128)(2,1)S(1)}, bf16[1,193,256]{2,1,0:T(8,128)(2,1)S(1)}, u32[]{:S(2)}, u32[]{:S(2)}) %collective-permute-start.12) | collective-permute-done | bytes 98848 | tf_op jit(solution)/shard_map/ppermute | solution.py:20
  84.3 1.9 collective-permute-start.13
  86.3 10.6 %collective-permute-done.13 = bf16[2,1,193,256]{3,2,0,1:T(8,128)(2,1)S(1)} collective-permute-done((bf16[2,1,193,256]{3,2,0,1:T(8,128)(2,1)S(1)}, bf16[2,1,193,256]{3,2,0,1:T(8,128)(2,1)S(1)}, u32[]{:S(2)}, u32[]{:S(2)}) %collective-permute-start.13) | collective-permute-done | bytes 197664 | tf_op jit(solution)/shard_map/ppermute | solution.py:20
  97.0 1.9 collective-permute-start.14
  99.0 11.3 %collective-permute-done.14 = bf16[2,2,1,193,256]{4,3,1,0,2:T(8,128)(2,1)S(1)} collective-permute-done((bf16[2,2,1,193,256]{4,3,1,0,2:T(8,128)(2,1)S(1)}, bf16[2,2,1,193,256]{4,3,1,0,2:T(8,128)(2,1)S(1)}, u32[]{:S(2)}, u32[]{:S(2)}) %collective-permute-start.14) | collective-permute-done | bytes 395296 | tf_op jit(solution)/shard_map/ppermute | solution.py:20
  111.0 1.9 collective-permute-start.15
  113.7 1.6 reshape_squeeze.7
  118.5 2.0 fusion.7
  120.5 3.4 %select_reduce_fusion = f32[192,4]{0,1:T(4,128)S(1)} fusion(f32[3072,192,4]{0,1,2:T(8,128)S(1)} %get-tuple-element.26, f32[192,4]{0,1:T(4,128)S(1)} %get-tuple-element.25, pred[192,3072]{1,0:T(8,128)(4,1)S(1)} %broadcast_compare_fusion.1), kind=kLoop, calls=%fused_computation.8 | loop fusion | flops 11795712 | bytes 10033152 | tf_op jit(solution)/shard_map/reduce_sum | solution.py:105
  123.9 2.9 %fusion.33 = f32[192,4]{0,1:T(4,128)S(1)} fusion(bf16[3072,128,1]{1,0,2:T(8,128)(2,1)S(1)} %bitcast.364, f32[3072,192,4]{0,1,2:T(8,128)S(1)} %get-tuple-element.26, f32[192,4]{0,1:T(4,128)S(1)} %log_add_fusion, pred[192,3072]{1,0:T(8,128)(4,1)S(1)} %broadcast_compare_fusion.1, bf16[192,4,128]{2,1,0:T(4,128)(2,1)S(1)} %copy-done.8), kind=kOutput, calls=%fused_computation.38 | convolution fusion | flops 616267008 | bytes 11016192 | tf_op jit(solution)/shard_map/qgk,kd->qgd/dot_general | solution.py:109
  126.8 5.3 %fusion.3 = bf16[192,4,3072]{2,0,1:T(8,128)(2,1)} fusion(f32[3072,192,4]{0,1,2:T(8,128)S(1)} %get-tuple-element.26, bf16[3072,128,1]{1,0,2:T(8,128)(2,1)S(1)} %bitcast.365, f32[192,4]{0,1:T(4,128)S(1)} %fusion.33, f32[192,4]{0,1:T(4,128)S(1)} %log_add_fusion, pred[192,3072]{1,0:T(8,128)(4,1)S(1)} %broadcast_compare_fusion.1, ...), kind=kOutput, calls=%fused_computation.5 | convolution fusion | flops 620494848 | bytes 15734784 | tf_op jit(solution)/shard_map/qgd,kd->qgk/dot_general | solution.py:114
  132.2 3.9 %fusion.2 = bf16[3072,4,192]{0,2,1:T(8,128)(2,1)} fusion(f32[3072,192,4]{0,1,2:T(8,128)S(1)} %get-tuple-element.26, f32[4,192]{1,0:T(4,128)S(1)} %bitcast.393, pred[3072,192]{0,1:T(8,128)(4,1)S(1)} %broadcast_compare_fusion), kind=kLoop, calls=%fused_computation.3 | loop fusion | flops 11796480 | bytes 14748672 | tf_op jit(solution)/shard_map/convert_element_type | solution.py:108
  136.1 16.2 %dot_general.34 = bf16[2,2,2,2,192,4,192]{4,3,2,1,0,6,5:T(2,128)(2,1)} reshape(bf16[3072,4,192]{0,2,1:T(8,128)(2,1)} %fusion.2) | data formatting | bytes 9437184 | tf_op jit(solution)/shard_map/qgk,qgd->kd/dot_general | solution.py:113
  152.3 3.9 %fusion.12 = bf16[3072,128]{1,0:T(8,128)(2,1)S(1)} fusion(bf16[192,4,3072]{2,0,1:T(8,128)(2,1)} %fusion.3, bf16[192,4,128]{2,1,0:T(4,128)(2,1)S(1)} %copy-done.10), kind=kOutput, calls=%fused_computation.18 | convolution fusion | flops 604766208 | bytes 5701632 | tf_op jit(solution)/shard_map/qgk,qgd->kd/dot_general | solution.py:119
  156.5 4.2 %bitcast_convert_fusion = bf16[2,2,2,2,192,128]{5,4,3,2,1,0:T(8,128)(2,1)S(1)} fusion(bf16[2,2,2,2,192,4,192]{4,3,2,1,0,6,5:T(2,128)(2,1)S(1)} %copy-done.6, bf16[192,4,128,1,1,1,1]{2,1,0,6,5,4,3:T(4,128)(2,1)S(1)} %bitcast.378), kind=kOutput, calls=%fused_computation.29 | convolution fusion | flops 604372992 | bytes 5701632 | tf_op jit(solution)/shard_map/qgk,qgd->kd/dot_general | solution.py:113
  160.9 2.4 collective-permute-start.16
  163.3 1.9 collective-permute-done.16
  165.6 2.2 collective-permute-start.17
  167.8 11.1 %collective-permute-done.17 = bf16[2,2,192,256]{3,2,1,0:T(8,128)(2,1)S(1)} collective-permute-done((bf16[2,2,192,256]{3,2,1,0:T(8,128)(2,1)S(1)}, bf16[2,2,192,256]{3,2,1,0:T(8,128)(2,1)S(1)}, u32[]{:S(2)}, u32[]{:S(2)}) %collective-permute-start.17) | collective-permute-done | bytes 393248 | tf_op jit(solution)/shard_map/ppermute | solution.py:20
  179.1 1.9 collective-permute-start.18
  181.0 11.2 %collective-permute-done.18 = bf16[2,192,256]{2,1,0:T(8,128)(2,1)S(1)} collective-permute-done((bf16[2,192,256]{2,1,0:T(8,128)(2,1)S(1)}, bf16[2,192,256]{2,1,0:T(8,128)(2,1)S(1)}, u32[]{:S(2)}, u32[]{:S(2)}) %collective-permute-start.18) | collective-permute-done | bytes 196640 | tf_op jit(solution)/shard_map/ppermute | solution.py:20
  192.3 1.9 collective-permute-start.19
  194.2 11.7 %collective-permute-done.19 = bf16[192,256]{1,0:T(8,128)(2,1)S(1)} collective-permute-done((bf16[192,256]{1,0:T(8,128)(2,1)S(1)}, bf16[192,256]{1,0:T(8,128)(2,1)S(1)}, u32[]{:S(2)}, u32[]{:S(2)}) %collective-permute-start.19) | collective-permute-done | bytes 98336 | tf_op jit(solution)/shard_map/ppermute | solution.py:20
  206.7 2.3 fusion.87
  208.9 2.9 %copy.141 = f32[4096,128]{1,0:T(8,128)} copy(f32[4096,128]{0,1:T(8,128)} %get-tuple-element.4) | data formatting | bytes 4194304 | tf_op jit(solution)/shard_map/slice | solution.py:126
  211.9 1.7 fusion.89
  214.9 1.9 collective-permute-start.20
  216.8 2.9 %copy.156 = f32[4096,128]{1,0:T(8,128)} copy(f32[4096,128]{0,1:T(8,128)} %get-tuple-element.3) | data formatting | bytes 4194304 | tf_op jit(solution)/shard_map/slice | solution.py:127
  219.7 1.8 fusion.88
  221.8 2.5 collective-permute-start.26
  224.3 1.5 bitcast_add_fusion.1
  226.8 2.6 collective-permute-start.21
  231.6 1.9 collective-permute-start.27
  233.5 1.4 fusion.23
  235.8 7.0 %collective-permute-done.21 = f32[2,2,2,2,64,128]{5,4,1,0,2,3:T(8,128)} collective-permute-done((f32[2,2,2,2,64,128]{5,4,1,0,2,3:T(8,128)}, f32[2,2,2,2,64,128]{5,4,1,0,2,3:T(8,128)}, u32[]{:S(2)}, u32[]{:S(2)}) %collective-permute-start.21) | collective-permute-done | bytes 524320 | tf_op jit(solution)/shard_map/ppermute | solution.py:20
  244.0 1.9 collective-permute-start.22
  245.9 1.4 collective-permute-done.27
  247.3 1.5 bitcast_add_fusion.2
  248.8 3.4 %collective-permute-start.28 = (f32[2,2,2,64,128]{4,3,1,0,2:T(8,128)S(1)}, f32[2,2,2,64,128]{4,3,1,0,2:T(8,128)S(1)}, u32[]{:S(2)}, u32[]{:S(2)}) collective-permute-start(f32[2,2,2,64,128]{4,3,1,0,2:T(8,128)S(1)} %select_bitcast_fusion.4), channel_id=1, source_target_pairs={{0,128},{128,0},{256,384},{384,256},{1,129},{129,1},{257,385},{385... | collective-permute-start | bytes 786440 | tf_op jit(solution)/shard_map/ppermute | solution.py:20
  253.4 4.4 %collective-permute-start.23 = (f32[2,2,64,128]{3,2,1,0:T(8,128)S(1)}, f32[2,2,64,128]{3,2,1,0:T(8,128)S(1)}, u32[]{:S(2)}, u32[]{:S(2)}) collective-permute-start(f32[2,2,64,128]{3,2,1,0:T(8,128)S(1)} %fusion.67), channel_id=1, source_target_pairs={{0,256},{128,384},{256,0},{384,128},{1,257},{129,385},{257,1},{385... | collective-permute-start | bytes 393224 | tf_op jit(solution)/shard_map/ppermute | solution.py:20
  258.5 1.9 collective-permute-start.29
  260.5 1.6 collective-permute-done.23
  262.1 3.2 %collective-permute-start.24 = (f32[2,64,128]{2,1,0:T(8,128)S(1)}, f32[2,64,128]{2,1,0:T(8,128)S(1)}, u32[]{:S(2)}, u32[]{:S(2)}) collective-permute-start(f32[2,64,128]{2,1,0:T(8,128)S(1)} %select_bitcast_fusion.10), channel_id=1, source_target_pairs={{0,32},{8,40},{16,48},{24,56},{32,0},{40,8},{48,16},{56,24},{64,96... | collective-permute-start | bytes 196616 | tf_op jit(solution)/shard_map/ppermute | solution.py:20
  265.4 4.5 %collective-permute-done.29 = f32[2,2,64,128]{3,2,1,0:T(8,128)S(1)} collective-permute-done((f32[2,2,64,128]{3,2,1,0:T(8,128)S(1)}, f32[2,2,64,128]{3,2,1,0:T(8,128)S(1)}, u32[]{:S(2)}, u32[]{:S(2)}) %collective-permute-start.29) | collective-permute-done | bytes 131104 | tf_op jit(solution)/shard_map/ppermute | solution.py:20
  269.9 4.3 %collective-permute-start.30 = (f32[2,64,128]{2,1,0:T(8,128)S(1)}, f32[2,64,128]{2,1,0:T(8,128)S(1)}, u32[]{:S(2)}, u32[]{:S(2)}) collective-permute-start(f32[2,64,128]{2,1,0:T(8,128)S(1)} %select_bitcast_fusion.9), channel_id=1, source_target_pairs={{0,256},{128,384},{256,0},{384,128},{1,257},{129,385},{257,1},{385... | collective-permute-start | bytes 196616 | tf_op jit(solution)/shard_map/ppermute | solution.py:20
  274.3 2.4 collective-permute-start.25
  277.6 6.5 %collective-permute-start.31 = (f32[64,128]{1,0:T(8,128)S(1)}, f32[64,128]{1,0:T(8,128)S(1)}, u32[]{:S(2)}, u32[]{:S(2)}) collective-permute-start(f32[64,128]{1,0:T(8,128)S(1)} %select_bitcast_fusion.11), channel_id=1, source_target_pairs={{0,64},{8,72},{16,80},{24,88},{32,96},{40,104},{48,112},{56,120},{... | collective-permute-start | bytes 98312 | tf_op jit(solution)/shard_map/ppermute | solution.py:20
  284.8 2.5 collective-permute-done.31
  (133 shorter events, 29.7 us)
Async XLA Ops:
  0.6 65.5 %copy-start = (bf16[1,192,4096]{2,1,0:T(8,128)(2,1)S(1)}, bf16[1,192,4096]{2,1,0:T(8,128)(2,1)}, u32[]{:S(2)}) copy-start(bf16[1,192,4096]{2,1,0:T(8,128)(2,1)} %param.6) | copy-start | bytes 4718596
  0.6 62.1 %copy-start.11 = (s32[1,192]{1,0:T(1,128)S(1)}, s32[1,192]{1,0:T(1,128)}, u32[]{:S(2)}) copy-start(s32[1,192]{1,0:T(1,128)} %param.9) | copy-start | bytes 2308
  0.7 11.2 %collective-permute-start.6 = (bf16[64,128]{1,0:T(8,128)(2,1)}, bf16[64,128]{1,0:T(8,128)(2,1)S(1)}, u32[]{:S(2)}, u32[]{:S(2)}) collective-permute-start(bf16[64,128]{1,0:T(8,128)(2,1)} %param.11), channel_id=1, source_target_pairs={{0,64},{8,72},{16,80},{24,88},{32,96},{40,104},{48,112},{56,120},{... | collective-permute-start | bytes 49160 | tf_op jit(solution)/shard_map/ppermute | solution.py:20
  9.9 9.9 %collective-permute-start = (bf16[64,128]{1,0:T(8,128)(2,1)}, bf16[64,128]{1,0:T(8,128)(2,1)S(1)}, u32[]{:S(2)}, u32[]{:S(2)}) collective-permute-start(bf16[64,128]{1,0:T(8,128)(2,1)} %param.10), channel_id=1, source_target_pairs={{0,64},{8,72},{16,80},{24,88},{32,96},{40,104},{48,112},{56,120},{... | collective-permute-start | bytes 49160 | tf_op jit(solution)/shard_map/ppermute | solution.py:20
  22.2 10.9 %collective-permute-start.7 = (bf16[2,64,128]{2,1,0:T(8,128)(2,1)S(1)}, bf16[2,64,128]{2,1,0:T(8,128)(2,1)S(1)}, u32[]{:S(2)}, u32[]{:S(2)}) collective-permute-start(bf16[2,64,128]{2,1,0:T(8,128)(2,1)S(1)} %maximum_select_fusion.22), channel_id=1, source_target_pairs={{0,256},{128,384},{256,0},{384,128},{1,257},{129,385},{257,1},{385... | collective-permute-start | bytes 98312 | tf_op jit(solution)/shard_map/ppermute | solution.py:20
  27.9 7.1 %collective-permute-start.1 = (bf16[2,64,128]{2,1,0:T(8,128)(2,1)S(1)}, bf16[2,64,128]{2,1,0:T(8,128)(2,1)S(1)}, u32[]{:S(2)}, u32[]{:S(2)}) collective-permute-start(bf16[2,64,128]{2,1,0:T(8,128)(2,1)S(1)} %maximum_select_fusion.21), channel_id=1, source_target_pairs={{0,32},{8,40},{16,48},{24,56},{32,0},{40,8},{48,16},{56,24},{64,96... | collective-permute-start | bytes 98312 | tf_op jit(solution)/shard_map/ppermute | solution.py:20
  33.1 7.1 %collective-permute-start.8 = (bf16[2,2,64,128]{3,2,1,0:T(8,128)(2,1)S(1)}, bf16[2,2,64,128]{3,2,1,0:T(8,128)(2,1)S(1)}, u32[]{:S(2)}, u32[]{:S(2)}) collective-permute-start(bf16[2,2,64,128]{3,2,1,0:T(8,128)(2,1)S(1)} %maximum_select_fusion.19), channel_id=1, source_target_pairs={{0,32},{8,40},{16,48},{24,56},{32,0},{40,8},{48,16},{56,24},{64,96... | collective-permute-start | bytes 196616 | tf_op jit(solution)/shard_map/ppermute | solution.py:20
  35.1 8.4 %collective-permute-start.2 = (bf16[2,2,64,128]{3,2,0,1:T(8,128)(2,1)S(1)}, bf16[2,2,64,128]{3,2,0,1:T(8,128)(2,1)S(1)}, u32[]{:S(2)}, u32[]{:S(2)}) collective-permute-start(bf16[2,2,64,128]{3,2,0,1:T(8,128)(2,1)S(1)} %maximum_select_fusion.18), channel_id=1, source_target_pairs={{0,256},{128,384},{256,0},{384,128},{1,257},{129,385},{257,1},{385... | collective-permute-start | bytes 196616 | tf_op jit(solution)/shard_map/ppermute | solution.py:20
  40.2 7.0 %collective-permute-start.9 = (bf16[2,2,2,64,128]{4,3,2,1,0:T(8,128)(2,1)S(1)}, bf16[2,2,2,64,128]{4,3,2,1,0:T(8,128)(2,1)S(1)}, u32[]{:S(2)}, u32[]{:S(2)}) collective-permute-start(bf16[2,2,2,64,128]{4,3,2,1,0:T(8,128)(2,1)S(1)} %maximum_select_fusion.16), channel_id=1, source_target_pairs={{0,128},{128,0},{256,384},{384,256},{1,129},{129,1},{257,385},{385... | collective-permute-start | bytes 393224 | tf_op jit(solution)/shard_map/ppermute | solution.py:20
  43.4 8.2 %collective-permute-start.3 = (bf16[2,2,2,64,128]{4,3,1,2,0:T(8,128)(2,1)S(1)}, bf16[2,2,2,64,128]{4,3,1,2,0:T(8,128)(2,1)S(1)}, u32[]{:S(2)}, u32[]{:S(2)}) collective-permute-start(bf16[2,2,2,64,128]{4,3,1,2,0:T(8,128)(2,1)S(1)} %maximum_select_fusion.15), channel_id=1, source_target_pairs={{0,16},{8,24},{16,0},{24,8},{32,48},{40,56},{48,32},{56,40},{64,80... | collective-permute-start | bytes 393224 | tf_op jit(solution)/shard_map/ppermute | solution.py:20
  47.2 8.3 %collective-permute-start.10 = (bf16[2,2,2,2,64,128]{5,4,3,2,1,0:T(8,128)(2,1)S(1)}, bf16[2,2,2,2,64,128]{5,4,3,2,1,0:T(8,128)(2,1)S(1)}, u32[]{:S(2)}, u32[]{:S(2)}) collective-permute-start(bf16[2,2,2,2,64,128]{5,4,3,2,1,0:T(8,128)(2,1)S(1)} %maximum_select_fusion.12), channel_id=1, source_target_pairs={{0,16},{8,24},{16,0},{24,8},{32,48},{40,56},{48,32},{56,40},{64,80... | collective-permute-start | bytes 786440 | tf_op jit(solution)/shard_map/ppermute | solution.py:20
  51.7 8.3 %collective-permute-start.4 = (bf16[2,2,2,2,64,128]{5,4,0,2,3,1:T(8,128)(2,1)S(1)}, bf16[2,2,2,2,64,128]{5,4,0,2,3,1:T(8,128)(2,1)S(1)}, u32[]{:S(2)}, u32[]{:S(2)}) collective-permute-start(bf16[2,2,2,2,64,128]{5,4,0,2,3,1:T(8,128)(2,1)S(1)} %maximum_select_fusion.11), channel_id=1, source_target_pairs={{0,128},{128,0},{256,384},{384,256},{1,129},{129,1},{257,385},{385... | collective-permute-start | bytes 786440 | tf_op jit(solution)/shard_map/ppermute | solution.py:20
  56.4 6.6 %collective-permute-start.11 = (bf16[2,2,2,2,2,64,128]{6,5,4,3,2,1,0:T(8,128)(2,1)}, bf16[2,2,2,2,2,64,128]{6,5,4,3,2,1,0:T(8,128)(2,1)S(1)}, u32[]{:S(2)}, u32[]{:S(2)}) collective-permute-start(bf16[2,2,2,2,2,64,128]{6,5,4,3,2,1,0:T(8,128)(2,1)} %maximum_select_fusion.7), channel_id=1, source_target_pairs={{0,8},{8,0},{16,24},{24,16},{32,40},{40,32},{48,56},{56,48},{64,72... | collective-permute-start | bytes 1572872 | tf_op jit(solution)/shard_map/ppermute | solution.py:20
  60.8 4.1 %collective-permute-start.5 = (bf16[2,2,2,2,2,64,128]{6,5,1,3,4,2,0:T(8,128)(2,1)}, bf16[2,2,2,2,2,64,128]{6,5,1,3,4,2,0:T(8,128)(2,1)}, u32[]{:S(2)}, u32[]{:S(2)}) collective-permute-start(bf16[2,2,2,2,2,64,128]{6,5,1,3,4,2,0:T(8,128)(2,1)} %maximum_select_fusion.5), channel_id=1, source_target_pairs={{0,8},{8,0},{16,24},{24,16},{32,40},{40,32},{48,56},{56,48},{64,72... | collective-permute-start | bytes 1572872 | tf_op jit(solution)/shard_map/ppermute | solution.py:20
  66.8 46.1 %copy-start.7 = (bf16[1,192,512]{2,1,0:T(8,128)(2,1)S(1)}, bf16[1,192,512]{2,1,0:T(8,128)(2,1)}, u32[]{:S(2)}) copy-start(bf16[1,192,512]{2,1,0:T(8,128)(2,1)} %param.7) | copy-start | bytes 589828
  66.8 17.4 %collective-permute-start.12 = (bf16[1,193,256]{2,1,0:T(8,128)(2,1)S(1)}, bf16[1,193,256]{2,1,0:T(8,128)(2,1)S(1)}, u32[]{:S(2)}, u32[]{:S(2)}) collective-permute-start(bf16[1,193,256]{2,1,0:T(8,128)(2,1)S(1)} %get-tuple-element.22), channel_id=1, source_target_pairs={{0,64},{8,72},{16,80},{24,88},{32,96},{40,104},{48,112},{56,120},{... | collective-permute-start | bytes 296456 | tf_op jit(solution)/shard_map/ppermute | solution.py:20
  84.3 12.6 %collective-permute-start.13 = (bf16[2,1,193,256]{3,2,0,1:T(8,128)(2,1)S(1)}, bf16[2,1,193,256]{3,2,0,1:T(8,128)(2,1)S(1)}, u32[]{:S(2)}, u32[]{:S(2)}) collective-permute-start(bf16[2,1,193,256]{3,2,0,1:T(8,128)(2,1)S(1)} %maximum_select_fusion.14), channel_id=1, source_target_pairs={{0,32},{8,40},{16,48},{24,56},{32,0},{40,8},{48,16},{56,24},{64,96... | collective-permute-start | bytes 592904 | tf_op jit(solution)/shard_map/ppermute | solution.py:20
  97.0 13.3 %collective-permute-start.14 = (bf16[2,2,1,193,256]{4,3,1,0,2:T(8,128)(2,1)S(1)}, bf16[2,2,1,193,256]{4,3,1,0,2:T(8,128)(2,1)S(1)}, u32[]{:S(2)}, u32[]{:S(2)}) collective-permute-start(bf16[2,2,1,193,256]{4,3,1,0,2:T(8,128)(2,1)S(1)} %maximum_select_fusion.9), channel_id=1, source_target_pairs={{0,16},{8,24},{16,0},{24,8},{32,48},{40,56},{48,32},{56,40},{64,80... | collective-permute-start | bytes 1185800 | tf_op jit(solution)/shard_map/ppermute | solution.py:20
  111.0 4.4 %collective-permute-start.15 = (bf16[2,2,2,1,193,256]{5,2,4,3,1,0:T(2,128)(2,1)S(1)}, bf16[2,2,2,1,193,256]{5,2,4,3,1,0:T(2,128)(2,1)}, u32[]{:S(2)}, u32[]{:S(2)}) collective-permute-start(bf16[2,2,2,1,193,256]{5,2,4,3,1,0:T(2,128)(2,1)S(1)} %copy.119), channel_id=1, source_target_pairs={{0,8},{8,0},{16,24},{24,16},{32,40},{40,32},{48,56},{56,48},{64,72... | collective-permute-start | bytes 2371592 | tf_op jit(solution)/shard_map/ppermute | solution.py:20
  117.0 1.5 copy-start.9
  120.5 3.4 %copy-start.8 = (bf16[192,4,128]{2,1,0:T(4,128)(2,1)S(1)}, bf16[192,4,128]{2,1,0:T(4,128)(2,1)}, u32[]{:S(2)}) copy-start(bf16[192,4,128]{2,1,0:T(4,128)(2,1)} %reshape_squeeze.7) | copy-start | bytes 589828
  136.1 16.2 %copy-start.10 = (bf16[192,4,128]{2,1,0:T(4,128)(2,1)S(1)}, bf16[192,4,128]{2,1,0:T(4,128)(2,1)}, u32[]{:S(2)}) copy-start(bf16[192,4,128]{2,1,0:T(4,128)(2,1)} %reshape_squeeze.6) | copy-start | bytes 589828
  152.3 4.2 %copy-start.6 = (bf16[2,2,2,2,192,4,192]{4,3,2,1,0,6,5:T(2,128)(2,1)S(1)}, bf16[2,2,2,2,192,4,192]{4,3,2,1,0,6,5:T(2,128)(2,1)}, u32[]{:S(2)}) copy-start(bf16[2,2,2,2,192,4,192]{4,3,2,1,0,6,5:T(2,128)(2,1)} %dot_general.34) | copy-start | bytes 14155780
  160.9 4.3 %collective-permute-start.16 = (bf16[2,2,2,192,256]{4,3,2,1,0:T(8,128)(2,1)S(1)}, bf16[2,2,2,192,256]{4,3,2,1,0:T(8,128)(2,1)S(1)}, u32[]{:S(2)}, u32[]{:S(2)}) collective-permute-start(bf16[2,2,2,192,256]{4,3,2,1,0:T(8,128)(2,1)S(1)} %fusion.48), channel_id=1, source_target_pairs={{0,8},{8,0},{16,24},{24,16},{32,40},{40,32},{48,56},{56,48},{64,72... | collective-permute-start | bytes 2359304 | tf_op jit(solution)/shard_map/ppermute | solution.py:20
  165.6 13.3 %collective-permute-start.17 = (bf16[2,2,192,256]{3,2,1,0:T(8,128)(2,1)S(1)}, bf16[2,2,192,256]{3,2,1,0:T(8,128)(2,1)S(1)}, u32[]{:S(2)}, u32[]{:S(2)}) collective-permute-start(bf16[2,2,192,256]{3,2,1,0:T(8,128)(2,1)S(1)} %fusion.54), channel_id=1, source_target_pairs={{0,16},{8,24},{16,0},{24,8},{32,48},{40,56},{48,32},{56,40},{64,80... | collective-permute-start | bytes 1179656 | tf_op jit(solution)/shard_map/ppermute | solution.py:20
  179.1 13.1 %collective-permute-start.18 = (bf16[2,192,256]{2,1,0:T(8,128)(2,1)S(1)}, bf16[2,192,256]{2,1,0:T(8,128)(2,1)S(1)}, u32[]{:S(2)}, u32[]{:S(2)}) collective-permute-start(bf16[2,192,256]{2,1,0:T(8,128)(2,1)S(1)} %fusion.58), channel_id=1, source_target_pairs={{0,32},{8,40},{16,48},{24,56},{32,0},{40,8},{48,16},{56,24},{64,96... | collective-permute-start | bytes 589832 | tf_op jit(solution)/shard_map/ppermute | solution.py:20
  192.3 13.6 %collective-permute-start.19 = (bf16[192,256]{1,0:T(8,128)(2,1)S(1)}, bf16[192,256]{1,0:T(8,128)(2,1)S(1)}, u32[]{:S(2)}, u32[]{:S(2)}) collective-permute-start(bf16[192,256]{1,0:T(8,128)(2,1)S(1)} %select_bitcast_fusion.8), channel_id=1, source_target_pairs={{0,64},{8,72},{16,80},{24,88},{32,96},{40,104},{48,112},{56,120},{... | collective-permute-start | bytes 294920 | tf_op jit(solution)/shard_map/ppermute | solution.py:20
  213.6 1.0 copy-start.2
  213.6 1.3 copy-start.4
  214.9 9.4 %collective-permute-start.20 = (f32[2,2,2,2,2,64,128]{6,5,2,0,3,1,4:T(8,128)S(1)}, f32[2,2,2,2,2,64,128]{6,5,2,0,3,1,4:T(8,128)}, u32[]{:S(2)}, u32[]{:S(2)}) collective-permute-start(f32[2,2,2,2,2,64,128]{6,5,2,0,3,1,4:T(8,128)S(1)} %select_bitcast_fusion.1), channel_id=1, source_target_pairs={{0,8},{8,0},{16,24},{24,16},{32,40},{40,32},{48,56},{56,48},{64,72... | collective-permute-start | bytes 3145736 | tf_op jit(solution)/shard_map/ppermute | solution.py:20
  219.7 4.6 %copy-start.3 = (f32[2,2,2,2,2,1,64,128]{7,6,5,4,3,2,1,0:T(8,128)S(1)}, f32[2,2,2,2,2,1,64,128]{7,6,5,4,3,2,1,0:T(8,128)}, u32[]{:S(2)}) copy-start(f32[2,2,2,2,2,1,64,128]{7,6,5,4,3,2,1,0:T(8,128)} %copy-done.2) | copy-start | bytes 3145732
  219.7 4.6 %copy-start.5 = (f32[2,2,2,2,2,1,64,128]{7,6,5,4,3,2,1,0:T(8,128)S(1)}, f32[2,2,2,2,2,1,64,128]{7,6,5,4,3,2,1,0:T(8,128)}, u32[]{:S(2)}) copy-start(f32[2,2,2,2,2,1,64,128]{7,6,5,4,3,2,1,0:T(8,128)} %copy-done.4) | copy-start | bytes 3145732
  219.7 13.7 %slice-start = ((s8[4718592]{0:T(1024)(128)(4,1)}), s8[4194304]{0:T(1024)(128)(4,1)S(1)}, s32[]{:S(2)}) async-start(s8[4718592]{0:T(1024)(128)(4,1)} %bitcast.394), calls=%async_computation | async-start | bytes 8388608
  221.8 11.7 %slice-start.1 = ((s8[4718592]{0:T(1024)(128)(4,1)}), s8[524288]{0:T(1024)(128)(4,1)S(1)}, s32[]{:S(2)}) async-start(s8[4718592]{0:T(1024)(128)(4,1)} %bitcast.394), calls=%async_computation.1 | async-start | bytes 1048576
  221.8 7.6 %collective-permute-start.26 = (f32[2,2,2,2,2,64,128]{6,5,2,0,3,1,4:T(8,128)S(1)}, f32[2,2,2,2,2,64,128]{6,5,2,0,3,1,4:T(8,128)S(1)}, u32[]{:S(2)}, u32[]{:S(2)}) collective-permute-start(f32[2,2,2,2,2,64,128]{6,5,2,0,3,1,4:T(8,128)S(1)} %select_bitcast_fusion), channel_id=1, source_target_pairs={{0,8},{8,0},{16,24},{24,16},{32,40},{40,32},{48,56},{56,48},{64,72... | collective-permute-start | bytes 3145736 | tf_op jit(solution)/shard_map/ppermute | solution.py:20
  226.8 16.0 %collective-permute-start.21 = (f32[2,2,2,2,64,128]{5,4,1,0,2,3:T(8,128)}, f32[2,2,2,2,64,128]{5,4,1,0,2,3:T(8,128)}, u32[]{:S(2)}, u32[]{:S(2)}) collective-permute-start(f32[2,2,2,2,64,128]{5,4,1,0,2,3:T(8,128)} %select_bitcast_fusion.3), channel_id=1, source_target_pairs={{0,128},{128,0},{256,384},{384,256},{1,129},{129,1},{257,385},{385... | collective-permute-start | bytes 1572872 | tf_op jit(solution)/shard_map/ppermute | solution.py:20
  229.7 1.0 copy-start.1
  231.6 15.8 %collective-permute-start.27 = (f32[2,2,2,2,64,128]{5,4,2,0,3,1:T(8,128)}, f32[2,2,2,2,64,128]{5,4,2,0,3,1:T(8,128)}, u32[]{:S(2)}, u32[]{:S(2)}) collective-permute-start(f32[2,2,2,2,64,128]{5,4,2,0,3,1:T(8,128)} %select_bitcast_fusion.2), channel_id=1, source_target_pairs={{0,16},{8,24},{16,0},{24,8},{32,48},{40,56},{48,32},{56,40},{64,80... | collective-permute-start | bytes 1572872 | tf_op jit(solution)/shard_map/ppermute | solution.py:20
  244.0 9.3 %collective-permute-start.22 = (f32[2,2,2,64,128]{4,3,1,0,2:T(8,128)S(1)}, f32[2,2,2,64,128]{4,3,1,0,2:T(8,128)S(1)}, u32[]{:S(2)}, u32[]{:S(2)}) collective-permute-start(f32[2,2,2,64,128]{4,3,1,0,2:T(8,128)S(1)} %select_bitcast_fusion.5), channel_id=1, source_target_pairs={{0,16},{8,24},{16,0},{24,8},{32,48},{40,56},{48,32},{56,40},{64,80... | collective-permute-start | bytes 786440 | tf_op jit(solution)/shard_map/ppermute | solution.py:20
  248.8 9.6 %collective-permute-start.28 = (f32[2,2,2,64,128]{4,3,1,0,2:T(8,128)S(1)}, f32[2,2,2,64,128]{4,3,1,0,2:T(8,128)S(1)}, u32[]{:S(2)}, u32[]{:S(2)}) collective-permute-start(f32[2,2,2,64,128]{4,3,1,0,2:T(8,128)S(1)} %select_bitcast_fusion.4), channel_id=1, source_target_pairs={{0,128},{128,0},{256,384},{384,256},{1,129},{129,1},{257,385},{385... | collective-permute-start | bytes 786440 | tf_op jit(solution)/shard_map/ppermute | solution.py:20
  253.4 8.7 %collective-permute-start.23 = (f32[2,2,64,128]{3,2,1,0:T(8,128)S(1)}, f32[2,2,64,128]{3,2,1,0:T(8,128)S(1)}, u32[]{:S(2)}, u32[]{:S(2)}) collective-permute-start(f32[2,2,64,128]{3,2,1,0:T(8,128)S(1)} %fusion.67), channel_id=1, source_target_pairs={{0,256},{128,384},{256,0},{384,128},{1,257},{129,385},{257,1},{385... | collective-permute-start | bytes 393224 | tf_op jit(solution)/shard_map/ppermute | solution.py:20
  258.5 11.3 %collective-permute-start.29 = (f32[2,2,64,128]{3,2,1,0:T(8,128)S(1)}, f32[2,2,64,128]{3,2,1,0:T(8,128)S(1)}, u32[]{:S(2)}, u32[]{:S(2)}) collective-permute-start(f32[2,2,64,128]{3,2,1,0:T(8,128)S(1)} %select_bitcast_fusion.6), channel_id=1, source_target_pairs={{0,32},{8,40},{16,48},{24,56},{32,0},{40,8},{48,16},{56,24},{64,96... | collective-permute-start | bytes 393224 | tf_op jit(solution)/shard_map/ppermute | solution.py:20
  262.1 12.1 %collective-permute-start.24 = (f32[2,64,128]{2,1,0:T(8,128)S(1)}, f32[2,64,128]{2,1,0:T(8,128)S(1)}, u32[]{:S(2)}, u32[]{:S(2)}) collective-permute-start(f32[2,64,128]{2,1,0:T(8,128)S(1)} %select_bitcast_fusion.10), channel_id=1, source_target_pairs={{0,32},{8,40},{16,48},{24,56},{32,0},{40,8},{48,16},{56,24},{64,96... | collective-permute-start | bytes 196616 | tf_op jit(solution)/shard_map/ppermute | solution.py:20
  269.9 7.7 %collective-permute-start.30 = (f32[2,64,128]{2,1,0:T(8,128)S(1)}, f32[2,64,128]{2,1,0:T(8,128)S(1)}, u32[]{:S(2)}, u32[]{:S(2)}) collective-permute-start(f32[2,64,128]{2,1,0:T(8,128)S(1)} %select_bitcast_fusion.9), channel_id=1, source_target_pairs={{0,256},{128,384},{256,0},{384,128},{1,257},{129,385},{257,1},{385... | collective-permute-start | bytes 196616 | tf_op jit(solution)/shard_map/ppermute | solution.py:20
  274.3 9.9 %collective-permute-start.25 = (f32[64,128]{1,0:T(8,128)S(1)}, f32[64,128]{1,0:T(8,128)S(1)}, u32[]{:S(2)}, u32[]{:S(2)}) collective-permute-start(f32[64,128]{1,0:T(8,128)S(1)} %select_bitcast_fusion.12), channel_id=1, source_target_pairs={{0,64},{8,72},{16,80},{24,88},{32,96},{40,104},{48,112},{56,120},{... | collective-permute-start | bytes 98312 | tf_op jit(solution)/shard_map/ppermute | solution.py:20
  277.6 9.7 %collective-permute-start.31 = (f32[64,128]{1,0:T(8,128)S(1)}, f32[64,128]{1,0:T(8,128)S(1)}, u32[]{:S(2)}, u32[]{:S(2)}) collective-permute-start(f32[64,128]{1,0:T(8,128)S(1)} %select_bitcast_fusion.11), channel_id=1, source_target_pairs={{0,64},{8,72},{16,80},{24,88},{32,96},{40,104},{48,112},{56,120},{... | collective-permute-start | bytes 98312 | tf_op jit(solution)/shard_map/ppermute | solution.py:20

commit v4 on v3

--- a/solution.py
+++ b/solution.py
@@ -1,6 +1,8 @@
 import jax
 import jax.numpy as jnp
 from jax import lax
+from jax.experimental import pallas as pl
+from jax.experimental.pallas import tpu as pltpu
 from jax.sharding import PartitionSpec as P
 
 HEADS = 32
@@ -56,6 +58,65 @@
     return cur
 
 
+def _attention_kernel(q_ref, do_ref, k_ref, v_ref, mq_ref, mk_ref, gq_ref, dkv_ref, dk_acc, dv_acc):
+    scale = HEAD_DIM ** (-0.5)
+    keys = k_ref[...]
+    values = v_ref[...]
+    same = mq_ref[...] == mk_ref[...]
+    dk_acc[...] = jnp.zeros_like(dk_acc)
+    dv_acc[...] = jnp.zeros_like(dv_acc)
+    nt = (((1,), (1,)), ((), ()))
+    for h in range(q_ref.shape[1] // HEAD_DIM):
+        cols = slice(h * HEAD_DIM, (h + 1) * HEAD_DIM)
+        qh = q_ref[:, cols]
+        doh = do_ref[:, cols]
+        raw = lax.dot_general(qh, keys, nt, preferred_element_type=jnp.float32) * scale
+        raw = jnp.where(same, raw, far_below)
+        top = jnp.max(raw, axis=1, keepdims=True)
+        total = jnp.sum(jnp.exp(raw - top), axis=1, keepdims=True)
+        probs = jnp.exp(raw - (top + jnp.log(total)))
+        probs_b = probs.astype(jnp.bfloat16)
+        out = jnp.dot(probs_b, values, preferred_element_type=jnp.float32).astype(jnp.bfloat16)
+        delta = jnp.sum(doh.astype(jnp.float32) * out.astype(jnp.float32), axis=1, keepdims=True)
+        dv_acc[...] += jnp.dot(probs.T.astype(jnp.bfloat16), doh, preferred_element_type=jnp.float32)
+        prob_grad = lax.dot_general(doh, values, nt, preferred_element_type=jnp.float32)
+        dscores = probs * (prob_grad - delta)
+        gq_ref[:, cols] = (
+            jnp.dot(dscores.astype(jnp.bfloat16), keys, preferred_element_type=jnp.float32) * scale
+        ).astype(gq_ref.dtype)
+        dk_acc[...] += jnp.dot(
+            dscores.T.astype(jnp.bfloat16), qh, preferred_element_type=jnp.float32
+        ) * scale
+    dkv_ref[:, :HEAD_DIM] = dk_acc[...].astype(dkv_ref.dtype)
+    dkv_ref[:, HEAD_DIM:] = dv_acc[...].astype(dkv_ref.dtype)
+
+
+def attention_block(q, do, keys, values, mq, mk):
+    rows, width = q.shape
+    n_keys = keys.shape[0]
+    heads = width // HEAD_DIM
+    flops = 2 * rows * n_keys * HEAD_DIM * heads * 6
+    vmem = pltpu.VMEM
+    return pl.pallas_call(
+        _attention_kernel,
+        out_shape=(
+            jax.ShapeDtypeStruct((rows, width), jnp.bfloat16),
+            jax.ShapeDtypeStruct((n_keys, 2 * HEAD_DIM), jnp.bfloat16),
+        ),
+        in_specs=[pl.BlockSpec(memory_space=vmem)] * 6,
+        out_specs=(pl.BlockSpec(memory_space=vmem), pl.BlockSpec(memory_space=vmem)),
+        scratch_shapes=[
+            pltpu.VMEM((n_keys, HEAD_DIM), jnp.float32),
+            pltpu.VMEM((n_keys, HEAD_DIM), jnp.float32),
+        ],
+        cost_estimate=pl.CostEstimate(
+            flops=flops,
+            transcendentals=2 * rows * n_keys * heads,
+            bytes_accessed=4 * rows * width * 2 + 4 * n_keys * HEAD_DIM * 2,
+        ),
+    )(q, do, keys, values, mq, mk)
+
+
 def body(hidden, queries, grad_out, segment, key_proj, value_proj):
     tok_rows = hidden.shape[1]
     n_dp = lax.axis_size("dp")
@@ -96,36 +157,16 @@
     values = kvm_all[:, :tok_rows, HEAD_DIM:].reshape(-1, HEAD_DIM)
     marks_all = kvm_all[:, tok_rows, :tok_rows].reshape(-1)
 
-    q = queries[0].reshape(tok_rows, group, HEAD_DIM)
-    do = grad_out[0].reshape(tok_rows, group, HEAD_DIM)
-    same = (marks[:, None] == marks_all[None, :])[:, None, :]
-    raw = jnp.einsum("qgd,kd->qgk", q, keys, preferred_element_type=jnp.float32) * scale
-    raw = jnp.where(same, raw, far_below)
-    top = jnp.max(raw, axis=-1)
-    total = jnp.sum(jnp.where(same, jnp.exp(raw - top[..., None]), 0.0), axis=-1)
-    log_total = top + jnp.log(total)
-    probs = jnp.where(same, jnp.exp(raw - log_total[..., None]), 0.0)
-    probs_b = probs.astype(jnp.bfloat16)
-    output = jnp.einsum("qgk,kd->qgd", probs_b, values, preferred_element_type=jnp.float32).astype(
-        jnp.bfloat16
-    )
-    delta = jnp.sum(do.astype(jnp.float32) * output.astype(jnp.float32), axis=-1)
-    value_part = jnp.einsum("qgk,qgd->kd", probs_b, do, preferred_element_type=jnp.float32)
-    prob_grad = jnp.einsum("qgd,kd->qgk", do, values, preferred_element_type=jnp.float32)
-    dscores = (probs * (prob_grad - delta[..., None])).astype(jnp.bfloat16)
-    grad_q = (
-        jnp.einsum("qgk,kd->qgd", dscores, keys, preferred_element_type=jnp.float32) * scale
-    ).astype(jnp.bfloat16)
-    key_part = jnp.einsum("qgk,qgd->kd", dscores, q, preferred_element_type=jnp.float32) * scale
-
-    kv_part = jnp.concatenate([key_part, value_part], axis=1).astype(jnp.bfloat16)
+    mq = marks.astype(jnp.float32)[:, None]
+    mk = marks_all.astype(jnp.float32)[None, :]
+    grad_q, kv_part = attention_block(queries[0], grad_out[0], keys, values, mq, mk)
     ctx_near_first = ctx_far_first[::-1]
     kv_grad = scatter_sum(kv_part, ctx_near_first, ctx_canon, jnp.float32).astype(jnp.bfloat16)
 
     proj_part = jnp.einsum("td,tc->dc", local_rows, kv_grad, preferred_element_type=jnp.float32)
     key_sum = scatter_sum(proj_part[:, :width_kv], order_a[::-1], both_canon)
     value_sum = scatter_sum(proj_part[:, width_kv:], order_b[::-1], both_canon)
-    grad_queries = grad_q.reshape(1, tok_rows, group * HEAD_DIM)
+    grad_queries = grad_q[None]
     return (grad_queries, key_sum, value_sum)
 
 

time: 290 us -> 265 us (0.914)
  matrix products: 21.1 us -> 1.36 us
  local copies, waits for them, and re-layouts: 37.2 us -> 18.8 us
  Pallas kernels: 0 us -> 15.4 us
  starting transfers between devices: 97.4 us -> 108 us
  other arithmetic: 25.1 us -> 15.4 us
  waiting for transfers between devices: 105 us -> 101 us
    dot_general x6 -> x0, matrix products: 19.8 us -> none  [the longest x1 5.32 us: body(): jnp.einsum('qgd,kd->qgk', do, values, preferred_element_type=jnp.float32)]
    dot_general x1 -> x0, local copies, waits for them, and re-layouts: 16.2 us -> none  [body(): jnp.einsum('qgk,qgd->kd', probs_b, do, preferred_element_type=jnp.float32)]
    pallas_call x0 -> x1, Pallas kernels: none -> 15.4 us  [attention_block(): pl.pallas_call(_attention_kernel, out_shape=(jax.ShapeDtypeStruct((rows,...]
    ppermute x32, starting transfers between devices: 97.4 us -> 108 us  [_exchange(): return lax.ppermute(x, axis, perm)]
    ppermute x32, waiting for transfers between devices: 105 us -> 101 us  [_exchange(): return lax.ppermute(x, axis, perm)]
    convert_element_type x1 -> x2, other arithmetic: 3.9 us -> 0.05 us  [the longest x1 0.04 us: body(): mk = marks_all.astype(jnp.float32)[None, :]]
    reduce_sum x1 -> x0, other arithmetic: 3.41 us -> none  [body(): jnp.sum(jnp.where(same, jnp.exp(raw - top[..., None]), 0.0), axis=-1)]
  transfers between devices with their start and end apart: 32 -> 32, of which waited for: 23 -> 20; matrix products, arithmetic and copies ran while one was open for 8% -> 5% of each run, Pallas kernels for 0% -> 0%
where the time goes in v4:
time: 265 us; the launch traced here: 262 us
  starting transfers between devices  108 us (41%)
  waiting for transfers between devices  101 us (38%)
  local copies, waits for them, and re-layouts  18.8 us (7%)
  other arithmetic  15.4 us (6%)
  Pallas kernels  15.4 us (6%)
    ppermute x32, starting transfers between devices, _exchange(): return lax.ppermute(x, axis, perm)  108 us
    ppermute x32, waiting for transfers between devices, _exchange(): return lax.ppermute(x, axis, perm)  101 us
    pallas_call x1, Pallas kernels, attention_block(): pl.pallas_call(_attention_kernel, out_shape=(jax.ShapeDtypeStruct((rows,...  15.4 us
    select_n x24, other arithmetic, gather_blocks(): cur = jnp.where(mine, jnp.stack([recv, cur]), jnp.stack([cur, recv]))  5.64 us
  transfers between devices with their start and end apart: 32, of which 20 were waited for; matrix products, arithmetic and copies ran while one was open for 5% of the time, Pallas kernels for 0%

profile of v4, /device:TPU:24, one launch (start us, length us, event | category | flops | bytes accessed | tf_op | source)
XLA Modules:
  0.0 261.8 jit_solution(7554782767875719958)
XLA Ops:
  0.6 9.2 %collective-permute-start.6 = (bf16[64,128]{1,0:T(8,128)(2,1)}, bf16[64,128]{1,0:T(8,128)(2,1)S(1)}, u32[]{:S(2)}, u32[]{:S(2)}) collective-permute-start(bf16[64,128]{1,0:T(8,128)(2,1)} %param.11), channel_id=1, source_target_pairs={{0,64},{8,72},{16,80},{24,88},{32,96},{40,104},{48,112},{56,120},{... | collective-permute-start | bytes 49160 | tf_op jit(solution)/shard_map/ppermute | solution.py:22
  9.9 1.9 collective-permute-start
  13.4 6.3 %collective-permute-done = bf16[64,128]{1,0:T(8,128)(2,1)S(1)} collective-permute-done((bf16[64,128]{1,0:T(8,128)(2,1)}, bf16[64,128]{1,0:T(8,128)(2,1)S(1)}, u32[]{:S(2)}, u32[]{:S(2)}) %collective-permute-start) | collective-permute-done | bytes 16416 | tf_op jit(solution)/shard_map/ppermute | solution.py:22
  22.1 4.9 %collective-permute-start.7 = (bf16[2,64,128]{2,1,0:T(8,128)(2,1)S(1)}, bf16[2,64,128]{2,1,0:T(8,128)(2,1)S(1)}, u32[]{:S(2)}, u32[]{:S(2)}) collective-permute-start(bf16[2,64,128]{2,1,0:T(8,128)(2,1)S(1)} %maximum_select_fusion.22), channel_id=1, source_target_pairs={{0,256},{128,384},{256,0},{384,128},{1,257},{129,385},{257,1},{385... | collective-permute-start | bytes 98312 | tf_op jit(solution)/shard_map/ppermute | solution.py:22
  27.9 5.2 %collective-permute-start.1 = (bf16[2,64,128]{2,1,0:T(8,128)(2,1)S(1)}, bf16[2,64,128]{2,1,0:T(8,128)(2,1)S(1)}, u32[]{:S(2)}, u32[]{:S(2)}) collective-permute-start(bf16[2,64,128]{2,1,0:T(8,128)(2,1)S(1)} %maximum_select_fusion.21), channel_id=1, source_target_pairs={{0,32},{8,40},{16,48},{24,56},{32,0},{40,8},{48,16},{56,24},{64,96... | collective-permute-start | bytes 98312 | tf_op jit(solution)/shard_map/ppermute | solution.py:22
  33.1 1.9 collective-permute-start.8
  35.0 4.6 %collective-permute-start.2 = (bf16[2,2,64,128]{3,2,0,1:T(8,128)(2,1)S(1)}, bf16[2,2,64,128]{3,2,0,1:T(8,128)(2,1)S(1)}, u32[]{:S(2)}, u32[]{:S(2)}) collective-permute-start(bf16[2,2,64,128]{3,2,0,1:T(8,128)(2,1)S(1)} %maximum_select_fusion.18), channel_id=1, source_target_pairs={{0,256},{128,384},{256,0},{384,128},{1,257},{129,385},{257,1},{385... | collective-permute-start | bytes 196616 | tf_op jit(solution)/shard_map/ppermute | solution.py:22
  40.2 2.5 collective-permute-done.2
  42.7 3.7 %collective-permute-start.3 = (bf16[2,2,2,64,128]{4,3,1,2,0:T(8,128)(2,1)S(1)}, bf16[2,2,2,64,128]{4,3,1,2,0:T(8,128)(2,1)S(1)}, u32[]{:S(2)}, u32[]{:S(2)}) collective-permute-start(bf16[2,2,2,64,128]{4,3,1,2,0:T(8,128)(2,1)S(1)} %maximum_select_fusion.15), channel_id=1, source_target_pairs={{0,16},{8,24},{16,0},{24,8},{32,48},{40,56},{48,32},{56,40},{64,80... | collective-permute-start | bytes 393224 | tf_op jit(solution)/shard_map/ppermute | solution.py:22
  46.5 3.0 %collective-permute-start.9 = (bf16[2,2,2,64,128]{4,3,2,1,0:T(8,128)(2,1)S(1)}, bf16[2,2,2,64,128]{4,3,2,1,0:T(8,128)(2,1)S(1)}, u32[]{:S(2)}, u32[]{:S(2)}) collective-permute-start(bf16[2,2,2,64,128]{4,3,2,1,0:T(8,128)(2,1)S(1)} %maximum_select_fusion.16), channel_id=1, source_target_pairs={{0,128},{128,0},{256,384},{384,256},{1,129},{129,1},{257,385},{385... | collective-permute-start | bytes 393224 | tf_op jit(solution)/shard_map/ppermute | solution.py:22
  49.6 3.8 %collective-permute-done.9 = bf16[2,2,2,64,128]{4,3,2,1,0:T(8,128)(2,1)S(1)} collective-permute-done((bf16[2,2,2,64,128]{4,3,2,1,0:T(8,128)(2,1)S(1)}, bf16[2,2,2,64,128]{4,3,2,1,0:T(8,128)(2,1)S(1)}, u32[]{:S(2)}, u32[]{:S(2)}) %collective-permute-start.9) | collective-permute-done | bytes 131104 | tf_op jit(solution)/shard_map/ppermute | solution.py:22
  53.4 2.1 collective-permute-start.10
  55.5 3.0 %collective-permute-start.4 = (bf16[2,2,2,2,64,128]{5,4,0,2,3,1:T(8,128)(2,1)S(1)}, bf16[2,2,2,2,64,128]{5,4,0,2,3,1:T(8,128)(2,1)S(1)}, u32[]{:S(2)}, u32[]{:S(2)}) collective-permute-start(bf16[2,2,2,2,64,128]{5,4,0,2,3,1:T(8,128)(2,1)S(1)} %maximum_select_fusion.11), channel_id=1, source_target_pairs={{0,128},{128,0},{256,384},{384,256},{1,129},{129,1},{257,385},{385... | collective-permute-start | bytes 786440 | tf_op jit(solution)/shard_map/ppermute | solution.py:22
  58.7 2.9 %collective-permute-done.10 = bf16[2,2,2,2,64,128]{5,4,3,2,1,0:T(8,128)(2,1)S(1)} collective-permute-done((bf16[2,2,2,2,64,128]{5,4,3,2,1,0:T(8,128)(2,1)S(1)}, bf16[2,2,2,2,64,128]{5,4,3,2,1,0:T(8,128)(2,1)S(1)}, u32[]{:S(2)}, u32[]{:S(2)}) %collective-permute-start.10) | collective-permute-done | bytes 262176 | tf_op jit(solution)/shard_map/ppermute | solution.py:22
  62.5 1.9 collective-permute-start.11
  64.4 0.9 maximum_select_fusion.5
  65.3 2.4 collective-permute-start.5
  68.3 1.3 collective-permute-done.5
  69.6 1.1 copy.175
  71.4 1.9 collective-permute-start.12
  73.4 15.7 %collective-permute-done.12 = bf16[1,193,256]{2,1,0:T(8,128)(2,1)S(1)} collective-permute-done((bf16[1,193,256]{2,1,0:T(8,128)(2,1)S(1)}, bf16[1,193,256]{2,1,0:T(8,128)(2,1)S(1)}, u32[]{:S(2)}, u32[]{:S(2)}) %collective-permute-start.12) | collective-permute-done | bytes 98848 | tf_op jit(solution)/shard_map/ppermute | solution.py:22
  89.1 1.9 collective-permute-start.13
  91.1 7.5 %collective-permute-done.13 = bf16[2,1,193,256]{3,2,0,1:T(8,128)(2,1)S(1)} collective-permute-done((bf16[2,1,193,256]{3,2,0,1:T(8,128)(2,1)S(1)}, bf16[2,1,193,256]{3,2,0,1:T(8,128)(2,1)S(1)}, u32[]{:S(2)}, u32[]{:S(2)}) %collective-permute-start.13) | collective-permute-done | bytes 197664 | tf_op jit(solution)/shard_map/ppermute | solution.py:22
  98.6 1.9 collective-permute-start.14
  100.6 10.1 %collective-permute-done.14 = bf16[2,2,1,193,256]{4,3,1,0,2:T(8,128)(2,1)S(1)} collective-permute-done((bf16[2,2,1,193,256]{4,3,1,0,2:T(8,128)(2,1)S(1)}, bf16[2,2,1,193,256]{4,3,1,0,2:T(8,128)(2,1)S(1)}, u32[]{:S(2)}, u32[]{:S(2)}) %collective-permute-start.14) | collective-permute-done | bytes 395296 | tf_op jit(solution)/shard_map/ppermute | solution.py:22
  111.5 2.1 collective-permute-start.15
  114.5 1.3 collective-permute-done.15
  115.8 1.2 copy.174
  117.5 1.6 fusion.54
  119.8 15.4 %shard_map.85 = (bf16[192,512]{1,0:T(8,128)(2,1)}, bf16[3072,256]{1,0:T(8,128)(2,1)}) custom-call(bf16[192,512]{1,0:T(8,128)(2,1)} %bitcast.342, bf16[192,512]{1,0:T(8,128)(2,1)} %bitcast.343, bf16[3072,128]{1,0:T(8,128)(2,1)} %bitcast.315, bf16[3072,128]{1,0:T(8,128)(2,1)} %bitcast.314, f32[192,1]{1,0:T(8,128)} %copy.115.mq_ref, f32[1,3072]{1,0:T(1,128)} %reshape.1979.mk_ref), custom_call_target="tpu_custom_call" | custom-call | flops 3623878656 | bytes 3932160 | tf_op jit(solution)/shard_map/pallas_call | solution.py:100
  135.2 1.6 fusion.20
  136.8 2.0 collective-permute-start.16
  138.8 2.1 collective-permute-done.16
  141.4 2.2 collective-permute-start.17
  143.6 10.9 %collective-permute-done.17 = bf16[2,2,192,256]{3,2,1,0:T(8,128)(2,1)S(1)} collective-permute-done((bf16[2,2,192,256]{3,2,1,0:T(8,128)(2,1)S(1)}, bf16[2,2,192,256]{3,2,1,0:T(8,128)(2,1)S(1)}, u32[]{:S(2)}, u32[]{:S(2)}) %collective-permute-start.17) | collective-permute-done | bytes 393248 | tf_op jit(solution)/shard_map/ppermute | solution.py:22
  154.6 2.5 collective-permute-start.18
  157.1 10.3 %collective-permute-done.18 = bf16[2,192,256]{2,1,0:T(8,128)(2,1)S(1)} collective-permute-done((bf16[2,192,256]{2,1,0:T(8,128)(2,1)S(1)}, bf16[2,192,256]{2,1,0:T(8,128)(2,1)S(1)}, u32[]{:S(2)}, u32[]{:S(2)}) %collective-permute-start.18) | collective-permute-done | bytes 196640 | tf_op jit(solution)/shard_map/ppermute | solution.py:22
  167.6 6.2 %collective-permute-start.19 = (bf16[192,256]{1,0:T(8,128)(2,1)S(1)}, bf16[192,256]{1,0:T(8,128)(2,1)S(1)}, u32[]{:S(2)}, u32[]{:S(2)}) collective-permute-start(bf16[192,256]{1,0:T(8,128)(2,1)S(1)} %select_bitcast_fusion.8), channel_id=1, source_target_pairs={{0,64},{8,72},{16,80},{24,88},{32,96},{40,104},{48,112},{56,120},{... | collective-permute-start | bytes 294920 | tf_op jit(solution)/shard_map/ppermute | solution.py:22
  173.7 8.3 %collective-permute-done.19 = bf16[192,256]{1,0:T(8,128)(2,1)S(1)} collective-permute-done((bf16[192,256]{1,0:T(8,128)(2,1)S(1)}, bf16[192,256]{1,0:T(8,128)(2,1)S(1)}, u32[]{:S(2)}, u32[]{:S(2)}) %collective-permute-start.19) | collective-permute-done | bytes 98336 | tf_op jit(solution)/shard_map/ppermute | solution.py:22
  182.7 2.4 fusion.51
  185.1 2.9 %copy.143 = f32[4096,128]{1,0:T(8,128)} copy(f32[4096,128]{0,1:T(8,128)} %get-tuple-element.7) | data formatting | bytes 4194304 | tf_op jit(solution)/shard_map/slice | solution.py:168
  188.0 1.7 fusion.52
  189.7 1.0 copy-done.1
  190.7 1.1 select_bitcast_fusion
  191.9 1.9 collective-permute-start.26
  193.8 2.9 %copy.128 = f32[4096,128]{1,0:T(8,128)} copy(f32[4096,128]{0,1:T(8,128)} %get-tuple-element.8) | data formatting | bytes 4194304 | tf_op jit(solution)/shard_map/slice | solution.py:167
  196.7 1.7 fusion.53
  198.6 2.5 collective-permute-start.20
  201.2 1.5 bitcast_add_fusion
  202.8 1.9 collective-permute-start.27
  205.1 5.0 %collective-permute-start.21 = (f32[2,2,2,2,64,128]{5,4,1,0,2,3:T(8,128)S(1)}, f32[2,2,2,2,64,128]{5,4,1,0,2,3:T(8,128)S(1)}, u32[]{:S(2)}, u32[]{:S(2)}) collective-permute-start(f32[2,2,2,2,64,128]{5,4,1,0,2,3:T(8,128)S(1)} %select_bitcast_fusion.3), channel_id=1, source_target_pairs={{0,128},{128,0},{256,384},{384,256},{1,129},{129,1},{257,385},{385... | collective-permute-start | bytes 1572872 | tf_op jit(solution)/shard_map/ppermute | solution.py:22
  210.1 8.4 %collective-permute-done.27 = f32[2,2,2,2,64,128]{5,4,2,0,3,1:T(8,128)S(1)} collective-permute-done((f32[2,2,2,2,64,128]{5,4,2,0,3,1:T(8,128)S(1)}, f32[2,2,2,2,64,128]{5,4,2,0,3,1:T(8,128)S(1)}, u32[]{:S(2)}, u32[]{:S(2)}) %collective-permute-start.27) | collective-permute-done | bytes 524320 | tf_op jit(solution)/shard_map/ppermute | solution.py:22
  218.7 5.0 %collective-permute-start.28 = (f32[2,2,2,64,128]{4,3,1,0,2:T(8,128)S(1)}, f32[2,2,2,64,128]{4,3,1,0,2:T(8,128)S(1)}, u32[]{:S(2)}, u32[]{:S(2)}) collective-permute-start(f32[2,2,2,64,128]{4,3,1,0,2:T(8,128)S(1)} %select_bitcast_fusion.4), channel_id=1, source_target_pairs={{0,128},{128,0},{256,384},{384,256},{1,129},{129,1},{257,385},{385... | collective-permute-start | bytes 786440 | tf_op jit(solution)/shard_map/ppermute | solution.py:22
  223.8 2.2 collective-permute-start.22
  226.0 3.3 %collective-permute-done.28 = f32[2,2,2,64,128]{4,3,1,0,2:T(8,128)S(1)} collective-permute-done((f32[2,2,2,64,128]{4,3,1,0,2:T(8,128)S(1)}, f32[2,2,2,64,128]{4,3,1,0,2:T(8,128)S(1)}, u32[]{:S(2)}, u32[]{:S(2)}) %collective-permute-start.28) | collective-permute-done | bytes 262176 | tf_op jit(solution)/shard_map/ppermute | solution.py:22
  229.3 1.9 collective-permute-start.29
  231.3 1.5 collective-permute-done.22
  232.9 5.1 %collective-permute-start.23 = (f32[2,2,64,128]{3,2,1,0:T(8,128)S(1)}, f32[2,2,64,128]{3,2,1,0:T(8,128)S(1)}, u32[]{:S(2)}, u32[]{:S(2)}) collective-permute-start(f32[2,2,64,128]{3,2,1,0:T(8,128)S(1)} %fusion.33), channel_id=1, source_target_pairs={{0,256},{128,384},{256,0},{384,128},{1,257},{129,385},{257,1},{385... | collective-permute-start | bytes 393224 | tf_op jit(solution)/shard_map/ppermute | solution.py:22
  238.0 0.9 collective-permute-done.29
  238.9 5.4 %collective-permute-start.30 = (f32[2,64,128]{2,1,0:T(8,128)S(1)}, f32[2,64,128]{2,1,0:T(8,128)S(1)}, u32[]{:S(2)}, u32[]{:S(2)}) collective-permute-start(f32[2,64,128]{2,1,0:T(8,128)S(1)} %select_bitcast_fusion.9), channel_id=1, source_target_pairs={{0,256},{128,384},{256,0},{384,128},{1,257},{129,385},{257,1},{385... | collective-permute-start | bytes 196616 | tf_op jit(solution)/shard_map/ppermute | solution.py:22
  244.4 1.9 collective-permute-start.24
  246.6 4.8 %collective-permute-start.31 = (f32[64,128]{1,0:T(8,128)S(1)}, f32[64,128]{1,0:T(8,128)S(1)}, u32[]{:S(2)}, u32[]{:S(2)}) collective-permute-start(f32[64,128]{1,0:T(8,128)S(1)} %select_bitcast_fusion.11), channel_id=1, source_target_pairs={{0,64},{8,72},{16,80},{24,88},{32,96},{40,104},{48,112},{56,120},{... | collective-permute-start | bytes 98312 | tf_op jit(solution)/shard_map/ppermute | solution.py:22
  251.5 5.5 %collective-permute-start.25 = (f32[64,128]{1,0:T(8,128)S(1)}, f32[64,128]{1,0:T(8,128)S(1)}, u32[]{:S(2)}, u32[]{:S(2)}) collective-permute-start(f32[64,128]{1,0:T(8,128)S(1)} %select_bitcast_fusion.12), channel_id=1, source_target_pairs={{0,64},{8,72},{16,80},{24,88},{32,96},{40,104},{48,112},{56,120},{... | collective-permute-start | bytes 98312 | tf_op jit(solution)/shard_map/ppermute | solution.py:22
  257.6 3.6 %collective-permute-done.25 = f32[64,128]{1,0:T(8,128)S(1)} collective-permute-done((f32[64,128]{1,0:T(8,128)S(1)}, f32[64,128]{1,0:T(8,128)S(1)}, u32[]{:S(2)}, u32[]{:S(2)}) %collective-permute-start.25) | collective-permute-done | bytes 32800 | tf_op jit(solution)/shard_map/ppermute | solution.py:22
  (101 shorter events, 14.7 us)
Async XLA Ops:
  0.6 70.1 %copy-start = (bf16[1,192,4096]{2,1,0:T(8,128)(2,1)S(1)}, bf16[1,192,4096]{2,1,0:T(8,128)(2,1)}, u32[]{:S(2)}) copy-start(bf16[1,192,4096]{2,1,0:T(8,128)(2,1)} %param.6) | copy-start | bytes 4718596
  0.6 11.2 %collective-permute-start.6 = (bf16[64,128]{1,0:T(8,128)(2,1)}, bf16[64,128]{1,0:T(8,128)(2,1)S(1)}, u32[]{:S(2)}, u32[]{:S(2)}) collective-permute-start(bf16[64,128]{1,0:T(8,128)(2,1)} %param.11), channel_id=1, source_target_pairs={{0,64},{8,72},{16,80},{24,88},{32,96},{40,104},{48,112},{56,120},{... | collective-permute-start | bytes 49160 | tf_op jit(solution)/shard_map/ppermute | solution.py:22
  9.9 9.9 %collective-permute-start = (bf16[64,128]{1,0:T(8,128)(2,1)}, bf16[64,128]{1,0:T(8,128)(2,1)S(1)}, u32[]{:S(2)}, u32[]{:S(2)}) collective-permute-start(bf16[64,128]{1,0:T(8,128)(2,1)} %param.10), channel_id=1, source_target_pairs={{0,64},{8,72},{16,80},{24,88},{32,96},{40,104},{48,112},{56,120},{... | collective-permute-start | bytes 49160 | tf_op jit(solution)/shard_map/ppermute | solution.py:22
  22.1 10.9 %collective-permute-start.7 = (bf16[2,64,128]{2,1,0:T(8,128)(2,1)S(1)}, bf16[2,64,128]{2,1,0:T(8,128)(2,1)S(1)}, u32[]{:S(2)}, u32[]{:S(2)}) collective-permute-start(bf16[2,64,128]{2,1,0:T(8,128)(2,1)S(1)} %maximum_select_fusion.22), channel_id=1, source_target_pairs={{0,256},{128,384},{256,0},{384,128},{1,257},{129,385},{257,1},{385... | collective-permute-start | bytes 98312 | tf_op jit(solution)/shard_map/ppermute | solution.py:22
  27.9 7.1 %collective-permute-start.1 = (bf16[2,64,128]{2,1,0:T(8,128)(2,1)S(1)}, bf16[2,64,128]{2,1,0:T(8,128)(2,1)S(1)}, u32[]{:S(2)}, u32[]{:S(2)}) collective-permute-start(bf16[2,64,128]{2,1,0:T(8,128)(2,1)S(1)} %maximum_select_fusion.21), channel_id=1, source_target_pairs={{0,32},{8,40},{16,48},{24,56},{32,0},{40,8},{48,16},{56,24},{64,96... | collective-permute-start | bytes 98312 | tf_op jit(solution)/shard_map/ppermute | solution.py:22
  33.1 7.1 %collective-permute-start.8 = (bf16[2,2,64,128]{3,2,1,0:T(8,128)(2,1)S(1)}, bf16[2,2,64,128]{3,2,1,0:T(8,128)(2,1)S(1)}, u32[]{:S(2)}, u32[]{:S(2)}) collective-permute-start(bf16[2,2,64,128]{3,2,1,0:T(8,128)(2,1)S(1)} %maximum_select_fusion.19), channel_id=1, source_target_pairs={{0,32},{8,40},{16,48},{24,56},{32,0},{40,8},{48,16},{56,24},{64,96... | collective-permute-start | bytes 196616 | tf_op jit(solution)/shard_map/ppermute | solution.py:22
  35.0 7.7 %collective-permute-start.2 = (bf16[2,2,64,128]{3,2,0,1:T(8,128)(2,1)S(1)}, bf16[2,2,64,128]{3,2,0,1:T(8,128)(2,1)S(1)}, u32[]{:S(2)}, u32[]{:S(2)}) collective-permute-start(bf16[2,2,64,128]{3,2,0,1:T(8,128)(2,1)S(1)} %maximum_select_fusion.18), channel_id=1, source_target_pairs={{0,256},{128,384},{256,0},{384,128},{1,257},{129,385},{257,1},{385... | collective-permute-start | bytes 196616 | tf_op jit(solution)/shard_map/ppermute | solution.py:22
  42.7 12.8 %collective-permute-start.3 = (bf16[2,2,2,64,128]{4,3,1,2,0:T(8,128)(2,1)S(1)}, bf16[2,2,2,64,128]{4,3,1,2,0:T(8,128)(2,1)S(1)}, u32[]{:S(2)}, u32[]{:S(2)}) collective-permute-start(bf16[2,2,2,64,128]{4,3,1,2,0:T(8,128)(2,1)S(1)} %maximum_select_fusion.15), channel_id=1, source_target_pairs={{0,16},{8,24},{16,0},{24,8},{32,48},{40,56},{48,32},{56,40},{64,80... | collective-permute-start | bytes 393224 | tf_op jit(solution)/shard_map/ppermute | solution.py:22
  46.5 6.9 %collective-permute-start.9 = (bf16[2,2,2,64,128]{4,3,2,1,0:T(8,128)(2,1)S(1)}, bf16[2,2,2,64,128]{4,3,2,1,0:T(8,128)(2,1)S(1)}, u32[]{:S(2)}, u32[]{:S(2)}) collective-permute-start(bf16[2,2,2,64,128]{4,3,2,1,0:T(8,128)(2,1)S(1)} %maximum_select_fusion.16), channel_id=1, source_target_pairs={{0,128},{128,0},{256,384},{384,256},{1,129},{129,1},{257,385},{385... | collective-permute-start | bytes 393224 | tf_op jit(solution)/shard_map/ppermute | solution.py:22
  53.4 8.3 %collective-permute-start.10 = (bf16[2,2,2,2,64,128]{5,4,3,2,1,0:T(8,128)(2,1)S(1)}, bf16[2,2,2,2,64,128]{5,4,3,2,1,0:T(8,128)(2,1)S(1)}, u32[]{:S(2)}, u32[]{:S(2)}) collective-permute-start(bf16[2,2,2,2,64,128]{5,4,3,2,1,0:T(8,128)(2,1)S(1)} %maximum_select_fusion.12), channel_id=1, source_target_pairs={{0,16},{8,24},{16,0},{24,8},{32,48},{40,56},{48,32},{56,40},{64,80... | collective-permute-start | bytes 786440 | tf_op jit(solution)/shard_map/ppermute | solution.py:22
  55.5 8.9 %collective-permute-start.4 = (bf16[2,2,2,2,64,128]{5,4,0,2,3,1:T(8,128)(2,1)S(1)}, bf16[2,2,2,2,64,128]{5,4,0,2,3,1:T(8,128)(2,1)S(1)}, u32[]{:S(2)}, u32[]{:S(2)}) collective-permute-start(bf16[2,2,2,2,64,128]{5,4,0,2,3,1:T(8,128)(2,1)S(1)} %maximum_select_fusion.11), channel_id=1, source_target_pairs={{0,128},{128,0},{256,384},{384,256},{1,129},{129,1},{257,385},{385... | collective-permute-start | bytes 786440 | tf_op jit(solution)/shard_map/ppermute | solution.py:22
  58.6 9.1 %copy-start.4 = (s32[1,192]{1,0:T(1,128)S(1)}, s32[1,192]{1,0:T(1,128)}, u32[]{:S(2)}) copy-start(s32[1,192]{1,0:T(1,128)} %param.9) | copy-start | bytes 2308
  62.5 5.5 %collective-permute-start.11 = (bf16[2,2,2,2,2,64,128]{6,5,4,3,2,1,0:T(8,128)(2,1)}, bf16[2,2,2,2,2,64,128]{6,5,4,3,2,1,0:T(8,128)(2,1)S(1)}, u32[]{:S(2)}, u32[]{:S(2)}) collective-permute-start(bf16[2,2,2,2,2,64,128]{6,5,4,3,2,1,0:T(8,128)(2,1)} %maximum_select_fusion.7), channel_id=1, source_target_pairs={{0,8},{8,0},{16,24},{24,16},{32,40},{40,32},{48,56},{56,48},{64,72... | collective-permute-start | bytes 1572872 | tf_op jit(solution)/shard_map/ppermute | solution.py:22
  65.3 4.3 %collective-permute-start.5 = (bf16[2,2,2,2,2,64,128]{6,5,1,3,4,2,0:T(8,128)(2,1)}, bf16[2,2,2,2,2,64,128]{6,5,1,3,4,2,0:T(8,128)(2,1)}, u32[]{:S(2)}, u32[]{:S(2)}) collective-permute-start(bf16[2,2,2,2,2,64,128]{6,5,1,3,4,2,0:T(8,128)(2,1)} %maximum_select_fusion.5), channel_id=1, source_target_pairs={{0,8},{8,0},{16,24},{24,16},{32,40},{40,32},{48,56},{56,48},{64,72... | collective-permute-start | bytes 1572872 | tf_op jit(solution)/shard_map/ppermute | solution.py:22
  71.4 17.6 %collective-permute-start.12 = (bf16[1,193,256]{2,1,0:T(8,128)(2,1)S(1)}, bf16[1,193,256]{2,1,0:T(8,128)(2,1)S(1)}, u32[]{:S(2)}, u32[]{:S(2)}) collective-permute-start(bf16[1,193,256]{2,1,0:T(8,128)(2,1)S(1)} %get-tuple-element.26), channel_id=1, source_target_pairs={{0,64},{8,72},{16,80},{24,88},{32,96},{40,104},{48,112},{56,120},{... | collective-permute-start | bytes 296456 | tf_op jit(solution)/shard_map/ppermute | solution.py:22
  89.1 9.5 %collective-permute-start.13 = (bf16[2,1,193,256]{3,2,0,1:T(8,128)(2,1)S(1)}, bf16[2,1,193,256]{3,2,0,1:T(8,128)(2,1)S(1)}, u32[]{:S(2)}, u32[]{:S(2)}) collective-permute-start(bf16[2,1,193,256]{3,2,0,1:T(8,128)(2,1)S(1)} %maximum_select_fusion.14), channel_id=1, source_target_pairs={{0,32},{8,40},{16,48},{24,56},{32,0},{40,8},{48,16},{56,24},{64,96... | collective-permute-start | bytes 592904 | tf_op jit(solution)/shard_map/ppermute | solution.py:22
  98.6 12.1 %collective-permute-start.14 = (bf16[2,2,1,193,256]{4,3,1,0,2:T(8,128)(2,1)S(1)}, bf16[2,2,1,193,256]{4,3,1,0,2:T(8,128)(2,1)S(1)}, u32[]{:S(2)}, u32[]{:S(2)}) collective-permute-start(bf16[2,2,1,193,256]{4,3,1,0,2:T(8,128)(2,1)S(1)} %maximum_select_fusion.9), channel_id=1, source_target_pairs={{0,16},{8,24},{16,0},{24,8},{32,48},{40,56},{48,32},{56,40},{64,80... | collective-permute-start | bytes 1185800 | tf_op jit(solution)/shard_map/ppermute | solution.py:22
  111.5 4.3 %collective-permute-start.15 = (bf16[2,2,2,1,193,256]{5,2,4,3,1,0:T(2,128)(2,1)S(1)}, bf16[2,2,2,1,193,256]{5,2,4,3,1,0:T(2,128)(2,1)}, u32[]{:S(2)}, u32[]{:S(2)}) collective-permute-start(bf16[2,2,2,1,193,256]{5,2,4,3,1,0:T(2,128)(2,1)S(1)} %copy.112), channel_id=1, source_target_pairs={{0,8},{8,0},{16,24},{24,16},{32,40},{40,32},{48,56},{56,48},{64,72... | collective-permute-start | bytes 2371592 | tf_op jit(solution)/shard_map/ppermute | solution.py:22
  135.2 5.8 %copy-start.3 = (bf16[3072,256]{1,0:T(8,128)(2,1)S(1)}, bf16[3072,256]{1,0:T(8,128)(2,1)}, u32[]{:S(2)}) copy-start(bf16[3072,256]{1,0:T(8,128)(2,1)} %get-tuple-element.6) | copy-start | bytes 4718596
  136.8 4.2 %collective-permute-start.16 = (bf16[2,2,2,192,256]{4,3,2,1,0:T(8,128)(2,1)S(1)}, bf16[2,2,2,192,256]{4,3,2,1,0:T(8,128)(2,1)S(1)}, u32[]{:S(2)}, u32[]{:S(2)}) collective-permute-start(bf16[2,2,2,192,256]{4,3,2,1,0:T(8,128)(2,1)S(1)} %fusion.20), channel_id=1, source_target_pairs={{0,8},{8,0},{16,24},{24,16},{32,40},{40,32},{48,56},{56,48},{64,72... | collective-permute-start | bytes 2359304 | tf_op jit(solution)/shard_map/ppermute | solution.py:22
  141.4 13.1 %collective-permute-start.17 = (bf16[2,2,192,256]{3,2,1,0:T(8,128)(2,1)S(1)}, bf16[2,2,192,256]{3,2,1,0:T(8,128)(2,1)S(1)}, u32[]{:S(2)}, u32[]{:S(2)}) collective-permute-start(bf16[2,2,192,256]{3,2,1,0:T(8,128)(2,1)S(1)} %fusion.25), channel_id=1, source_target_pairs={{0,16},{8,24},{16,0},{24,8},{32,48},{40,56},{48,32},{56,40},{64,80... | collective-permute-start | bytes 1179656 | tf_op jit(solution)/shard_map/ppermute | solution.py:22
  154.6 12.9 %collective-permute-start.18 = (bf16[2,192,256]{2,1,0:T(8,128)(2,1)S(1)}, bf16[2,192,256]{2,1,0:T(8,128)(2,1)S(1)}, u32[]{:S(2)}, u32[]{:S(2)}) collective-permute-start(bf16[2,192,256]{2,1,0:T(8,128)(2,1)S(1)} %fusion.29), channel_id=1, source_target_pairs={{0,32},{8,40},{16,48},{24,56},{32,0},{40,8},{48,16},{56,24},{64,96... | collective-permute-start | bytes 589832 | tf_op jit(solution)/shard_map/ppermute | solution.py:22
  167.6 14.4 %collective-permute-start.19 = (bf16[192,256]{1,0:T(8,128)(2,1)S(1)}, bf16[192,256]{1,0:T(8,128)(2,1)S(1)}, u32[]{:S(2)}, u32[]{:S(2)}) collective-permute-start(bf16[192,256]{1,0:T(8,128)(2,1)S(1)} %select_bitcast_fusion.8), channel_id=1, source_target_pairs={{0,64},{8,72},{16,80},{24,88},{32,96},{40,104},{48,112},{56,120},{... | collective-permute-start | bytes 294920 | tf_op jit(solution)/shard_map/ppermute | solution.py:22
  189.7 1.0 copy-start.1
  191.9 9.3 %collective-permute-start.26 = (f32[2,2,2,2,2,64,128]{6,5,2,0,3,1,4:T(8,128)}, f32[2,2,2,2,2,64,128]{6,5,2,0,3,1,4:T(8,128)}, u32[]{:S(2)}, u32[]{:S(2)}) collective-permute-start(f32[2,2,2,2,2,64,128]{6,5,2,0,3,1,4:T(8,128)} %select_bitcast_fusion), channel_id=1, source_target_pairs={{0,8},{8,0},{16,24},{24,16},{32,40},{40,32},{48,56},{56,48},{64,72... | collective-permute-start | bytes 3145736 | tf_op jit(solution)/shard_map/ppermute | solution.py:22
  198.4 2.7 %copy-start.2 = (f32[2,2,2,2,2,1,64,128]{7,6,5,4,3,2,1,0:T(8,128)S(1)}, f32[2,2,2,2,2,1,64,128]{7,6,5,4,3,2,1,0:T(8,128)}, u32[]{:S(2)}) copy-start(f32[2,2,2,2,2,1,64,128]{7,6,5,4,3,2,1,0:T(8,128)} %copy-done.1) | copy-start | bytes 3145732
  198.6 6.1 %collective-permute-start.20 = (f32[2,2,2,2,2,64,128]{6,5,2,0,3,1,4:T(8,128)S(1)}, f32[2,2,2,2,2,64,128]{6,5,2,0,3,1,4:T(8,128)S(1)}, u32[]{:S(2)}, u32[]{:S(2)}) collective-permute-start(f32[2,2,2,2,2,64,128]{6,5,2,0,3,1,4:T(8,128)S(1)} %select_bitcast_fusion.1), channel_id=1, source_target_pairs={{0,8},{8,0},{16,24},{24,16},{32,40},{40,32},{48,56},{56,48},{64,72... | collective-permute-start | bytes 3145736 | tf_op jit(solution)/shard_map/ppermute | solution.py:22
  202.8 15.7 %collective-permute-start.27 = (f32[2,2,2,2,64,128]{5,4,2,0,3,1:T(8,128)S(1)}, f32[2,2,2,2,64,128]{5,4,2,0,3,1:T(8,128)S(1)}, u32[]{:S(2)}, u32[]{:S(2)}) collective-permute-start(f32[2,2,2,2,64,128]{5,4,2,0,3,1:T(8,128)S(1)} %select_bitcast_fusion.2), channel_id=1, source_target_pairs={{0,16},{8,24},{16,0},{24,8},{32,48},{40,56},{48,32},{56,40},{64,80... | collective-permute-start | bytes 1572872 | tf_op jit(solution)/shard_map/ppermute | solution.py:22
  205.1 18.5 %collective-permute-start.21 = (f32[2,2,2,2,64,128]{5,4,1,0,2,3:T(8,128)S(1)}, f32[2,2,2,2,64,128]{5,4,1,0,2,3:T(8,128)S(1)}, u32[]{:S(2)}, u32[]{:S(2)}) collective-permute-start(f32[2,2,2,2,64,128]{5,4,1,0,2,3:T(8,128)S(1)} %select_bitcast_fusion.3), channel_id=1, source_target_pairs={{0,128},{128,0},{256,384},{384,256},{1,129},{129,1},{257,385},{385... | collective-permute-start | bytes 1572872 | tf_op jit(solution)/shard_map/ppermute | solution.py:22
  218.7 10.6 %collective-permute-start.28 = (f32[2,2,2,64,128]{4,3,1,0,2:T(8,128)S(1)}, f32[2,2,2,64,128]{4,3,1,0,2:T(8,128)S(1)}, u32[]{:S(2)}, u32[]{:S(2)}) collective-permute-start(f32[2,2,2,64,128]{4,3,1,0,2:T(8,128)S(1)} %select_bitcast_fusion.4), channel_id=1, source_target_pairs={{0,128},{128,0},{256,384},{384,256},{1,129},{129,1},{257,385},{385... | collective-permute-start | bytes 786440 | tf_op jit(solution)/shard_map/ppermute | solution.py:22
  223.8 9.0 %collective-permute-start.22 = (f32[2,2,2,64,128]{4,3,1,0,2:T(8,128)S(1)}, f32[2,2,2,64,128]{4,3,1,0,2:T(8,128)S(1)}, u32[]{:S(2)}, u32[]{:S(2)}) collective-permute-start(f32[2,2,2,64,128]{4,3,1,0,2:T(8,128)S(1)} %select_bitcast_fusion.5), channel_id=1, source_target_pairs={{0,16},{8,24},{16,0},{24,8},{32,48},{40,56},{48,32},{56,40},{64,80... | collective-permute-start | bytes 786440 | tf_op jit(solution)/shard_map/ppermute | solution.py:22
  229.3 9.5 %collective-permute-start.29 = (f32[2,2,64,128]{3,2,1,0:T(8,128)S(1)}, f32[2,2,64,128]{3,2,1,0:T(8,128)S(1)}, u32[]{:S(2)}, u32[]{:S(2)}) collective-permute-start(f32[2,2,64,128]{3,2,1,0:T(8,128)S(1)} %select_bitcast_fusion.6), channel_id=1, source_target_pairs={{0,32},{8,40},{16,48},{24,56},{32,0},{40,8},{48,16},{56,24},{64,96... | collective-permute-start | bytes 393224 | tf_op jit(solution)/shard_map/ppermute | solution.py:22
  232.9 11.4 %collective-permute-start.23 = (f32[2,2,64,128]{3,2,1,0:T(8,128)S(1)}, f32[2,2,64,128]{3,2,1,0:T(8,128)S(1)}, u32[]{:S(2)}, u32[]{:S(2)}) collective-permute-start(f32[2,2,64,128]{3,2,1,0:T(8,128)S(1)} %fusion.33), channel_id=1, source_target_pairs={{0,256},{128,384},{256,0},{384,128},{1,257},{129,385},{257,1},{385... | collective-permute-start | bytes 393224 | tf_op jit(solution)/shard_map/ppermute | solution.py:22
  238.9 7.7 %collective-permute-start.30 = (f32[2,64,128]{2,1,0:T(8,128)S(1)}, f32[2,64,128]{2,1,0:T(8,128)S(1)}, u32[]{:S(2)}, u32[]{:S(2)}) collective-permute-start(f32[2,64,128]{2,1,0:T(8,128)S(1)} %select_bitcast_fusion.9), channel_id=1, source_target_pairs={{0,256},{128,384},{256,0},{384,128},{1,257},{129,385},{257,1},{385... | collective-permute-start | bytes 196616 | tf_op jit(solution)/shard_map/ppermute | solution.py:22
  244.4 7.1 %collective-permute-start.24 = (f32[2,64,128]{2,1,0:T(8,128)S(1)}, f32[2,64,128]{2,1,0:T(8,128)S(1)}, u32[]{:S(2)}, u32[]{:S(2)}) collective-permute-start(f32[2,64,128]{2,1,0:T(8,128)S(1)} %select_bitcast_fusion.10), channel_id=1, source_target_pairs={{0,32},{8,40},{16,48},{24,56},{32,0},{40,8},{48,16},{56,24},{64,96... | collective-permute-start | bytes 196616 | tf_op jit(solution)/shard_map/ppermute | solution.py:22
  246.6 10.3 %collective-permute-start.31 = (f32[64,128]{1,0:T(8,128)S(1)}, f32[64,128]{1,0:T(8,128)S(1)}, u32[]{:S(2)}, u32[]{:S(2)}) collective-permute-start(f32[64,128]{1,0:T(8,128)S(1)} %select_bitcast_fusion.11), channel_id=1, source_target_pairs={{0,64},{8,72},{16,80},{24,88},{32,96},{40,104},{48,112},{56,120},{... | collective-permute-start | bytes 98312 | tf_op jit(solution)/shard_map/ppermute | solution.py:22
  251.5 9.7 %collective-permute-start.25 = (f32[64,128]{1,0:T(8,128)S(1)}, f32[64,128]{1,0:T(8,128)S(1)}, u32[]{:S(2)}, u32[]{:S(2)}) collective-permute-start(f32[64,128]{1,0:T(8,128)S(1)} %select_bitcast_fusion.12), channel_id=1, source_target_pairs={{0,64},{8,72},{16,80},{24,88},{32,96},{40,104},{48,112},{56,120},{... | collective-permute-start | bytes 98312 | tf_op jit(solution)/shard_map/ppermute | solution.py:22

commit v5 on v4

--- a/solution.py
+++ b/solution.py
@@ -53,6 +53,26 @@
         keep = jnp.where(mine, hi, lo)
         send = jnp.where(mine, lo, hi)
         total = keep.astype(acc) + _exchange(send, axis, size, bit).astype(acc)
+        cur = total if len(dims) == 1 else total.astype(x.dtype)
+        dims.pop(at)
+    return cur
+
+
+def gather_relative(x, steps):
+    cur = x
+    for axis, size, bit in steps:
+        cur = jnp.stack([cur, _exchange(cur, axis, size, bit)])
+    return cur
+
+
+def scatter_relative(x, steps):
+    dims = [bit for _, _, bit in steps][::-1]
+    cur = x
+    for axis, size, bit in steps[::-1]:
+        at = dims.index(bit)
+        keep = lax.index_in_dim(cur, 0, at, keepdims=False)
+        send = lax.index_in_dim(cur, 1, at, keepdims=False)
+        total = keep.astype(jnp.float32) + _exchange(send, axis, size, bit).astype(jnp.float32)
         cur = total if len(dims) == 1 else total.astype(x.dtype)
         dims.pop(at)
     return cur
@@ -144,15 +164,14 @@
     order_a = ctx_far[:1] + interleave(ctx_far[1:-1], dp_far) + ctx_far[-1:]
     order_b = ctx_far[:1] + interleave(dp_far, ctx_far[1:-1]) + ctx_far[-1:]
 
-    key_all = gather_blocks(key_proj, order_a, both_canon)
-    value_all = gather_blocks(value_proj, order_b, both_canon)
-    proj_all = jnp.concatenate([key_all, value_all], axis=1)
+    far_first = ctx_far[:1] + interleave(ctx_far[1:-1], dp_far) + ctx_far[-1:]
+    proj = jnp.concatenate([key_proj, value_proj], axis=1)
+    proj_all = gather_blocks(proj, far_first, both_canon)
     kv = jnp.dot(local_rows, proj_all, preferred_element_type=jnp.float32).astype(jnp.bfloat16)
     marks = segment[0].astype(jnp.bfloat16)
     marks_row = jnp.pad(marks, (0, 2 * HEAD_DIM - tok_rows))[None, :]
     kvm = jnp.concatenate([kv, marks_row], axis=0)[None]
-    ctx_far_first = ctx_far
-    kvm_all = gather_blocks(kvm, ctx_far_first, ctx_canon)
+    kvm_all = gather_relative(kvm, ctx_far).reshape((-1,) + kvm.shape[1:])
     keys = kvm_all[:, :tok_rows, :HEAD_DIM].reshape(-1, HEAD_DIM)
     values = kvm_all[:, :tok_rows, HEAD_DIM:].reshape(-1, HEAD_DIM)
     marks_all = kvm_all[:, tok_rows, :tok_rows].reshape(-1)
@@ -160,8 +179,8 @@
     mq = marks.astype(jnp.float32)[:, None]
     mk = marks_all.astype(jnp.float32)[None, :]
     grad_q, kv_part = attention_block(queries[0], grad_out[0], keys, values, mq, mk)
-    ctx_near_first = ctx_far_first[::-1]
-    kv_grad = scatter_sum(kv_part, ctx_near_first, ctx_canon, jnp.float32).astype(jnp.bfloat16)
+    kv_blocks = kv_part.reshape((2,) * len(ctx_far) + (tok_rows, kv_part.shape[1]))
+    kv_grad = scatter_relative(kv_blocks, ctx_far).astype(jnp.bfloat16)
 
     proj_part = jnp.einsum("td,tc->dc", local_rows, kv_grad, preferred_element_type=jnp.float32)
     key_sum = scatter_sum(proj_part[:, :width_kv], order_a[::-1], both_canon)

time: 265 us -> 255 us (0.962)
  other arithmetic: 15.4 us -> 9.35 us
  starting transfers between devices: 108 us -> 102 us
    ppermute x32 -> x26, starting transfers between devices: 108 us -> 102 us  [_exchange(): return lax.ppermute(x, axis, perm)]
    select_n x24 -> x11, other arithmetic: 5.64 us -> 1.69 us  [gather_blocks(): cur = jnp.where(mine, jnp.stack([recv, cur]), jnp.stack([cur, recv]))]
    ppermute x32 -> x26, waiting for transfers between devices: 101 us -> 103 us  [_exchange(): return lax.ppermute(x, axis, perm)]
  transfers between devices with their start and end apart: 32 -> 26, of which waited for: 20 -> 20; matrix products, arithmetic and copies ran while one was open for 5% -> 4% of each run, Pallas kernels for 0% -> 0%
where the time goes in v5:
time: 255 us; the launch traced here: 253 us
  waiting for transfers between devices  103 us (40%)
  starting transfers between devices  102 us (40%)
  local copies, waits for them, and re-layouts  20.2 us (8%)
  Pallas kernels  15.4 us (6%)
  other arithmetic  9.35 us (4%)
    ppermute x26, waiting for transfers between devices, _exchange(): return lax.ppermute(x, axis, perm)  103 us
    ppermute x26, starting transfers between devices, _exchange(): return lax.ppermute(x, axis, perm)  102 us
    pallas_call x1, Pallas kernels, attention_block(): pl.pallas_call(_attention_kernel, out_shape=(jax.ShapeDtypeStruct((rows,...  15.4 us
    slice x2, local copies, waits for them, and re-layouts, body(): value_sum = scatter_sum(proj_part[:, width_kv:], order_b[::-1], both_canon)  5.29 us
  transfers between devices with their start and end apart: 26, of which 20 were waited for; matrix products, arithmetic and copies ran while one was open for 4% of the time, Pallas kernels for 0%

profile of v5, /device:TPU:24, one launch (start us, length us, event | category | flops | bytes accessed | tf_op | source)
XLA Modules:
  0.0 252.5 jit_solution(12088782429160601272)
XLA Ops:
  0.6 0.8 constant_dynamic-update-slice_fusion.1
  1.5 0.7 constant_dynamic-update-slice_fusion
  2.2 9.1 %collective-permute-start = (bf16[64,256]{1,0:T(8,128)(2,1)S(1)}, bf16[64,256]{1,0:T(8,128)(2,1)S(1)}, u32[]{:S(2)}, u32[]{:S(2)}) collective-permute-start(bf16[64,256]{1,0:T(8,128)(2,1)S(1)} %constant_dynamic-update-slice_fusion), channel_id=1, source_target_pairs={{0,64},{8,72},{16,80},{24,88},{32,96},{40,104},{48,112},{56,120},{... | collective-permute-start | bytes 98312 | tf_op jit(solution)/shard_map/ppermute | solution.py:22
  11.3 1.9 collective-permute-done
  13.2 5.2 %collective-permute-start.1 = (bf16[2,64,256]{2,1,0:T(8,128)(2,1)S(1)}, bf16[2,64,256]{2,1,0:T(8,128)(2,1)S(1)}, u32[]{:S(2)}, u32[]{:S(2)}) collective-permute-start(bf16[2,64,256]{2,1,0:T(8,128)(2,1)S(1)} %maximum_select_fusion.6), channel_id=1, source_target_pairs={{0,32},{8,40},{16,48},{24,56},{32,0},{40,8},{48,16},{56,24},{64,96... | collective-permute-start | bytes 196616 | tf_op jit(solution)/shard_map/ppermute | solution.py:22
  18.4 3.6 %collective-permute-done.1 = bf16[2,64,256]{2,1,0:T(8,128)(2,1)S(1)} collective-permute-done((bf16[2,64,256]{2,1,0:T(8,128)(2,1)S(1)}, bf16[2,64,256]{2,1,0:T(8,128)(2,1)S(1)}, u32[]{:S(2)}, u32[]{:S(2)}) %collective-permute-start.1) | collective-permute-done | bytes 65568 | tf_op jit(solution)/shard_map/ppermute | solution.py:22
  22.0 4.9 %collective-permute-start.2 = (bf16[2,2,64,256]{3,2,0,1:T(8,128)(2,1)S(1)}, bf16[2,2,64,256]{3,2,0,1:T(8,128)(2,1)S(1)}, u32[]{:S(2)}, u32[]{:S(2)}) collective-permute-start(bf16[2,2,64,256]{3,2,0,1:T(8,128)(2,1)S(1)} %maximum_select_fusion.5), channel_id=1, source_target_pairs={{0,256},{128,384},{256,0},{384,128},{1,257},{129,385},{257,1},{385... | collective-permute-start | bytes 393224 | tf_op jit(solution)/shard_map/ppermute | solution.py:22
  27.0 3.4 %collective-permute-done.2 = bf16[2,2,64,256]{3,2,0,1:T(8,128)(2,1)S(1)} collective-permute-done((bf16[2,2,64,256]{3,2,0,1:T(8,128)(2,1)S(1)}, bf16[2,2,64,256]{3,2,0,1:T(8,128)(2,1)S(1)}, u32[]{:S(2)}, u32[]{:S(2)}) %collective-permute-start.2) | collective-permute-done | bytes 131104 | tf_op jit(solution)/shard_map/ppermute | solution.py:22
  30.4 2.4 collective-permute-start.3
  32.9 5.8 %collective-permute-done.3 = bf16[2,2,2,64,256]{4,3,1,2,0:T(8,128)(2,1)S(1)} collective-permute-done((bf16[2,2,2,64,256]{4,3,1,2,0:T(8,128)(2,1)S(1)}, bf16[2,2,2,64,256]{4,3,1,2,0:T(8,128)(2,1)S(1)}, u32[]{:S(2)}, u32[]{:S(2)}) %collective-permute-start.3) | collective-permute-done | bytes 262176 | tf_op jit(solution)/shard_map/ppermute | solution.py:22
  38.8 3.4 %collective-permute-start.4 = (bf16[2,2,2,2,64,256]{5,4,0,2,3,1:T(8,128)(2,1)S(1)}, bf16[2,2,2,2,64,256]{5,4,0,2,3,1:T(8,128)(2,1)S(1)}, u32[]{:S(2)}, u32[]{:S(2)}) collective-permute-start(bf16[2,2,2,2,64,256]{5,4,0,2,3,1:T(8,128)(2,1)S(1)} %maximum_select_fusion.3), channel_id=1, source_target_pairs={{0,128},{128,0},{256,384},{384,256},{1,129},{129,1},{257,385},{385... | collective-permute-start | bytes 1572872 | tf_op jit(solution)/shard_map/ppermute | solution.py:22
  42.4 7.5 %collective-permute-done.4 = bf16[2,2,2,2,64,256]{5,4,0,2,3,1:T(8,128)(2,1)S(1)} collective-permute-done((bf16[2,2,2,2,64,256]{5,4,0,2,3,1:T(8,128)(2,1)S(1)}, bf16[2,2,2,2,64,256]{5,4,0,2,3,1:T(8,128)(2,1)S(1)}, u32[]{:S(2)}, u32[]{:S(2)}) %collective-permute-start.4) | collective-permute-done | bytes 524320 | tf_op jit(solution)/shard_map/ppermute | solution.py:22
  49.8 1.1 maximum_select_fusion.1
  51.0 1.9 collective-permute-start.5
  53.1 2.8 %collective-permute-done.5 = bf16[2,2,2,2,2,64,256]{6,5,1,3,4,2,0:T(8,128)(2,1)} collective-permute-done((bf16[2,2,2,2,2,64,256]{6,5,1,3,4,2,0:T(8,128)(2,1)}, bf16[2,2,2,2,2,64,256]{6,5,1,3,4,2,0:T(8,128)(2,1)}, u32[]{:S(2)}, u32[]{:S(2)}) %collective-permute-start.5) | collective-permute-done | bytes 1048608 | tf_op jit(solution)/shard_map/ppermute | solution.py:22
  55.9 1.3 copy.113
  58.0 8.2 %collective-permute-start.6 = (bf16[1,193,256]{2,1,0:T(8,128)(2,1)S(1)}, bf16[1,193,256]{2,1,0:T(8,128)(2,1)S(1)}, u32[]{:S(2)}, u32[]{:S(2)}) collective-permute-start(bf16[1,193,256]{2,1,0:T(8,128)(2,1)S(1)} %get-tuple-element.29), channel_id=1, source_target_pairs={{0,64},{8,72},{16,80},{24,88},{32,96},{40,104},{48,112},{56,120},{... | collective-permute-start | bytes 296456 | tf_op jit(solution)/shard_map/ppermute | solution.py:22
  66.2 9.7 %collective-permute-done.6 = bf16[1,193,256]{2,1,0:T(8,128)(2,1)S(1)} collective-permute-done((bf16[1,193,256]{2,1,0:T(8,128)(2,1)S(1)}, bf16[1,193,256]{2,1,0:T(8,128)(2,1)S(1)}, u32[]{:S(2)}, u32[]{:S(2)}) %collective-permute-start.6) | collective-permute-done | bytes 98848 | tf_op jit(solution)/shard_map/ppermute | solution.py:22
  75.9 2.1 collective-permute-start.7
  78.0 9.8 %collective-permute-done.7 = bf16[2,1,193,256]{3,2,1,0:T(8,128)(2,1)S(1)} collective-permute-done((bf16[2,1,193,256]{3,2,1,0:T(8,128)(2,1)S(1)}, bf16[2,1,193,256]{3,2,1,0:T(8,128)(2,1)S(1)}, u32[]{:S(2)}, u32[]{:S(2)}) %collective-permute-start.7) | collective-permute-done | bytes 197664 | tf_op jit(solution)/shard_map/ppermute | solution.py:22
  87.9 2.1 collective-permute-start.8
  90.0 9.6 %collective-permute-done.8 = bf16[2,2,1,193,256]{4,3,1,2,0:T(8,128)(2,1)S(1)} collective-permute-done((bf16[2,2,1,193,256]{4,3,1,2,0:T(8,128)(2,1)S(1)}, bf16[2,2,1,193,256]{4,3,1,2,0:T(8,128)(2,1)S(1)}, u32[]{:S(2)}, u32[]{:S(2)}) %collective-permute-start.8) | collective-permute-done | bytes 395296 | tf_op jit(solution)/shard_map/ppermute | solution.py:22
  100.3 2.1 collective-permute-start.9
  102.4 0.8 copy.66.mq_ref
  103.2 1.4 collective-permute-done.9
  104.6 1.2 copy.114
  106.1 1.6 fusion.31
  107.7 0.7 reshape.648.mk_ref
  108.3 15.4 %shard_map.85 = (bf16[192,512]{1,0:T(8,128)(2,1)}, bf16[3072,256]{1,0:T(8,128)(2,1)}) custom-call(bf16[192,512]{1,0:T(8,128)(2,1)} %bitcast.239, bf16[192,512]{1,0:T(8,128)(2,1)} %bitcast.240, bf16[3072,128]{1,0:T(8,128)(2,1)} %bitcast.226, bf16[3072,128]{1,0:T(8,128)(2,1)} %bitcast.225, f32[192,1]{1,0:T(8,128)} %copy.66.mq_ref, f32[1,3072]{1,0:T(1,128)} %reshape.648.mk_ref), custom_call_target="tpu_custom_call" | custom-call | flops 3623878656 | bytes 3932160 | tf_op jit(solution)/shard_map/pallas_call | solution.py:120
  123.8 1.5 fusion.32
  125.2 2.0 collective-permute-start.10
  127.3 2.1 collective-permute-done.10
  129.7 3.6 %collective-permute-start.11 = (bf16[2,2,192,256]{3,2,1,0:T(8,128)(2,1)S(1)}, bf16[2,2,192,256]{3,2,1,0:T(8,128)(2,1)S(1)}, u32[]{:S(2)}, u32[]{:S(2)}) collective-permute-start(bf16[2,2,192,256]{3,2,1,0:T(8,128)(2,1)S(1)} %slice_bitcast_fusion), channel_id=1, source_target_pairs={{0,16},{8,24},{16,0},{24,8},{32,48},{40,56},{48,32},{56,40},{64,80... | collective-permute-start | bytes 1179656 | tf_op jit(solution)/shard_map/ppermute | solution.py:22
  133.3 9.4 %collective-permute-done.11 = bf16[2,2,192,256]{3,2,1,0:T(8,128)(2,1)S(1)} collective-permute-done((bf16[2,2,192,256]{3,2,1,0:T(8,128)(2,1)S(1)}, bf16[2,2,192,256]{3,2,1,0:T(8,128)(2,1)S(1)}, u32[]{:S(2)}, u32[]{:S(2)}) %collective-permute-start.11) | collective-permute-done | bytes 393248 | tf_op jit(solution)/shard_map/ppermute | solution.py:22
  142.8 5.3 %collective-permute-start.12 = (bf16[2,192,256]{2,1,0:T(8,128)(2,1)S(1)}, bf16[2,192,256]{2,1,0:T(8,128)(2,1)S(1)}, u32[]{:S(2)}, u32[]{:S(2)}) collective-permute-start(bf16[2,192,256]{2,1,0:T(8,128)(2,1)S(1)} %slice_bitcast_fusion.2), channel_id=1, source_target_pairs={{0,32},{8,40},{16,48},{24,56},{32,0},{40,8},{48,16},{56,24},{64,96... | collective-permute-start | bytes 589832 | tf_op jit(solution)/shard_map/ppermute | solution.py:22
  148.1 8.6 %collective-permute-done.12 = bf16[2,192,256]{2,1,0:T(8,128)(2,1)S(1)} collective-permute-done((bf16[2,192,256]{2,1,0:T(8,128)(2,1)S(1)}, bf16[2,192,256]{2,1,0:T(8,128)(2,1)S(1)}, u32[]{:S(2)}, u32[]{:S(2)}) %collective-permute-start.12) | collective-permute-done | bytes 196640 | tf_op jit(solution)/shard_map/ppermute | solution.py:22
  156.8 8.0 %collective-permute-start.13 = (bf16[192,256]{1,0:T(8,128)(2,1)S(1)}, bf16[192,256]{1,0:T(8,128)(2,1)S(1)}, u32[]{:S(2)}, u32[]{:S(2)}) collective-permute-start(bf16[192,256]{1,0:T(8,128)(2,1)S(1)} %slice_bitcast_fusion.4), channel_id=1, source_target_pairs={{0,64},{8,72},{16,80},{24,88},{32,96},{40,104},{48,112},{56,120},{... | collective-permute-start | bytes 294920 | tf_op jit(solution)/shard_map/ppermute | solution.py:22
  164.8 7.0 %collective-permute-done.13 = bf16[192,256]{1,0:T(8,128)(2,1)S(1)} collective-permute-done((bf16[192,256]{1,0:T(8,128)(2,1)S(1)}, bf16[192,256]{1,0:T(8,128)(2,1)S(1)}, u32[]{:S(2)}, u32[]{:S(2)}) %collective-permute-start.13) | collective-permute-done | bytes 98336 | tf_op jit(solution)/shard_map/ppermute | solution.py:22
  171.8 0.7 convolution_bitcast_fusion
  172.6 2.3 fusion.28
  174.9 3.0 %copy.85 = f32[4096,128]{1,0:T(8,128)} copy(f32[4096,128]{0,1:T(8,128)} %get-tuple-element.7) | data formatting | bytes 4194304 | tf_op jit(solution)/shard_map/slice | solution.py:187
  177.9 1.7 fusion.29
  179.6 1.0 copy-done.1
  180.6 1.1 select_bitcast_fusion
  181.7 1.9 collective-permute-start.20
  183.6 2.9 %copy.67 = f32[4096,128]{1,0:T(8,128)} copy(f32[4096,128]{0,1:T(8,128)} %get-tuple-element.8) | data formatting | bytes 4194304 | tf_op jit(solution)/shard_map/slice | solution.py:186
  186.5 2.0 fusion.30
  188.5 2.4 collective-permute-start.14
  191.0 1.5 bitcast_add_fusion
  192.5 1.9 collective-permute-start.21
  194.8 3.4 %collective-permute-start.15 = (f32[2,2,2,2,64,128]{5,4,3,2,1,0:T(8,128)S(1)}, f32[2,2,2,2,64,128]{5,4,3,2,1,0:T(8,128)S(1)}, u32[]{:S(2)}, u32[]{:S(2)}) collective-permute-start(f32[2,2,2,2,64,128]{5,4,3,2,1,0:T(8,128)S(1)} %select_bitcast_fusion.3), channel_id=1, source_target_pairs={{0,128},{128,0},{256,384},{384,256},{1,129},{129,1},{257,385},{385... | collective-permute-start | bytes 1572872 | tf_op jit(solution)/shard_map/ppermute | solution.py:22
  198.2 10.0 %collective-permute-done.21 = f32[2,2,2,2,64,128]{5,4,2,0,3,1:T(8,128)S(1)} collective-permute-done((f32[2,2,2,2,64,128]{5,4,2,0,3,1:T(8,128)S(1)}, f32[2,2,2,2,64,128]{5,4,2,0,3,1:T(8,128)S(1)}, u32[]{:S(2)}, u32[]{:S(2)}) %collective-permute-start.21) | collective-permute-done | bytes 524320 | tf_op jit(solution)/shard_map/ppermute | solution.py:22
  208.4 3.4 %collective-permute-start.22 = (f32[2,2,2,64,128]{4,3,1,0,2:T(8,128)S(1)}, f32[2,2,2,64,128]{4,3,1,0,2:T(8,128)S(1)}, u32[]{:S(2)}, u32[]{:S(2)}) collective-permute-start(f32[2,2,2,64,128]{4,3,1,0,2:T(8,128)S(1)} %select_bitcast_fusion.4), channel_id=1, source_target_pairs={{0,128},{128,0},{256,384},{384,256},{1,129},{129,1},{257,385},{385... | collective-permute-start | bytes 786440 | tf_op jit(solution)/shard_map/ppermute | solution.py:22
  212.0 2.4 collective-permute-start.16
  214.4 3.3 %collective-permute-done.22 = f32[2,2,2,64,128]{4,3,1,0,2:T(8,128)S(1)} collective-permute-done((f32[2,2,2,64,128]{4,3,1,0,2:T(8,128)S(1)}, f32[2,2,2,64,128]{4,3,1,0,2:T(8,128)S(1)}, u32[]{:S(2)}, u32[]{:S(2)}) %collective-permute-start.22) | collective-permute-done | bytes 262176 | tf_op jit(solution)/shard_map/ppermute | solution.py:22
  217.7 2.9 %collective-permute-start.23 = (f32[2,2,64,128]{3,2,1,0:T(8,128)S(1)}, f32[2,2,64,128]{3,2,1,0:T(8,128)S(1)}, u32[]{:S(2)}, u32[]{:S(2)}) collective-permute-start(f32[2,2,64,128]{3,2,1,0:T(8,128)S(1)} %select_bitcast_fusion.6), channel_id=1, source_target_pairs={{0,32},{8,40},{16,48},{24,56},{32,0},{40,8},{48,16},{56,24},{64,96... | collective-permute-start | bytes 393224 | tf_op jit(solution)/shard_map/ppermute | solution.py:22
  221.0 4.7 %collective-permute-start.17 = (f32[2,2,64,128]{3,2,1,0:T(8,128)S(1)}, f32[2,2,64,128]{3,2,1,0:T(8,128)S(1)}, u32[]{:S(2)}, u32[]{:S(2)}) collective-permute-start(f32[2,2,64,128]{3,2,1,0:T(8,128)S(1)} %select_bitcast_fusion.7), channel_id=1, source_target_pairs={{0,256},{128,384},{256,0},{384,128},{1,257},{129,385},{257,1},{385... | collective-permute-start | bytes 393224 | tf_op jit(solution)/shard_map/ppermute | solution.py:22
  225.7 1.3 collective-permute-done.23
  227.0 4.9 %collective-permute-start.24 = (f32[2,64,128]{2,1,0:T(8,128)S(1)}, f32[2,64,128]{2,1,0:T(8,128)S(1)}, u32[]{:S(2)}, u32[]{:S(2)}) collective-permute-start(f32[2,64,128]{2,1,0:T(8,128)S(1)} %select_bitcast_fusion.8), channel_id=1, source_target_pairs={{0,256},{128,384},{256,0},{384,128},{1,257},{129,385},{257,1},{385... | collective-permute-start | bytes 196616 | tf_op jit(solution)/shard_map/ppermute | solution.py:22
  232.0 1.9 collective-permute-start.18
  234.0 0.7 collective-permute-done.24
  234.7 7.4 %collective-permute-start.25 = (f32[64,128]{1,0:T(8,128)S(1)}, f32[64,128]{1,0:T(8,128)S(1)}, u32[]{:S(2)}, u32[]{:S(2)}) collective-permute-start(f32[64,128]{1,0:T(8,128)S(1)} %select_bitcast_fusion.10), channel_id=1, source_target_pairs={{0,64},{8,72},{16,80},{24,88},{32,96},{40,104},{48,112},{56,120},{... | collective-permute-start | bytes 98312 | tf_op jit(solution)/shard_map/ppermute | solution.py:22
  242.2 4.7 %collective-permute-start.19 = (f32[64,128]{1,0:T(8,128)S(1)}, f32[64,128]{1,0:T(8,128)S(1)}, u32[]{:S(2)}, u32[]{:S(2)}) collective-permute-start(f32[64,128]{1,0:T(8,128)S(1)} %select_bitcast_fusion.11), channel_id=1, source_target_pairs={{0,64},{8,72},{16,80},{24,88},{32,96},{40,104},{48,112},{56,120},{... | collective-permute-start | bytes 98312 | tf_op jit(solution)/shard_map/ppermute | solution.py:22
  247.5 4.4 %collective-permute-done.19 = f32[64,128]{1,0:T(8,128)S(1)} collective-permute-done((f32[64,128]{1,0:T(8,128)S(1)}, f32[64,128]{1,0:T(8,128)S(1)}, u32[]{:S(2)}, u32[]{:S(2)}) %collective-permute-start.19) | collective-permute-done | bytes 32800 | tf_op jit(solution)/shard_map/ppermute | solution.py:22
  (68 shorter events, 5.2 us)
Async XLA Ops:
  0.6 56.7 %copy-start = (bf16[1,192,4096]{2,1,0:T(8,128)(2,1)S(1)}, bf16[1,192,4096]{2,1,0:T(8,128)(2,1)}, u32[]{:S(2)}) copy-start(bf16[1,192,4096]{2,1,0:T(8,128)(2,1)} %param.6) | copy-start | bytes 4718596
  2.2 11.0 %collective-permute-start = (bf16[64,256]{1,0:T(8,128)(2,1)S(1)}, bf16[64,256]{1,0:T(8,128)(2,1)S(1)}, u32[]{:S(2)}, u32[]{:S(2)}) collective-permute-start(bf16[64,256]{1,0:T(8,128)(2,1)S(1)} %constant_dynamic-update-slice_fusion), channel_id=1, source_target_pairs={{0,64},{8,72},{16,80},{24,88},{32,96},{40,104},{48,112},{56,120},{... | collective-permute-start | bytes 98312 | tf_op jit(solution)/shard_map/ppermute | solution.py:22
  13.2 8.8 %collective-permute-start.1 = (bf16[2,64,256]{2,1,0:T(8,128)(2,1)S(1)}, bf16[2,64,256]{2,1,0:T(8,128)(2,1)S(1)}, u32[]{:S(2)}, u32[]{:S(2)}) collective-permute-start(bf16[2,64,256]{2,1,0:T(8,128)(2,1)S(1)} %maximum_select_fusion.6), channel_id=1, source_target_pairs={{0,32},{8,40},{16,48},{24,56},{32,0},{40,8},{48,16},{56,24},{64,96... | collective-permute-start | bytes 196616 | tf_op jit(solution)/shard_map/ppermute | solution.py:22
  22.0 8.4 %collective-permute-start.2 = (bf16[2,2,64,256]{3,2,0,1:T(8,128)(2,1)S(1)}, bf16[2,2,64,256]{3,2,0,1:T(8,128)(2,1)S(1)}, u32[]{:S(2)}, u32[]{:S(2)}) collective-permute-start(bf16[2,2,64,256]{3,2,0,1:T(8,128)(2,1)S(1)} %maximum_select_fusion.5), channel_id=1, source_target_pairs={{0,256},{128,384},{256,0},{384,128},{1,257},{129,385},{257,1},{385... | collective-permute-start | bytes 393224 | tf_op jit(solution)/shard_map/ppermute | solution.py:22
  30.4 8.3 %collective-permute-start.3 = (bf16[2,2,2,64,256]{4,3,1,2,0:T(8,128)(2,1)S(1)}, bf16[2,2,2,64,256]{4,3,1,2,0:T(8,128)(2,1)S(1)}, u32[]{:S(2)}, u32[]{:S(2)}) collective-permute-start(bf16[2,2,2,64,256]{4,3,1,2,0:T(8,128)(2,1)S(1)} %maximum_select_fusion.4), channel_id=1, source_target_pairs={{0,16},{8,24},{16,0},{24,8},{32,48},{40,56},{48,32},{56,40},{64,80... | collective-permute-start | bytes 786440 | tf_op jit(solution)/shard_map/ppermute | solution.py:22
  38.8 11.1 %collective-permute-start.4 = (bf16[2,2,2,2,64,256]{5,4,0,2,3,1:T(8,128)(2,1)S(1)}, bf16[2,2,2,2,64,256]{5,4,0,2,3,1:T(8,128)(2,1)S(1)}, u32[]{:S(2)}, u32[]{:S(2)}) collective-permute-start(bf16[2,2,2,2,64,256]{5,4,0,2,3,1:T(8,128)(2,1)S(1)} %maximum_select_fusion.3), channel_id=1, source_target_pairs={{0,128},{128,0},{256,384},{384,256},{1,129},{129,1},{257,385},{385... | collective-permute-start | bytes 1572872 | tf_op jit(solution)/shard_map/ppermute | solution.py:22
  42.3 10.6 %copy-start.3 = (s32[1,192]{1,0:T(1,128)S(1)}, s32[1,192]{1,0:T(1,128)}, u32[]{:S(2)}) copy-start(s32[1,192]{1,0:T(1,128)} %param.9) | copy-start | bytes 2308
  51.0 4.9 %collective-permute-start.5 = (bf16[2,2,2,2,2,64,256]{6,5,1,3,4,2,0:T(8,128)(2,1)}, bf16[2,2,2,2,2,64,256]{6,5,1,3,4,2,0:T(8,128)(2,1)}, u32[]{:S(2)}, u32[]{:S(2)}) collective-permute-start(bf16[2,2,2,2,2,64,256]{6,5,1,3,4,2,0:T(8,128)(2,1)} %maximum_select_fusion.1), channel_id=1, source_target_pairs={{0,8},{8,0},{16,24},{24,16},{32,40},{40,32},{48,56},{56,48},{64,72... | collective-permute-start | bytes 3145736 | tf_op jit(solution)/shard_map/ppermute | solution.py:22
  58.0 17.9 %collective-permute-start.6 = (bf16[1,193,256]{2,1,0:T(8,128)(2,1)S(1)}, bf16[1,193,256]{2,1,0:T(8,128)(2,1)S(1)}, u32[]{:S(2)}, u32[]{:S(2)}) collective-permute-start(bf16[1,193,256]{2,1,0:T(8,128)(2,1)S(1)} %get-tuple-element.29), channel_id=1, source_target_pairs={{0,64},{8,72},{16,80},{24,88},{32,96},{40,104},{48,112},{56,120},{... | collective-permute-start | bytes 296456 | tf_op jit(solution)/shard_map/ppermute | solution.py:22
  75.9 11.9 %collective-permute-start.7 = (bf16[2,1,193,256]{3,2,1,0:T(8,128)(2,1)S(1)}, bf16[2,1,193,256]{3,2,1,0:T(8,128)(2,1)S(1)}, u32[]{:S(2)}, u32[]{:S(2)}) collective-permute-start(bf16[2,1,193,256]{3,2,1,0:T(8,128)(2,1)S(1)} %get-tuple-element.25), channel_id=1, source_target_pairs={{0,32},{8,40},{16,48},{24,56},{32,0},{40,8},{48,16},{56,24},{64,96... | collective-permute-start | bytes 592904 | tf_op jit(solution)/shard_map/ppermute | solution.py:22
  87.9 11.7 %collective-permute-start.8 = (bf16[2,2,1,193,256]{4,3,1,2,0:T(8,128)(2,1)S(1)}, bf16[2,2,1,193,256]{4,3,1,2,0:T(8,128)(2,1)S(1)}, u32[]{:S(2)}, u32[]{:S(2)}) collective-permute-start(bf16[2,2,1,193,256]{4,3,1,2,0:T(8,128)(2,1)S(1)} %get-tuple-element.23), channel_id=1, source_target_pairs={{0,16},{8,24},{16,0},{24,8},{32,48},{40,56},{48,32},{56,40},{64,80... | collective-permute-start | bytes 1185800 | tf_op jit(solution)/shard_map/ppermute | solution.py:22
  100.3 4.3 %collective-permute-start.9 = (bf16[2,2,2,1,193,256]{5,2,4,3,1,0:T(2,128)(2,1)S(1)}, bf16[2,2,2,1,193,256]{5,2,4,3,1,0:T(2,128)(2,1)}, u32[]{:S(2)}, u32[]{:S(2)}) collective-permute-start(bf16[2,2,2,1,193,256]{5,2,4,3,1,0:T(2,128)(2,1)S(1)} %copy.63), channel_id=1, source_target_pairs={{0,8},{8,0},{16,24},{24,16},{32,40},{40,32},{48,56},{56,48},{64,72... | collective-permute-start | bytes 2371592 | tf_op jit(solution)/shard_map/ppermute | solution.py:22
  125.2 4.2 %collective-permute-start.10 = (bf16[2,2,2,192,256]{4,3,2,1,0:T(8,128)(2,1)S(1)}, bf16[2,2,2,192,256]{4,3,2,1,0:T(8,128)(2,1)S(1)}, u32[]{:S(2)}, u32[]{:S(2)}) collective-permute-start(bf16[2,2,2,192,256]{4,3,2,1,0:T(8,128)(2,1)S(1)} %bitcast.227), channel_id=1, source_target_pairs={{0,8},{8,0},{16,24},{24,16},{32,40},{40,32},{48,56},{56,48},{64,72... | collective-permute-start | bytes 2359304 | tf_op jit(solution)/shard_map/ppermute | solution.py:22
  129.7 13.1 %collective-permute-start.11 = (bf16[2,2,192,256]{3,2,1,0:T(8,128)(2,1)S(1)}, bf16[2,2,192,256]{3,2,1,0:T(8,128)(2,1)S(1)}, u32[]{:S(2)}, u32[]{:S(2)}) collective-permute-start(bf16[2,2,192,256]{3,2,1,0:T(8,128)(2,1)S(1)} %slice_bitcast_fusion), channel_id=1, source_target_pairs={{0,16},{8,24},{16,0},{24,8},{32,48},{40,56},{48,32},{56,40},{64,80... | collective-permute-start | bytes 1179656 | tf_op jit(solution)/shard_map/ppermute | solution.py:22
  142.8 13.9 %collective-permute-start.12 = (bf16[2,192,256]{2,1,0:T(8,128)(2,1)S(1)}, bf16[2,192,256]{2,1,0:T(8,128)(2,1)S(1)}, u32[]{:S(2)}, u32[]{:S(2)}) collective-permute-start(bf16[2,192,256]{2,1,0:T(8,128)(2,1)S(1)} %slice_bitcast_fusion.2), channel_id=1, source_target_pairs={{0,32},{8,40},{16,48},{24,56},{32,0},{40,8},{48,16},{56,24},{64,96... | collective-permute-start | bytes 589832 | tf_op jit(solution)/shard_map/ppermute | solution.py:22
  156.8 15.0 %collective-permute-start.13 = (bf16[192,256]{1,0:T(8,128)(2,1)S(1)}, bf16[192,256]{1,0:T(8,128)(2,1)S(1)}, u32[]{:S(2)}, u32[]{:S(2)}) collective-permute-start(bf16[192,256]{1,0:T(8,128)(2,1)S(1)} %slice_bitcast_fusion.4), channel_id=1, source_target_pairs={{0,64},{8,72},{16,80},{24,88},{32,96},{40,104},{48,112},{56,120},{... | collective-permute-start | bytes 294920 | tf_op jit(solution)/shard_map/ppermute | solution.py:22
  179.6 1.0 copy-start.1
  181.7 9.3 %collective-permute-start.20 = (f32[2,2,2,2,2,64,128]{6,5,2,0,3,1,4:T(8,128)}, f32[2,2,2,2,2,64,128]{6,5,2,0,3,1,4:T(8,128)}, u32[]{:S(2)}, u32[]{:S(2)}) collective-permute-start(f32[2,2,2,2,2,64,128]{6,5,2,0,3,1,4:T(8,128)} %select_bitcast_fusion), channel_id=1, source_target_pairs={{0,8},{8,0},{16,24},{24,16},{32,40},{40,32},{48,56},{56,48},{64,72... | collective-permute-start | bytes 3145736 | tf_op jit(solution)/shard_map/ppermute | solution.py:22
  186.5 4.4 %copy-start.2 = (f32[2,2,2,2,2,1,64,128]{7,6,5,4,3,2,1,0:T(8,128)S(1)}, f32[2,2,2,2,2,1,64,128]{7,6,5,4,3,2,1,0:T(8,128)}, u32[]{:S(2)}) copy-start(f32[2,2,2,2,2,1,64,128]{7,6,5,4,3,2,1,0:T(8,128)} %copy-done.1) | copy-start | bytes 3145732
  188.5 5.9 %collective-permute-start.14 = (f32[2,2,2,2,2,64,128]{6,5,4,3,2,1,0:T(8,128)S(1)}, f32[2,2,2,2,2,64,128]{6,5,4,3,2,1,0:T(8,128)S(1)}, u32[]{:S(2)}, u32[]{:S(2)}) collective-permute-start(f32[2,2,2,2,2,64,128]{6,5,4,3,2,1,0:T(8,128)S(1)} %get-tuple-element.12), channel_id=1, source_target_pairs={{0,8},{8,0},{16,24},{24,16},{32,40},{40,32},{48,56},{56,48},{64,72... | collective-permute-start | bytes 3145736 | tf_op jit(solution)/shard_map/ppermute | solution.py:22
  192.5 15.7 %collective-permute-start.21 = (f32[2,2,2,2,64,128]{5,4,2,0,3,1:T(8,128)S(1)}, f32[2,2,2,2,64,128]{5,4,2,0,3,1:T(8,128)S(1)}, u32[]{:S(2)}, u32[]{:S(2)}) collective-permute-start(f32[2,2,2,2,64,128]{5,4,2,0,3,1:T(8,128)S(1)} %select_bitcast_fusion.2), channel_id=1, source_target_pairs={{0,16},{8,24},{16,0},{24,8},{32,48},{40,56},{48,32},{56,40},{64,80... | collective-permute-start | bytes 1572872 | tf_op jit(solution)/shard_map/ppermute | solution.py:22
  194.8 17.0 %collective-permute-start.15 = (f32[2,2,2,2,64,128]{5,4,3,2,1,0:T(8,128)S(1)}, f32[2,2,2,2,64,128]{5,4,3,2,1,0:T(8,128)S(1)}, u32[]{:S(2)}, u32[]{:S(2)}) collective-permute-start(f32[2,2,2,2,64,128]{5,4,3,2,1,0:T(8,128)S(1)} %select_bitcast_fusion.3), channel_id=1, source_target_pairs={{0,128},{128,0},{256,384},{384,256},{1,129},{129,1},{257,385},{385... | collective-permute-start | bytes 1572872 | tf_op jit(solution)/shard_map/ppermute | solution.py:22
  208.4 9.3 %collective-permute-start.22 = (f32[2,2,2,64,128]{4,3,1,0,2:T(8,128)S(1)}, f32[2,2,2,64,128]{4,3,1,0,2:T(8,128)S(1)}, u32[]{:S(2)}, u32[]{:S(2)}) collective-permute-start(f32[2,2,2,64,128]{4,3,1,0,2:T(8,128)S(1)} %select_bitcast_fusion.4), channel_id=1, source_target_pairs={{0,128},{128,0},{256,384},{384,256},{1,129},{129,1},{257,385},{385... | collective-permute-start | bytes 786440 | tf_op jit(solution)/shard_map/ppermute | solution.py:22
  212.0 9.0 %collective-permute-start.16 = (f32[2,2,2,64,128]{4,3,2,1,0:T(8,128)S(1)}, f32[2,2,2,64,128]{4,3,2,1,0:T(8,128)S(1)}, u32[]{:S(2)}, u32[]{:S(2)}) collective-permute-start(f32[2,2,2,64,128]{4,3,2,1,0:T(8,128)S(1)} %select_bitcast_fusion.5), channel_id=1, source_target_pairs={{0,16},{8,24},{16,0},{24,8},{32,48},{40,56},{48,32},{56,40},{64,80... | collective-permute-start | bytes 786440 | tf_op jit(solution)/shard_map/ppermute | solution.py:22
  217.7 9.2 %collective-permute-start.23 = (f32[2,2,64,128]{3,2,1,0:T(8,128)S(1)}, f32[2,2,64,128]{3,2,1,0:T(8,128)S(1)}, u32[]{:S(2)}, u32[]{:S(2)}) collective-permute-start(f32[2,2,64,128]{3,2,1,0:T(8,128)S(1)} %select_bitcast_fusion.6), channel_id=1, source_target_pairs={{0,32},{8,40},{16,48},{24,56},{32,0},{40,8},{48,16},{56,24},{64,96... | collective-permute-start | bytes 393224 | tf_op jit(solution)/shard_map/ppermute | solution.py:22
  221.0 10.9 %collective-permute-start.17 = (f32[2,2,64,128]{3,2,1,0:T(8,128)S(1)}, f32[2,2,64,128]{3,2,1,0:T(8,128)S(1)}, u32[]{:S(2)}, u32[]{:S(2)}) collective-permute-start(f32[2,2,64,128]{3,2,1,0:T(8,128)S(1)} %select_bitcast_fusion.7), channel_id=1, source_target_pairs={{0,256},{128,384},{256,0},{384,128},{1,257},{129,385},{257,1},{385... | collective-permute-start | bytes 393224 | tf_op jit(solution)/shard_map/ppermute | solution.py:22
  227.0 7.7 %collective-permute-start.24 = (f32[2,64,128]{2,1,0:T(8,128)S(1)}, f32[2,64,128]{2,1,0:T(8,128)S(1)}, u32[]{:S(2)}, u32[]{:S(2)}) collective-permute-start(f32[2,64,128]{2,1,0:T(8,128)S(1)} %select_bitcast_fusion.8), channel_id=1, source_target_pairs={{0,256},{128,384},{256,0},{384,128},{1,257},{129,385},{257,1},{385... | collective-permute-start | bytes 196616 | tf_op jit(solution)/shard_map/ppermute | solution.py:22
  232.0 10.1 %collective-permute-start.18 = (f32[2,64,128]{2,1,0:T(8,128)S(1)}, f32[2,64,128]{2,1,0:T(8,128)S(1)}, u32[]{:S(2)}, u32[]{:S(2)}) collective-permute-start(f32[2,64,128]{2,1,0:T(8,128)S(1)} %select_bitcast_fusion.9), channel_id=1, source_target_pairs={{0,32},{8,40},{16,48},{24,56},{32,0},{40,8},{48,16},{56,24},{64,96... | collective-permute-start | bytes 196616 | tf_op jit(solution)/shard_map/ppermute | solution.py:22
  234.7 12.1 %collective-permute-start.25 = (f32[64,128]{1,0:T(8,128)S(1)}, f32[64,128]{1,0:T(8,128)S(1)}, u32[]{:S(2)}, u32[]{:S(2)}) collective-permute-start(f32[64,128]{1,0:T(8,128)S(1)} %select_bitcast_fusion.10), channel_id=1, source_target_pairs={{0,64},{8,72},{16,80},{24,88},{32,96},{40,104},{48,112},{56,120},{... | collective-permute-start | bytes 98312 | tf_op jit(solution)/shard_map/ppermute | solution.py:22
  242.2 9.7 %collective-permute-start.19 = (f32[64,128]{1,0:T(8,128)S(1)}, f32[64,128]{1,0:T(8,128)S(1)}, u32[]{:S(2)}, u32[]{:S(2)}) collective-permute-start(f32[64,128]{1,0:T(8,128)S(1)} %select_bitcast_fusion.11), channel_id=1, source_target_pairs={{0,64},{8,72},{16,80},{24,88},{32,96},{40,104},{48,112},{56,120},{... | collective-permute-start | bytes 98312 | tf_op jit(solution)/shard_map/ppermute | solution.py:22

commit v6 on v5

--- a/solution.py
+++ b/solution.py
@@ -182,9 +182,11 @@
     kv_blocks = kv_part.reshape((2,) * len(ctx_far) + (tok_rows, kv_part.shape[1]))
     kv_grad = scatter_relative(kv_blocks, ctx_far).astype(jnp.bfloat16)
 
-    proj_part = jnp.einsum("td,tc->dc", local_rows, kv_grad, preferred_element_type=jnp.float32)
-    key_sum = scatter_sum(proj_part[:, :width_kv], order_a[::-1], both_canon)
-    value_sum = scatter_sum(proj_part[:, width_kv:], order_b[::-1], both_canon)
+    dims_t = (((0,), (0,)), ((), ()))
+    key_part = lax.dot_general(local_rows, kv_grad[:, :width_kv], dims_t, preferred_element_type=jnp.float32)
+    value_part = lax.dot_general(local_rows, kv_grad[:, width_kv:], dims_t, preferred_element_type=jnp.float32)
+    key_sum = scatter_sum(key_part.astype(jnp.bfloat16), order_a[::-1], both_canon, jnp.float32)
+    value_sum = scatter_sum(value_part.astype(jnp.bfloat16), order_b[::-1], both_canon, jnp.float32)
     grad_queries = grad_q[None]
     return (grad_queries, key_sum, value_sum)
 

time: 255 us -> 237 us (0.929)
  waiting for transfers between devices: 103 us -> 96.6 us
  local copies, waits for them, and re-layouts: 20.2 us -> 14.2 us
  starting transfers between devices: 102 us -> 99.2 us
    slice x3 -> x0, local copies, waits for them, and re-layouts: 8.2 us -> none  [the longest x2 5.29 us: body(): value_sum = scatter_sum(proj_part[:, width_kv:], order_b[::-1], both_canon)]
    ppermute x26, waiting for transfers between devices: 103 us -> 96.6 us  [_exchange(): return lax.ppermute(x, axis, perm)]
    convert_element_type x0 -> x2, local copies, waits for them, and re-layouts: none -> 3.58 us  [the longest x1 2.26 us: body(): key_part.astype(jnp.bfloat16)]
    ppermute x26, starting transfers between devices: 102 us -> 99.2 us  [_exchange(): return lax.ppermute(x, axis, perm)]
  transfers between devices with their start and end apart: 26 -> 26, of which waited for: 20 -> 19; matrix products, arithmetic and copies ran while one was open for 4% -> 3% of each run, Pallas kernels for 0% -> 0%
where the time goes in v6:
time: 237 us; the launch traced here: 236 us
  starting transfers between devices  99.2 us (42%)
  waiting for transfers between devices  96.6 us (41%)
  Pallas kernels  15.4 us (6%)
  local copies, waits for them, and re-layouts  14.2 us (6%)
  other arithmetic  7.18 us (3%)
  matrix products  2.47 us (1%)
    ppermute x26, starting transfers between devices, _exchange(): return lax.ppermute(x, axis, perm)  99.2 us
    ppermute x26, waiting for transfers between devices, _exchange(): return lax.ppermute(x, axis, perm)  96.6 us
    pallas_call x1, Pallas kernels, attention_block(): pl.pallas_call(_attention_kernel, out_shape=(jax.ShapeDtypeStruct((rows,...  15.4 us
  transfers between devices with their start and end apart: 26, of which 19 were waited for; matrix products, arithmetic and copies ran while one was open for 3% of the time, Pallas kernels for 0%

profile of v6, /device:TPU:24, one launch (start us, length us, event | category | flops | bytes accessed | tf_op | source)
XLA Modules:
  0.0 236.3 jit_solution(9553182446985585352)
XLA Ops:
  0.6 0.8 constant_dynamic-update-slice_fusion.1
  1.5 0.7 constant_dynamic-update-slice_fusion
  2.2 9.1 %collective-permute-start = (bf16[64,256]{1,0:T(8,128)(2,1)S(1)}, bf16[64,256]{1,0:T(8,128)(2,1)S(1)}, u32[]{:S(2)}, u32[]{:S(2)}) collective-permute-start(bf16[64,256]{1,0:T(8,128)(2,1)S(1)} %constant_dynamic-update-slice_fusion), channel_id=1, source_target_pairs={{0,64},{8,72},{16,80},{24,88},{32,96},{40,104},{48,112},{56,120},{... | collective-permute-start | bytes 98312 | tf_op jit(solution)/shard_map/ppermute | solution.py:22
  11.3 1.9 collective-permute-done
  13.2 5.2 %collective-permute-start.1 = (bf16[2,64,256]{2,1,0:T(8,128)(2,1)S(1)}, bf16[2,64,256]{2,1,0:T(8,128)(2,1)S(1)}, u32[]{:S(2)}, u32[]{:S(2)}) collective-permute-start(bf16[2,64,256]{2,1,0:T(8,128)(2,1)S(1)} %maximum_select_fusion.6), channel_id=1, source_target_pairs={{0,32},{8,40},{16,48},{24,56},{32,0},{40,8},{48,16},{56,24},{64,96... | collective-permute-start | bytes 196616 | tf_op jit(solution)/shard_map/ppermute | solution.py:22
  18.4 3.6 %collective-permute-done.1 = bf16[2,64,256]{2,1,0:T(8,128)(2,1)S(1)} collective-permute-done((bf16[2,64,256]{2,1,0:T(8,128)(2,1)S(1)}, bf16[2,64,256]{2,1,0:T(8,128)(2,1)S(1)}, u32[]{:S(2)}, u32[]{:S(2)}) %collective-permute-start.1) | collective-permute-done | bytes 65568 | tf_op jit(solution)/shard_map/ppermute | solution.py:22
  22.0 4.9 %collective-permute-start.2 = (bf16[2,2,64,256]{3,2,0,1:T(8,128)(2,1)S(1)}, bf16[2,2,64,256]{3,2,0,1:T(8,128)(2,1)S(1)}, u32[]{:S(2)}, u32[]{:S(2)}) collective-permute-start(bf16[2,2,64,256]{3,2,0,1:T(8,128)(2,1)S(1)} %maximum_select_fusion.5), channel_id=1, source_target_pairs={{0,256},{128,384},{256,0},{384,128},{1,257},{129,385},{257,1},{385... | collective-permute-start | bytes 393224 | tf_op jit(solution)/shard_map/ppermute | solution.py:22
  27.0 3.4 %collective-permute-done.2 = bf16[2,2,64,256]{3,2,0,1:T(8,128)(2,1)S(1)} collective-permute-done((bf16[2,2,64,256]{3,2,0,1:T(8,128)(2,1)S(1)}, bf16[2,2,64,256]{3,2,0,1:T(8,128)(2,1)S(1)}, u32[]{:S(2)}, u32[]{:S(2)}) %collective-permute-start.2) | collective-permute-done | bytes 131104 | tf_op jit(solution)/shard_map/ppermute | solution.py:22
  30.4 2.4 %collective-permute-start.3 = (bf16[2,2,2,64,256]{4,3,1,2,0:T(8,128)(2,1)S(1)}, bf16[2,2,2,64,256]{4,3,1,2,0:T(8,128)(2,1)S(1)}, u32[]{:S(2)}, u32[]{:S(2)}) collective-permute-start(bf16[2,2,2,64,256]{4,3,1,2,0:T(8,128)(2,1)S(1)} %maximum_select_fusion.4), channel_id=1, source_target_pairs={{0,16},{8,24},{16,0},{24,8},{32,48},{40,56},{48,32},{56,40},{64,80... | collective-permute-start | bytes 786440 | tf_op jit(solution)/shard_map/ppermute | solution.py:22
  32.9 5.8 %collective-permute-done.3 = bf16[2,2,2,64,256]{4,3,1,2,0:T(8,128)(2,1)S(1)} collective-permute-done((bf16[2,2,2,64,256]{4,3,1,2,0:T(8,128)(2,1)S(1)}, bf16[2,2,2,64,256]{4,3,1,2,0:T(8,128)(2,1)S(1)}, u32[]{:S(2)}, u32[]{:S(2)}) %collective-permute-start.3) | collective-permute-done | bytes 262176 | tf_op jit(solution)/shard_map/ppermute | solution.py:22
  38.8 3.4 %collective-permute-start.4 = (bf16[2,2,2,2,64,256]{5,4,0,2,3,1:T(8,128)(2,1)S(1)}, bf16[2,2,2,2,64,256]{5,4,0,2,3,1:T(8,128)(2,1)S(1)}, u32[]{:S(2)}, u32[]{:S(2)}) collective-permute-start(bf16[2,2,2,2,64,256]{5,4,0,2,3,1:T(8,128)(2,1)S(1)} %maximum_select_fusion.3), channel_id=1, source_target_pairs={{0,128},{128,0},{256,384},{384,256},{1,129},{129,1},{257,385},{385... | collective-permute-start | bytes 1572872 | tf_op jit(solution)/shard_map/ppermute | solution.py:22
  42.4 7.5 %collective-permute-done.4 = bf16[2,2,2,2,64,256]{5,4,0,2,3,1:T(8,128)(2,1)S(1)} collective-permute-done((bf16[2,2,2,2,64,256]{5,4,0,2,3,1:T(8,128)(2,1)S(1)}, bf16[2,2,2,2,64,256]{5,4,0,2,3,1:T(8,128)(2,1)S(1)}, u32[]{:S(2)}, u32[]{:S(2)}) %collective-permute-start.4) | collective-permute-done | bytes 524320 | tf_op jit(solution)/shard_map/ppermute | solution.py:22
  49.8 1.1 maximum_select_fusion.1
  51.0 1.9 collective-permute-start.5
  53.1 2.8 %collective-permute-done.5 = bf16[2,2,2,2,2,64,256]{6,5,1,3,4,2,0:T(8,128)(2,1)} collective-permute-done((bf16[2,2,2,2,2,64,256]{6,5,1,3,4,2,0:T(8,128)(2,1)}, bf16[2,2,2,2,2,64,256]{6,5,1,3,4,2,0:T(8,128)(2,1)}, u32[]{:S(2)}, u32[]{:S(2)}) %collective-permute-start.5) | collective-permute-done | bytes 1048608 | tf_op jit(solution)/shard_map/ppermute | solution.py:22
  55.9 1.3 copy.117
  58.0 8.2 %collective-permute-start.6 = (bf16[1,193,256]{2,1,0:T(8,128)(2,1)S(1)}, bf16[1,193,256]{2,1,0:T(8,128)(2,1)S(1)}, u32[]{:S(2)}, u32[]{:S(2)}) collective-permute-start(bf16[1,193,256]{2,1,0:T(8,128)(2,1)S(1)} %get-tuple-element.27), channel_id=1, source_target_pairs={{0,64},{8,72},{16,80},{24,88},{32,96},{40,104},{48,112},{56,120},{... | collective-permute-start | bytes 296456 | tf_op jit(solution)/shard_map/ppermute | solution.py:22
  66.2 9.8 %collective-permute-done.6 = bf16[1,193,256]{2,1,0:T(8,128)(2,1)S(1)} collective-permute-done((bf16[1,193,256]{2,1,0:T(8,128)(2,1)S(1)}, bf16[1,193,256]{2,1,0:T(8,128)(2,1)S(1)}, u32[]{:S(2)}, u32[]{:S(2)}) %collective-permute-start.6) | collective-permute-done | bytes 98848 | tf_op jit(solution)/shard_map/ppermute | solution.py:22
  75.9 2.1 collective-permute-start.7
  78.0 9.8 %collective-permute-done.7 = bf16[2,1,193,256]{3,2,1,0:T(8,128)(2,1)S(1)} collective-permute-done((bf16[2,1,193,256]{3,2,1,0:T(8,128)(2,1)S(1)}, bf16[2,1,193,256]{3,2,1,0:T(8,128)(2,1)S(1)}, u32[]{:S(2)}, u32[]{:S(2)}) %collective-permute-start.7) | collective-permute-done | bytes 197664 | tf_op jit(solution)/shard_map/ppermute | solution.py:22
  87.9 2.1 collective-permute-start.8
  89.9 9.6 %collective-permute-done.8 = bf16[2,2,1,193,256]{4,3,1,2,0:T(8,128)(2,1)S(1)} collective-permute-done((bf16[2,2,1,193,256]{4,3,1,2,0:T(8,128)(2,1)S(1)}, bf16[2,2,1,193,256]{4,3,1,2,0:T(8,128)(2,1)S(1)}, u32[]{:S(2)}, u32[]{:S(2)}) %collective-permute-start.8) | collective-permute-done | bytes 395296 | tf_op jit(solution)/shard_map/ppermute | solution.py:22
  99.7 0.6 copy.63
  100.3 2.1 collective-permute-start.9
  102.4 0.8 copy.66.mq_ref
  103.2 1.4 collective-permute-done.9
  104.6 1.2 copy.118
  106.0 1.6 fusion.43
  107.7 0.7 reshape.672.mk_ref
  108.3 15.4 %shard_map.85 = (bf16[192,512]{1,0:T(8,128)(2,1)}, bf16[3072,256]{1,0:T(8,128)(2,1)}) custom-call(bf16[192,512]{1,0:T(8,128)(2,1)} %bitcast.262, bf16[192,512]{1,0:T(8,128)(2,1)} %bitcast.263, bf16[3072,128]{1,0:T(8,128)(2,1)} %bitcast.249, bf16[3072,128]{1,0:T(8,128)(2,1)} %bitcast.248, f32[192,1]{1,0:T(8,128)} %copy.66.mq_ref, f32[1,3072]{1,0:T(1,128)} %reshape.672.mk_ref), custom_call_target="tpu_custom_call" | custom-call | flops 3623878656 | bytes 3932160 | tf_op jit(solution)/shard_map/pallas_call | solution.py:120
  123.7 1.5 fusion.44
  125.2 2.0 collective-permute-start.10
  127.3 2.1 collective-permute-done.10
  129.6 3.6 %collective-permute-start.11 = (bf16[2,2,192,256]{3,2,1,0:T(8,128)(2,1)S(1)}, bf16[2,2,192,256]{3,2,1,0:T(8,128)(2,1)S(1)}, u32[]{:S(2)}, u32[]{:S(2)}) collective-permute-start(bf16[2,2,192,256]{3,2,1,0:T(8,128)(2,1)S(1)} %slice_bitcast_fusion), channel_id=1, source_target_pairs={{0,16},{8,24},{16,0},{24,8},{32,48},{40,56},{48,32},{56,40},{64,80... | collective-permute-start | bytes 1179656 | tf_op jit(solution)/shard_map/ppermute | solution.py:22
  133.3 9.4 %collective-permute-done.11 = bf16[2,2,192,256]{3,2,1,0:T(8,128)(2,1)S(1)} collective-permute-done((bf16[2,2,192,256]{3,2,1,0:T(8,128)(2,1)S(1)}, bf16[2,2,192,256]{3,2,1,0:T(8,128)(2,1)S(1)}, u32[]{:S(2)}, u32[]{:S(2)}) %collective-permute-start.11) | collective-permute-done | bytes 393248 | tf_op jit(solution)/shard_map/ppermute | solution.py:22
  142.8 5.3 %collective-permute-start.12 = (bf16[2,192,256]{2,1,0:T(8,128)(2,1)S(1)}, bf16[2,192,256]{2,1,0:T(8,128)(2,1)S(1)}, u32[]{:S(2)}, u32[]{:S(2)}) collective-permute-start(bf16[2,192,256]{2,1,0:T(8,128)(2,1)S(1)} %slice_bitcast_fusion.2), channel_id=1, source_target_pairs={{0,32},{8,40},{16,48},{24,56},{32,0},{40,8},{48,16},{56,24},{64,96... | collective-permute-start | bytes 589832 | tf_op jit(solution)/shard_map/ppermute | solution.py:22
  148.1 8.6 %collective-permute-done.12 = bf16[2,192,256]{2,1,0:T(8,128)(2,1)S(1)} collective-permute-done((bf16[2,192,256]{2,1,0:T(8,128)(2,1)S(1)}, bf16[2,192,256]{2,1,0:T(8,128)(2,1)S(1)}, u32[]{:S(2)}, u32[]{:S(2)}) %collective-permute-start.12) | collective-permute-done | bytes 196640 | tf_op jit(solution)/shard_map/ppermute | solution.py:22
  156.8 8.0 %collective-permute-start.13 = (bf16[192,256]{1,0:T(8,128)(2,1)S(1)}, bf16[192,256]{1,0:T(8,128)(2,1)S(1)}, u32[]{:S(2)}, u32[]{:S(2)}) collective-permute-start(bf16[192,256]{1,0:T(8,128)(2,1)S(1)} %slice_bitcast_fusion.4), channel_id=1, source_target_pairs={{0,64},{8,72},{16,80},{24,88},{32,96},{40,104},{48,112},{56,120},{... | collective-permute-start | bytes 294920 | tf_op jit(solution)/shard_map/ppermute | solution.py:22
  164.8 7.0 %collective-permute-done.13 = bf16[192,256]{1,0:T(8,128)(2,1)S(1)} collective-permute-done((bf16[192,256]{1,0:T(8,128)(2,1)S(1)}, bf16[192,256]{1,0:T(8,128)(2,1)S(1)}, u32[]{:S(2)}, u32[]{:S(2)}) %collective-permute-start.13) | collective-permute-done | bytes 98336 | tf_op jit(solution)/shard_map/ppermute | solution.py:22
  172.3 1.3 copy.85
  173.6 1.3 fusion.45
  174.9 0.9 select_bitcast_fusion
  175.8 1.9 collective-permute-start.20
  177.7 1.4 fusion
  179.1 2.3 copy.67
  181.4 1.3 select_bitcast_fusion.1
  182.7 2.4 %collective-permute-start.14 = (bf16[2,2,2,2,2,64,128]{6,5,4,3,2,1,0:T(8,128)(2,1)S(1)}, bf16[2,2,2,2,2,64,128]{6,5,4,3,2,1,0:T(8,128)(2,1)S(1)}, u32[]{:S(2)}, u32[]{:S(2)}) collective-permute-start(bf16[2,2,2,2,2,64,128]{6,5,4,3,2,1,0:T(8,128)(2,1)S(1)} %get-tuple-element.13), channel_id=1, source_target_pairs={{0,8},{8,0},{16,24},{24,16},{32,40},{40,32},{48,56},{56,48},{64,72... | collective-permute-start | bytes 1572872 | tf_op jit(solution)/shard_map/ppermute | solution.py:22
  185.4 1.9 collective-permute-start.21
  187.7 3.4 %collective-permute-start.15 = (bf16[2,2,2,2,64,128]{5,4,3,2,1,0:T(8,128)(2,1)S(1)}, bf16[2,2,2,2,64,128]{5,4,3,2,1,0:T(8,128)(2,1)S(1)}, u32[]{:S(2)}, u32[]{:S(2)}) collective-permute-start(bf16[2,2,2,2,64,128]{5,4,3,2,1,0:T(8,128)(2,1)S(1)} %fusion.21), channel_id=1, source_target_pairs={{0,128},{128,0},{256,384},{384,256},{1,129},{129,1},{257,385},{385... | collective-permute-start | bytes 786440 | tf_op jit(solution)/shard_map/ppermute | solution.py:22
  191.1 4.4 %collective-permute-done.21 = bf16[2,2,2,2,64,128]{5,4,2,0,3,1:T(8,128)(2,1)S(1)} collective-permute-done((bf16[2,2,2,2,64,128]{5,4,2,0,3,1:T(8,128)(2,1)S(1)}, bf16[2,2,2,2,64,128]{5,4,2,0,3,1:T(8,128)(2,1)S(1)}, u32[]{:S(2)}, u32[]{:S(2)}) %collective-permute-start.21) | collective-permute-done | bytes 262176 | tf_op jit(solution)/shard_map/ppermute | solution.py:22
  195.7 3.4 %collective-permute-start.22 = (bf16[2,2,2,64,128]{4,3,1,0,2:T(8,128)(2,1)S(1)}, bf16[2,2,2,64,128]{4,3,1,0,2:T(8,128)(2,1)S(1)}, u32[]{:S(2)}, u32[]{:S(2)}) collective-permute-start(bf16[2,2,2,64,128]{4,3,1,0,2:T(8,128)(2,1)S(1)} %select_bitcast_fusion.3), channel_id=1, source_target_pairs={{0,128},{128,0},{256,384},{384,256},{1,129},{129,1},{257,385},{385... | collective-permute-start | bytes 393224 | tf_op jit(solution)/shard_map/ppermute | solution.py:22
  199.3 2.3 collective-permute-start.16
  201.6 0.9 collective-permute-done.22
  202.7 3.0 %collective-permute-start.23 = (bf16[2,2,64,128]{3,2,1,0:T(8,128)(2,1)S(1)}, bf16[2,2,64,128]{3,2,1,0:T(8,128)(2,1)S(1)}, u32[]{:S(2)}, u32[]{:S(2)}) collective-permute-start(bf16[2,2,64,128]{3,2,1,0:T(8,128)(2,1)S(1)} %select_bitcast_fusion.4), channel_id=1, source_target_pairs={{0,32},{8,40},{16,48},{24,56},{32,0},{40,8},{48,16},{56,24},{64,96... | collective-permute-start | bytes 196616 | tf_op jit(solution)/shard_map/ppermute | solution.py:22
  205.6 1.3 collective-permute-done.16
  207.0 3.9 %collective-permute-start.17 = (bf16[2,2,64,128]{3,2,1,0:T(8,128)(2,1)S(1)}, bf16[2,2,64,128]{3,2,1,0:T(8,128)(2,1)S(1)}, u32[]{:S(2)}, u32[]{:S(2)}) collective-permute-start(bf16[2,2,64,128]{3,2,1,0:T(8,128)(2,1)S(1)} %select_bitcast_fusion.5), channel_id=1, source_target_pairs={{0,256},{128,384},{256,0},{384,128},{1,257},{129,385},{257,1},{385... | collective-permute-start | bytes 196616 | tf_op jit(solution)/shard_map/ppermute | solution.py:22
  210.9 4.3 %collective-permute-start.24 = (bf16[2,64,128]{2,1,0:T(8,128)(2,1)S(1)}, bf16[2,64,128]{2,1,0:T(8,128)(2,1)S(1)}, u32[]{:S(2)}, u32[]{:S(2)}) collective-permute-start(bf16[2,64,128]{2,1,0:T(8,128)(2,1)S(1)} %select_bitcast_fusion.6), channel_id=1, source_target_pairs={{0,256},{128,384},{256,0},{384,128},{1,257},{129,385},{257,1},{385... | collective-permute-start | bytes 98312 | tf_op jit(solution)/shard_map/ppermute | solution.py:22
  215.3 2.2 collective-permute-start.18
  217.5 0.8 collective-permute-done.24
  218.3 7.8 %collective-permute-start.25 = (bf16[64,128]{1,0:T(8,128)(2,1)S(1)}, bf16[64,128]{1,0:T(8,128)(2,1)S(1)}, u32[]{:S(2)}, u32[]{:S(2)}) collective-permute-start(bf16[64,128]{1,0:T(8,128)(2,1)S(1)} %select_bitcast_fusion.7), channel_id=1, source_target_pairs={{0,64},{8,72},{16,80},{24,88},{32,96},{40,104},{48,112},{56,120},{... | collective-permute-start | bytes 49160 | tf_op jit(solution)/shard_map/ppermute | solution.py:22
  226.1 2.3 collective-permute-start.19
  228.5 0.6 convert_add_fusion.13
  229.1 6.6 %collective-permute-done.19 = bf16[64,128]{1,0:T(8,128)(2,1)S(1)} collective-permute-done((bf16[64,128]{1,0:T(8,128)(2,1)S(1)}, bf16[64,128]{1,0:T(8,128)(2,1)S(1)}, u32[]{:S(2)}, u32[]{:S(2)}) %collective-permute-start.19) | collective-permute-done | bytes 16416 | tf_op jit(solution)/shard_map/ppermute | solution.py:22
  235.7 0.6 convert_add_fusion.14
  (65 shorter events, 3.8 us)
Async XLA Ops:
  0.6 56.7 %copy-start = (bf16[1,192,4096]{2,1,0:T(8,128)(2,1)S(1)}, bf16[1,192,4096]{2,1,0:T(8,128)(2,1)}, u32[]{:S(2)}) copy-start(bf16[1,192,4096]{2,1,0:T(8,128)(2,1)} %param.6) | copy-start | bytes 4718596
  2.2 11.0 %collective-permute-start = (bf16[64,256]{1,0:T(8,128)(2,1)S(1)}, bf16[64,256]{1,0:T(8,128)(2,1)S(1)}, u32[]{:S(2)}, u32[]{:S(2)}) collective-permute-start(bf16[64,256]{1,0:T(8,128)(2,1)S(1)} %constant_dynamic-update-slice_fusion), channel_id=1, source_target_pairs={{0,64},{8,72},{16,80},{24,88},{32,96},{40,104},{48,112},{56,120},{... | collective-permute-start | bytes 98312 | tf_op jit(solution)/shard_map/ppermute | solution.py:22
  13.2 8.8 %collective-permute-start.1 = (bf16[2,64,256]{2,1,0:T(8,128)(2,1)S(1)}, bf16[2,64,256]{2,1,0:T(8,128)(2,1)S(1)}, u32[]{:S(2)}, u32[]{:S(2)}) collective-permute-start(bf16[2,64,256]{2,1,0:T(8,128)(2,1)S(1)} %maximum_select_fusion.6), channel_id=1, source_target_pairs={{0,32},{8,40},{16,48},{24,56},{32,0},{40,8},{48,16},{56,24},{64,96... | collective-permute-start | bytes 196616 | tf_op jit(solution)/shard_map/ppermute | solution.py:22
  22.0 8.4 %collective-permute-start.2 = (bf16[2,2,64,256]{3,2,0,1:T(8,128)(2,1)S(1)}, bf16[2,2,64,256]{3,2,0,1:T(8,128)(2,1)S(1)}, u32[]{:S(2)}, u32[]{:S(2)}) collective-permute-start(bf16[2,2,64,256]{3,2,0,1:T(8,128)(2,1)S(1)} %maximum_select_fusion.5), channel_id=1, source_target_pairs={{0,256},{128,384},{256,0},{384,128},{1,257},{129,385},{257,1},{385... | collective-permute-start | bytes 393224 | tf_op jit(solution)/shard_map/ppermute | solution.py:22
  30.4 8.3 %collective-permute-start.3 = (bf16[2,2,2,64,256]{4,3,1,2,0:T(8,128)(2,1)S(1)}, bf16[2,2,2,64,256]{4,3,1,2,0:T(8,128)(2,1)S(1)}, u32[]{:S(2)}, u32[]{:S(2)}) collective-permute-start(bf16[2,2,2,64,256]{4,3,1,2,0:T(8,128)(2,1)S(1)} %maximum_select_fusion.4), channel_id=1, source_target_pairs={{0,16},{8,24},{16,0},{24,8},{32,48},{40,56},{48,32},{56,40},{64,80... | collective-permute-start | bytes 786440 | tf_op jit(solution)/shard_map/ppermute | solution.py:22
  38.8 11.1 %collective-permute-start.4 = (bf16[2,2,2,2,64,256]{5,4,0,2,3,1:T(8,128)(2,1)S(1)}, bf16[2,2,2,2,64,256]{5,4,0,2,3,1:T(8,128)(2,1)S(1)}, u32[]{:S(2)}, u32[]{:S(2)}) collective-permute-start(bf16[2,2,2,2,64,256]{5,4,0,2,3,1:T(8,128)(2,1)S(1)} %maximum_select_fusion.3), channel_id=1, source_target_pairs={{0,128},{128,0},{256,384},{384,256},{1,129},{129,1},{257,385},{385... | collective-permute-start | bytes 1572872 | tf_op jit(solution)/shard_map/ppermute | solution.py:22
  42.3 10.6 %copy-start.1 = (s32[1,192]{1,0:T(1,128)S(1)}, s32[1,192]{1,0:T(1,128)}, u32[]{:S(2)}) copy-start(s32[1,192]{1,0:T(1,128)} %param.9) | copy-start | bytes 2308
  51.0 4.9 %collective-permute-start.5 = (bf16[2,2,2,2,2,64,256]{6,5,1,3,4,2,0:T(8,128)(2,1)}, bf16[2,2,2,2,2,64,256]{6,5,1,3,4,2,0:T(8,128)(2,1)}, u32[]{:S(2)}, u32[]{:S(2)}) collective-permute-start(bf16[2,2,2,2,2,64,256]{6,5,1,3,4,2,0:T(8,128)(2,1)} %maximum_select_fusion.1), channel_id=1, source_target_pairs={{0,8},{8,0},{16,24},{24,16},{32,40},{40,32},{48,56},{56,48},{64,72... | collective-permute-start | bytes 3145736 | tf_op jit(solution)/shard_map/ppermute | solution.py:22
  58.0 17.9 %collective-permute-start.6 = (bf16[1,193,256]{2,1,0:T(8,128)(2,1)S(1)}, bf16[1,193,256]{2,1,0:T(8,128)(2,1)S(1)}, u32[]{:S(2)}, u32[]{:S(2)}) collective-permute-start(bf16[1,193,256]{2,1,0:T(8,128)(2,1)S(1)} %get-tuple-element.27), channel_id=1, source_target_pairs={{0,64},{8,72},{16,80},{24,88},{32,96},{40,104},{48,112},{56,120},{... | collective-permute-start | bytes 296456 | tf_op jit(solution)/shard_map/ppermute | solution.py:22
  75.9 11.9 %collective-permute-start.7 = (bf16[2,1,193,256]{3,2,1,0:T(8,128)(2,1)S(1)}, bf16[2,1,193,256]{3,2,1,0:T(8,128)(2,1)S(1)}, u32[]{:S(2)}, u32[]{:S(2)}) collective-permute-start(bf16[2,1,193,256]{3,2,1,0:T(8,128)(2,1)S(1)} %get-tuple-element.23), channel_id=1, source_target_pairs={{0,32},{8,40},{16,48},{24,56},{32,0},{40,8},{48,16},{56,24},{64,96... | collective-permute-start | bytes 592904 | tf_op jit(solution)/shard_map/ppermute | solution.py:22
  87.9 11.7 %collective-permute-start.8 = (bf16[2,2,1,193,256]{4,3,1,2,0:T(8,128)(2,1)S(1)}, bf16[2,2,1,193,256]{4,3,1,2,0:T(8,128)(2,1)S(1)}, u32[]{:S(2)}, u32[]{:S(2)}) collective-permute-start(bf16[2,2,1,193,256]{4,3,1,2,0:T(8,128)(2,1)S(1)} %get-tuple-element.21), channel_id=1, source_target_pairs={{0,16},{8,24},{16,0},{24,8},{32,48},{40,56},{48,32},{56,40},{64,80... | collective-permute-start | bytes 1185800 | tf_op jit(solution)/shard_map/ppermute | solution.py:22
  100.3 4.3 %collective-permute-start.9 = (bf16[2,2,2,1,193,256]{5,2,4,3,1,0:T(2,128)(2,1)S(1)}, bf16[2,2,2,1,193,256]{5,2,4,3,1,0:T(2,128)(2,1)}, u32[]{:S(2)}, u32[]{:S(2)}) collective-permute-start(bf16[2,2,2,1,193,256]{5,2,4,3,1,0:T(2,128)(2,1)S(1)} %copy.63), channel_id=1, source_target_pairs={{0,8},{8,0},{16,24},{24,16},{32,40},{40,32},{48,56},{56,48},{64,72... | collective-permute-start | bytes 2371592 | tf_op jit(solution)/shard_map/ppermute | solution.py:22
  125.2 4.2 %collective-permute-start.10 = (bf16[2,2,2,192,256]{4,3,2,1,0:T(8,128)(2,1)S(1)}, bf16[2,2,2,192,256]{4,3,2,1,0:T(8,128)(2,1)S(1)}, u32[]{:S(2)}, u32[]{:S(2)}) collective-permute-start(bf16[2,2,2,192,256]{4,3,2,1,0:T(8,128)(2,1)S(1)} %bitcast.250), channel_id=1, source_target_pairs={{0,8},{8,0},{16,24},{24,16},{32,40},{40,32},{48,56},{56,48},{64,72... | collective-permute-start | bytes 2359304 | tf_op jit(solution)/shard_map/ppermute | solution.py:22
  129.6 13.1 %collective-permute-start.11 = (bf16[2,2,192,256]{3,2,1,0:T(8,128)(2,1)S(1)}, bf16[2,2,192,256]{3,2,1,0:T(8,128)(2,1)S(1)}, u32[]{:S(2)}, u32[]{:S(2)}) collective-permute-start(bf16[2,2,192,256]{3,2,1,0:T(8,128)(2,1)S(1)} %slice_bitcast_fusion), channel_id=1, source_target_pairs={{0,16},{8,24},{16,0},{24,8},{32,48},{40,56},{48,32},{56,40},{64,80... | collective-permute-start | bytes 1179656 | tf_op jit(solution)/shard_map/ppermute | solution.py:22
  142.8 13.9 %collective-permute-start.12 = (bf16[2,192,256]{2,1,0:T(8,128)(2,1)S(1)}, bf16[2,192,256]{2,1,0:T(8,128)(2,1)S(1)}, u32[]{:S(2)}, u32[]{:S(2)}) collective-permute-start(bf16[2,192,256]{2,1,0:T(8,128)(2,1)S(1)} %slice_bitcast_fusion.2), channel_id=1, source_target_pairs={{0,32},{8,40},{16,48},{24,56},{32,0},{40,8},{48,16},{56,24},{64,96... | collective-permute-start | bytes 589832 | tf_op jit(solution)/shard_map/ppermute | solution.py:22
  156.8 15.0 %collective-permute-start.13 = (bf16[192,256]{1,0:T(8,128)(2,1)S(1)}, bf16[192,256]{1,0:T(8,128)(2,1)S(1)}, u32[]{:S(2)}, u32[]{:S(2)}) collective-permute-start(bf16[192,256]{1,0:T(8,128)(2,1)S(1)} %slice_bitcast_fusion.4), channel_id=1, source_target_pairs={{0,64},{8,72},{16,80},{24,88},{32,96},{40,104},{48,112},{56,120},{... | collective-permute-start | bytes 294920 | tf_op jit(solution)/shard_map/ppermute | solution.py:22
  175.8 9.4 %collective-permute-start.20 = (bf16[2,2,2,2,2,64,128]{6,5,2,0,3,1,4:T(8,128)(2,1)}, bf16[2,2,2,2,2,64,128]{6,5,2,0,3,1,4:T(8,128)(2,1)S(1)}, u32[]{:S(2)}, u32[]{:S(2)}) collective-permute-start(bf16[2,2,2,2,2,64,128]{6,5,2,0,3,1,4:T(8,128)(2,1)} %select_bitcast_fusion), channel_id=1, source_target_pairs={{0,8},{8,0},{16,24},{24,16},{32,40},{40,32},{48,56},{56,48},{64,72... | collective-permute-start | bytes 1572872 | tf_op jit(solution)/shard_map/ppermute | solution.py:22
  182.7 4.7 %collective-permute-start.14 = (bf16[2,2,2,2,2,64,128]{6,5,4,3,2,1,0:T(8,128)(2,1)S(1)}, bf16[2,2,2,2,2,64,128]{6,5,4,3,2,1,0:T(8,128)(2,1)S(1)}, u32[]{:S(2)}, u32[]{:S(2)}) collective-permute-start(bf16[2,2,2,2,2,64,128]{6,5,4,3,2,1,0:T(8,128)(2,1)S(1)} %get-tuple-element.13), channel_id=1, source_target_pairs={{0,8},{8,0},{16,24},{24,16},{32,40},{40,32},{48,56},{56,48},{64,72... | collective-permute-start | bytes 1572872 | tf_op jit(solution)/shard_map/ppermute | solution.py:22
  185.4 10.1 %collective-permute-start.21 = (bf16[2,2,2,2,64,128]{5,4,2,0,3,1:T(8,128)(2,1)S(1)}, bf16[2,2,2,2,64,128]{5,4,2,0,3,1:T(8,128)(2,1)S(1)}, u32[]{:S(2)}, u32[]{:S(2)}) collective-permute-start(bf16[2,2,2,2,64,128]{5,4,2,0,3,1:T(8,128)(2,1)S(1)} %select_bitcast_fusion.2), channel_id=1, source_target_pairs={{0,16},{8,24},{16,0},{24,8},{32,48},{40,56},{48,32},{56,40},{64,80... | collective-permute-start | bytes 786440 | tf_op jit(solution)/shard_map/ppermute | solution.py:22
  187.7 11.4 %collective-permute-start.15 = (bf16[2,2,2,2,64,128]{5,4,3,2,1,0:T(8,128)(2,1)S(1)}, bf16[2,2,2,2,64,128]{5,4,3,2,1,0:T(8,128)(2,1)S(1)}, u32[]{:S(2)}, u32[]{:S(2)}) collective-permute-start(bf16[2,2,2,2,64,128]{5,4,3,2,1,0:T(8,128)(2,1)S(1)} %fusion.21), channel_id=1, source_target_pairs={{0,128},{128,0},{256,384},{384,256},{1,129},{129,1},{257,385},{385... | collective-permute-start | bytes 786440 | tf_op jit(solution)/shard_map/ppermute | solution.py:22
  195.7 6.9 %collective-permute-start.22 = (bf16[2,2,2,64,128]{4,3,1,0,2:T(8,128)(2,1)S(1)}, bf16[2,2,2,64,128]{4,3,1,0,2:T(8,128)(2,1)S(1)}, u32[]{:S(2)}, u32[]{:S(2)}) collective-permute-start(bf16[2,2,2,64,128]{4,3,1,0,2:T(8,128)(2,1)S(1)} %select_bitcast_fusion.3), channel_id=1, source_target_pairs={{0,128},{128,0},{256,384},{384,256},{1,129},{129,1},{257,385},{385... | collective-permute-start | bytes 393224 | tf_op jit(solution)/shard_map/ppermute | solution.py:22
  199.3 7.6 %collective-permute-start.16 = (bf16[2,2,2,64,128]{4,3,2,1,0:T(8,128)(2,1)S(1)}, bf16[2,2,2,64,128]{4,3,2,1,0:T(8,128)(2,1)S(1)}, u32[]{:S(2)}, u32[]{:S(2)}) collective-permute-start(bf16[2,2,2,64,128]{4,3,2,1,0:T(8,128)(2,1)S(1)} %fusion.27), channel_id=1, source_target_pairs={{0,16},{8,24},{16,0},{24,8},{32,48},{40,56},{48,32},{56,40},{64,80... | collective-permute-start | bytes 393224 | tf_op jit(solution)/shard_map/ppermute | solution.py:22
  202.7 8.2 %collective-permute-start.23 = (bf16[2,2,64,128]{3,2,1,0:T(8,128)(2,1)S(1)}, bf16[2,2,64,128]{3,2,1,0:T(8,128)(2,1)S(1)}, u32[]{:S(2)}, u32[]{:S(2)}) collective-permute-start(bf16[2,2,64,128]{3,2,1,0:T(8,128)(2,1)S(1)} %select_bitcast_fusion.4), channel_id=1, source_target_pairs={{0,32},{8,40},{16,48},{24,56},{32,0},{40,8},{48,16},{56,24},{64,96... | collective-permute-start | bytes 196616 | tf_op jit(solution)/shard_map/ppermute | solution.py:22
  207.0 8.3 %collective-permute-start.17 = (bf16[2,2,64,128]{3,2,1,0:T(8,128)(2,1)S(1)}, bf16[2,2,64,128]{3,2,1,0:T(8,128)(2,1)S(1)}, u32[]{:S(2)}, u32[]{:S(2)}) collective-permute-start(bf16[2,2,64,128]{3,2,1,0:T(8,128)(2,1)S(1)} %select_bitcast_fusion.5), channel_id=1, source_target_pairs={{0,256},{128,384},{256,0},{384,128},{1,257},{129,385},{257,1},{385... | collective-permute-start | bytes 196616 | tf_op jit(solution)/shard_map/ppermute | solution.py:22
  210.9 7.3 %collective-permute-start.24 = (bf16[2,64,128]{2,1,0:T(8,128)(2,1)S(1)}, bf16[2,64,128]{2,1,0:T(8,128)(2,1)S(1)}, u32[]{:S(2)}, u32[]{:S(2)}) collective-permute-start(bf16[2,64,128]{2,1,0:T(8,128)(2,1)S(1)} %select_bitcast_fusion.6), channel_id=1, source_target_pairs={{0,256},{128,384},{256,0},{384,128},{1,257},{129,385},{257,1},{385... | collective-permute-start | bytes 98312 | tf_op jit(solution)/shard_map/ppermute | solution.py:22
  215.3 10.8 %collective-permute-start.18 = (bf16[2,64,128]{2,1,0:T(8,128)(2,1)S(1)}, bf16[2,64,128]{2,1,0:T(8,128)(2,1)S(1)}, u32[]{:S(2)}, u32[]{:S(2)}) collective-permute-start(bf16[2,64,128]{2,1,0:T(8,128)(2,1)S(1)} %fusion.38), channel_id=1, source_target_pairs={{0,32},{8,40},{16,48},{24,56},{32,0},{40,8},{48,16},{56,24},{64,96... | collective-permute-start | bytes 98312 | tf_op jit(solution)/shard_map/ppermute | solution.py:22
  218.3 10.2 %collective-permute-start.25 = (bf16[64,128]{1,0:T(8,128)(2,1)S(1)}, bf16[64,128]{1,0:T(8,128)(2,1)S(1)}, u32[]{:S(2)}, u32[]{:S(2)}) collective-permute-start(bf16[64,128]{1,0:T(8,128)(2,1)S(1)} %select_bitcast_fusion.7), channel_id=1, source_target_pairs={{0,64},{8,72},{16,80},{24,88},{32,96},{40,104},{48,112},{56,120},{... | collective-permute-start | bytes 49160 | tf_op jit(solution)/shard_map/ppermute | solution.py:22
  226.1 9.5 %collective-permute-start.19 = (bf16[64,128]{1,0:T(8,128)(2,1)S(1)}, bf16[64,128]{1,0:T(8,128)(2,1)S(1)}, u32[]{:S(2)}, u32[]{:S(2)}) collective-permute-start(bf16[64,128]{1,0:T(8,128)(2,1)S(1)} %select_bitcast_fusion.8), channel_id=1, source_target_pairs={{0,64},{8,72},{16,80},{24,88},{32,96},{40,104},{48,112},{56,120},{... | collective-permute-start | bytes 49160 | tf_op jit(solution)/shard_map/ppermute | solution.py:22

commit v7 on v6

--- a/solution.py
+++ b/solution.py
@@ -1,3 +1,5 @@
+import functools
+
 import jax
 import jax.numpy as jnp
 from jax import lax
@@ -76,6 +78,55 @@
         cur = total if len(dims) == 1 else total.astype(x.dtype)
         dims.pop(at)
     return cur
+
+
+def _gather_kernel(bits, x_ref, o_ref, held, send_sems, recv_sems, local_sem):
+    me = lax.axis_index("context")
+    partners = [lax.bitwise_xor(me, 1 << b) for b in bits]
+    barrier = pltpu.get_barrier_semaphore()
+    for p in partners:
+        pl.semaphore_signal(barrier, inc=1, device_id={"context": p},
+                            device_id_type=pl.DeviceIdType.MESH)
+    pl.semaphore_wait(barrier, len(partners))
+    local = pltpu.make_async_copy(x_ref, held.at[0:1], local_sem)
+    local.start()
+    for k, p in enumerate(partners):
+        n = 1 << k
+        if k == 1:
+            local.wait()
+        copy = pltpu.make_async_remote_copy(
+            src_ref=x_ref if k == 0 else held.at[0:n],
+            dst_ref=held.at[n:2 * n],
+            send_sem=send_sems.at[k],
+            recv_sem=recv_sems.at[k],
+            device_id={"context": p},
+            device_id_type=pl.DeviceIdType.MESH,
+        )
+        copy.start()
+        copy.wait()
+    if len(partners) < 2:
+        local.wait()
+    out = pltpu.make_async_copy(held, o_ref, local_sem)
+    out.start()
+    out.wait()
+
+
+def context_gather(x, bits):
+    n = 1 << len(bits)
+    shape = (n,) + x.shape[1:]
+    return pl.pallas_call(
+        functools.partial(_gather_kernel, bits),
+        out_shape=jax.ShapeDtypeStruct(shape, x.dtype),
+        in_specs=[pl.BlockSpec(memory_space=pltpu.VMEM)],
+        out_specs=pl.BlockSpec(memory_space=pltpu.VMEM),
+        scratch_shapes=[
+            pltpu.VMEM(shape, x.dtype),
+            pltpu.SemaphoreType.DMA((len(bits),)),
+            pltpu.SemaphoreType.DMA((len(bits),)),
+            pltpu.SemaphoreType.DMA,
+        ],
+        compiler_params=pltpu.CompilerParams(collective_id=0, has_side_effects=True),
+    )(x)
 
 
 def _attention_kernel(q_ref, do_ref, k_ref, v_ref, mq_ref, mk_ref, gq_ref, dkv_ref, dk_acc, dv_acc):
@@ -171,7 +222,7 @@
     marks = segment[0].astype(jnp.bfloat16)
     marks_row = jnp.pad(marks, (0, 2 * HEAD_DIM - tok_rows))[None, :]
     kvm = jnp.concatenate([kv, marks_row], axis=0)[None]
-    kvm_all = gather_relative(kvm, ctx_far).reshape((-1,) + kvm.shape[1:])
+    kvm_all = context_gather(kvm, [bit for _, _, bit in ctx_far])
     keys = kvm_all[:, :tok_rows, :HEAD_DIM].reshape(-1, HEAD_DIM)
     values = kvm_all[:, :tok_rows, HEAD_DIM:].reshape(-1, HEAD_DIM)
     marks_all = kvm_all[:, tok_rows, :tok_rows].reshape(-1)

time: 237 us -> 231 us (0.975)
  Pallas kernels: 15.4 us -> 59 us
  waiting for transfers between devices: 96.6 us -> 66.6 us
  starting transfers between devices: 99.2 us -> 79.4 us
    pallas_call x0 -> x1, Pallas kernels: none -> 43.6 us  [context_gather(): pl.pallas_call(functools.partial(_gather_kernel, bits), out_shape=jax.Sha...]
    ppermute x26 -> x22, waiting for transfers between devices: 96.6 us -> 66.6 us  [_exchange(): return lax.ppermute(x, axis, perm)]
    ppermute x26 -> x22, starting transfers between devices: 99.2 us -> 79.4 us  [_exchange(): return lax.ppermute(x, axis, perm)]
  transfers between devices with their start and end apart: 26 -> 22, of which waited for: 19 -> 15; matrix products, arithmetic and copies ran while one was open for 3% -> 3% of each run, Pallas kernels for 0% -> 0%
where the time goes in v7:
time: 231 us; the launch traced here: 230 us
  starting transfers between devices  79.4 us (34%)
  waiting for transfers between devices  66.6 us (29%)
  Pallas kernels  59 us (26%)
  local copies, waits for them, and re-layouts  13.3 us (6%)
  other arithmetic  8.35 us (4%)
  matrix products  2.53 us (1%)
    ppermute x22, starting transfers between devices, _exchange(): return lax.ppermute(x, axis, perm)  79.4 us
    ppermute x22, waiting for transfers between devices, _exchange(): return lax.ppermute(x, axis, perm)  66.6 us
    pallas_call x1, Pallas kernels, context_gather(): pl.pallas_call(functools.partial(_gather_kernel, bits), out_shape=jax.Sha...  43.6 us
    pallas_call x1, Pallas kernels, attention_block(): pl.pallas_call(_attention_kernel, out_shape=(jax.ShapeDtypeStruct((rows,...  15.4 us
  transfers between devices with their start and end apart: 22, of which 15 were waited for; matrix products, arithmetic and copies ran while one was open for 3% of the time, Pallas kernels for 0%

profile of v7, /device:TPU:24, one launch (start us, length us, event | category | flops | bytes accessed | tf_op | source)
XLA Modules:
  0.0 230.4 jit_solution(13028971646559569366)
XLA Ops:
  0.6 0.8 constant_dynamic-update-slice_fusion.1
  1.5 0.7 constant_dynamic-update-slice_fusion
  2.2 9.1 %collective-permute-start = (bf16[64,256]{1,0:T(8,128)(2,1)S(1)}, bf16[64,256]{1,0:T(8,128)(2,1)S(1)}, u32[]{:S(2)}, u32[]{:S(2)}) collective-permute-start(bf16[64,256]{1,0:T(8,128)(2,1)S(1)} %constant_dynamic-update-slice_fusion), channel_id=1, source_target_pairs={{0,64},{8,72},{16,80},{24,88},{32,96},{40,104},{48,112},{56,120},{... | collective-permute-start | bytes 98312 | tf_op jit(solution)/shard_map/ppermute | solution.py:24
  11.3 1.9 collective-permute-done
  13.2 5.2 %collective-permute-start.1 = (bf16[2,64,256]{2,1,0:T(8,128)(2,1)S(1)}, bf16[2,64,256]{2,1,0:T(8,128)(2,1)S(1)}, u32[]{:S(2)}, u32[]{:S(2)}) collective-permute-start(bf16[2,64,256]{2,1,0:T(8,128)(2,1)S(1)} %maximum_select_fusion.6), channel_id=1, source_target_pairs={{0,32},{8,40},{16,48},{24,56},{32,0},{40,8},{48,16},{56,24},{64,96... | collective-permute-start | bytes 196616 | tf_op jit(solution)/shard_map/ppermute | solution.py:24
  18.4 3.6 %collective-permute-done.1 = bf16[2,64,256]{2,1,0:T(8,128)(2,1)S(1)} collective-permute-done((bf16[2,64,256]{2,1,0:T(8,128)(2,1)S(1)}, bf16[2,64,256]{2,1,0:T(8,128)(2,1)S(1)}, u32[]{:S(2)}, u32[]{:S(2)}) %collective-permute-start.1) | collective-permute-done | bytes 65568 | tf_op jit(solution)/shard_map/ppermute | solution.py:24
  22.0 4.9 %collective-permute-start.2 = (bf16[2,2,64,256]{3,2,0,1:T(8,128)(2,1)S(1)}, bf16[2,2,64,256]{3,2,0,1:T(8,128)(2,1)S(1)}, u32[]{:S(2)}, u32[]{:S(2)}) collective-permute-start(bf16[2,2,64,256]{3,2,0,1:T(8,128)(2,1)S(1)} %maximum_select_fusion.5), channel_id=1, source_target_pairs={{0,256},{128,384},{256,0},{384,128},{1,257},{129,385},{257,1},{385... | collective-permute-start | bytes 393224 | tf_op jit(solution)/shard_map/ppermute | solution.py:24
  27.0 3.4 %collective-permute-done.2 = bf16[2,2,64,256]{3,2,0,1:T(8,128)(2,1)S(1)} collective-permute-done((bf16[2,2,64,256]{3,2,0,1:T(8,128)(2,1)S(1)}, bf16[2,2,64,256]{3,2,0,1:T(8,128)(2,1)S(1)}, u32[]{:S(2)}, u32[]{:S(2)}) %collective-permute-start.2) | collective-permute-done | bytes 131104 | tf_op jit(solution)/shard_map/ppermute | solution.py:24
  30.4 2.4 %collective-permute-start.3 = (bf16[2,2,2,64,256]{4,3,1,2,0:T(8,128)(2,1)S(1)}, bf16[2,2,2,64,256]{4,3,1,2,0:T(8,128)(2,1)S(1)}, u32[]{:S(2)}, u32[]{:S(2)}) collective-permute-start(bf16[2,2,2,64,256]{4,3,1,2,0:T(8,128)(2,1)S(1)} %maximum_select_fusion.4), channel_id=1, source_target_pairs={{0,16},{8,24},{16,0},{24,8},{32,48},{40,56},{48,32},{56,40},{64,80... | collective-permute-start | bytes 786440 | tf_op jit(solution)/shard_map/ppermute | solution.py:24
  32.9 5.8 %collective-permute-done.3 = bf16[2,2,2,64,256]{4,3,1,2,0:T(8,128)(2,1)S(1)} collective-permute-done((bf16[2,2,2,64,256]{4,3,1,2,0:T(8,128)(2,1)S(1)}, bf16[2,2,2,64,256]{4,3,1,2,0:T(8,128)(2,1)S(1)}, u32[]{:S(2)}, u32[]{:S(2)}) %collective-permute-start.3) | collective-permute-done | bytes 262176 | tf_op jit(solution)/shard_map/ppermute | solution.py:24
  38.8 3.4 %collective-permute-start.4 = (bf16[2,2,2,2,64,256]{5,4,0,2,3,1:T(8,128)(2,1)S(1)}, bf16[2,2,2,2,64,256]{5,4,0,2,3,1:T(8,128)(2,1)S(1)}, u32[]{:S(2)}, u32[]{:S(2)}) collective-permute-start(bf16[2,2,2,2,64,256]{5,4,0,2,3,1:T(8,128)(2,1)S(1)} %maximum_select_fusion.3), channel_id=1, source_target_pairs={{0,128},{128,0},{256,384},{384,256},{1,129},{129,1},{257,385},{385... | collective-permute-start | bytes 1572872 | tf_op jit(solution)/shard_map/ppermute | solution.py:24
  42.4 7.5 %collective-permute-done.4 = bf16[2,2,2,2,64,256]{5,4,0,2,3,1:T(8,128)(2,1)S(1)} collective-permute-done((bf16[2,2,2,2,64,256]{5,4,0,2,3,1:T(8,128)(2,1)S(1)}, bf16[2,2,2,2,64,256]{5,4,0,2,3,1:T(8,128)(2,1)S(1)}, u32[]{:S(2)}, u32[]{:S(2)}) %collective-permute-start.4) | collective-permute-done | bytes 524320 | tf_op jit(solution)/shard_map/ppermute | solution.py:24
  49.8 1.2 maximum_select_fusion.1
  51.0 1.9 collective-permute-start.5
  53.0 0.8 copy.30.mq_ref
  53.7 0.1 maximum_select_fusion.2
  53.9 2.0 collective-permute-done.5
  55.9 1.3 copy.78
  57.2 0.2 maximum_select_fusion
  57.4 0.6 fusion.10
  58.0 0.7 maximum_bitcast_fusion.2.x_ref
  58.6 43.6 %shard_map.85 = bf16[16,193,256]{2,1,0:T(8,128)(2,1)} custom-call(bf16[1,193,256]{2,1,0:T(8,128)(2,1)} %maximum_bitcast_fusion.2.x_ref), custom_call_target="tpu_custom_call" | custom-call | tf_op jit(solution)/shard_map/pallas_call | solution.py:117
  102.2 2.6 %fusion.38 = (bf16[16,192,128]{2,1,0:T(8,128)(2,1)}, bf16[16,192,128]{2,1,0:T(8,128)(2,1)}) fusion(bf16[16,193,256]{2,1,0:T(8,128)(2,1)} %shard_map.85), kind=kLoop, calls=%fused_computation.98 | loop fusion | bytes 3145728 | tf_op jit(solution)/shard_map/slice | solution.py:227
  104.8 0.9 convert_reduce_fusion
  105.7 0.7 reshape.668.mk_ref
  106.4 15.4 %shard_map.86 = (bf16[192,512]{1,0:T(8,128)(2,1)}, bf16[3072,256]{1,0:T(8,128)(2,1)}) custom-call(bf16[192,512]{1,0:T(8,128)(2,1)} %bitcast.239, bf16[192,512]{1,0:T(8,128)(2,1)} %bitcast.240, bf16[3072,128]{1,0:T(8,128)(2,1)} %bitcast.229, bf16[3072,128]{1,0:T(8,128)(2,1)} %bitcast.228, f32[192,1]{1,0:T(8,128)} %copy.30.mq_ref, f32[1,3072]{1,0:T(1,128)} %reshape.668.mk_ref), custom_call_target="tpu_custom_call" | custom-call | flops 3623878656 | bytes 3932160 | tf_op jit(solution)/shard_map/pallas_call | solution.py:171
  121.8 1.5 fusion.39
  123.3 2.3 collective-permute-start.6
  125.6 1.9 collective-permute-done.6
  127.5 0.2 fusion.2
  127.7 4.4 %collective-permute-start.7 = (bf16[2,2,192,256]{3,2,1,0:T(8,128)(2,1)S(1)}, bf16[2,2,192,256]{3,2,1,0:T(8,128)(2,1)S(1)}, u32[]{:S(2)}, u32[]{:S(2)}) collective-permute-start(bf16[2,2,192,256]{3,2,1,0:T(8,128)(2,1)S(1)} %slice_bitcast_fusion), channel_id=1, source_target_pairs={{0,16},{8,24},{16,0},{24,8},{32,48},{40,56},{48,32},{56,40},{64,80... | collective-permute-start | bytes 1179656 | tf_op jit(solution)/shard_map/ppermute | solution.py:24
  132.1 9.6 %collective-permute-done.7 = bf16[2,2,192,256]{3,2,1,0:T(8,128)(2,1)S(1)} collective-permute-done((bf16[2,2,192,256]{3,2,1,0:T(8,128)(2,1)S(1)}, bf16[2,2,192,256]{3,2,1,0:T(8,128)(2,1)S(1)}, u32[]{:S(2)}, u32[]{:S(2)}) %collective-permute-start.7) | collective-permute-done | bytes 393248 | tf_op jit(solution)/shard_map/ppermute | solution.py:24
  141.9 4.0 %collective-permute-start.8 = (bf16[2,192,256]{2,1,0:T(8,128)(2,1)S(1)}, bf16[2,192,256]{2,1,0:T(8,128)(2,1)S(1)}, u32[]{:S(2)}, u32[]{:S(2)}) collective-permute-start(bf16[2,192,256]{2,1,0:T(8,128)(2,1)S(1)} %slice_bitcast_fusion.2), channel_id=1, source_target_pairs={{0,32},{8,40},{16,48},{24,56},{32,0},{40,8},{48,16},{56,24},{64,96... | collective-permute-start | bytes 589832 | tf_op jit(solution)/shard_map/ppermute | solution.py:24
  145.8 9.6 %collective-permute-done.8 = bf16[2,192,256]{2,1,0:T(8,128)(2,1)S(1)} collective-permute-done((bf16[2,192,256]{2,1,0:T(8,128)(2,1)S(1)}, bf16[2,192,256]{2,1,0:T(8,128)(2,1)S(1)}, u32[]{:S(2)}, u32[]{:S(2)}) %collective-permute-start.8) | collective-permute-done | bytes 196640 | tf_op jit(solution)/shard_map/ppermute | solution.py:24
  155.5 3.9 %collective-permute-start.9 = (bf16[192,256]{1,0:T(8,128)(2,1)S(1)}, bf16[192,256]{1,0:T(8,128)(2,1)S(1)}, u32[]{:S(2)}, u32[]{:S(2)}) collective-permute-start(bf16[192,256]{1,0:T(8,128)(2,1)S(1)} %slice_bitcast_fusion.4), channel_id=1, source_target_pairs={{0,64},{8,72},{16,80},{24,88},{32,96},{40,104},{48,112},{56,120},{... | collective-permute-start | bytes 294920 | tf_op jit(solution)/shard_map/ppermute | solution.py:24
  159.5 10.4 %collective-permute-done.9 = bf16[192,256]{1,0:T(8,128)(2,1)S(1)} collective-permute-done((bf16[192,256]{1,0:T(8,128)(2,1)S(1)}, bf16[192,256]{1,0:T(8,128)(2,1)S(1)}, u32[]{:S(2)}, u32[]{:S(2)}) %collective-permute-start.9) | collective-permute-done | bytes 98336 | tf_op jit(solution)/shard_map/ppermute | solution.py:24
  169.9 0.5 fusion.1
  170.4 1.3 copy.49
  171.7 1.3 fusion.40
  173.0 0.9 select_bitcast_fusion
  173.8 1.9 collective-permute-start.16
  175.7 1.5 fusion
  177.2 2.3 copy.31
  179.5 1.3 select_bitcast_fusion.1
  180.8 2.4 %collective-permute-start.10 = (bf16[2,2,2,2,2,64,128]{6,5,4,3,2,1,0:T(8,128)(2,1)S(1)}, bf16[2,2,2,2,2,64,128]{6,5,4,3,2,1,0:T(8,128)(2,1)S(1)}, u32[]{:S(2)}, u32[]{:S(2)}) collective-permute-start(bf16[2,2,2,2,2,64,128]{6,5,4,3,2,1,0:T(8,128)(2,1)S(1)} %get-tuple-element.13), channel_id=1, source_target_pairs={{0,8},{8,0},{16,24},{24,16},{32,40},{40,32},{48,56},{56,48},{64,72... | collective-permute-start | bytes 1572872 | tf_op jit(solution)/shard_map/ppermute | solution.py:24
  183.2 0.3 fusion.13
  183.5 1.9 collective-permute-start.17
  185.4 0.3 fusion.14
  185.8 3.4 %collective-permute-start.11 = (bf16[2,2,2,2,64,128]{5,4,3,2,1,0:T(8,128)(2,1)S(1)}, bf16[2,2,2,2,64,128]{5,4,3,2,1,0:T(8,128)(2,1)S(1)}, u32[]{:S(2)}, u32[]{:S(2)}) collective-permute-start(bf16[2,2,2,2,64,128]{5,4,3,2,1,0:T(8,128)(2,1)S(1)} %fusion.21), channel_id=1, source_target_pairs={{0,128},{128,0},{256,384},{384,256},{1,129},{129,1},{257,385},{385... | collective-permute-start | bytes 786440 | tf_op jit(solution)/shard_map/ppermute | solution.py:24
  189.2 4.4 %collective-permute-done.17 = bf16[2,2,2,2,64,128]{5,4,2,0,3,1:T(8,128)(2,1)S(1)} collective-permute-done((bf16[2,2,2,2,64,128]{5,4,2,0,3,1:T(8,128)(2,1)S(1)}, bf16[2,2,2,2,64,128]{5,4,2,0,3,1:T(8,128)(2,1)S(1)}, u32[]{:S(2)}, u32[]{:S(2)}) %collective-permute-start.17) | collective-permute-done | bytes 262176 | tf_op jit(solution)/shard_map/ppermute | solution.py:24
  193.8 3.4 %collective-permute-start.18 = (bf16[2,2,2,64,128]{4,3,1,0,2:T(8,128)(2,1)S(1)}, bf16[2,2,2,64,128]{4,3,1,0,2:T(8,128)(2,1)S(1)}, u32[]{:S(2)}, u32[]{:S(2)}) collective-permute-start(bf16[2,2,2,64,128]{4,3,1,0,2:T(8,128)(2,1)S(1)} %select_bitcast_fusion.3), channel_id=1, source_target_pairs={{0,128},{128,0},{256,384},{384,256},{1,129},{129,1},{257,385},{385... | collective-permute-start | bytes 393224 | tf_op jit(solution)/shard_map/ppermute | solution.py:24
  197.4 2.3 %collective-permute-start.12 = (bf16[2,2,2,64,128]{4,3,2,1,0:T(8,128)(2,1)S(1)}, bf16[2,2,2,64,128]{4,3,2,1,0:T(8,128)(2,1)S(1)}, u32[]{:S(2)}, u32[]{:S(2)}) collective-permute-start(bf16[2,2,2,64,128]{4,3,2,1,0:T(8,128)(2,1)S(1)} %fusion.27), channel_id=1, source_target_pairs={{0,16},{8,24},{16,0},{24,8},{32,48},{40,56},{48,32},{56,40},{64,80... | collective-permute-start | bytes 393224 | tf_op jit(solution)/shard_map/ppermute | solution.py:24
  199.7 0.9 collective-permute-done.18
  200.7 1.9 collective-permute-start.19
  202.7 1.6 collective-permute-done.12
  204.3 4.6 %collective-permute-start.13 = (bf16[2,2,64,128]{3,2,1,0:T(8,128)(2,1)S(1)}, bf16[2,2,64,128]{3,2,1,0:T(8,128)(2,1)S(1)}, u32[]{:S(2)}, u32[]{:S(2)}) collective-permute-start(bf16[2,2,64,128]{3,2,1,0:T(8,128)(2,1)S(1)} %select_bitcast_fusion.5), channel_id=1, source_target_pairs={{0,256},{128,384},{256,0},{384,128},{1,257},{129,385},{257,1},{385... | collective-permute-start | bytes 196616 | tf_op jit(solution)/shard_map/ppermute | solution.py:24
  209.0 4.3 %collective-permute-start.20 = (bf16[2,64,128]{2,1,0:T(8,128)(2,1)S(1)}, bf16[2,64,128]{2,1,0:T(8,128)(2,1)S(1)}, u32[]{:S(2)}, u32[]{:S(2)}) collective-permute-start(bf16[2,64,128]{2,1,0:T(8,128)(2,1)S(1)} %select_bitcast_fusion.6), channel_id=1, source_target_pairs={{0,256},{128,384},{256,0},{384,128},{1,257},{129,385},{257,1},{385... | collective-permute-start | bytes 98312 | tf_op jit(solution)/shard_map/ppermute | solution.py:24
  213.4 1.9 collective-permute-start.14
  215.3 1.0 collective-permute-done.20
  216.4 3.8 %collective-permute-start.21 = (bf16[64,128]{1,0:T(8,128)(2,1)S(1)}, bf16[64,128]{1,0:T(8,128)(2,1)S(1)}, u32[]{:S(2)}, u32[]{:S(2)}) collective-permute-start(bf16[64,128]{1,0:T(8,128)(2,1)S(1)} %select_bitcast_fusion.7), channel_id=1, source_target_pairs={{0,64},{8,72},{16,80},{24,88},{32,96},{40,104},{48,112},{56,120},{... | collective-permute-start | bytes 49160 | tf_op jit(solution)/shard_map/ppermute | solution.py:24
  220.3 5.9 %collective-permute-start.15 = (bf16[64,128]{1,0:T(8,128)(2,1)S(1)}, bf16[64,128]{1,0:T(8,128)(2,1)S(1)}, u32[]{:S(2)}, u32[]{:S(2)}) collective-permute-start(bf16[64,128]{1,0:T(8,128)(2,1)S(1)} %select_bitcast_fusion.8), channel_id=1, source_target_pairs={{0,64},{8,72},{16,80},{24,88},{32,96},{40,104},{48,112},{56,120},{... | collective-permute-start | bytes 49160 | tf_op jit(solution)/shard_map/ppermute | solution.py:24
  226.2 0.6 convert_add_fusion.13
  226.8 3.0 %collective-permute-done.15 = bf16[64,128]{1,0:T(8,128)(2,1)S(1)} collective-permute-done((bf16[64,128]{1,0:T(8,128)(2,1)S(1)}, bf16[64,128]{1,0:T(8,128)(2,1)S(1)}, u32[]{:S(2)}, u32[]{:S(2)}) %collective-permute-start.15) | collective-permute-done | bytes 16416 | tf_op jit(solution)/shard_map/ppermute | solution.py:24
  229.8 0.6 convert_add_fusion.14
  (51 shorter events, 1.3 us)
Async XLA Ops:
  0.6 56.7 %copy-start = (bf16[1,192,4096]{2,1,0:T(8,128)(2,1)S(1)}, bf16[1,192,4096]{2,1,0:T(8,128)(2,1)}, u32[]{:S(2)}) copy-start(bf16[1,192,4096]{2,1,0:T(8,128)(2,1)} %param.6) | copy-start | bytes 4718596
  2.2 11.0 %collective-permute-start = (bf16[64,256]{1,0:T(8,128)(2,1)S(1)}, bf16[64,256]{1,0:T(8,128)(2,1)S(1)}, u32[]{:S(2)}, u32[]{:S(2)}) collective-permute-start(bf16[64,256]{1,0:T(8,128)(2,1)S(1)} %constant_dynamic-update-slice_fusion), channel_id=1, source_target_pairs={{0,64},{8,72},{16,80},{24,88},{32,96},{40,104},{48,112},{56,120},{... | collective-permute-start | bytes 98312 | tf_op jit(solution)/shard_map/ppermute | solution.py:24
  13.2 8.8 %collective-permute-start.1 = (bf16[2,64,256]{2,1,0:T(8,128)(2,1)S(1)}, bf16[2,64,256]{2,1,0:T(8,128)(2,1)S(1)}, u32[]{:S(2)}, u32[]{:S(2)}) collective-permute-start(bf16[2,64,256]{2,1,0:T(8,128)(2,1)S(1)} %maximum_select_fusion.6), channel_id=1, source_target_pairs={{0,32},{8,40},{16,48},{24,56},{32,0},{40,8},{48,16},{56,24},{64,96... | collective-permute-start | bytes 196616 | tf_op jit(solution)/shard_map/ppermute | solution.py:24
  22.0 8.4 %collective-permute-start.2 = (bf16[2,2,64,256]{3,2,0,1:T(8,128)(2,1)S(1)}, bf16[2,2,64,256]{3,2,0,1:T(8,128)(2,1)S(1)}, u32[]{:S(2)}, u32[]{:S(2)}) collective-permute-start(bf16[2,2,64,256]{3,2,0,1:T(8,128)(2,1)S(1)} %maximum_select_fusion.5), channel_id=1, source_target_pairs={{0,256},{128,384},{256,0},{384,128},{1,257},{129,385},{257,1},{385... | collective-permute-start | bytes 393224 | tf_op jit(solution)/shard_map/ppermute | solution.py:24
  30.4 8.3 %collective-permute-start.3 = (bf16[2,2,2,64,256]{4,3,1,2,0:T(8,128)(2,1)S(1)}, bf16[2,2,2,64,256]{4,3,1,2,0:T(8,128)(2,1)S(1)}, u32[]{:S(2)}, u32[]{:S(2)}) collective-permute-start(bf16[2,2,2,64,256]{4,3,1,2,0:T(8,128)(2,1)S(1)} %maximum_select_fusion.4), channel_id=1, source_target_pairs={{0,16},{8,24},{16,0},{24,8},{32,48},{40,56},{48,32},{56,40},{64,80... | collective-permute-start | bytes 786440 | tf_op jit(solution)/shard_map/ppermute | solution.py:24
  38.8 11.1 %collective-permute-start.4 = (bf16[2,2,2,2,64,256]{5,4,0,2,3,1:T(8,128)(2,1)S(1)}, bf16[2,2,2,2,64,256]{5,4,0,2,3,1:T(8,128)(2,1)S(1)}, u32[]{:S(2)}, u32[]{:S(2)}) collective-permute-start(bf16[2,2,2,2,64,256]{5,4,0,2,3,1:T(8,128)(2,1)S(1)} %maximum_select_fusion.3), channel_id=1, source_target_pairs={{0,128},{128,0},{256,384},{384,256},{1,129},{129,1},{257,385},{385... | collective-permute-start | bytes 1572872 | tf_op jit(solution)/shard_map/ppermute | solution.py:24
  42.3 10.6 %copy-start.1 = (s32[1,192]{1,0:T(1,128)S(1)}, s32[1,192]{1,0:T(1,128)}, u32[]{:S(2)}) copy-start(s32[1,192]{1,0:T(1,128)} %param.9) | copy-start | bytes 2308
  51.0 4.9 %collective-permute-start.5 = (bf16[2,2,2,2,2,64,256]{6,5,1,3,4,2,0:T(8,128)(2,1)}, bf16[2,2,2,2,2,64,256]{6,5,1,3,4,2,0:T(8,128)(2,1)}, u32[]{:S(2)}, u32[]{:S(2)}) collective-permute-start(bf16[2,2,2,2,2,64,256]{6,5,1,3,4,2,0:T(8,128)(2,1)} %maximum_select_fusion.1), channel_id=1, source_target_pairs={{0,8},{8,0},{16,24},{24,16},{32,40},{40,32},{48,56},{56,48},{64,72... | collective-permute-start | bytes 3145736 | tf_op jit(solution)/shard_map/ppermute | solution.py:24
  123.3 4.2 %collective-permute-start.6 = (bf16[2,2,2,192,256]{4,3,2,1,0:T(8,128)(2,1)S(1)}, bf16[2,2,2,192,256]{4,3,2,1,0:T(8,128)(2,1)S(1)}, u32[]{:S(2)}, u32[]{:S(2)}) collective-permute-start(bf16[2,2,2,192,256]{4,3,2,1,0:T(8,128)(2,1)S(1)} %bitcast.230), channel_id=1, source_target_pairs={{0,8},{8,0},{16,24},{24,16},{32,40},{40,32},{48,56},{56,48},{64,72... | collective-permute-start | bytes 2359304 | tf_op jit(solution)/shard_map/ppermute | solution.py:24
  127.7 14.0 %collective-permute-start.7 = (bf16[2,2,192,256]{3,2,1,0:T(8,128)(2,1)S(1)}, bf16[2,2,192,256]{3,2,1,0:T(8,128)(2,1)S(1)}, u32[]{:S(2)}, u32[]{:S(2)}) collective-permute-start(bf16[2,2,192,256]{3,2,1,0:T(8,128)(2,1)S(1)} %slice_bitcast_fusion), channel_id=1, source_target_pairs={{0,16},{8,24},{16,0},{24,8},{32,48},{40,56},{48,32},{56,40},{64,80... | collective-permute-start | bytes 1179656 | tf_op jit(solution)/shard_map/ppermute | solution.py:24
  141.9 13.6 %collective-permute-start.8 = (bf16[2,192,256]{2,1,0:T(8,128)(2,1)S(1)}, bf16[2,192,256]{2,1,0:T(8,128)(2,1)S(1)}, u32[]{:S(2)}, u32[]{:S(2)}) collective-permute-start(bf16[2,192,256]{2,1,0:T(8,128)(2,1)S(1)} %slice_bitcast_fusion.2), channel_id=1, source_target_pairs={{0,32},{8,40},{16,48},{24,56},{32,0},{40,8},{48,16},{56,24},{64,96... | collective-permute-start | bytes 589832 | tf_op jit(solution)/shard_map/ppermute | solution.py:24
  155.5 14.3 %collective-permute-start.9 = (bf16[192,256]{1,0:T(8,128)(2,1)S(1)}, bf16[192,256]{1,0:T(8,128)(2,1)S(1)}, u32[]{:S(2)}, u32[]{:S(2)}) collective-permute-start(bf16[192,256]{1,0:T(8,128)(2,1)S(1)} %slice_bitcast_fusion.4), channel_id=1, source_target_pairs={{0,64},{8,72},{16,80},{24,88},{32,96},{40,104},{48,112},{56,120},{... | collective-permute-start | bytes 294920 | tf_op jit(solution)/shard_map/ppermute | solution.py:24
  173.8 9.4 %collective-permute-start.16 = (bf16[2,2,2,2,2,64,128]{6,5,2,0,3,1,4:T(8,128)(2,1)}, bf16[2,2,2,2,2,64,128]{6,5,2,0,3,1,4:T(8,128)(2,1)S(1)}, u32[]{:S(2)}, u32[]{:S(2)}) collective-permute-start(bf16[2,2,2,2,2,64,128]{6,5,2,0,3,1,4:T(8,128)(2,1)} %select_bitcast_fusion), channel_id=1, source_target_pairs={{0,8},{8,0},{16,24},{24,16},{32,40},{40,32},{48,56},{56,48},{64,72... | collective-permute-start | bytes 1572872 | tf_op jit(solution)/shard_map/ppermute | solution.py:24
  180.8 4.7 %collective-permute-start.10 = (bf16[2,2,2,2,2,64,128]{6,5,4,3,2,1,0:T(8,128)(2,1)S(1)}, bf16[2,2,2,2,2,64,128]{6,5,4,3,2,1,0:T(8,128)(2,1)S(1)}, u32[]{:S(2)}, u32[]{:S(2)}) collective-permute-start(bf16[2,2,2,2,2,64,128]{6,5,4,3,2,1,0:T(8,128)(2,1)S(1)} %get-tuple-element.13), channel_id=1, source_target_pairs={{0,8},{8,0},{16,24},{24,16},{32,40},{40,32},{48,56},{56,48},{64,72... | collective-permute-start | bytes 1572872 | tf_op jit(solution)/shard_map/ppermute | solution.py:24
  183.5 10.1 %collective-permute-start.17 = (bf16[2,2,2,2,64,128]{5,4,2,0,3,1:T(8,128)(2,1)S(1)}, bf16[2,2,2,2,64,128]{5,4,2,0,3,1:T(8,128)(2,1)S(1)}, u32[]{:S(2)}, u32[]{:S(2)}) collective-permute-start(bf16[2,2,2,2,64,128]{5,4,2,0,3,1:T(8,128)(2,1)S(1)} %select_bitcast_fusion.2), channel_id=1, source_target_pairs={{0,16},{8,24},{16,0},{24,8},{32,48},{40,56},{48,32},{56,40},{64,80... | collective-permute-start | bytes 786440 | tf_op jit(solution)/shard_map/ppermute | solution.py:24
  185.8 11.4 %collective-permute-start.11 = (bf16[2,2,2,2,64,128]{5,4,3,2,1,0:T(8,128)(2,1)S(1)}, bf16[2,2,2,2,64,128]{5,4,3,2,1,0:T(8,128)(2,1)S(1)}, u32[]{:S(2)}, u32[]{:S(2)}) collective-permute-start(bf16[2,2,2,2,64,128]{5,4,3,2,1,0:T(8,128)(2,1)S(1)} %fusion.21), channel_id=1, source_target_pairs={{0,128},{128,0},{256,384},{384,256},{1,129},{129,1},{257,385},{385... | collective-permute-start | bytes 786440 | tf_op jit(solution)/shard_map/ppermute | solution.py:24
  193.8 6.9 %collective-permute-start.18 = (bf16[2,2,2,64,128]{4,3,1,0,2:T(8,128)(2,1)S(1)}, bf16[2,2,2,64,128]{4,3,1,0,2:T(8,128)(2,1)S(1)}, u32[]{:S(2)}, u32[]{:S(2)}) collective-permute-start(bf16[2,2,2,64,128]{4,3,1,0,2:T(8,128)(2,1)S(1)} %select_bitcast_fusion.3), channel_id=1, source_target_pairs={{0,128},{128,0},{256,384},{384,256},{1,129},{129,1},{257,385},{385... | collective-permute-start | bytes 393224 | tf_op jit(solution)/shard_map/ppermute | solution.py:24
  197.4 6.9 %collective-permute-start.12 = (bf16[2,2,2,64,128]{4,3,2,1,0:T(8,128)(2,1)S(1)}, bf16[2,2,2,64,128]{4,3,2,1,0:T(8,128)(2,1)S(1)}, u32[]{:S(2)}, u32[]{:S(2)}) collective-permute-start(bf16[2,2,2,64,128]{4,3,2,1,0:T(8,128)(2,1)S(1)} %fusion.27), channel_id=1, source_target_pairs={{0,16},{8,24},{16,0},{24,8},{32,48},{40,56},{48,32},{56,40},{64,80... | collective-permute-start | bytes 393224 | tf_op jit(solution)/shard_map/ppermute | solution.py:24
  200.7 8.2 %collective-permute-start.19 = (bf16[2,2,64,128]{3,2,1,0:T(8,128)(2,1)S(1)}, bf16[2,2,64,128]{3,2,1,0:T(8,128)(2,1)S(1)}, u32[]{:S(2)}, u32[]{:S(2)}) collective-permute-start(bf16[2,2,64,128]{3,2,1,0:T(8,128)(2,1)S(1)} %select_bitcast_fusion.4), channel_id=1, source_target_pairs={{0,32},{8,40},{16,48},{24,56},{32,0},{40,8},{48,16},{56,24},{64,96... | collective-permute-start | bytes 196616 | tf_op jit(solution)/shard_map/ppermute | solution.py:24
  204.3 9.0 %collective-permute-start.13 = (bf16[2,2,64,128]{3,2,1,0:T(8,128)(2,1)S(1)}, bf16[2,2,64,128]{3,2,1,0:T(8,128)(2,1)S(1)}, u32[]{:S(2)}, u32[]{:S(2)}) collective-permute-start(bf16[2,2,64,128]{3,2,1,0:T(8,128)(2,1)S(1)} %select_bitcast_fusion.5), channel_id=1, source_target_pairs={{0,256},{128,384},{256,0},{384,128},{1,257},{129,385},{257,1},{385... | collective-permute-start | bytes 196616 | tf_op jit(solution)/shard_map/ppermute | solution.py:24
  209.0 7.3 %collective-permute-start.20 = (bf16[2,64,128]{2,1,0:T(8,128)(2,1)S(1)}, bf16[2,64,128]{2,1,0:T(8,128)(2,1)S(1)}, u32[]{:S(2)}, u32[]{:S(2)}) collective-permute-start(bf16[2,64,128]{2,1,0:T(8,128)(2,1)S(1)} %select_bitcast_fusion.6), channel_id=1, source_target_pairs={{0,256},{128,384},{256,0},{384,128},{1,257},{129,385},{257,1},{385... | collective-permute-start | bytes 98312 | tf_op jit(solution)/shard_map/ppermute | solution.py:24
  213.4 6.8 %collective-permute-start.14 = (bf16[2,64,128]{2,1,0:T(8,128)(2,1)S(1)}, bf16[2,64,128]{2,1,0:T(8,128)(2,1)S(1)}, u32[]{:S(2)}, u32[]{:S(2)}) collective-permute-start(bf16[2,64,128]{2,1,0:T(8,128)(2,1)S(1)} %fusion.36), channel_id=1, source_target_pairs={{0,32},{8,40},{16,48},{24,56},{32,0},{40,8},{48,16},{56,24},{64,96... | collective-permute-start | bytes 98312 | tf_op jit(solution)/shard_map/ppermute | solution.py:24
  216.4 9.8 %collective-permute-start.21 = (bf16[64,128]{1,0:T(8,128)(2,1)S(1)}, bf16[64,128]{1,0:T(8,128)(2,1)S(1)}, u32[]{:S(2)}, u32[]{:S(2)}) collective-permute-start(bf16[64,128]{1,0:T(8,128)(2,1)S(1)} %select_bitcast_fusion.7), channel_id=1, source_target_pairs={{0,64},{8,72},{16,80},{24,88},{32,96},{40,104},{48,112},{56,120},{... | collective-permute-start | bytes 49160 | tf_op jit(solution)/shard_map/ppermute | solution.py:24
  220.3 9.5 %collective-permute-start.15 = (bf16[64,128]{1,0:T(8,128)(2,1)S(1)}, bf16[64,128]{1,0:T(8,128)(2,1)S(1)}, u32[]{:S(2)}, u32[]{:S(2)}) collective-permute-start(bf16[64,128]{1,0:T(8,128)(2,1)S(1)} %select_bitcast_fusion.8), channel_id=1, source_target_pairs={{0,64},{8,72},{16,80},{24,88},{32,96},{40,104},{48,112},{56,120},{... | collective-permute-start | bytes 49160 | tf_op jit(solution)/shard_map/ppermute | solution.py:24

commit v8 on v7

--- a/solution.py
+++ b/solution.py
@@ -83,29 +83,46 @@
 def _gather_kernel(bits, x_ref, o_ref, held, send_sems, recv_sems, local_sem):
     me = lax.axis_index("context")
     partners = [lax.bitwise_xor(me, 1 << b) for b in bits]
+    mesh = pl.DeviceIdType.MESH
     barrier = pltpu.get_barrier_semaphore()
     for p in partners:
-        pl.semaphore_signal(barrier, inc=1, device_id={"context": p},
-                            device_id_type=pl.DeviceIdType.MESH)
+        pl.semaphore_signal(barrier, inc=1, device_id={"context": p}, device_id_type=mesh)
     pl.semaphore_wait(barrier, len(partners))
     local = pltpu.make_async_copy(x_ref, held.at[0:1], local_sem)
     local.start()
-    for k, p in enumerate(partners):
-        n = 1 << k
-        if k == 1:
-            local.wait()
+    sends = []
+
+    def push(src, lo, hi, j):
+        base = 1 << j
         copy = pltpu.make_async_remote_copy(
-            src_ref=x_ref if k == 0 else held.at[0:n],
-            dst_ref=held.at[n:2 * n],
-            send_sem=send_sems.at[k],
-            recv_sem=recv_sems.at[k],
-            device_id={"context": p},
-            device_id_type=pl.DeviceIdType.MESH,
+            src_ref=src,
+            dst_ref=held.at[base + lo:base + hi],
+            send_sem=send_sems.at[len(sends)],
+            recv_sem=recv_sems.at[j],
+            device_id={"context": partners[j]},
+            device_id_type=mesh,
         )
         copy.start()
-        copy.wait()
-    if len(partners) < 2:
-        local.wait()
+        sends.append(copy)
+
+    for j in range(len(partners)):
+        push(x_ref, 0, 1, j)
+    for i in range(len(partners)):
+        lo, hi = 1 << i, 2 << i
+        arrived = pltpu.make_async_remote_copy(
+            src_ref=held.at[lo:hi],
+            dst_ref=held.at[lo:hi],
+            send_sem=send_sems.at[0],
+            recv_sem=recv_sems.at[i],
+            device_id={"context": partners[i]},
+            device_id_type=mesh,
+        )
+        arrived.wait_recv()
+        for j in range(i + 1, len(partners)):
+            push(held.at[lo:hi], lo, hi, j)
+    for copy in sends:
+        copy.wait_send()
+    local.wait()
     out = pltpu.make_async_copy(held, o_ref, local_sem)
     out.start()
     out.wait()
@@ -121,7 +138,7 @@
         out_specs=pl.BlockSpec(memory_space=pltpu.VMEM),
         scratch_shapes=[
             pltpu.VMEM(shape, x.dtype),
-            pltpu.SemaphoreType.DMA((len(bits),)),
+            pltpu.SemaphoreType.DMA((len(bits) * (len(bits) + 1) // 2,)),
             pltpu.SemaphoreType.DMA((len(bits),)),
             pltpu.SemaphoreType.DMA,
         ],

time: 231 us -> 223 us (0.965)
  Pallas kernels: 59 us -> 50.4 us
    pallas_call x1, Pallas kernels: 43.6 us -> 35 us  [context_gather(): pl.pallas_call(functools.partial(_gather_kernel, bits), out_shape=jax.Sha...]
  transfers between devices with their start and end apart: 22 -> 22, of which waited for: 15 -> 16; matrix products, arithmetic and copies ran while one was open for 3% -> 4% of each run, Pallas kernels for 0% -> 0%
where the time goes in v8:
time: 223 us; the launch traced here: 222 us
  starting transfers between devices  78.6 us (35%)
  waiting for transfers between devices  67.2 us (30%)
  Pallas kernels  50.4 us (23%)
  local copies, waits for them, and re-layouts  13.3 us (6%)
  other arithmetic  8.35 us (4%)
  matrix products  2.53 us (1%)
    ppermute x22, starting transfers between devices, _exchange(): return lax.ppermute(x, axis, perm)  78.6 us
    ppermute x22, waiting for transfers between devices, _exchange(): return lax.ppermute(x, axis, perm)  67.2 us
    pallas_call x1, Pallas kernels, context_gather(): pl.pallas_call(functools.partial(_gather_kernel, bits), out_shape=jax.Sha...  35 us
    pallas_call x1, Pallas kernels, attention_block(): pl.pallas_call(_attention_kernel, out_shape=(jax.ShapeDtypeStruct((rows,...  15.4 us
  transfers between devices with their start and end apart: 22, of which 16 were waited for; matrix products, arithmetic and copies ran while one was open for 4% of the time, Pallas kernels for 0%

profile of v8, /device:TPU:24, one launch (start us, length us, event | category | flops | bytes accessed | tf_op | source)
XLA Modules:
  0.0 221.6 jit_solution(13874955535911014812)
XLA Ops:
  0.6 0.8 constant_dynamic-update-slice_fusion.1
  1.5 0.7 constant_dynamic-update-slice_fusion
  2.2 9.1 %collective-permute-start = (bf16[64,256]{1,0:T(8,128)(2,1)S(1)}, bf16[64,256]{1,0:T(8,128)(2,1)S(1)}, u32[]{:S(2)}, u32[]{:S(2)}) collective-permute-start(bf16[64,256]{1,0:T(8,128)(2,1)S(1)} %constant_dynamic-update-slice_fusion), channel_id=1, source_target_pairs={{0,64},{8,72},{16,80},{24,88},{32,96},{40,104},{48,112},{56,120},{... | collective-permute-start | bytes 98312 | tf_op jit(solution)/shard_map/ppermute | solution.py:24
  11.3 1.9 collective-permute-done
  13.2 5.2 %collective-permute-start.1 = (bf16[2,64,256]{2,1,0:T(8,128)(2,1)S(1)}, bf16[2,64,256]{2,1,0:T(8,128)(2,1)S(1)}, u32[]{:S(2)}, u32[]{:S(2)}) collective-permute-start(bf16[2,64,256]{2,1,0:T(8,128)(2,1)S(1)} %maximum_select_fusion.6), channel_id=1, source_target_pairs={{0,32},{8,40},{16,48},{24,56},{32,0},{40,8},{48,16},{56,24},{64,96... | collective-permute-start | bytes 196616 | tf_op jit(solution)/shard_map/ppermute | solution.py:24
  18.4 3.6 %collective-permute-done.1 = bf16[2,64,256]{2,1,0:T(8,128)(2,1)S(1)} collective-permute-done((bf16[2,64,256]{2,1,0:T(8,128)(2,1)S(1)}, bf16[2,64,256]{2,1,0:T(8,128)(2,1)S(1)}, u32[]{:S(2)}, u32[]{:S(2)}) %collective-permute-start.1) | collective-permute-done | bytes 65568 | tf_op jit(solution)/shard_map/ppermute | solution.py:24
  22.0 4.9 %collective-permute-start.2 = (bf16[2,2,64,256]{3,2,0,1:T(8,128)(2,1)S(1)}, bf16[2,2,64,256]{3,2,0,1:T(8,128)(2,1)S(1)}, u32[]{:S(2)}, u32[]{:S(2)}) collective-permute-start(bf16[2,2,64,256]{3,2,0,1:T(8,128)(2,1)S(1)} %maximum_select_fusion.5), channel_id=1, source_target_pairs={{0,256},{128,384},{256,0},{384,128},{1,257},{129,385},{257,1},{385... | collective-permute-start | bytes 393224 | tf_op jit(solution)/shard_map/ppermute | solution.py:24
  27.0 3.4 %collective-permute-done.2 = bf16[2,2,64,256]{3,2,0,1:T(8,128)(2,1)S(1)} collective-permute-done((bf16[2,2,64,256]{3,2,0,1:T(8,128)(2,1)S(1)}, bf16[2,2,64,256]{3,2,0,1:T(8,128)(2,1)S(1)}, u32[]{:S(2)}, u32[]{:S(2)}) %collective-permute-start.2) | collective-permute-done | bytes 131104 | tf_op jit(solution)/shard_map/ppermute | solution.py:24
  30.4 2.4 %collective-permute-start.3 = (bf16[2,2,2,64,256]{4,3,1,2,0:T(8,128)(2,1)S(1)}, bf16[2,2,2,64,256]{4,3,1,2,0:T(8,128)(2,1)S(1)}, u32[]{:S(2)}, u32[]{:S(2)}) collective-permute-start(bf16[2,2,2,64,256]{4,3,1,2,0:T(8,128)(2,1)S(1)} %maximum_select_fusion.4), channel_id=1, source_target_pairs={{0,16},{8,24},{16,0},{24,8},{32,48},{40,56},{48,32},{56,40},{64,80... | collective-permute-start | bytes 786440 | tf_op jit(solution)/shard_map/ppermute | solution.py:24
  32.9 5.8 %collective-permute-done.3 = bf16[2,2,2,64,256]{4,3,1,2,0:T(8,128)(2,1)S(1)} collective-permute-done((bf16[2,2,2,64,256]{4,3,1,2,0:T(8,128)(2,1)S(1)}, bf16[2,2,2,64,256]{4,3,1,2,0:T(8,128)(2,1)S(1)}, u32[]{:S(2)}, u32[]{:S(2)}) %collective-permute-start.3) | collective-permute-done | bytes 262176 | tf_op jit(solution)/shard_map/ppermute | solution.py:24
  38.8 3.4 %collective-permute-start.4 = (bf16[2,2,2,2,64,256]{5,4,0,2,3,1:T(8,128)(2,1)S(1)}, bf16[2,2,2,2,64,256]{5,4,0,2,3,1:T(8,128)(2,1)S(1)}, u32[]{:S(2)}, u32[]{:S(2)}) collective-permute-start(bf16[2,2,2,2,64,256]{5,4,0,2,3,1:T(8,128)(2,1)S(1)} %maximum_select_fusion.3), channel_id=1, source_target_pairs={{0,128},{128,0},{256,384},{384,256},{1,129},{129,1},{257,385},{385... | collective-permute-start | bytes 1572872 | tf_op jit(solution)/shard_map/ppermute | solution.py:24
  42.4 7.5 %collective-permute-done.4 = bf16[2,2,2,2,64,256]{5,4,0,2,3,1:T(8,128)(2,1)S(1)} collective-permute-done((bf16[2,2,2,2,64,256]{5,4,0,2,3,1:T(8,128)(2,1)S(1)}, bf16[2,2,2,2,64,256]{5,4,0,2,3,1:T(8,128)(2,1)S(1)}, u32[]{:S(2)}, u32[]{:S(2)}) %collective-permute-start.4) | collective-permute-done | bytes 524320 | tf_op jit(solution)/shard_map/ppermute | solution.py:24
  49.8 1.2 maximum_select_fusion.1
  51.0 1.9 collective-permute-start.5
  53.0 0.8 copy.30.mq_ref
  53.7 0.1 maximum_select_fusion.2
  53.9 2.0 collective-permute-done.5
  55.9 1.3 copy.78
  57.2 0.2 maximum_select_fusion
  57.4 0.6 fusion.10
  58.0 0.7 maximum_bitcast_fusion.2.x_ref
  58.6 35.0 %shard_map.85 = bf16[16,193,256]{2,1,0:T(8,128)(2,1)} custom-call(bf16[1,193,256]{2,1,0:T(8,128)(2,1)} %maximum_bitcast_fusion.2.x_ref), custom_call_target="tpu_custom_call" | custom-call | tf_op jit(solution)/shard_map/pallas_call | solution.py:134
  93.6 2.6 %fusion.38 = (bf16[16,192,128]{2,1,0:T(8,128)(2,1)}, bf16[16,192,128]{2,1,0:T(8,128)(2,1)}) fusion(bf16[16,193,256]{2,1,0:T(8,128)(2,1)} %shard_map.85), kind=kLoop, calls=%fused_computation.98 | loop fusion | bytes 3145728 | tf_op jit(solution)/shard_map/slice | solution.py:244
  96.2 0.9 convert_reduce_fusion
  97.1 0.7 reshape.668.mk_ref
  97.8 15.4 %shard_map.86 = (bf16[192,512]{1,0:T(8,128)(2,1)}, bf16[3072,256]{1,0:T(8,128)(2,1)}) custom-call(bf16[192,512]{1,0:T(8,128)(2,1)} %bitcast.239, bf16[192,512]{1,0:T(8,128)(2,1)} %bitcast.240, bf16[3072,128]{1,0:T(8,128)(2,1)} %bitcast.229, bf16[3072,128]{1,0:T(8,128)(2,1)} %bitcast.228, f32[192,1]{1,0:T(8,128)} %copy.30.mq_ref, f32[1,3072]{1,0:T(1,128)} %reshape.668.mk_ref), custom_call_target="tpu_custom_call" | custom-call | flops 3623878656 | bytes 3932160 | tf_op jit(solution)/shard_map/pallas_call | solution.py:188
  113.2 1.5 fusion.39
  114.7 2.3 %collective-permute-start.6 = (bf16[2,2,2,192,256]{4,3,2,1,0:T(8,128)(2,1)S(1)}, bf16[2,2,2,192,256]{4,3,2,1,0:T(8,128)(2,1)S(1)}, u32[]{:S(2)}, u32[]{:S(2)}) collective-permute-start(bf16[2,2,2,192,256]{4,3,2,1,0:T(8,128)(2,1)S(1)} %bitcast.230), channel_id=1, source_target_pairs={{0,8},{8,0},{16,24},{24,16},{32,40},{40,32},{48,56},{56,48},{64,72... | collective-permute-start | bytes 2359304 | tf_op jit(solution)/shard_map/ppermute | solution.py:24
  117.0 1.9 collective-permute-done.6
  118.9 0.2 fusion.2
  119.1 3.0 %collective-permute-start.7 = (bf16[2,2,192,256]{3,2,1,0:T(8,128)(2,1)S(1)}, bf16[2,2,192,256]{3,2,1,0:T(8,128)(2,1)S(1)}, u32[]{:S(2)}, u32[]{:S(2)}) collective-permute-start(bf16[2,2,192,256]{3,2,1,0:T(8,128)(2,1)S(1)} %slice_bitcast_fusion), channel_id=1, source_target_pairs={{0,16},{8,24},{16,0},{24,8},{32,48},{40,56},{48,32},{56,40},{64,80... | collective-permute-start | bytes 1179656 | tf_op jit(solution)/shard_map/ppermute | solution.py:24
  122.1 10.3 %collective-permute-done.7 = bf16[2,2,192,256]{3,2,1,0:T(8,128)(2,1)S(1)} collective-permute-done((bf16[2,2,192,256]{3,2,1,0:T(8,128)(2,1)S(1)}, bf16[2,2,192,256]{3,2,1,0:T(8,128)(2,1)S(1)}, u32[]{:S(2)}, u32[]{:S(2)}) %collective-permute-start.7) | collective-permute-done | bytes 393248 | tf_op jit(solution)/shard_map/ppermute | solution.py:24
  132.5 3.6 %collective-permute-start.8 = (bf16[2,192,256]{2,1,0:T(8,128)(2,1)S(1)}, bf16[2,192,256]{2,1,0:T(8,128)(2,1)S(1)}, u32[]{:S(2)}, u32[]{:S(2)}) collective-permute-start(bf16[2,192,256]{2,1,0:T(8,128)(2,1)S(1)} %slice_bitcast_fusion.2), channel_id=1, source_target_pairs={{0,32},{8,40},{16,48},{24,56},{32,0},{40,8},{48,16},{56,24},{64,96... | collective-permute-start | bytes 589832 | tf_op jit(solution)/shard_map/ppermute | solution.py:24
  136.1 9.8 %collective-permute-done.8 = bf16[2,192,256]{2,1,0:T(8,128)(2,1)S(1)} collective-permute-done((bf16[2,192,256]{2,1,0:T(8,128)(2,1)S(1)}, bf16[2,192,256]{2,1,0:T(8,128)(2,1)S(1)}, u32[]{:S(2)}, u32[]{:S(2)}) %collective-permute-start.8) | collective-permute-done | bytes 196640 | tf_op jit(solution)/shard_map/ppermute | solution.py:24
  146.0 5.0 %collective-permute-start.9 = (bf16[192,256]{1,0:T(8,128)(2,1)S(1)}, bf16[192,256]{1,0:T(8,128)(2,1)S(1)}, u32[]{:S(2)}, u32[]{:S(2)}) collective-permute-start(bf16[192,256]{1,0:T(8,128)(2,1)S(1)} %slice_bitcast_fusion.4), channel_id=1, source_target_pairs={{0,64},{8,72},{16,80},{24,88},{32,96},{40,104},{48,112},{56,120},{... | collective-permute-start | bytes 294920 | tf_op jit(solution)/shard_map/ppermute | solution.py:24
  151.0 10.2 %collective-permute-done.9 = bf16[192,256]{1,0:T(8,128)(2,1)S(1)} collective-permute-done((bf16[192,256]{1,0:T(8,128)(2,1)S(1)}, bf16[192,256]{1,0:T(8,128)(2,1)S(1)}, u32[]{:S(2)}, u32[]{:S(2)}) %collective-permute-start.9) | collective-permute-done | bytes 98336 | tf_op jit(solution)/shard_map/ppermute | solution.py:24
  161.3 0.5 fusion.1
  161.7 1.3 copy.49
  163.0 1.3 fusion.40
  164.3 0.9 select_bitcast_fusion
  165.2 1.9 collective-permute-start.16
  167.1 1.5 fusion
  168.6 2.3 %copy.31 = bf16[4096,128]{1,0:T(8,128)(2,1)} copy(bf16[4096,128]{0,1:T(8,128)(2,1)} %fusion) | data formatting | bytes 2097152 | tf_op jit(solution)/shard_map/convert_element_type | solution.py:256
  170.9 1.3 select_bitcast_fusion.1
  172.2 2.4 %collective-permute-start.10 = (bf16[2,2,2,2,2,64,128]{6,5,4,3,2,1,0:T(8,128)(2,1)S(1)}, bf16[2,2,2,2,2,64,128]{6,5,4,3,2,1,0:T(8,128)(2,1)S(1)}, u32[]{:S(2)}, u32[]{:S(2)}) collective-permute-start(bf16[2,2,2,2,2,64,128]{6,5,4,3,2,1,0:T(8,128)(2,1)S(1)} %get-tuple-element.13), channel_id=1, source_target_pairs={{0,8},{8,0},{16,24},{24,16},{32,40},{40,32},{48,56},{56,48},{64,72... | collective-permute-start | bytes 1572872 | tf_op jit(solution)/shard_map/ppermute | solution.py:24
  174.6 0.3 fusion.13
  174.9 1.9 collective-permute-start.17
  176.8 0.3 fusion.14
  177.1 3.4 %collective-permute-start.11 = (bf16[2,2,2,2,64,128]{5,4,3,2,1,0:T(8,128)(2,1)S(1)}, bf16[2,2,2,2,64,128]{5,4,3,2,1,0:T(8,128)(2,1)S(1)}, u32[]{:S(2)}, u32[]{:S(2)}) collective-permute-start(bf16[2,2,2,2,64,128]{5,4,3,2,1,0:T(8,128)(2,1)S(1)} %fusion.21), channel_id=1, source_target_pairs={{0,128},{128,0},{256,384},{384,256},{1,129},{129,1},{257,385},{385... | collective-permute-start | bytes 786440 | tf_op jit(solution)/shard_map/ppermute | solution.py:24
  180.5 4.5 %collective-permute-done.17 = bf16[2,2,2,2,64,128]{5,4,2,0,3,1:T(8,128)(2,1)S(1)} collective-permute-done((bf16[2,2,2,2,64,128]{5,4,2,0,3,1:T(8,128)(2,1)S(1)}, bf16[2,2,2,2,64,128]{5,4,2,0,3,1:T(8,128)(2,1)S(1)}, u32[]{:S(2)}, u32[]{:S(2)}) %collective-permute-start.17) | collective-permute-done | bytes 262176 | tf_op jit(solution)/shard_map/ppermute | solution.py:24
  185.2 3.3 %collective-permute-start.18 = (bf16[2,2,2,64,128]{4,3,1,0,2:T(8,128)(2,1)S(1)}, bf16[2,2,2,64,128]{4,3,1,0,2:T(8,128)(2,1)S(1)}, u32[]{:S(2)}, u32[]{:S(2)}) collective-permute-start(bf16[2,2,2,64,128]{4,3,1,0,2:T(8,128)(2,1)S(1)} %select_bitcast_fusion.3), channel_id=1, source_target_pairs={{0,128},{128,0},{256,384},{384,256},{1,129},{129,1},{257,385},{385... | collective-permute-start | bytes 393224 | tf_op jit(solution)/shard_map/ppermute | solution.py:24
  188.7 2.4 %collective-permute-start.12 = (bf16[2,2,2,64,128]{4,3,2,1,0:T(8,128)(2,1)S(1)}, bf16[2,2,2,64,128]{4,3,2,1,0:T(8,128)(2,1)S(1)}, u32[]{:S(2)}, u32[]{:S(2)}) collective-permute-start(bf16[2,2,2,64,128]{4,3,2,1,0:T(8,128)(2,1)S(1)} %fusion.27), channel_id=1, source_target_pairs={{0,16},{8,24},{16,0},{24,8},{32,48},{40,56},{48,32},{56,40},{64,80... | collective-permute-start | bytes 393224 | tf_op jit(solution)/shard_map/ppermute | solution.py:24
  191.1 0.9 collective-permute-done.18
  192.1 1.9 collective-permute-start.19
  194.1 1.5 collective-permute-done.12
  195.6 4.7 %collective-permute-start.13 = (bf16[2,2,64,128]{3,2,1,0:T(8,128)(2,1)S(1)}, bf16[2,2,64,128]{3,2,1,0:T(8,128)(2,1)S(1)}, u32[]{:S(2)}, u32[]{:S(2)}) collective-permute-start(bf16[2,2,64,128]{3,2,1,0:T(8,128)(2,1)S(1)} %select_bitcast_fusion.5), channel_id=1, source_target_pairs={{0,256},{128,384},{256,0},{384,128},{1,257},{129,385},{257,1},{385... | collective-permute-start | bytes 196616 | tf_op jit(solution)/shard_map/ppermute | solution.py:24
  200.4 4.3 %collective-permute-start.20 = (bf16[2,64,128]{2,1,0:T(8,128)(2,1)S(1)}, bf16[2,64,128]{2,1,0:T(8,128)(2,1)S(1)}, u32[]{:S(2)}, u32[]{:S(2)}) collective-permute-start(bf16[2,64,128]{2,1,0:T(8,128)(2,1)S(1)} %select_bitcast_fusion.6), channel_id=1, source_target_pairs={{0,256},{128,384},{256,0},{384,128},{1,257},{129,385},{257,1},{385... | collective-permute-start | bytes 98312 | tf_op jit(solution)/shard_map/ppermute | solution.py:24
  204.7 1.9 collective-permute-start.14
  206.7 1.0 collective-permute-done.20
  207.7 3.6 %collective-permute-start.21 = (bf16[64,128]{1,0:T(8,128)(2,1)S(1)}, bf16[64,128]{1,0:T(8,128)(2,1)S(1)}, u32[]{:S(2)}, u32[]{:S(2)}) collective-permute-start(bf16[64,128]{1,0:T(8,128)(2,1)S(1)} %select_bitcast_fusion.7), channel_id=1, source_target_pairs={{0,64},{8,72},{16,80},{24,88},{32,96},{40,104},{48,112},{56,120},{... | collective-permute-start | bytes 49160 | tf_op jit(solution)/shard_map/ppermute | solution.py:24
  211.5 6.1 %collective-permute-start.15 = (bf16[64,128]{1,0:T(8,128)(2,1)S(1)}, bf16[64,128]{1,0:T(8,128)(2,1)S(1)}, u32[]{:S(2)}, u32[]{:S(2)}) collective-permute-start(bf16[64,128]{1,0:T(8,128)(2,1)S(1)} %select_bitcast_fusion.8), channel_id=1, source_target_pairs={{0,64},{8,72},{16,80},{24,88},{32,96},{40,104},{48,112},{56,120},{... | collective-permute-start | bytes 49160 | tf_op jit(solution)/shard_map/ppermute | solution.py:24
  217.6 0.6 convert_add_fusion.13
  218.2 2.8 %collective-permute-done.15 = bf16[64,128]{1,0:T(8,128)(2,1)S(1)} collective-permute-done((bf16[64,128]{1,0:T(8,128)(2,1)S(1)}, bf16[64,128]{1,0:T(8,128)(2,1)S(1)}, u32[]{:S(2)}, u32[]{:S(2)}) %collective-permute-start.15) | collective-permute-done | bytes 16416 | tf_op jit(solution)/shard_map/ppermute | solution.py:24
  221.0 0.6 convert_add_fusion.14
  (51 shorter events, 1.4 us)
Async XLA Ops:
  0.6 56.7 %copy-start = (bf16[1,192,4096]{2,1,0:T(8,128)(2,1)S(1)}, bf16[1,192,4096]{2,1,0:T(8,128)(2,1)}, u32[]{:S(2)}) copy-start(bf16[1,192,4096]{2,1,0:T(8,128)(2,1)} %param.6) | copy-start | bytes 4718596
  2.2 11.0 %collective-permute-start = (bf16[64,256]{1,0:T(8,128)(2,1)S(1)}, bf16[64,256]{1,0:T(8,128)(2,1)S(1)}, u32[]{:S(2)}, u32[]{:S(2)}) collective-permute-start(bf16[64,256]{1,0:T(8,128)(2,1)S(1)} %constant_dynamic-update-slice_fusion), channel_id=1, source_target_pairs={{0,64},{8,72},{16,80},{24,88},{32,96},{40,104},{48,112},{56,120},{... | collective-permute-start | bytes 98312 | tf_op jit(solution)/shard_map/ppermute | solution.py:24
  13.2 8.8 %collective-permute-start.1 = (bf16[2,64,256]{2,1,0:T(8,128)(2,1)S(1)}, bf16[2,64,256]{2,1,0:T(8,128)(2,1)S(1)}, u32[]{:S(2)}, u32[]{:S(2)}) collective-permute-start(bf16[2,64,256]{2,1,0:T(8,128)(2,1)S(1)} %maximum_select_fusion.6), channel_id=1, source_target_pairs={{0,32},{8,40},{16,48},{24,56},{32,0},{40,8},{48,16},{56,24},{64,96... | collective-permute-start | bytes 196616 | tf_op jit(solution)/shard_map/ppermute | solution.py:24
  22.0 8.4 %collective-permute-start.2 = (bf16[2,2,64,256]{3,2,0,1:T(8,128)(2,1)S(1)}, bf16[2,2,64,256]{3,2,0,1:T(8,128)(2,1)S(1)}, u32[]{:S(2)}, u32[]{:S(2)}) collective-permute-start(bf16[2,2,64,256]{3,2,0,1:T(8,128)(2,1)S(1)} %maximum_select_fusion.5), channel_id=1, source_target_pairs={{0,256},{128,384},{256,0},{384,128},{1,257},{129,385},{257,1},{385... | collective-permute-start | bytes 393224 | tf_op jit(solution)/shard_map/ppermute | solution.py:24
  30.4 8.3 %collective-permute-start.3 = (bf16[2,2,2,64,256]{4,3,1,2,0:T(8,128)(2,1)S(1)}, bf16[2,2,2,64,256]{4,3,1,2,0:T(8,128)(2,1)S(1)}, u32[]{:S(2)}, u32[]{:S(2)}) collective-permute-start(bf16[2,2,2,64,256]{4,3,1,2,0:T(8,128)(2,1)S(1)} %maximum_select_fusion.4), channel_id=1, source_target_pairs={{0,16},{8,24},{16,0},{24,8},{32,48},{40,56},{48,32},{56,40},{64,80... | collective-permute-start | bytes 786440 | tf_op jit(solution)/shard_map/ppermute | solution.py:24
  38.8 11.1 %collective-permute-start.4 = (bf16[2,2,2,2,64,256]{5,4,0,2,3,1:T(8,128)(2,1)S(1)}, bf16[2,2,2,2,64,256]{5,4,0,2,3,1:T(8,128)(2,1)S(1)}, u32[]{:S(2)}, u32[]{:S(2)}) collective-permute-start(bf16[2,2,2,2,64,256]{5,4,0,2,3,1:T(8,128)(2,1)S(1)} %maximum_select_fusion.3), channel_id=1, source_target_pairs={{0,128},{128,0},{256,384},{384,256},{1,129},{129,1},{257,385},{385... | collective-permute-start | bytes 1572872 | tf_op jit(solution)/shard_map/ppermute | solution.py:24
  42.3 10.6 %copy-start.1 = (s32[1,192]{1,0:T(1,128)S(1)}, s32[1,192]{1,0:T(1,128)}, u32[]{:S(2)}) copy-start(s32[1,192]{1,0:T(1,128)} %param.9) | copy-start | bytes 2308
  51.0 4.9 %collective-permute-start.5 = (bf16[2,2,2,2,2,64,256]{6,5,1,3,4,2,0:T(8,128)(2,1)}, bf16[2,2,2,2,2,64,256]{6,5,1,3,4,2,0:T(8,128)(2,1)}, u32[]{:S(2)}, u32[]{:S(2)}) collective-permute-start(bf16[2,2,2,2,2,64,256]{6,5,1,3,4,2,0:T(8,128)(2,1)} %maximum_select_fusion.1), channel_id=1, source_target_pairs={{0,8},{8,0},{16,24},{24,16},{32,40},{40,32},{48,56},{56,48},{64,72... | collective-permute-start | bytes 3145736 | tf_op jit(solution)/shard_map/ppermute | solution.py:24
  114.7 4.2 %collective-permute-start.6 = (bf16[2,2,2,192,256]{4,3,2,1,0:T(8,128)(2,1)S(1)}, bf16[2,2,2,192,256]{4,3,2,1,0:T(8,128)(2,1)S(1)}, u32[]{:S(2)}, u32[]{:S(2)}) collective-permute-start(bf16[2,2,2,192,256]{4,3,2,1,0:T(8,128)(2,1)S(1)} %bitcast.230), channel_id=1, source_target_pairs={{0,8},{8,0},{16,24},{24,16},{32,40},{40,32},{48,56},{56,48},{64,72... | collective-permute-start | bytes 2359304 | tf_op jit(solution)/shard_map/ppermute | solution.py:24
  119.1 13.3 %collective-permute-start.7 = (bf16[2,2,192,256]{3,2,1,0:T(8,128)(2,1)S(1)}, bf16[2,2,192,256]{3,2,1,0:T(8,128)(2,1)S(1)}, u32[]{:S(2)}, u32[]{:S(2)}) collective-permute-start(bf16[2,2,192,256]{3,2,1,0:T(8,128)(2,1)S(1)} %slice_bitcast_fusion), channel_id=1, source_target_pairs={{0,16},{8,24},{16,0},{24,8},{32,48},{40,56},{48,32},{56,40},{64,80... | collective-permute-start | bytes 1179656 | tf_op jit(solution)/shard_map/ppermute | solution.py:24
  132.5 13.4 %collective-permute-start.8 = (bf16[2,192,256]{2,1,0:T(8,128)(2,1)S(1)}, bf16[2,192,256]{2,1,0:T(8,128)(2,1)S(1)}, u32[]{:S(2)}, u32[]{:S(2)}) collective-permute-start(bf16[2,192,256]{2,1,0:T(8,128)(2,1)S(1)} %slice_bitcast_fusion.2), channel_id=1, source_target_pairs={{0,32},{8,40},{16,48},{24,56},{32,0},{40,8},{48,16},{56,24},{64,96... | collective-permute-start | bytes 589832 | tf_op jit(solution)/shard_map/ppermute | solution.py:24
  146.0 15.2 %collective-permute-start.9 = (bf16[192,256]{1,0:T(8,128)(2,1)S(1)}, bf16[192,256]{1,0:T(8,128)(2,1)S(1)}, u32[]{:S(2)}, u32[]{:S(2)}) collective-permute-start(bf16[192,256]{1,0:T(8,128)(2,1)S(1)} %slice_bitcast_fusion.4), channel_id=1, source_target_pairs={{0,64},{8,72},{16,80},{24,88},{32,96},{40,104},{48,112},{56,120},{... | collective-permute-start | bytes 294920 | tf_op jit(solution)/shard_map/ppermute | solution.py:24
  165.2 9.4 %collective-permute-start.16 = (bf16[2,2,2,2,2,64,128]{6,5,2,0,3,1,4:T(8,128)(2,1)}, bf16[2,2,2,2,2,64,128]{6,5,2,0,3,1,4:T(8,128)(2,1)S(1)}, u32[]{:S(2)}, u32[]{:S(2)}) collective-permute-start(bf16[2,2,2,2,2,64,128]{6,5,2,0,3,1,4:T(8,128)(2,1)} %select_bitcast_fusion), channel_id=1, source_target_pairs={{0,8},{8,0},{16,24},{24,16},{32,40},{40,32},{48,56},{56,48},{64,72... | collective-permute-start | bytes 1572872 | tf_op jit(solution)/shard_map/ppermute | solution.py:24
  172.2 4.6 %collective-permute-start.10 = (bf16[2,2,2,2,2,64,128]{6,5,4,3,2,1,0:T(8,128)(2,1)S(1)}, bf16[2,2,2,2,2,64,128]{6,5,4,3,2,1,0:T(8,128)(2,1)S(1)}, u32[]{:S(2)}, u32[]{:S(2)}) collective-permute-start(bf16[2,2,2,2,2,64,128]{6,5,4,3,2,1,0:T(8,128)(2,1)S(1)} %get-tuple-element.13), channel_id=1, source_target_pairs={{0,8},{8,0},{16,24},{24,16},{32,40},{40,32},{48,56},{56,48},{64,72... | collective-permute-start | bytes 1572872 | tf_op jit(solution)/shard_map/ppermute | solution.py:24
  174.9 10.2 %collective-permute-start.17 = (bf16[2,2,2,2,64,128]{5,4,2,0,3,1:T(8,128)(2,1)S(1)}, bf16[2,2,2,2,64,128]{5,4,2,0,3,1:T(8,128)(2,1)S(1)}, u32[]{:S(2)}, u32[]{:S(2)}) collective-permute-start(bf16[2,2,2,2,64,128]{5,4,2,0,3,1:T(8,128)(2,1)S(1)} %select_bitcast_fusion.2), channel_id=1, source_target_pairs={{0,16},{8,24},{16,0},{24,8},{32,48},{40,56},{48,32},{56,40},{64,80... | collective-permute-start | bytes 786440 | tf_op jit(solution)/shard_map/ppermute | solution.py:24
  177.1 11.4 %collective-permute-start.11 = (bf16[2,2,2,2,64,128]{5,4,3,2,1,0:T(8,128)(2,1)S(1)}, bf16[2,2,2,2,64,128]{5,4,3,2,1,0:T(8,128)(2,1)S(1)}, u32[]{:S(2)}, u32[]{:S(2)}) collective-permute-start(bf16[2,2,2,2,64,128]{5,4,3,2,1,0:T(8,128)(2,1)S(1)} %fusion.21), channel_id=1, source_target_pairs={{0,128},{128,0},{256,384},{384,256},{1,129},{129,1},{257,385},{385... | collective-permute-start | bytes 786440 | tf_op jit(solution)/shard_map/ppermute | solution.py:24
  185.2 6.9 %collective-permute-start.18 = (bf16[2,2,2,64,128]{4,3,1,0,2:T(8,128)(2,1)S(1)}, bf16[2,2,2,64,128]{4,3,1,0,2:T(8,128)(2,1)S(1)}, u32[]{:S(2)}, u32[]{:S(2)}) collective-permute-start(bf16[2,2,2,64,128]{4,3,1,0,2:T(8,128)(2,1)S(1)} %select_bitcast_fusion.3), channel_id=1, source_target_pairs={{0,128},{128,0},{256,384},{384,256},{1,129},{129,1},{257,385},{385... | collective-permute-start | bytes 393224 | tf_op jit(solution)/shard_map/ppermute | solution.py:24
  188.7 6.9 %collective-permute-start.12 = (bf16[2,2,2,64,128]{4,3,2,1,0:T(8,128)(2,1)S(1)}, bf16[2,2,2,64,128]{4,3,2,1,0:T(8,128)(2,1)S(1)}, u32[]{:S(2)}, u32[]{:S(2)}) collective-permute-start(bf16[2,2,2,64,128]{4,3,2,1,0:T(8,128)(2,1)S(1)} %fusion.27), channel_id=1, source_target_pairs={{0,16},{8,24},{16,0},{24,8},{32,48},{40,56},{48,32},{56,40},{64,80... | collective-permute-start | bytes 393224 | tf_op jit(solution)/shard_map/ppermute | solution.py:24
  192.1 8.2 %collective-permute-start.19 = (bf16[2,2,64,128]{3,2,1,0:T(8,128)(2,1)S(1)}, bf16[2,2,64,128]{3,2,1,0:T(8,128)(2,1)S(1)}, u32[]{:S(2)}, u32[]{:S(2)}) collective-permute-start(bf16[2,2,64,128]{3,2,1,0:T(8,128)(2,1)S(1)} %select_bitcast_fusion.4), channel_id=1, source_target_pairs={{0,32},{8,40},{16,48},{24,56},{32,0},{40,8},{48,16},{56,24},{64,96... | collective-permute-start | bytes 196616 | tf_op jit(solution)/shard_map/ppermute | solution.py:24
  195.6 9.0 %collective-permute-start.13 = (bf16[2,2,64,128]{3,2,1,0:T(8,128)(2,1)S(1)}, bf16[2,2,64,128]{3,2,1,0:T(8,128)(2,1)S(1)}, u32[]{:S(2)}, u32[]{:S(2)}) collective-permute-start(bf16[2,2,64,128]{3,2,1,0:T(8,128)(2,1)S(1)} %select_bitcast_fusion.5), channel_id=1, source_target_pairs={{0,256},{128,384},{256,0},{384,128},{1,257},{129,385},{257,1},{385... | collective-permute-start | bytes 196616 | tf_op jit(solution)/shard_map/ppermute | solution.py:24
  200.4 7.3 %collective-permute-start.20 = (bf16[2,64,128]{2,1,0:T(8,128)(2,1)S(1)}, bf16[2,64,128]{2,1,0:T(8,128)(2,1)S(1)}, u32[]{:S(2)}, u32[]{:S(2)}) collective-permute-start(bf16[2,64,128]{2,1,0:T(8,128)(2,1)S(1)} %select_bitcast_fusion.6), channel_id=1, source_target_pairs={{0,256},{128,384},{256,0},{384,128},{1,257},{129,385},{257,1},{385... | collective-permute-start | bytes 98312 | tf_op jit(solution)/shard_map/ppermute | solution.py:24
  204.7 6.7 %collective-permute-start.14 = (bf16[2,64,128]{2,1,0:T(8,128)(2,1)S(1)}, bf16[2,64,128]{2,1,0:T(8,128)(2,1)S(1)}, u32[]{:S(2)}, u32[]{:S(2)}) collective-permute-start(bf16[2,64,128]{2,1,0:T(8,128)(2,1)S(1)} %fusion.36), channel_id=1, source_target_pairs={{0,32},{8,40},{16,48},{24,56},{32,0},{40,8},{48,16},{56,24},{64,96... | collective-permute-start | bytes 98312 | tf_op jit(solution)/shard_map/ppermute | solution.py:24
  207.7 9.8 %collective-permute-start.21 = (bf16[64,128]{1,0:T(8,128)(2,1)S(1)}, bf16[64,128]{1,0:T(8,128)(2,1)S(1)}, u32[]{:S(2)}, u32[]{:S(2)}) collective-permute-start(bf16[64,128]{1,0:T(8,128)(2,1)S(1)} %select_bitcast_fusion.7), channel_id=1, source_target_pairs={{0,64},{8,72},{16,80},{24,88},{32,96},{40,104},{48,112},{56,120},{... | collective-permute-start | bytes 49160 | tf_op jit(solution)/shard_map/ppermute | solution.py:24
  211.5 9.5 %collective-permute-start.15 = (bf16[64,128]{1,0:T(8,128)(2,1)S(1)}, bf16[64,128]{1,0:T(8,128)(2,1)S(1)}, u32[]{:S(2)}, u32[]{:S(2)}) collective-permute-start(bf16[64,128]{1,0:T(8,128)(2,1)S(1)} %select_bitcast_fusion.8), channel_id=1, source_target_pairs={{0,64},{8,72},{16,80},{24,88},{32,96},{40,104},{48,112},{56,120},{... | collective-permute-start | bytes 49160 | tf_op jit(solution)/shard_map/ppermute | solution.py:24

commit v9 on v8

--- a/solution.py
+++ b/solution.py
@@ -80,13 +80,12 @@
     return cur
 
 
-def _gather_kernel(bits, x_ref, o_ref, held, send_sems, recv_sems, local_sem):
-    me = lax.axis_index("context")
-    partners = [lax.bitwise_xor(me, 1 << b) for b in bits]
+def _gather_kernel(steps, canonical, x_ref, o_ref, held, send_sems, recv_sems, local_sem):
     mesh = pl.DeviceIdType.MESH
+    partners = [{axis: lax.bitwise_xor(lax.axis_index(axis), 1 << bit)} for axis, _, bit in steps]
     barrier = pltpu.get_barrier_semaphore()
     for p in partners:
-        pl.semaphore_signal(barrier, inc=1, device_id={"context": p}, device_id_type=mesh)
+        pl.semaphore_signal(barrier, inc=1, device_id=p, device_id_type=mesh)
     pl.semaphore_wait(barrier, len(partners))
     local = pltpu.make_async_copy(x_ref, held.at[0:1], local_sem)
     local.start()
@@ -99,7 +98,7 @@
             dst_ref=held.at[base + lo:base + hi],
             send_sem=send_sems.at[len(sends)],
             recv_sem=recv_sems.at[j],
-            device_id={"context": partners[j]},
+            device_id=partners[j],
             device_id_type=mesh,
         )
         copy.start()
@@ -114,7 +113,7 @@
             dst_ref=held.at[lo:hi],
             send_sem=send_sems.at[0],
             recv_sem=recv_sems.at[i],
-            device_id={"context": partners[i]},
+            device_id=partners[i],
             device_id_type=mesh,
         )
         arrived.wait_recv()
@@ -123,26 +122,43 @@
     for copy in sends:
         copy.wait_send()
     local.wait()
-    out = pltpu.make_async_copy(held, o_ref, local_sem)
-    out.start()
-    out.wait()
-
-
-def context_gather(x, bits):
-    n = 1 << len(bits)
+    if canonical is None:
+        out = pltpu.make_async_copy(held, o_ref, local_sem)
+        out.start()
+        out.wait()
+        return
+    weights = []
+    me = 0
+    for axis, size, bit in steps:
+        idx = lax.axis_index(axis)
+        mine = (idx // (1 << bit)) % 2
+        weights.append(canonical[(axis, bit)] * (1 - 2 * mine))
+    for axis, stride in canonical["origin"]:
+        me = me + lax.axis_index(axis) * stride
+    for r in range(1 << len(steps)):
+        at = me
+        for k in range(len(steps)):
+            if (r >> k) & 1:
+                at = at + weights[k]
+        pltpu.make_async_copy(held.at[r:r + 1], o_ref.at[pl.ds(at, 1)], local_sem).start()
+    pltpu.make_async_copy(held, o_ref, local_sem).wait()
+
+
+def pair_gather(x, steps, collective_id, canonical=None):
+    n = 1 << len(steps)
     shape = (n,) + x.shape[1:]
     return pl.pallas_call(
-        functools.partial(_gather_kernel, bits),
+        functools.partial(_gather_kernel, steps, canonical),
         out_shape=jax.ShapeDtypeStruct(shape, x.dtype),
         in_specs=[pl.BlockSpec(memory_space=pltpu.VMEM)],
         out_specs=pl.BlockSpec(memory_space=pltpu.VMEM),
         scratch_shapes=[
             pltpu.VMEM(shape, x.dtype),
-            pltpu.SemaphoreType.DMA((len(bits) * (len(bits) + 1) // 2,)),
-            pltpu.SemaphoreType.DMA((len(bits),)),
+            pltpu.SemaphoreType.DMA((len(steps) * (len(steps) + 1) // 2,)),
+            pltpu.SemaphoreType.DMA((len(steps),)),
             pltpu.SemaphoreType.DMA,
         ],
-        compiler_params=pltpu.CompilerParams(collective_id=0, has_side_effects=True),
+        compiler_params=pltpu.CompilerParams(collective_id=collective_id, has_side_effects=True),
     )(x)
 
 
@@ -234,12 +250,15 @@
 
     far_first = ctx_far[:1] + interleave(ctx_far[1:-1], dp_far) + ctx_far[-1:]
     proj = jnp.concatenate([key_proj, value_proj], axis=1)
-    proj_all = gather_blocks(proj, far_first, both_canon)
+    canonical = {("dp", b): n_ctx << b for b in range(_bits(n_dp))}
+    canonical.update({("context", b): 1 << b for b in range(_bits(n_ctx))})
+    canonical["origin"] = (("dp", n_ctx), ("context", 1))
+    proj_all = pair_gather(proj[None], far_first, 1, canonical).reshape(-1, proj.shape[1])
     kv = jnp.dot(local_rows, proj_all, preferred_element_type=jnp.float32).astype(jnp.bfloat16)
     marks = segment[0].astype(jnp.bfloat16)
     marks_row = jnp.pad(marks, (0, 2 * HEAD_DIM - tok_rows))[None, :]
     kvm = jnp.concatenate([kv, marks_row], axis=0)[None]
-    kvm_all = context_gather(kvm, [bit for _, _, bit in ctx_far])
+    kvm_all = pair_gather(kvm, ctx_far, 0)
     keys = kvm_all[:, :tok_rows, :HEAD_DIM].reshape(-1, HEAD_DIM)
     values = kvm_all[:, :tok_rows, HEAD_DIM:].reshape(-1, HEAD_DIM)
     marks_all = kvm_all[:, tok_rows, :tok_rows].reshape(-1)

time: 223 us -> 208 us (0.933)
  Pallas kernels: 50.4 us -> 84 us
  starting transfers between devices: 78.6 us -> 53.8 us
  waiting for transfers between devices: 67.2 us -> 42.6 us
  local copies, waits for them, and re-layouts: 13.3 us -> 10.5 us
  other arithmetic: 8.35 us -> 11.1 us
    pallas_call x1 -> x2, Pallas kernels: 35 us -> 68.7 us  [pair_gather(): pl.pallas_call(functools.partial(_gather_kernel, steps, canonical), out_s...]
    ppermute x22 -> x16, starting transfers between devices: 78.6 us -> 53.8 us  [_exchange(): return lax.ppermute(x, axis, perm)]
    ppermute x22 -> x16, waiting for transfers between devices: 67.2 us -> 42.6 us  [_exchange(): return lax.ppermute(x, axis, perm)]
  transfers between devices with their start and end apart: 22 -> 16, of which waited for: 16 -> 8; matrix products, arithmetic and copies ran while one was open for 4% -> 5% of each run, Pallas kernels for 0% -> 0%
where the time goes in v9:
time: 208 us; the launch traced here: 207 us
  Pallas kernels  84 us (40%)
  starting transfers between devices  53.8 us (26%)
  waiting for transfers between devices  42.6 us (20%)
  other arithmetic  11.1 us (5%)
  local copies, waits for them, and re-layouts  10.5 us (5%)
  matrix products  4.08 us (2%)
    pallas_call x2, Pallas kernels, pair_gather(): pl.pallas_call(functools.partial(_gather_kernel, steps, canonical), out_s...  68.7 us
    ppermute x16, starting transfers between devices, _exchange(): return lax.ppermute(x, axis, perm)  53.8 us
    ppermute x16, waiting for transfers between devices, _exchange(): return lax.ppermute(x, axis, perm)  42.6 us
    pallas_call x1, Pallas kernels, attention_block(): pl.pallas_call(_attention_kernel, out_shape=(jax.ShapeDtypeStruct((rows,...  15.3 us
  transfers between devices with their start and end apart: 16, of which 8 were waited for; matrix products, arithmetic and copies ran while one was open for 5% of the time, Pallas kernels for 0%

profile of v9, /device:TPU:24, one launch (start us, length us, event | category | flops | bytes accessed | tf_op | source)
XLA Modules:
  0.0 207.2 jit_solution(15337052970421087111)
XLA Ops:
  0.6 0.0 copy-start
  0.6 0.0 copy-start.2
  0.7 1.5 maximum_bitcast_fusion.1.x_ref
  2.1 38.8 %shard_map.85 = bf16[64,64,256]{2,1,0:T(8,128)(2,1)} custom-call(bf16[1,64,256]{2,1,0:T(8,128)(2,1)} %maximum_bitcast_fusion.1.x_ref), custom_call_target="tpu_custom_call" | custom-call | tf_op jit(solution)/shard_map/pallas_call | solution.py:150
  41.0 0.0 copy-done.2
  41.0 0.0 copy-done
  41.1 2.2 %fusion.10 = bf16[192,256]{1,0:T(8,128)(2,1)S(1)} fusion(bf16[4096,256]{1,0:T(8,128)(2,1)} %bitcast.171, bf16[1,192,4096]{2,1,0:T(8,128)(2,1)S(1)} %copy-done), kind=kOutput, calls=%fused_computation.11 | convolution fusion | flops 402702336 | bytes 3768320 | tf_op jit(solution)/shard_map/dot_general | solution.py:257
  43.2 0.7 maximum_bitcast_fusion.x_ref
  43.9 29.8 %shard_map.86 = bf16[16,193,256]{2,1,0:T(8,128)(2,1)} custom-call(bf16[1,193,256]{2,1,0:T(8,128)(2,1)} %maximum_bitcast_fusion.x_ref), custom_call_target="tpu_custom_call" | custom-call | tf_op jit(solution)/shard_map/pallas_call | solution.py:150
  73.7 2.7 %fusion.36 = (bf16[16,192,128]{2,1,0:T(8,128)(2,1)}, bf16[16,192,128]{2,1,0:T(8,128)(2,1)}) fusion(bf16[16,193,256]{2,1,0:T(8,128)(2,1)} %shard_map.86), kind=kLoop, calls=%fused_computation.77 | loop fusion | bytes 3145728 | tf_op jit(solution)/shard_map/slice | solution.py:263
  76.4 0.9 convert_reduce_fusion
  77.3 0.7 reshape.141.mk_ref
  78.0 0.8 copy.21.mq_ref
  78.7 15.3 %shard_map.87 = (bf16[192,512]{1,0:T(8,128)(2,1)}, bf16[3072,256]{1,0:T(8,128)(2,1)}) custom-call(bf16[192,512]{1,0:T(8,128)(2,1)} %bitcast.175, bf16[192,512]{1,0:T(8,128)(2,1)} %bitcast.176, bf16[3072,128]{1,0:T(8,128)(2,1)} %bitcast.173, bf16[3072,128]{1,0:T(8,128)(2,1)} %bitcast.172, f32[192,1]{1,0:T(8,128)} %copy.21.mq_ref, f32[1,3072]{1,0:T(1,128)} %reshape.141.mk_ref), custom_call_target="tpu_custom_call" | custom-call | flops 3623878656 | bytes 3932160 | tf_op jit(solution)/shard_map/pallas_call | solution.py:204
  94.1 1.5 fusion.37
  95.5 2.3 %collective-permute-start = (bf16[2,2,2,192,256]{4,3,2,1,0:T(8,128)(2,1)S(1)}, bf16[2,2,2,192,256]{4,3,2,1,0:T(8,128)(2,1)S(1)}, u32[]{:S(2)}, u32[]{:S(2)}) collective-permute-start(bf16[2,2,2,192,256]{4,3,2,1,0:T(8,128)(2,1)S(1)} %bitcast.174), channel_id=1, source_target_pairs={{0,8},{8,0},{16,24},{24,16},{32,40},{40,32},{48,56},{56,48},{64,72... | collective-permute-start | bytes 2359304 | tf_op jit(solution)/shard_map/ppermute | solution.py:24
  97.8 1.9 collective-permute-done
  99.7 0.2 fusion.2
  100.0 4.5 %collective-permute-start.1 = (bf16[2,2,192,256]{3,2,1,0:T(8,128)(2,1)S(1)}, bf16[2,2,192,256]{3,2,1,0:T(8,128)(2,1)S(1)}, u32[]{:S(2)}, u32[]{:S(2)}) collective-permute-start(bf16[2,2,192,256]{3,2,1,0:T(8,128)(2,1)S(1)} %slice_bitcast_fusion), channel_id=1, source_target_pairs={{0,16},{8,24},{16,0},{24,8},{32,48},{40,56},{48,32},{56,40},{64,80... | collective-permute-start | bytes 1179656 | tf_op jit(solution)/shard_map/ppermute | solution.py:24
  104.5 9.6 %collective-permute-done.1 = bf16[2,2,192,256]{3,2,1,0:T(8,128)(2,1)S(1)} collective-permute-done((bf16[2,2,192,256]{3,2,1,0:T(8,128)(2,1)S(1)}, bf16[2,2,192,256]{3,2,1,0:T(8,128)(2,1)S(1)}, u32[]{:S(2)}, u32[]{:S(2)}) %collective-permute-start.1) | collective-permute-done | bytes 393248 | tf_op jit(solution)/shard_map/ppermute | solution.py:24
  114.2 0.1 fusion.15
  114.3 2.4 %collective-permute-start.2 = (bf16[2,192,256]{2,1,0:T(8,128)(2,1)S(1)}, bf16[2,192,256]{2,1,0:T(8,128)(2,1)S(1)}, u32[]{:S(2)}, u32[]{:S(2)}) collective-permute-start(bf16[2,192,256]{2,1,0:T(8,128)(2,1)S(1)} %slice_bitcast_fusion.2), channel_id=1, source_target_pairs={{0,32},{8,40},{16,48},{24,56},{32,0},{40,8},{48,16},{56,24},{64,96... | collective-permute-start | bytes 589832 | tf_op jit(solution)/shard_map/ppermute | solution.py:24
  116.7 11.2 %collective-permute-done.2 = bf16[2,192,256]{2,1,0:T(8,128)(2,1)S(1)} collective-permute-done((bf16[2,192,256]{2,1,0:T(8,128)(2,1)S(1)}, bf16[2,192,256]{2,1,0:T(8,128)(2,1)S(1)}, u32[]{:S(2)}, u32[]{:S(2)}) %collective-permute-start.2) | collective-permute-done | bytes 196640 | tf_op jit(solution)/shard_map/ppermute | solution.py:24
  128.0 4.8 %collective-permute-start.3 = (bf16[192,256]{1,0:T(8,128)(2,1)S(1)}, bf16[192,256]{1,0:T(8,128)(2,1)S(1)}, u32[]{:S(2)}, u32[]{:S(2)}) collective-permute-start(bf16[192,256]{1,0:T(8,128)(2,1)S(1)} %slice_bitcast_fusion.4), channel_id=1, source_target_pairs={{0,64},{8,72},{16,80},{24,88},{32,96},{40,104},{48,112},{56,120},{... | collective-permute-start | bytes 294920 | tf_op jit(solution)/shard_map/ppermute | solution.py:24
  132.8 9.9 %collective-permute-done.3 = bf16[192,256]{1,0:T(8,128)(2,1)S(1)} collective-permute-done((bf16[192,256]{1,0:T(8,128)(2,1)S(1)}, bf16[192,256]{1,0:T(8,128)(2,1)S(1)}, u32[]{:S(2)}, u32[]{:S(2)}) %collective-permute-start.3) | collective-permute-done | bytes 98336 | tf_op jit(solution)/shard_map/ppermute | solution.py:24
  142.8 0.5 fusion.1
  143.3 1.3 copy.40
  144.6 1.3 fusion.38
  145.9 0.9 select_bitcast_fusion
  146.7 1.9 collective-permute-start.10
  148.7 1.5 fusion
  150.1 2.3 %copy.22 = bf16[4096,128]{1,0:T(8,128)(2,1)} copy(bf16[4096,128]{0,1:T(8,128)(2,1)} %fusion) | data formatting | bytes 2097152 | tf_op jit(solution)/shard_map/convert_element_type | solution.py:275
  152.4 2.3 %select_bitcast_fusion.1 = (bf16[2,2,2,2,2,64,128]{6,5,4,3,2,1,0:T(8,128)(2,1)}, bf16[2,2,2,2,2,1,64,128]{7,6,5,4,3,2,1,0:T(8,128)(2,1)S(1)}, bf16[2,2,2,2,2,1,64,128]{7,6,5,4,3,2,1,0:T(8,128)(2,1)}) fusion(pred[]{:T(512)S(6)} %eq.29, bf16[2,2,2,2,2,2,64,128]{7,6,5,4,3,2,1,0:T(8,128)(2,1)} %bitcast.168), kind=kLoop, calls=%fused_computation.26 | loop fusion | flops 262144 | bytes 2621441 | tf_op jit(solution)/shard_map/jit(_where)/select_n | solution.py:56
  154.7 2.4 %collective-permute-start.4 = (bf16[2,2,2,2,2,64,128]{6,5,4,3,2,1,0:T(8,128)(2,1)}, bf16[2,2,2,2,2,64,128]{6,5,4,3,2,1,0:T(8,128)(2,1)}, u32[]{:S(2)}, u32[]{:S(2)}) collective-permute-start(bf16[2,2,2,2,2,64,128]{6,5,4,3,2,1,0:T(8,128)(2,1)} %get-tuple-element.13), channel_id=1, source_target_pairs={{0,8},{8,0},{16,24},{24,16},{32,40},{40,32},{48,56},{56,48},{64,72... | collective-permute-start | bytes 1572872 | tf_op jit(solution)/shard_map/ppermute | solution.py:24
  157.2 0.0 collective-permute-done.10
  157.2 1.4 fusion.13
  158.6 1.9 collective-permute-start.11
  160.5 0.0 collective-permute-done.4
  160.5 1.3 fusion.14
  161.9 3.3 %collective-permute-start.5 = (bf16[2,2,2,2,64,128]{5,4,3,2,1,0:T(8,128)(2,1)S(1)}, bf16[2,2,2,2,64,128]{5,4,3,2,1,0:T(8,128)(2,1)S(1)}, u32[]{:S(2)}, u32[]{:S(2)}) collective-permute-start(bf16[2,2,2,2,64,128]{5,4,3,2,1,0:T(8,128)(2,1)S(1)} %fusion.21), channel_id=1, source_target_pairs={{0,128},{128,0},{256,384},{384,256},{1,129},{129,1},{257,385},{385... | collective-permute-start | bytes 786440 | tf_op jit(solution)/shard_map/ppermute | solution.py:24
  165.2 3.5 %collective-permute-done.11 = bf16[2,2,2,2,64,128]{5,4,2,0,3,1:T(8,128)(2,1)S(1)} collective-permute-done((bf16[2,2,2,2,64,128]{5,4,2,0,3,1:T(8,128)(2,1)S(1)}, bf16[2,2,2,2,64,128]{5,4,2,0,3,1:T(8,128)(2,1)S(1)}, u32[]{:S(2)}, u32[]{:S(2)}) %collective-permute-start.11) | collective-permute-done | bytes 262176 | tf_op jit(solution)/shard_map/ppermute | solution.py:24
  168.7 0.1 fusion.18
  168.8 3.3 %collective-permute-start.12 = (bf16[2,2,2,64,128]{4,3,1,0,2:T(8,128)(2,1)S(1)}, bf16[2,2,2,64,128]{4,3,1,0,2:T(8,128)(2,1)S(1)}, u32[]{:S(2)}, u32[]{:S(2)}) collective-permute-start(bf16[2,2,2,64,128]{4,3,1,0,2:T(8,128)(2,1)S(1)} %select_bitcast_fusion.3), channel_id=1, source_target_pairs={{0,128},{128,0},{256,384},{384,256},{1,129},{129,1},{257,385},{385... | collective-permute-start | bytes 393224 | tf_op jit(solution)/shard_map/ppermute | solution.py:24
  172.1 0.0 collective-permute-done.5
  172.1 0.1 fusion.19
  172.3 4.0 %collective-permute-start.6 = (bf16[2,2,2,64,128]{4,3,2,1,0:T(8,128)(2,1)S(1)}, bf16[2,2,2,64,128]{4,3,2,1,0:T(8,128)(2,1)S(1)}, u32[]{:S(2)}, u32[]{:S(2)}) collective-permute-start(bf16[2,2,2,64,128]{4,3,2,1,0:T(8,128)(2,1)S(1)} %fusion.26), channel_id=1, source_target_pairs={{0,16},{8,24},{16,0},{24,8},{32,48},{40,56},{48,32},{56,40},{64,80... | collective-permute-start | bytes 393224 | tf_op jit(solution)/shard_map/ppermute | solution.py:24
  176.3 0.0 collective-permute-done.12
  176.3 0.1 fusion.23
  176.4 1.9 collective-permute-start.13
  178.3 0.9 collective-permute-done.6
  179.2 0.1 fusion.24
  179.3 4.0 %collective-permute-start.7 = (bf16[2,2,64,128]{3,2,1,0:T(8,128)(2,1)S(1)}, bf16[2,2,64,128]{3,2,1,0:T(8,128)(2,1)S(1)}, u32[]{:S(2)}, u32[]{:S(2)}) collective-permute-start(bf16[2,2,64,128]{3,2,1,0:T(8,128)(2,1)S(1)} %select_bitcast_fusion.5), channel_id=1, source_target_pairs={{0,256},{128,384},{256,0},{384,128},{1,257},{129,385},{257,1},{385... | collective-permute-start | bytes 196616 | tf_op jit(solution)/shard_map/ppermute | solution.py:24
  183.3 0.5 collective-permute-done.13
  183.8 4.0 %collective-permute-start.14 = (bf16[2,64,128]{2,1,0:T(8,128)(2,1)S(1)}, bf16[2,64,128]{2,1,0:T(8,128)(2,1)S(1)}, u32[]{:S(2)}, u32[]{:S(2)}) collective-permute-start(bf16[2,64,128]{2,1,0:T(8,128)(2,1)S(1)} %select_bitcast_fusion.6), channel_id=1, source_target_pairs={{0,256},{128,384},{256,0},{384,128},{1,257},{129,385},{257,1},{385... | collective-permute-start | bytes 98312 | tf_op jit(solution)/shard_map/ppermute | solution.py:24
  187.8 0.0 collective-permute-done.7
  187.9 3.3 %collective-permute-start.8 = (bf16[2,64,128]{2,1,0:T(8,128)(2,1)S(1)}, bf16[2,64,128]{2,1,0:T(8,128)(2,1)S(1)}, u32[]{:S(2)}, u32[]{:S(2)}) collective-permute-start(bf16[2,64,128]{2,1,0:T(8,128)(2,1)S(1)} %fusion.34), channel_id=1, source_target_pairs={{0,32},{8,40},{16,48},{24,56},{32,0},{40,8},{48,16},{56,24},{64,96... | collective-permute-start | bytes 98312 | tf_op jit(solution)/shard_map/ppermute | solution.py:24
  191.2 0.0 collective-permute-done.14
  191.3 5.7 %collective-permute-start.15 = (bf16[64,128]{1,0:T(8,128)(2,1)S(1)}, bf16[64,128]{1,0:T(8,128)(2,1)S(1)}, u32[]{:S(2)}, u32[]{:S(2)}) collective-permute-start(bf16[64,128]{1,0:T(8,128)(2,1)S(1)} %select_bitcast_fusion.7), channel_id=1, source_target_pairs={{0,64},{8,72},{16,80},{24,88},{32,96},{40,104},{48,112},{56,120},{... | collective-permute-start | bytes 49160 | tf_op jit(solution)/shard_map/ppermute | solution.py:24
  196.9 0.0 collective-permute-done.8
  197.0 4.1 %collective-permute-start.9 = (bf16[64,128]{1,0:T(8,128)(2,1)S(1)}, bf16[64,128]{1,0:T(8,128)(2,1)S(1)}, u32[]{:S(2)}, u32[]{:S(2)}) collective-permute-start(bf16[64,128]{1,0:T(8,128)(2,1)S(1)} %select_bitcast_fusion.8), channel_id=1, source_target_pairs={{0,64},{8,72},{16,80},{24,88},{32,96},{40,104},{48,112},{56,120},{... | collective-permute-start | bytes 49160 | tf_op jit(solution)/shard_map/ppermute | solution.py:24
  201.1 0.0 collective-permute-done.15
  201.1 0.6 convert_add_fusion.13
  201.7 4.9 %collective-permute-done.9 = bf16[64,128]{1,0:T(8,128)(2,1)S(1)} collective-permute-done((bf16[64,128]{1,0:T(8,128)(2,1)S(1)}, bf16[64,128]{1,0:T(8,128)(2,1)S(1)}, u32[]{:S(2)}, u32[]{:S(2)}) %collective-permute-start.9) | collective-permute-done | bytes 16416 | tf_op jit(solution)/shard_map/ppermute | solution.py:24
  206.6 0.6 convert_add_fusion.14
  (25 shorter events, 0.4 us)
Async XLA Ops:
  0.6 40.4 %copy-start = (bf16[1,192,4096]{2,1,0:T(8,128)(2,1)S(1)}, bf16[1,192,4096]{2,1,0:T(8,128)(2,1)}, u32[]{:S(2)}) copy-start(bf16[1,192,4096]{2,1,0:T(8,128)(2,1)} %param.6) | copy-start | bytes 4718596
  0.6 40.3 %copy-start.2 = (s32[1,192]{1,0:T(1,128)S(1)}, s32[1,192]{1,0:T(1,128)}, u32[]{:S(2)}) copy-start(s32[1,192]{1,0:T(1,128)} %param.9) | copy-start | bytes 2308
  95.5 4.2 %collective-permute-start = (bf16[2,2,2,192,256]{4,3,2,1,0:T(8,128)(2,1)S(1)}, bf16[2,2,2,192,256]{4,3,2,1,0:T(8,128)(2,1)S(1)}, u32[]{:S(2)}, u32[]{:S(2)}) collective-permute-start(bf16[2,2,2,192,256]{4,3,2,1,0:T(8,128)(2,1)S(1)} %bitcast.174), channel_id=1, source_target_pairs={{0,8},{8,0},{16,24},{24,16},{32,40},{40,32},{48,56},{56,48},{64,72... | collective-permute-start | bytes 2359304 | tf_op jit(solution)/shard_map/ppermute | solution.py:24
  100.0 14.2 %collective-permute-start.1 = (bf16[2,2,192,256]{3,2,1,0:T(8,128)(2,1)S(1)}, bf16[2,2,192,256]{3,2,1,0:T(8,128)(2,1)S(1)}, u32[]{:S(2)}, u32[]{:S(2)}) collective-permute-start(bf16[2,2,192,256]{3,2,1,0:T(8,128)(2,1)S(1)} %slice_bitcast_fusion), channel_id=1, source_target_pairs={{0,16},{8,24},{16,0},{24,8},{32,48},{40,56},{48,32},{56,40},{64,80... | collective-permute-start | bytes 1179656 | tf_op jit(solution)/shard_map/ppermute | solution.py:24
  114.3 13.6 %collective-permute-start.2 = (bf16[2,192,256]{2,1,0:T(8,128)(2,1)S(1)}, bf16[2,192,256]{2,1,0:T(8,128)(2,1)S(1)}, u32[]{:S(2)}, u32[]{:S(2)}) collective-permute-start(bf16[2,192,256]{2,1,0:T(8,128)(2,1)S(1)} %slice_bitcast_fusion.2), channel_id=1, source_target_pairs={{0,32},{8,40},{16,48},{24,56},{32,0},{40,8},{48,16},{56,24},{64,96... | collective-permute-start | bytes 589832 | tf_op jit(solution)/shard_map/ppermute | solution.py:24
  128.0 14.8 %collective-permute-start.3 = (bf16[192,256]{1,0:T(8,128)(2,1)S(1)}, bf16[192,256]{1,0:T(8,128)(2,1)S(1)}, u32[]{:S(2)}, u32[]{:S(2)}) collective-permute-start(bf16[192,256]{1,0:T(8,128)(2,1)S(1)} %slice_bitcast_fusion.4), channel_id=1, source_target_pairs={{0,64},{8,72},{16,80},{24,88},{32,96},{40,104},{48,112},{56,120},{... | collective-permute-start | bytes 294920 | tf_op jit(solution)/shard_map/ppermute | solution.py:24
  146.7 10.4 %collective-permute-start.10 = (bf16[2,2,2,2,2,64,128]{6,5,2,0,3,1,4:T(8,128)(2,1)}, bf16[2,2,2,2,2,64,128]{6,5,2,0,3,1,4:T(8,128)(2,1)}, u32[]{:S(2)}, u32[]{:S(2)}) collective-permute-start(bf16[2,2,2,2,2,64,128]{6,5,2,0,3,1,4:T(8,128)(2,1)} %select_bitcast_fusion), channel_id=1, source_target_pairs={{0,8},{8,0},{16,24},{24,16},{32,40},{40,32},{48,56},{56,48},{64,72... | collective-permute-start | bytes 1572872 | tf_op jit(solution)/shard_map/ppermute | solution.py:24
  154.7 5.8 %collective-permute-start.4 = (bf16[2,2,2,2,2,64,128]{6,5,4,3,2,1,0:T(8,128)(2,1)}, bf16[2,2,2,2,2,64,128]{6,5,4,3,2,1,0:T(8,128)(2,1)}, u32[]{:S(2)}, u32[]{:S(2)}) collective-permute-start(bf16[2,2,2,2,2,64,128]{6,5,4,3,2,1,0:T(8,128)(2,1)} %get-tuple-element.13), channel_id=1, source_target_pairs={{0,8},{8,0},{16,24},{24,16},{32,40},{40,32},{48,56},{56,48},{64,72... | collective-permute-start | bytes 1572872 | tf_op jit(solution)/shard_map/ppermute | solution.py:24
  157.1 3.4 %copy-start.1 = (bf16[2,2,2,2,2,1,64,128]{7,6,5,4,3,2,1,0:T(8,128)(2,1)S(1)}, bf16[2,2,2,2,2,1,64,128]{7,6,5,4,3,2,1,0:T(8,128)(2,1)}, u32[]{:S(2)}) copy-start(bf16[2,2,2,2,2,1,64,128]{7,6,5,4,3,2,1,0:T(8,128)(2,1)} %get-tuple-element.15) | copy-start | bytes 1572868
  158.6 10.1 %collective-permute-start.11 = (bf16[2,2,2,2,64,128]{5,4,2,0,3,1:T(8,128)(2,1)S(1)}, bf16[2,2,2,2,64,128]{5,4,2,0,3,1:T(8,128)(2,1)S(1)}, u32[]{:S(2)}, u32[]{:S(2)}) collective-permute-start(bf16[2,2,2,2,64,128]{5,4,2,0,3,1:T(8,128)(2,1)S(1)} %select_bitcast_fusion.2), channel_id=1, source_target_pairs={{0,16},{8,24},{16,0},{24,8},{32,48},{40,56},{48,32},{56,40},{64,80... | collective-permute-start | bytes 786440 | tf_op jit(solution)/shard_map/ppermute | solution.py:24
  161.9 10.3 %collective-permute-start.5 = (bf16[2,2,2,2,64,128]{5,4,3,2,1,0:T(8,128)(2,1)S(1)}, bf16[2,2,2,2,64,128]{5,4,3,2,1,0:T(8,128)(2,1)S(1)}, u32[]{:S(2)}, u32[]{:S(2)}) collective-permute-start(bf16[2,2,2,2,64,128]{5,4,3,2,1,0:T(8,128)(2,1)S(1)} %fusion.21), channel_id=1, source_target_pairs={{0,128},{128,0},{256,384},{384,256},{1,129},{129,1},{257,385},{385... | collective-permute-start | bytes 786440 | tf_op jit(solution)/shard_map/ppermute | solution.py:24
  168.8 7.5 %collective-permute-start.12 = (bf16[2,2,2,64,128]{4,3,1,0,2:T(8,128)(2,1)S(1)}, bf16[2,2,2,64,128]{4,3,1,0,2:T(8,128)(2,1)S(1)}, u32[]{:S(2)}, u32[]{:S(2)}) collective-permute-start(bf16[2,2,2,64,128]{4,3,1,0,2:T(8,128)(2,1)S(1)} %select_bitcast_fusion.3), channel_id=1, source_target_pairs={{0,128},{128,0},{256,384},{384,256},{1,129},{129,1},{257,385},{385... | collective-permute-start | bytes 393224 | tf_op jit(solution)/shard_map/ppermute | solution.py:24
  172.3 6.9 %collective-permute-start.6 = (bf16[2,2,2,64,128]{4,3,2,1,0:T(8,128)(2,1)S(1)}, bf16[2,2,2,64,128]{4,3,2,1,0:T(8,128)(2,1)S(1)}, u32[]{:S(2)}, u32[]{:S(2)}) collective-permute-start(bf16[2,2,2,64,128]{4,3,2,1,0:T(8,128)(2,1)S(1)} %fusion.26), channel_id=1, source_target_pairs={{0,16},{8,24},{16,0},{24,8},{32,48},{40,56},{48,32},{56,40},{64,80... | collective-permute-start | bytes 393224 | tf_op jit(solution)/shard_map/ppermute | solution.py:24
  176.4 7.4 %collective-permute-start.13 = (bf16[2,2,64,128]{3,2,1,0:T(8,128)(2,1)S(1)}, bf16[2,2,64,128]{3,2,1,0:T(8,128)(2,1)S(1)}, u32[]{:S(2)}, u32[]{:S(2)}) collective-permute-start(bf16[2,2,64,128]{3,2,1,0:T(8,128)(2,1)S(1)} %select_bitcast_fusion.4), channel_id=1, source_target_pairs={{0,32},{8,40},{16,48},{24,56},{32,0},{40,8},{48,16},{56,24},{64,96... | collective-permute-start | bytes 196616 | tf_op jit(solution)/shard_map/ppermute | solution.py:24
  179.3 8.5 %collective-permute-start.7 = (bf16[2,2,64,128]{3,2,1,0:T(8,128)(2,1)S(1)}, bf16[2,2,64,128]{3,2,1,0:T(8,128)(2,1)S(1)}, u32[]{:S(2)}, u32[]{:S(2)}) collective-permute-start(bf16[2,2,64,128]{3,2,1,0:T(8,128)(2,1)S(1)} %select_bitcast_fusion.5), channel_id=1, source_target_pairs={{0,256},{128,384},{256,0},{384,128},{1,257},{129,385},{257,1},{385... | collective-permute-start | bytes 196616 | tf_op jit(solution)/shard_map/ppermute | solution.py:24
  183.8 7.4 %collective-permute-start.14 = (bf16[2,64,128]{2,1,0:T(8,128)(2,1)S(1)}, bf16[2,64,128]{2,1,0:T(8,128)(2,1)S(1)}, u32[]{:S(2)}, u32[]{:S(2)}) collective-permute-start(bf16[2,64,128]{2,1,0:T(8,128)(2,1)S(1)} %select_bitcast_fusion.6), channel_id=1, source_target_pairs={{0,256},{128,384},{256,0},{384,128},{1,257},{129,385},{257,1},{385... | collective-permute-start | bytes 98312 | tf_op jit(solution)/shard_map/ppermute | solution.py:24
  187.9 9.1 %collective-permute-start.8 = (bf16[2,64,128]{2,1,0:T(8,128)(2,1)S(1)}, bf16[2,64,128]{2,1,0:T(8,128)(2,1)S(1)}, u32[]{:S(2)}, u32[]{:S(2)}) collective-permute-start(bf16[2,64,128]{2,1,0:T(8,128)(2,1)S(1)} %fusion.34), channel_id=1, source_target_pairs={{0,32},{8,40},{16,48},{24,56},{32,0},{40,8},{48,16},{56,24},{64,96... | collective-permute-start | bytes 98312 | tf_op jit(solution)/shard_map/ppermute | solution.py:24
  191.3 9.8 %collective-permute-start.15 = (bf16[64,128]{1,0:T(8,128)(2,1)S(1)}, bf16[64,128]{1,0:T(8,128)(2,1)S(1)}, u32[]{:S(2)}, u32[]{:S(2)}) collective-permute-start(bf16[64,128]{1,0:T(8,128)(2,1)S(1)} %select_bitcast_fusion.7), channel_id=1, source_target_pairs={{0,64},{8,72},{16,80},{24,88},{32,96},{40,104},{48,112},{56,120},{... | collective-permute-start | bytes 49160 | tf_op jit(solution)/shard_map/ppermute | solution.py:24
  197.0 9.6 %collective-permute-start.9 = (bf16[64,128]{1,0:T(8,128)(2,1)S(1)}, bf16[64,128]{1,0:T(8,128)(2,1)S(1)}, u32[]{:S(2)}, u32[]{:S(2)}) collective-permute-start(bf16[64,128]{1,0:T(8,128)(2,1)S(1)} %select_bitcast_fusion.8), channel_id=1, source_target_pairs={{0,64},{8,72},{16,80},{24,88},{32,96},{40,104},{48,112},{56,120},{... | collective-permute-start | bytes 49160 | tf_op jit(solution)/shard_map/ppermute | solution.py:24

commit v10 on v9

--- a/solution.py
+++ b/solution.py
@@ -162,6 +162,63 @@
     )(x)
 
 
+def _scatter_kernel(steps, x_ref, o_ref, acc, rbuf, sbuf, staged, send_sems, recv_sems, local_sem):
+    mesh = pl.DeviceIdType.MESH
+    partners = [{axis: lax.bitwise_xor(lax.axis_index(axis), 1 << bit)} for axis, _, bit in steps]
+    barrier = pltpu.get_barrier_semaphore()
+    for p in partners:
+        pl.semaphore_signal(barrier, inc=1, device_id=p, device_id_type=mesh)
+    pl.semaphore_wait(barrier, len(partners))
+    for k in reversed(range(len(steps))):
+        half = 1 << k
+        off = half - 1
+        if k == len(steps) - 1:
+            src = x_ref.at[half:2 * half]
+        else:
+            sbuf[off:off + half] = acc[half:2 * half].astype(sbuf.dtype)
+            stage = pltpu.make_async_copy(sbuf.at[off:off + half], staged.at[off:off + half], local_sem)
+            stage.start()
+            stage.wait()
+            src = staged.at[off:off + half]
+        copy = pltpu.make_async_remote_copy(
+            src_ref=src,
+            dst_ref=rbuf.at[off:off + half],
+            send_sem=send_sems.at[k],
+            recv_sem=recv_sems.at[k],
+            device_id=partners[k],
+            device_id_type=mesh,
+        )
+        copy.start()
+        copy.wait()
+        got = rbuf[off:off + half].astype(jnp.float32)
+        if k == len(steps) - 1:
+            acc[0:half] = x_ref[0:half].astype(jnp.float32) + got
+        else:
+            acc[0:half] = acc[0:half] + got
+    o_ref[...] = acc[0]
+
+
+def pair_scatter(x, steps, collective_id):
+    n = x.shape[0]
+    block = x.shape[1:]
+    return pl.pallas_call(
+        functools.partial(_scatter_kernel, steps),
+        out_shape=jax.ShapeDtypeStruct(block, jnp.float32),
+        in_specs=[pl.BlockSpec(memory_space=pltpu.VMEM)],
+        out_specs=pl.BlockSpec(memory_space=pltpu.VMEM),
+        scratch_shapes=[
+            pltpu.VMEM((n // 2,) + block, jnp.float32),
+            pltpu.VMEM((n - 1,) + block, x.dtype),
+            pltpu.VMEM((n - 1,) + block, x.dtype),
+            pltpu.VMEM((n - 1,) + block, x.dtype),
+            pltpu.SemaphoreType.DMA((len(steps),)),
+            pltpu.SemaphoreType.DMA((len(steps),)),
+            pltpu.SemaphoreType.DMA,
+        ],
+        compiler_params=pltpu.CompilerParams(collective_id=collective_id, has_side_effects=True),
+    )(x)
+
+
 def _attention_kernel(q_ref, do_ref, k_ref, v_ref, mq_ref, mk_ref, gq_ref, dkv_ref, dk_acc, dv_acc):
     scale = HEAD_DIM ** (-0.5)
     keys = k_ref[...]
@@ -266,8 +323,8 @@
     mq = marks.astype(jnp.float32)[:, None]
     mk = marks_all.astype(jnp.float32)[None, :]
     grad_q, kv_part = attention_block(queries[0], grad_out[0], keys, values, mq, mk)
-    kv_blocks = kv_part.reshape((2,) * len(ctx_far) + (tok_rows, kv_part.shape[1]))
-    kv_grad = scatter_relative(kv_blocks, ctx_far).astype(jnp.bfloat16)
+    kv_blocks = kv_part.reshape((-1, tok_rows, kv_part.shape[1]))
+    kv_grad = pair_scatter(kv_blocks, ctx_far, 2).astype(jnp.bfloat16)
 
     dims_t = (((0,), (0,)), ((), ()))
     key_part = lax.dot_general(local_rows, kv_grad[:, :width_kv], dims_t, preferred_element_type=jnp.float32)

time: 208 us -> 201 us (0.966)
  Pallas kernels: 84 us -> 125 us
  waiting for transfers between devices: 42.6 us -> 9.49 us
  starting transfers between devices: 53.8 us -> 39.4 us
    pallas_call x0 -> x1, Pallas kernels: none -> 40.8 us  [pair_scatter(): pl.pallas_call(functools.partial(_scatter_kernel, steps), out_shape=jax.S...]
    ppermute x16 -> x12, waiting for transfers between devices: 42.6 us -> 9.49 us  [_exchange(): return lax.ppermute(x, axis, perm)]
    ppermute x16 -> x12, starting transfers between devices: 53.8 us -> 39.4 us  [_exchange(): return lax.ppermute(x, axis, perm)]
  transfers between devices with their start and end apart: 16 -> 12, of which waited for: 8 -> 4; matrix products, arithmetic and copies ran while one was open for 5% -> 5% of each run, Pallas kernels for 0% -> 0%
where the time goes in v10:
time: 201 us; the launch traced here: 200 us
  Pallas kernels  125 us (62%)
  starting transfers between devices  39.4 us (20%)
  other arithmetic  11.7 us (6%)
  waiting for transfers between devices  9.49 us (5%)
  local copies, waits for them, and re-layouts  8.95 us (4%)
  matrix products  4.11 us (2%)
    pallas_call x2, Pallas kernels, pair_gather(): pl.pallas_call(functools.partial(_gather_kernel, steps, canonical), out_s...  68.7 us
    pallas_call x1, Pallas kernels, pair_scatter(): pl.pallas_call(functools.partial(_scatter_kernel, steps), out_shape=jax.S...  40.8 us
    ppermute x12, starting transfers between devices, _exchange(): return lax.ppermute(x, axis, perm)  39.4 us
    pallas_call x1, Pallas kernels, attention_block(): pl.pallas_call(_attention_kernel, out_shape=(jax.ShapeDtypeStruct((rows,...  15.3 us
    ppermute x12, waiting for transfers between devices, _exchange(): return lax.ppermute(x, axis, perm)  9.49 us
  transfers between devices with their start and end apart: 12, of which 4 were waited for; matrix products, arithmetic and copies ran while one was open for 5% of the time, Pallas kernels for 0%

profile of v10, /device:TPU:24, one launch (start us, length us, event | category | flops | bytes accessed | tf_op | source)
XLA Modules:
  0.0 199.6 jit_solution(14384184766185168216)
XLA Ops:
  0.6 0.0 copy-start
  0.6 0.0 copy-start.2
  0.7 1.5 maximum_bitcast_fusion.1.x_ref
  2.1 38.8 %shard_map.85 = bf16[64,64,256]{2,1,0:T(8,128)(2,1)} custom-call(bf16[1,64,256]{2,1,0:T(8,128)(2,1)} %maximum_bitcast_fusion.1.x_ref), custom_call_target="tpu_custom_call" | custom-call | tf_op jit(solution)/shard_map/pallas_call | solution.py:150
  41.0 0.0 copy-done.2
  41.0 0.0 copy-done
  41.0 2.2 %fusion.9 = bf16[192,256]{1,0:T(8,128)(2,1)S(1)} fusion(bf16[4096,256]{1,0:T(8,128)(2,1)} %bitcast.147, bf16[1,192,4096]{2,1,0:T(8,128)(2,1)S(1)} %copy-done), kind=kOutput, calls=%fused_computation.9 | convolution fusion | flops 402702336 | bytes 3768320 | tf_op jit(solution)/shard_map/dot_general | solution.py:314
  43.2 0.7 maximum_bitcast_fusion.x_ref
  43.9 29.9 %shard_map.86 = bf16[16,193,256]{2,1,0:T(8,128)(2,1)} custom-call(bf16[1,193,256]{2,1,0:T(8,128)(2,1)} %maximum_bitcast_fusion.x_ref), custom_call_target="tpu_custom_call" | custom-call | tf_op jit(solution)/shard_map/pallas_call | solution.py:150
  73.7 2.6 %fusion.32 = (bf16[16,192,128]{2,1,0:T(8,128)(2,1)}, bf16[16,192,128]{2,1,0:T(8,128)(2,1)}) fusion(bf16[16,193,256]{2,1,0:T(8,128)(2,1)} %shard_map.86), kind=kLoop, calls=%fused_computation.63 | loop fusion | bytes 3145728 | tf_op jit(solution)/shard_map/slice | solution.py:320
  76.4 0.9 convert_reduce_fusion
  77.3 0.7 reshape.132.mk_ref
  77.9 0.8 copy.21.mq_ref
  78.7 15.3 %shard_map.87 = (bf16[192,512]{1,0:T(8,128)(2,1)}, bf16[3072,256]{1,0:T(8,128)(2,1)}) custom-call(bf16[192,512]{1,0:T(8,128)(2,1)} %bitcast.151, bf16[192,512]{1,0:T(8,128)(2,1)} %bitcast.152, bf16[3072,128]{1,0:T(8,128)(2,1)} %bitcast.150, bf16[3072,128]{1,0:T(8,128)(2,1)} %bitcast.149, f32[192,1]{1,0:T(8,128)} %copy.21.mq_ref, f32[1,3072]{1,0:T(1,128)} %reshape.132.mk_ref), custom_call_target="tpu_custom_call" | custom-call | flops 3623878656 | bytes 3932160 | tf_op jit(solution)/shard_map/pallas_call | solution.py:261
  94.1 40.8 %shard_map.88 = f32[192,256]{1,0:T(8,128)} custom-call(bf16[16,192,256]{2,1,0:T(8,128)(2,1)} %bitcast.148), custom_call_target="tpu_custom_call" | custom-call | tf_op jit(solution)/shard_map/pallas_call | solution.py:204
  134.9 0.9 convert_element_type.209
  135.9 0.5 fusion.1
  136.3 1.3 copy.40
  137.6 1.3 fusion.33
  138.9 0.9 select_bitcast_fusion
  139.8 1.9 collective-permute-start.6
  141.7 1.5 fusion
  143.2 2.3 %copy.22 = bf16[4096,128]{1,0:T(8,128)(2,1)} copy(bf16[4096,128]{0,1:T(8,128)(2,1)} %fusion) | data formatting | bytes 2097152 | tf_op jit(solution)/shard_map/convert_element_type | solution.py:332
  145.5 2.3 %select_bitcast_fusion.1 = (bf16[2,2,2,2,2,64,128]{6,5,4,3,2,1,0:T(8,128)(2,1)}, bf16[2,2,2,2,2,1,64,128]{7,6,5,4,3,2,1,0:T(8,128)(2,1)S(1)}, bf16[2,2,2,2,2,1,64,128]{7,6,5,4,3,2,1,0:T(8,128)(2,1)}) fusion(pred[]{:T(512)S(6)} %eq.29, bf16[2,2,2,2,2,2,64,128]{7,6,5,4,3,2,1,0:T(8,128)(2,1)} %bitcast.145), kind=kLoop, calls=%fused_computation.22 | loop fusion | flops 262144 | bytes 2621441 | tf_op jit(solution)/shard_map/jit(_where)/select_n | solution.py:56
  147.8 2.4 %collective-permute-start = (bf16[2,2,2,2,2,64,128]{6,5,4,3,2,1,0:T(8,128)(2,1)}, bf16[2,2,2,2,2,64,128]{6,5,4,3,2,1,0:T(8,128)(2,1)}, u32[]{:S(2)}, u32[]{:S(2)}) collective-permute-start(bf16[2,2,2,2,2,64,128]{6,5,4,3,2,1,0:T(8,128)(2,1)} %get-tuple-element.11), channel_id=1, source_target_pairs={{0,8},{8,0},{16,24},{24,16},{32,40},{40,32},{48,56},{56,48},{64,72... | collective-permute-start | bytes 1572872 | tf_op jit(solution)/shard_map/ppermute | solution.py:24
  150.2 0.0 copy-start.1
  150.2 0.0 collective-permute-done.6
  150.2 1.4 fusion.12
  151.6 1.9 collective-permute-start.7
  153.5 0.0 collective-permute-done
  153.5 0.0 copy-done.1
  153.5 1.3 fusion.13
  154.9 3.2 %collective-permute-start.1 = (bf16[2,2,2,2,64,128]{5,4,3,2,1,0:T(8,128)(2,1)S(1)}, bf16[2,2,2,2,64,128]{5,4,3,2,1,0:T(8,128)(2,1)S(1)}, u32[]{:S(2)}, u32[]{:S(2)}) collective-permute-start(bf16[2,2,2,2,64,128]{5,4,3,2,1,0:T(8,128)(2,1)S(1)} %fusion.18), channel_id=1, source_target_pairs={{0,128},{128,0},{256,384},{384,256},{1,129},{129,1},{257,385},{385... | collective-permute-start | bytes 786440 | tf_op jit(solution)/shard_map/ppermute | solution.py:24
  158.1 3.6 %collective-permute-done.7 = bf16[2,2,2,2,64,128]{5,4,2,0,3,1:T(8,128)(2,1)S(1)} collective-permute-done((bf16[2,2,2,2,64,128]{5,4,2,0,3,1:T(8,128)(2,1)S(1)}, bf16[2,2,2,2,64,128]{5,4,2,0,3,1:T(8,128)(2,1)S(1)}, u32[]{:S(2)}, u32[]{:S(2)}) %collective-permute-start.7) | collective-permute-done | bytes 262176 | tf_op jit(solution)/shard_map/ppermute | solution.py:24
  161.7 0.1 fusion.16
  161.9 3.3 %collective-permute-start.8 = (bf16[2,2,2,64,128]{4,3,1,0,2:T(8,128)(2,1)S(1)}, bf16[2,2,2,64,128]{4,3,1,0,2:T(8,128)(2,1)S(1)}, u32[]{:S(2)}, u32[]{:S(2)}) collective-permute-start(bf16[2,2,2,64,128]{4,3,1,0,2:T(8,128)(2,1)S(1)} %select_bitcast_fusion.3), channel_id=1, source_target_pairs={{0,128},{128,0},{256,384},{384,256},{1,129},{129,1},{257,385},{385... | collective-permute-start | bytes 393224 | tf_op jit(solution)/shard_map/ppermute | solution.py:24
  165.1 0.0 collective-permute-done.1
  165.2 0.1 fusion.17
  165.3 4.0 %collective-permute-start.2 = (bf16[2,2,2,64,128]{4,3,2,1,0:T(8,128)(2,1)S(1)}, bf16[2,2,2,64,128]{4,3,2,1,0:T(8,128)(2,1)S(1)}, u32[]{:S(2)}, u32[]{:S(2)}) collective-permute-start(bf16[2,2,2,64,128]{4,3,2,1,0:T(8,128)(2,1)S(1)} %fusion.22), channel_id=1, source_target_pairs={{0,16},{8,24},{16,0},{24,8},{32,48},{40,56},{48,32},{56,40},{64,80... | collective-permute-start | bytes 393224 | tf_op jit(solution)/shard_map/ppermute | solution.py:24
  169.3 0.0 collective-permute-done.8
  169.4 0.1 fusion.20
  169.4 1.9 collective-permute-start.9
  171.4 0.9 collective-permute-done.2
  172.3 0.1 fusion.21
  172.4 3.6 %collective-permute-start.3 = (bf16[2,2,64,128]{3,2,1,0:T(8,128)(2,1)S(1)}, bf16[2,2,64,128]{3,2,1,0:T(8,128)(2,1)S(1)}, u32[]{:S(2)}, u32[]{:S(2)}) collective-permute-start(bf16[2,2,64,128]{3,2,1,0:T(8,128)(2,1)S(1)} %select_bitcast_fusion.5), channel_id=1, source_target_pairs={{0,256},{128,384},{256,0},{384,128},{1,257},{129,385},{257,1},{385... | collective-permute-start | bytes 196616 | tf_op jit(solution)/shard_map/ppermute | solution.py:24
  176.0 0.8 collective-permute-done.9
  176.9 3.6 %collective-permute-start.10 = (bf16[2,64,128]{2,1,0:T(8,128)(2,1)S(1)}, bf16[2,64,128]{2,1,0:T(8,128)(2,1)S(1)}, u32[]{:S(2)}, u32[]{:S(2)}) collective-permute-start(bf16[2,64,128]{2,1,0:T(8,128)(2,1)S(1)} %select_bitcast_fusion.6), channel_id=1, source_target_pairs={{0,256},{128,384},{256,0},{384,128},{1,257},{129,385},{257,1},{385... | collective-permute-start | bytes 98312 | tf_op jit(solution)/shard_map/ppermute | solution.py:24
  180.5 0.0 collective-permute-done.3
  180.6 3.7 %collective-permute-start.4 = (bf16[2,64,128]{2,1,0:T(8,128)(2,1)S(1)}, bf16[2,64,128]{2,1,0:T(8,128)(2,1)S(1)}, u32[]{:S(2)}, u32[]{:S(2)}) collective-permute-start(bf16[2,64,128]{2,1,0:T(8,128)(2,1)S(1)} %fusion.30), channel_id=1, source_target_pairs={{0,32},{8,40},{16,48},{24,56},{32,0},{40,8},{48,16},{56,24},{64,96... | collective-permute-start | bytes 98312 | tf_op jit(solution)/shard_map/ppermute | solution.py:24
  184.4 0.0 collective-permute-done.10
  184.4 5.0 %collective-permute-start.11 = (bf16[64,128]{1,0:T(8,128)(2,1)S(1)}, bf16[64,128]{1,0:T(8,128)(2,1)S(1)}, u32[]{:S(2)}, u32[]{:S(2)}) collective-permute-start(bf16[64,128]{1,0:T(8,128)(2,1)S(1)} %select_bitcast_fusion.7), channel_id=1, source_target_pairs={{0,64},{8,72},{16,80},{24,88},{32,96},{40,104},{48,112},{56,120},{... | collective-permute-start | bytes 49160 | tf_op jit(solution)/shard_map/ppermute | solution.py:24
  189.4 0.0 collective-permute-done.4
  189.4 4.8 %collective-permute-start.5 = (bf16[64,128]{1,0:T(8,128)(2,1)S(1)}, bf16[64,128]{1,0:T(8,128)(2,1)S(1)}, u32[]{:S(2)}, u32[]{:S(2)}) collective-permute-start(bf16[64,128]{1,0:T(8,128)(2,1)S(1)} %select_bitcast_fusion.8), channel_id=1, source_target_pairs={{0,64},{8,72},{16,80},{24,88},{32,96},{40,104},{48,112},{56,120},{... | collective-permute-start | bytes 49160 | tf_op jit(solution)/shard_map/ppermute | solution.py:24
  194.2 0.0 collective-permute-done.11
  194.2 0.6 convert_add_fusion.9
  194.9 4.1 %collective-permute-done.5 = bf16[64,128]{1,0:T(8,128)(2,1)S(1)} collective-permute-done((bf16[64,128]{1,0:T(8,128)(2,1)S(1)}, bf16[64,128]{1,0:T(8,128)(2,1)S(1)}, u32[]{:S(2)}, u32[]{:S(2)}) %collective-permute-start.5) | collective-permute-done | bytes 16416 | tf_op jit(solution)/shard_map/ppermute | solution.py:24
  199.0 0.6 convert_add_fusion.10
  (18 shorter events, 0.3 us)
Async XLA Ops:
  0.6 40.4 %copy-start = (bf16[1,192,4096]{2,1,0:T(8,128)(2,1)S(1)}, bf16[1,192,4096]{2,1,0:T(8,128)(2,1)}, u32[]{:S(2)}) copy-start(bf16[1,192,4096]{2,1,0:T(8,128)(2,1)} %param.6) | copy-start | bytes 4718596
  0.6 40.3 %copy-start.2 = (s32[1,192]{1,0:T(1,128)S(1)}, s32[1,192]{1,0:T(1,128)}, u32[]{:S(2)}) copy-start(s32[1,192]{1,0:T(1,128)} %param.9) | copy-start | bytes 2308
  139.8 10.4 %collective-permute-start.6 = (bf16[2,2,2,2,2,64,128]{6,5,2,0,3,1,4:T(8,128)(2,1)}, bf16[2,2,2,2,2,64,128]{6,5,2,0,3,1,4:T(8,128)(2,1)}, u32[]{:S(2)}, u32[]{:S(2)}) collective-permute-start(bf16[2,2,2,2,2,64,128]{6,5,2,0,3,1,4:T(8,128)(2,1)} %select_bitcast_fusion), channel_id=1, source_target_pairs={{0,8},{8,0},{16,24},{24,16},{32,40},{40,32},{48,56},{56,48},{64,72... | collective-permute-start | bytes 1572872 | tf_op jit(solution)/shard_map/ppermute | solution.py:24
  147.8 5.8 %collective-permute-start = (bf16[2,2,2,2,2,64,128]{6,5,4,3,2,1,0:T(8,128)(2,1)}, bf16[2,2,2,2,2,64,128]{6,5,4,3,2,1,0:T(8,128)(2,1)}, u32[]{:S(2)}, u32[]{:S(2)}) collective-permute-start(bf16[2,2,2,2,2,64,128]{6,5,4,3,2,1,0:T(8,128)(2,1)} %get-tuple-element.11), channel_id=1, source_target_pairs={{0,8},{8,0},{16,24},{24,16},{32,40},{40,32},{48,56},{56,48},{64,72... | collective-permute-start | bytes 1572872 | tf_op jit(solution)/shard_map/ppermute | solution.py:24
  150.2 3.4 %copy-start.1 = (bf16[2,2,2,2,2,1,64,128]{7,6,5,4,3,2,1,0:T(8,128)(2,1)S(1)}, bf16[2,2,2,2,2,1,64,128]{7,6,5,4,3,2,1,0:T(8,128)(2,1)}, u32[]{:S(2)}) copy-start(bf16[2,2,2,2,2,1,64,128]{7,6,5,4,3,2,1,0:T(8,128)(2,1)} %get-tuple-element.13) | copy-start | bytes 1572868
  151.6 10.1 %collective-permute-start.7 = (bf16[2,2,2,2,64,128]{5,4,2,0,3,1:T(8,128)(2,1)S(1)}, bf16[2,2,2,2,64,128]{5,4,2,0,3,1:T(8,128)(2,1)S(1)}, u32[]{:S(2)}, u32[]{:S(2)}) collective-permute-start(bf16[2,2,2,2,64,128]{5,4,2,0,3,1:T(8,128)(2,1)S(1)} %select_bitcast_fusion.2), channel_id=1, source_target_pairs={{0,16},{8,24},{16,0},{24,8},{32,48},{40,56},{48,32},{56,40},{64,80... | collective-permute-start | bytes 786440 | tf_op jit(solution)/shard_map/ppermute | solution.py:24
  154.9 10.3 %collective-permute-start.1 = (bf16[2,2,2,2,64,128]{5,4,3,2,1,0:T(8,128)(2,1)S(1)}, bf16[2,2,2,2,64,128]{5,4,3,2,1,0:T(8,128)(2,1)S(1)}, u32[]{:S(2)}, u32[]{:S(2)}) collective-permute-start(bf16[2,2,2,2,64,128]{5,4,3,2,1,0:T(8,128)(2,1)S(1)} %fusion.18), channel_id=1, source_target_pairs={{0,128},{128,0},{256,384},{384,256},{1,129},{129,1},{257,385},{385... | collective-permute-start | bytes 786440 | tf_op jit(solution)/shard_map/ppermute | solution.py:24
  161.9 7.5 %collective-permute-start.8 = (bf16[2,2,2,64,128]{4,3,1,0,2:T(8,128)(2,1)S(1)}, bf16[2,2,2,64,128]{4,3,1,0,2:T(8,128)(2,1)S(1)}, u32[]{:S(2)}, u32[]{:S(2)}) collective-permute-start(bf16[2,2,2,64,128]{4,3,1,0,2:T(8,128)(2,1)S(1)} %select_bitcast_fusion.3), channel_id=1, source_target_pairs={{0,128},{128,0},{256,384},{384,256},{1,129},{129,1},{257,385},{385... | collective-permute-start | bytes 393224 | tf_op jit(solution)/shard_map/ppermute | solution.py:24
  165.3 7.0 %collective-permute-start.2 = (bf16[2,2,2,64,128]{4,3,2,1,0:T(8,128)(2,1)S(1)}, bf16[2,2,2,64,128]{4,3,2,1,0:T(8,128)(2,1)S(1)}, u32[]{:S(2)}, u32[]{:S(2)}) collective-permute-start(bf16[2,2,2,64,128]{4,3,2,1,0:T(8,128)(2,1)S(1)} %fusion.22), channel_id=1, source_target_pairs={{0,16},{8,24},{16,0},{24,8},{32,48},{40,56},{48,32},{56,40},{64,80... | collective-permute-start | bytes 393224 | tf_op jit(solution)/shard_map/ppermute | solution.py:24
  169.4 7.4 %collective-permute-start.9 = (bf16[2,2,64,128]{3,2,1,0:T(8,128)(2,1)S(1)}, bf16[2,2,64,128]{3,2,1,0:T(8,128)(2,1)S(1)}, u32[]{:S(2)}, u32[]{:S(2)}) collective-permute-start(bf16[2,2,64,128]{3,2,1,0:T(8,128)(2,1)S(1)} %select_bitcast_fusion.4), channel_id=1, source_target_pairs={{0,32},{8,40},{16,48},{24,56},{32,0},{40,8},{48,16},{56,24},{64,96... | collective-permute-start | bytes 196616 | tf_op jit(solution)/shard_map/ppermute | solution.py:24
  172.4 8.2 %collective-permute-start.3 = (bf16[2,2,64,128]{3,2,1,0:T(8,128)(2,1)S(1)}, bf16[2,2,64,128]{3,2,1,0:T(8,128)(2,1)S(1)}, u32[]{:S(2)}, u32[]{:S(2)}) collective-permute-start(bf16[2,2,64,128]{3,2,1,0:T(8,128)(2,1)S(1)} %select_bitcast_fusion.5), channel_id=1, source_target_pairs={{0,256},{128,384},{256,0},{384,128},{1,257},{129,385},{257,1},{385... | collective-permute-start | bytes 196616 | tf_op jit(solution)/shard_map/ppermute | solution.py:24
  176.9 7.5 %collective-permute-start.10 = (bf16[2,64,128]{2,1,0:T(8,128)(2,1)S(1)}, bf16[2,64,128]{2,1,0:T(8,128)(2,1)S(1)}, u32[]{:S(2)}, u32[]{:S(2)}) collective-permute-start(bf16[2,64,128]{2,1,0:T(8,128)(2,1)S(1)} %select_bitcast_fusion.6), channel_id=1, source_target_pairs={{0,256},{128,384},{256,0},{384,128},{1,257},{129,385},{257,1},{385... | collective-permute-start | bytes 98312 | tf_op jit(solution)/shard_map/ppermute | solution.py:24
  180.6 8.8 %collective-permute-start.4 = (bf16[2,64,128]{2,1,0:T(8,128)(2,1)S(1)}, bf16[2,64,128]{2,1,0:T(8,128)(2,1)S(1)}, u32[]{:S(2)}, u32[]{:S(2)}) collective-permute-start(bf16[2,64,128]{2,1,0:T(8,128)(2,1)S(1)} %fusion.30), channel_id=1, source_target_pairs={{0,32},{8,40},{16,48},{24,56},{32,0},{40,8},{48,16},{56,24},{64,96... | collective-permute-start | bytes 98312 | tf_op jit(solution)/shard_map/ppermute | solution.py:24
  184.4 9.8 %collective-permute-start.11 = (bf16[64,128]{1,0:T(8,128)(2,1)S(1)}, bf16[64,128]{1,0:T(8,128)(2,1)S(1)}, u32[]{:S(2)}, u32[]{:S(2)}) collective-permute-start(bf16[64,128]{1,0:T(8,128)(2,1)S(1)} %select_bitcast_fusion.7), channel_id=1, source_target_pairs={{0,64},{8,72},{16,80},{24,88},{32,96},{40,104},{48,112},{56,120},{... | collective-permute-start | bytes 49160 | tf_op jit(solution)/shard_map/ppermute | solution.py:24
  189.4 9.5 %collective-permute-start.5 = (bf16[64,128]{1,0:T(8,128)(2,1)S(1)}, bf16[64,128]{1,0:T(8,128)(2,1)S(1)}, u32[]{:S(2)}, u32[]{:S(2)}) collective-permute-start(bf16[64,128]{1,0:T(8,128)(2,1)S(1)} %select_bitcast_fusion.8), channel_id=1, source_target_pairs={{0,64},{8,72},{16,80},{24,88},{32,96},{40,104},{48,112},{56,120},{... | collective-permute-start | bytes 49160 | tf_op jit(solution)/shard_map/ppermute | solution.py:24

commit v11 on v10

--- a/solution.py
+++ b/solution.py
@@ -162,9 +162,26 @@
     )(x)
 
 
-def _scatter_kernel(steps, x_ref, o_ref, acc, rbuf, sbuf, staged, send_sems, recv_sems, local_sem):
+def _scatter_kernel(steps, canonical, x_in, o_ref, acc, rbuf, sbuf, staged, rel, send_sems, recv_sems, local_sem):
     mesh = pl.DeviceIdType.MESH
     partners = [{axis: lax.bitwise_xor(lax.axis_index(axis), 1 << bit)} for axis, _, bit in steps]
+    x_ref = x_in
+    if canonical is not None:
+        weights = []
+        me = 0
+        for axis, size, bit in steps:
+            mine = (lax.axis_index(axis) // (1 << bit)) % 2
+            weights.append(canonical[(axis, bit)] * (1 - 2 * mine))
+        for axis, stride in canonical["origin"]:
+            me = me + lax.axis_index(axis) * stride
+        for r in range(1 << len(steps)):
+            at = me
+            for k in range(len(steps)):
+                if (r >> k) & 1:
+                    at = at + weights[k]
+            pltpu.make_async_copy(x_in.at[pl.ds(at, 1)], rel.at[r:r + 1], local_sem).start()
+        pltpu.make_async_copy(x_in, rel, local_sem).wait()
+        x_ref = rel
     barrier = pltpu.get_barrier_semaphore()
     for p in partners:
         pl.semaphore_signal(barrier, inc=1, device_id=p, device_id_type=mesh)
@@ -198,11 +215,11 @@
     o_ref[...] = acc[0]
 
 
-def pair_scatter(x, steps, collective_id):
+def pair_scatter(x, steps, collective_id, canonical=None):
     n = x.shape[0]
     block = x.shape[1:]
     return pl.pallas_call(
-        functools.partial(_scatter_kernel, steps),
+        functools.partial(_scatter_kernel, steps, canonical),
         out_shape=jax.ShapeDtypeStruct(block, jnp.float32),
         in_specs=[pl.BlockSpec(memory_space=pltpu.VMEM)],
         out_specs=pl.BlockSpec(memory_space=pltpu.VMEM),
@@ -211,6 +228,7 @@
             pltpu.VMEM((n - 1,) + block, x.dtype),
             pltpu.VMEM((n - 1,) + block, x.dtype),
             pltpu.VMEM((n - 1,) + block, x.dtype),
+            pltpu.VMEM((n if canonical else 1,) + block, x.dtype),
             pltpu.SemaphoreType.DMA((len(steps),)),
             pltpu.SemaphoreType.DMA((len(steps),)),
             pltpu.SemaphoreType.DMA,
@@ -329,8 +347,10 @@
     dims_t = (((0,), (0,)), ((), ()))
     key_part = lax.dot_general(local_rows, kv_grad[:, :width_kv], dims_t, preferred_element_type=jnp.float32)
     value_part = lax.dot_general(local_rows, kv_grad[:, width_kv:], dims_t, preferred_element_type=jnp.float32)
-    key_sum = scatter_sum(key_part.astype(jnp.bfloat16), order_a[::-1], both_canon, jnp.float32)
-    value_sum = scatter_sum(value_part.astype(jnp.bfloat16), order_b[::-1], both_canon, jnp.float32)
+    parts = jnp.concatenate([key_part, value_part], axis=1).astype(jnp.bfloat16)
+    parts = parts.reshape((-1, key_proj.shape[0], parts.shape[1]))
+    summed = pair_scatter(parts, far_first, 3, canonical)
+    key_sum, value_sum = summed[:, :width_kv], summed[:, width_kv:]
     grad_queries = grad_q[None]
     return (grad_queries, key_sum, value_sum)
 

time: 201 us -> 195 us (0.970)
  Pallas kernels: 125 us -> 171 us
  starting transfers between devices: 39.4 us -> 0 us
  waiting for transfers between devices: 9.49 us -> 0 us
  other arithmetic: 11.7 us -> 8.23 us
    pallas_call x1 -> x2, Pallas kernels: 40.8 us -> 86.9 us  [pair_scatter(): pl.pallas_call(functools.partial(_scatter_kernel, steps, canonical), out_...]
    ppermute x12 -> x0, starting transfers between devices: 39.4 us -> none  [_exchange(): return lax.ppermute(x, axis, perm)]
    ppermute x12 -> x0, waiting for transfers between devices: 9.49 us -> none  [_exchange(): return lax.ppermute(x, axis, perm)]
    dot_general x0 -> x2, local copies, waits for them, and re-layouts: none -> 3.89 us  [the longest x1 2.28 us: body(): lax.dot_general(local_rows, kv_grad[:, :width_kv], dims_t, preferred_elem...]
    convert_element_type x2 -> x0, local copies, waits for them, and re-layouts: 3.56 us -> none  [the longest x1 2.25 us: body(): key_part.astype(jnp.bfloat16)]
    select_n x12 -> x0, other arithmetic: 3.33 us -> none  [scatter_sum(): send = jnp.where(mine, lo, hi)]
    convert_element_type x10 -> x0, other arithmetic: 3.1 us -> none  [scatter_sum(): cur = total if len(dims) == 1 else total.astype(x.dtype)]
    concatenate x0 -> x1, other arithmetic: none -> 2.9 us  [body(): parts = jnp.concatenate([key_part, value_part], axis=1).astype(jnp.bfloat16)]
  transfers between devices with their start and end apart: 12 -> 0, of which waited for: 4 -> 0; matrix products, arithmetic and copies ran while one was open for 5% -> 0% of each run, Pallas kernels for 0% -> 0%
where the time goes in v11:
time: 195 us; the launch traced here: 194 us
  Pallas kernels  171 us (88%)
  local copies, waits for them, and re-layouts  9.4 us (5%)
  other arithmetic  8.23 us (4%)
  matrix products  5.08 us (3%)
    pallas_call x2, Pallas kernels, pair_scatter(): pl.pallas_call(functools.partial(_scatter_kernel, steps, canonical), out_...  86.9 us
    pallas_call x2, Pallas kernels, pair_gather(): pl.pallas_call(functools.partial(_gather_kernel, steps, canonical), out_s...  68.7 us
    pallas_call x1, Pallas kernels, attention_block(): pl.pallas_call(_attention_kernel, out_shape=(jax.ShapeDtypeStruct((rows,...  15.3 us

profile of v11, /device:TPU:24, one launch (start us, length us, event | category | flops | bytes accessed | tf_op | source)
XLA Modules:
  0.0 194.4 jit_solution(14700230104882799917)
XLA Ops:
  0.6 0.0 copy-start
  0.6 0.8 convert_reduce_fusion.1
  1.5 0.7 bitcast_convert_fusion
  2.2 1.4 maximum_bitcast_fusion.1.x_ref
  3.5 0.8 copy.11.mq_ref
  4.3 38.9 %shard_map.85 = bf16[64,64,256]{2,1,0:T(8,128)(2,1)} custom-call(bf16[1,64,256]{2,1,0:T(8,128)(2,1)} %maximum_bitcast_fusion.1.x_ref), custom_call_target="tpu_custom_call" | custom-call | tf_op jit(solution)/shard_map/pallas_call | solution.py:150
  43.2 0.0 copy-done
  43.2 2.2 %fusion.9 = bf16[192,256]{1,0:T(8,128)(2,1)S(1)} fusion(bf16[4096,256]{1,0:T(8,128)(2,1)} %bitcast.36, bf16[1,192,4096]{2,1,0:T(8,128)(2,1)S(1)} %copy-done), kind=kOutput, calls=%fused_computation.10 | convolution fusion | flops 402702336 | bytes 3768320 | tf_op jit(solution)/shard_map/dot_general | solution.py:332
  45.3 0.7 maximum_bitcast_fusion.x_ref
  46.0 29.9 %shard_map.86 = bf16[16,193,256]{2,1,0:T(8,128)(2,1)} custom-call(bf16[1,193,256]{2,1,0:T(8,128)(2,1)} %maximum_bitcast_fusion.x_ref), custom_call_target="tpu_custom_call" | custom-call | tf_op jit(solution)/shard_map/pallas_call | solution.py:150
  75.8 0.9 convert_reduce_fusion
  76.7 2.6 %fusion.14 = (bf16[16,192,128]{2,1,0:T(8,128)(2,1)}, bf16[16,192,128]{2,1,0:T(8,128)(2,1)}) fusion(bf16[16,193,256]{2,1,0:T(8,128)(2,1)} %shard_map.86), kind=kLoop, calls=%fused_computation.18 | loop fusion | bytes 3145728 | tf_op jit(solution)/shard_map/slice | solution.py:338
  79.4 0.7 reshape.57.mk_ref
  80.1 15.3 %shard_map.87 = (bf16[192,512]{1,0:T(8,128)(2,1)}, bf16[3072,256]{1,0:T(8,128)(2,1)}) custom-call(bf16[192,512]{1,0:T(8,128)(2,1)} %bitcast.40, bf16[192,512]{1,0:T(8,128)(2,1)} %bitcast.41, bf16[3072,128]{1,0:T(8,128)(2,1)} %bitcast.39, bf16[3072,128]{1,0:T(8,128)(2,1)} %bitcast.38, f32[192,1]{1,0:T(8,128)} %copy.11.mq_ref, f32[1,3072]{1,0:T(1,128)} %reshape.57.mk_ref), custom_call_target="tpu_custom_call" | custom-call | flops 3623878656 | bytes 3932160 | tf_op jit(solution)/shard_map/pallas_call | solution.py:279
  95.4 40.8 %shard_map.88 = f32[192,256]{1,0:T(8,128)} custom-call(bf16[16,192,256]{2,1,0:T(8,128)(2,1)} %bitcast.37), custom_call_target="tpu_custom_call" | custom-call | tf_op jit(solution)/shard_map/pallas_call | solution.py:221
  136.3 0.9 convert_element_type.61
  137.2 1.5 fusion.1
  138.7 1.6 copy.13
  140.3 1.4 fusion
  141.7 2.3 %copy.12 = bf16[4096,128]{1,0:T(8,128)(2,1)} copy(bf16[4096,128]{0,1:T(8,128)(2,1)} %fusion) | data formatting | bytes 2097152 | tf_op jit(solution)/shard_map/dot_general | solution.py:348
  144.0 2.9 %pad_maximum_fusion.x_in = bf16[64,64,256]{2,1,0:T(8,128)(2,1)} fusion(bf16[64,64,128]{2,1,0:T(8,128)(2,1)S(1)} %bitcast.34, bf16[64,64,128]{2,1,0:T(8,128)(2,1)} %bitcast.35), kind=kLoop, calls=%fused_computation.4 | loop fusion | flops 4194304 | bytes 4194304 | tf_op jit(solution)/shard_map/concatenate | solution.py:350
  146.9 46.1 %shard_map.89 = f32[64,256]{1,0:T(8,128)} custom-call(bf16[64,64,256]{2,1,0:T(8,128)(2,1)} %pad_maximum_fusion.x_in), custom_call_target="tpu_custom_call" | custom-call | tf_op jit(solution)/shard_map/pallas_call | solution.py:221
  193.0 1.4 fusion.15
  (2 shorter events, 0.0 us)
Async XLA Ops:
  0.6 42.5 %copy-start = (bf16[1,192,4096]{2,1,0:T(8,128)(2,1)S(1)}, bf16[1,192,4096]{2,1,0:T(8,128)(2,1)}, u32[]{:S(2)}) copy-start(bf16[1,192,4096]{2,1,0:T(8,128)(2,1)} %param.6) | copy-start | bytes 4718596

commit v12 on v11

--- a/solution.py
+++ b/solution.py
@@ -345,9 +345,8 @@
     kv_grad = pair_scatter(kv_blocks, ctx_far, 2).astype(jnp.bfloat16)
 
     dims_t = (((0,), (0,)), ((), ()))
-    key_part = lax.dot_general(local_rows, kv_grad[:, :width_kv], dims_t, preferred_element_type=jnp.float32)
-    value_part = lax.dot_general(local_rows, kv_grad[:, width_kv:], dims_t, preferred_element_type=jnp.float32)
-    parts = jnp.concatenate([key_part, value_part], axis=1).astype(jnp.bfloat16)
+    parts = lax.dot_general(local_rows, kv_grad, dims_t, preferred_element_type=jnp.float32)
+    parts = parts.astype(jnp.bfloat16)
     parts = parts.reshape((-1, key_proj.shape[0], parts.shape[1]))
     summed = pair_scatter(parts, far_first, 3, canonical)
     key_sum, value_sum = summed[:, :width_kv], summed[:, width_kv:]

time: 195 us -> 192 us (0.985)
  other arithmetic: 8.23 us -> 4.39 us
    convert_element_type x0 -> x1, local copies, waits for them, and re-layouts: none -> 4.08 us  [body(): parts = parts.astype(jnp.bfloat16)]
    dot_general x2 -> x0, local copies, waits for them, and re-layouts: 3.89 us -> none  [the longest x1 2.28 us: body(): lax.dot_general(local_rows, kv_grad[:, :width_kv], dims_t, preferred_elem...]
    concatenate x1 -> x0, other arithmetic: 2.9 us -> none  [body(): parts = jnp.concatenate([key_part, value_part], axis=1).astype(jnp.bfloat16)]
where the time goes in v12:
time: 192 us; the launch traced here: 191 us
  Pallas kernels  171 us (89%)
  local copies, waits for them, and re-layouts  9.59 us (5%)
  matrix products  5.18 us (3%)
  other arithmetic  4.39 us (2%)
    pallas_call x2, Pallas kernels, pair_scatter(): pl.pallas_call(functools.partial(_scatter_kernel, steps, canonical), out_...  86.9 us
    pallas_call x2, Pallas kernels, pair_gather(): pl.pallas_call(functools.partial(_gather_kernel, steps, canonical), out_s...  68.7 us
    pallas_call x1, Pallas kernels, attention_block(): pl.pallas_call(_attention_kernel, out_shape=(jax.ShapeDtypeStruct((rows,...  15.3 us
    convert_element_type x1, local copies, waits for them, and re-layouts, body(): parts = parts.astype(jnp.bfloat16)  4.08 us

profile of v12, /device:TPU:24, one launch (start us, length us, event | category | flops | bytes accessed | tf_op | source)
XLA Modules:
  0.0 190.9 jit_solution(7326696862356052245)
XLA Ops:
  0.6 0.0 copy-start
  0.6 0.8 convert_reduce_fusion.1
  1.5 0.7 bitcast_convert_fusion
  2.2 1.4 maximum_bitcast_fusion.1.x_ref
  3.5 0.8 copy.10.mq_ref
  4.3 38.9 %shard_map.85 = bf16[64,64,256]{2,1,0:T(8,128)(2,1)} custom-call(bf16[1,64,256]{2,1,0:T(8,128)(2,1)} %maximum_bitcast_fusion.1.x_ref), custom_call_target="tpu_custom_call" | custom-call | tf_op jit(solution)/shard_map/pallas_call | solution.py:150
  43.2 0.0 copy-done
  43.2 2.2 %fusion.7 = bf16[192,256]{1,0:T(8,128)(2,1)S(1)} fusion(bf16[4096,256]{1,0:T(8,128)(2,1)} %bitcast.30, bf16[1,192,4096]{2,1,0:T(8,128)(2,1)S(1)} %copy-done), kind=kOutput, calls=%fused_computation.6 | convolution fusion | flops 402702336 | bytes 3768320 | tf_op jit(solution)/shard_map/dot_general | solution.py:332
  45.3 0.7 maximum_bitcast_fusion.x_ref
  46.0 29.9 %shard_map.86 = bf16[16,193,256]{2,1,0:T(8,128)(2,1)} custom-call(bf16[1,193,256]{2,1,0:T(8,128)(2,1)} %maximum_bitcast_fusion.x_ref), custom_call_target="tpu_custom_call" | custom-call | tf_op jit(solution)/shard_map/pallas_call | solution.py:150
  75.8 0.9 convert_reduce_fusion
  76.7 2.6 %fusion.11 = (bf16[16,192,128]{2,1,0:T(8,128)(2,1)}, bf16[16,192,128]{2,1,0:T(8,128)(2,1)}) fusion(bf16[16,193,256]{2,1,0:T(8,128)(2,1)} %shard_map.86), kind=kLoop, calls=%fused_computation.13 | loop fusion | bytes 3145728 | tf_op jit(solution)/shard_map/slice | solution.py:338
  79.4 0.7 reshape.56.mk_ref
  80.1 15.3 %shard_map.87 = (bf16[192,512]{1,0:T(8,128)(2,1)}, bf16[3072,256]{1,0:T(8,128)(2,1)}) custom-call(bf16[192,512]{1,0:T(8,128)(2,1)} %bitcast.34, bf16[192,512]{1,0:T(8,128)(2,1)} %bitcast.35, bf16[3072,128]{1,0:T(8,128)(2,1)} %bitcast.33, bf16[3072,128]{1,0:T(8,128)(2,1)} %bitcast.32, f32[192,1]{1,0:T(8,128)} %copy.10.mq_ref, f32[1,3072]{1,0:T(1,128)} %reshape.56.mk_ref), custom_call_target="tpu_custom_call" | custom-call | flops 3623878656 | bytes 3932160 | tf_op jit(solution)/shard_map/pallas_call | solution.py:279
  95.4 40.9 %shard_map.88 = f32[192,256]{1,0:T(8,128)} custom-call(bf16[16,192,256]{2,1,0:T(8,128)(2,1)} %bitcast.31), custom_call_target="tpu_custom_call" | custom-call | tf_op jit(solution)/shard_map/pallas_call | solution.py:221
  136.3 3.0 %fusion = bf16[4096,256]{0,1:T(8,128)(2,1)} fusion(bf16[1,192,4096]{2,1,0:T(8,128)(2,1)S(1)} %copy-done, f32[192,256]{1,0:T(8,128)} %shard_map.88), kind=kOutput, calls=%fused_computation.1 | convolution fusion | flops 403750912 | bytes 3866624 | tf_op jit(solution)/shard_map/dot_general | solution.py:348
  139.3 4.1 %copy.11 = bf16[4096,256]{1,0:T(8,128)(2,1)} copy(bf16[4096,256]{0,1:T(8,128)(2,1)} %fusion) | data formatting | bytes 4194304 | tf_op jit(solution)/shard_map/convert_element_type | solution.py:349
  143.4 46.1 %shard_map.89 = f32[64,256]{1,0:T(8,128)} custom-call(bf16[64,64,256]{2,1,0:T(8,128)(2,1)} %bitcast.29), custom_call_target="tpu_custom_call" | custom-call | tf_op jit(solution)/shard_map/pallas_call | solution.py:221
  189.5 1.4 fusion.12
  (2 shorter events, 0.0 us)
Async XLA Ops:
  0.6 42.5 %copy-start = (bf16[1,192,4096]{2,1,0:T(8,128)(2,1)S(1)}, bf16[1,192,4096]{2,1,0:T(8,128)(2,1)}, u32[]{:S(2)}) copy-start(bf16[1,192,4096]{2,1,0:T(8,128)(2,1)} %param.6) | copy-start | bytes 4718596

commit v13 on v12

--- a/solution.py
+++ b/solution.py
@@ -237,10 +237,14 @@
     )(x)
 
 
-def _attention_kernel(q_ref, do_ref, k_ref, v_ref, mq_ref, mk_ref, gq_ref, dkv_ref, dk_acc, dv_acc):
+def _attention_kernel(q_ref, do_ref, kvm_ref, mq_ref, mk_ref, gq_ref, dkv_ref, dk_acc, dv_acc, k_scr, v_scr):
     scale = HEAD_DIM ** (-0.5)
-    keys = k_ref[...]
-    values = v_ref[...]
+    rows = q_ref.shape[0]
+    for j in range(kvm_ref.shape[0]):
+        k_scr[j * rows:(j + 1) * rows, :] = kvm_ref[j, 0:rows, 0:HEAD_DIM]
+        v_scr[j * rows:(j + 1) * rows, :] = kvm_ref[j, 0:rows, HEAD_DIM:2 * HEAD_DIM]
+    keys = k_scr[...]
+    values = v_scr[...]
     same = mq_ref[...] == mk_ref[...]
     dk_acc[...] = jnp.zeros_like(dk_acc)
     dv_acc[...] = jnp.zeros_like(dv_acc)
@@ -270,9 +274,9 @@
     dkv_ref[:, HEAD_DIM:] = dv_acc[...].astype(dkv_ref.dtype)
 
 
-def attention_block(q, do, keys, values, mq, mk):
+def attention_block(q, do, kvm, mq, mk):
     rows, width = q.shape
-    n_keys = keys.shape[0]
+    n_keys = kvm.shape[0] * rows
     heads = width // HEAD_DIM
     flops = 2 * rows * n_keys * HEAD_DIM * heads * 6
     vmem = pltpu.VMEM
@@ -282,18 +286,20 @@
             jax.ShapeDtypeStruct((rows, width), jnp.bfloat16),
             jax.ShapeDtypeStruct((n_keys, 2 * HEAD_DIM), jnp.bfloat16),
         ),
-        in_specs=[pl.BlockSpec(memory_space=vmem)] * 6,
+        in_specs=[pl.BlockSpec(memory_space=vmem)] * 5,
         out_specs=(pl.BlockSpec(memory_space=vmem), pl.BlockSpec(memory_space=vmem)),
         scratch_shapes=[
             pltpu.VMEM((n_keys, HEAD_DIM), jnp.float32),
             pltpu.VMEM((n_keys, HEAD_DIM), jnp.float32),
+            pltpu.VMEM((n_keys, HEAD_DIM), kvm.dtype),
+            pltpu.VMEM((n_keys, HEAD_DIM), kvm.dtype),
         ],
         cost_estimate=pl.CostEstimate(
             flops=flops,
             transcendentals=2 * rows * n_keys * heads,
             bytes_accessed=4 * rows * width * 2 + 4 * n_keys * HEAD_DIM * 2,
         ),
-    )(q, do, keys, values, mq, mk)
+    )(q, do, kvm, mq, mk)
 
 
 def body(hidden, queries, grad_out, segment, key_proj, value_proj):
@@ -334,13 +340,11 @@
     marks_row = jnp.pad(marks, (0, 2 * HEAD_DIM - tok_rows))[None, :]
     kvm = jnp.concatenate([kv, marks_row], axis=0)[None]
     kvm_all = pair_gather(kvm, ctx_far, 0)
-    keys = kvm_all[:, :tok_rows, :HEAD_DIM].reshape(-1, HEAD_DIM)
-    values = kvm_all[:, :tok_rows, HEAD_DIM:].reshape(-1, HEAD_DIM)
     marks_all = kvm_all[:, tok_rows, :tok_rows].reshape(-1)
 
     mq = marks.astype(jnp.float32)[:, None]
     mk = marks_all.astype(jnp.float32)[None, :]
-    grad_q, kv_part = attention_block(queries[0], grad_out[0], keys, values, mq, mk)
+    grad_q, kv_part = attention_block(queries[0], grad_out[0], kvm_all, mq, mk)
     kv_blocks = kv_part.reshape((-1, tok_rows, kv_part.shape[1]))
     kv_grad = pair_scatter(kv_blocks, ctx_far, 2).astype(jnp.bfloat16)
 

time: 192 us -> 189 us (0.984)
  local copies, waits for them, and re-layouts: 9.59 us -> 6.95 us
    slice x1 -> x0, local copies, waits for them, and re-layouts: 2.64 us -> none  [body(): values = kvm_all[:, :tok_rows, HEAD_DIM:].reshape(-1, HEAD_DIM)]
where the time goes in v13:
time: 189 us
  Pallas kernels  171 us (90%)
  local copies, waits for them, and re-layouts  6.95 us (4%)
  matrix products  5.18 us (3%)
  other arithmetic  4.39 us (2%)
    pallas_call x2, Pallas kernels, pair_scatter(): pl.pallas_call(functools.partial(_scatter_kernel, steps, canonical), out_...  86.9 us
    pallas_call x2, Pallas kernels, pair_gather(): pl.pallas_call(functools.partial(_gather_kernel, steps, canonical), out_s...  68.7 us
    pallas_call x1, Pallas kernels, attention_block(): pl.pallas_call(_attention_kernel, out_shape=(jax.ShapeDtypeStruct((rows,...  15.7 us
    convert_element_type x1, local copies, waits for them, and re-layouts, body(): parts = parts.astype(jnp.bfloat16)  4.08 us

profile of v13, /device:TPU:24, one launch (start us, length us, event | category | flops | bytes accessed | tf_op | source)
XLA Modules:
  0.0 188.6 jit_solution(5020034961744246051)
XLA Ops:
  0.6 0.0 copy-start
  0.6 0.8 convert_reduce_fusion.1
  1.5 0.7 bitcast_convert_fusion
  2.2 1.4 maximum_bitcast_fusion.1.x_ref
  3.5 0.8 copy.10.mq_ref
  4.3 38.9 %shard_map.85 = bf16[64,64,256]{2,1,0:T(8,128)(2,1)} custom-call(bf16[1,64,256]{2,1,0:T(8,128)(2,1)} %maximum_bitcast_fusion.1.x_ref), custom_call_target="tpu_custom_call" | custom-call | tf_op jit(solution)/shard_map/pallas_call | solution.py:150
  43.2 0.0 copy-done
  43.2 2.2 %fusion.7 = bf16[192,256]{1,0:T(8,128)(2,1)S(1)} fusion(bf16[4096,256]{1,0:T(8,128)(2,1)} %bitcast.28, bf16[1,192,4096]{2,1,0:T(8,128)(2,1)S(1)} %copy-done), kind=kOutput, calls=%fused_computation.6 | convolution fusion | flops 402702336 | bytes 3768320 | tf_op jit(solution)/shard_map/dot_general | solution.py:338
  45.3 0.7 maximum_bitcast_fusion.x_ref
  46.0 29.9 %shard_map.86.kvm_ref = bf16[16,193,256]{2,1,0:T(8,128)(2,1)} custom-call(bf16[1,193,256]{2,1,0:T(8,128)(2,1)} %maximum_bitcast_fusion.x_ref), custom_call_target="tpu_custom_call" | custom-call | tf_op jit(solution)/shard_map/pallas_call | solution.py:150
  75.8 0.9 convert_reduce_fusion
  76.7 0.7 reshape.48.mk_ref
  77.4 15.7 %shard_map.87 = (bf16[192,512]{1,0:T(8,128)(2,1)}, bf16[3072,256]{1,0:T(8,128)(2,1)}) custom-call(bf16[192,512]{1,0:T(8,128)(2,1)} %bitcast.30, bf16[192,512]{1,0:T(8,128)(2,1)} %bitcast.31, bf16[16,193,256]{2,1,0:T(8,128)(2,1)} %shard_map.86.kvm_ref, f32[192,1]{1,0:T(8,128)} %copy.10.mq_ref, f32[1,3072]{1,0:T(1,128)} %reshape.48.mk_ref), custom_call_target="tpu_custom_call" | custom-call | flops 3623878656 | bytes 3932160 | tf_op jit(solution)/shard_map/pallas_call | solution.py:283
  93.1 40.9 %shard_map.88 = f32[192,256]{1,0:T(8,128)} custom-call(bf16[16,192,256]{2,1,0:T(8,128)(2,1)} %bitcast.29), custom_call_target="tpu_custom_call" | custom-call | tf_op jit(solution)/shard_map/pallas_call | solution.py:221
  134.0 3.0 %fusion = bf16[4096,256]{0,1:T(8,128)(2,1)} fusion(bf16[1,192,4096]{2,1,0:T(8,128)(2,1)S(1)} %copy-done, f32[192,256]{1,0:T(8,128)} %shard_map.88), kind=kOutput, calls=%fused_computation.1 | convolution fusion | flops 403750912 | bytes 3866624 | tf_op jit(solution)/shard_map/dot_general | solution.py:352
  137.0 4.1 %copy.11 = bf16[4096,256]{1,0:T(8,128)(2,1)} copy(bf16[4096,256]{0,1:T(8,128)(2,1)} %fusion) | data formatting | bytes 4194304 | tf_op jit(solution)/shard_map/convert_element_type | solution.py:353
  141.1 46.1 %shard_map.89 = f32[64,256]{1,0:T(8,128)} custom-call(bf16[64,64,256]{2,1,0:T(8,128)(2,1)} %bitcast.27), custom_call_target="tpu_custom_call" | custom-call | tf_op jit(solution)/shard_map/pallas_call | solution.py:221
  187.2 1.4 fusion.11
  (2 shorter events, 0.0 us)
Async XLA Ops:
  0.6 42.5 %copy-start = (bf16[1,192,4096]{2,1,0:T(8,128)(2,1)S(1)}, bf16[1,192,4096]{2,1,0:T(8,128)(2,1)}, u32[]{:S(2)}) copy-start(bf16[1,192,4096]{2,1,0:T(8,128)(2,1)} %param.6) | copy-start | bytes 4718596

commit v14 on v13

--- a/solution.py
+++ b/solution.py
@@ -256,8 +256,9 @@
         raw = lax.dot_general(qh, keys, nt, preferred_element_type=jnp.float32) * scale
         raw = jnp.where(same, raw, far_below)
         top = jnp.max(raw, axis=1, keepdims=True)
-        total = jnp.sum(jnp.exp(raw - top), axis=1, keepdims=True)
-        probs = jnp.exp(raw - (top + jnp.log(total)))
+        weights = jnp.exp(raw - top)
+        total = jnp.sum(weights, axis=1, keepdims=True)
+        probs = weights / total
         probs_b = probs.astype(jnp.bfloat16)
         out = jnp.dot(probs_b, values, preferred_element_type=jnp.float32).astype(jnp.bfloat16)
         delta = jnp.sum(doh.astype(jnp.float32) * out.astype(jnp.float32), axis=1, keepdims=True)

time: 189 us -> 189 us (level)
  no operation moved by 1% of the time
where the time goes in v14:
time: 189 us; the launch traced here: 188 us
  Pallas kernels  171 us (90%)
  local copies, waits for them, and re-layouts  6.95 us (4%)
  matrix products  5.18 us (3%)
  other arithmetic  4.39 us (2%)
    pallas_call x2, Pallas kernels, pair_scatter(): pl.pallas_call(functools.partial(_scatter_kernel, steps, canonical), out_...  86.9 us
    pallas_call x2, Pallas kernels, pair_gather(): pl.pallas_call(functools.partial(_gather_kernel, steps, canonical), out_s...  68.7 us
    pallas_call x1, Pallas kernels, attention_block(): pl.pallas_call(_attention_kernel, out_shape=(jax.ShapeDtypeStruct((rows,...  15.3 us
    convert_element_type x1, local copies, waits for them, and re-layouts, body(): parts = parts.astype(jnp.bfloat16)  4.08 us

profile of v14, /device:TPU:24, one launch (start us, length us, event | category | flops | bytes accessed | tf_op | source)
XLA Modules:
  0.0 188.2 jit_solution(5234795413998276099)
XLA Ops:
  0.6 0.0 copy-start
  0.6 0.8 convert_reduce_fusion.1
  1.5 0.7 bitcast_convert_fusion
  2.2 1.4 maximum_bitcast_fusion.1.x_ref
  3.5 0.8 copy.10.mq_ref
  4.3 38.9 %shard_map.85 = bf16[64,64,256]{2,1,0:T(8,128)(2,1)} custom-call(bf16[1,64,256]{2,1,0:T(8,128)(2,1)} %maximum_bitcast_fusion.1.x_ref), custom_call_target="tpu_custom_call" | custom-call | tf_op jit(solution)/shard_map/pallas_call | solution.py:150
  43.2 0.0 copy-done
  43.2 2.2 %fusion.7 = bf16[192,256]{1,0:T(8,128)(2,1)S(1)} fusion(bf16[4096,256]{1,0:T(8,128)(2,1)} %bitcast.28, bf16[1,192,4096]{2,1,0:T(8,128)(2,1)S(1)} %copy-done), kind=kOutput, calls=%fused_computation.6 | convolution fusion | flops 402702336 | bytes 3768320 | tf_op jit(solution)/shard_map/dot_general | solution.py:339
  45.3 0.7 maximum_bitcast_fusion.x_ref
  46.0 29.9 %shard_map.86.kvm_ref = bf16[16,193,256]{2,1,0:T(8,128)(2,1)} custom-call(bf16[1,193,256]{2,1,0:T(8,128)(2,1)} %maximum_bitcast_fusion.x_ref), custom_call_target="tpu_custom_call" | custom-call | tf_op jit(solution)/shard_map/pallas_call | solution.py:150
  75.8 0.9 convert_reduce_fusion
  76.7 0.7 reshape.48.mk_ref
  77.4 15.3 %shard_map.87 = (bf16[192,512]{1,0:T(8,128)(2,1)}, bf16[3072,256]{1,0:T(8,128)(2,1)}) custom-call(bf16[192,512]{1,0:T(8,128)(2,1)} %bitcast.30, bf16[192,512]{1,0:T(8,128)(2,1)} %bitcast.31, bf16[16,193,256]{2,1,0:T(8,128)(2,1)} %shard_map.86.kvm_ref, f32[192,1]{1,0:T(8,128)} %copy.10.mq_ref, f32[1,3072]{1,0:T(1,128)} %reshape.48.mk_ref), custom_call_target="tpu_custom_call" | custom-call | flops 3623878656 | bytes 3932160 | tf_op jit(solution)/shard_map/pallas_call | solution.py:284
  92.7 40.8 %shard_map.88 = f32[192,256]{1,0:T(8,128)} custom-call(bf16[16,192,256]{2,1,0:T(8,128)(2,1)} %bitcast.29), custom_call_target="tpu_custom_call" | custom-call | tf_op jit(solution)/shard_map/pallas_call | solution.py:221
  133.6 3.0 %fusion = bf16[4096,256]{0,1:T(8,128)(2,1)} fusion(bf16[1,192,4096]{2,1,0:T(8,128)(2,1)S(1)} %copy-done, f32[192,256]{1,0:T(8,128)} %shard_map.88), kind=kOutput, calls=%fused_computation.1 | convolution fusion | flops 403750912 | bytes 3866624 | tf_op jit(solution)/shard_map/dot_general | solution.py:353
  136.6 4.1 %copy.11 = bf16[4096,256]{1,0:T(8,128)(2,1)} copy(bf16[4096,256]{0,1:T(8,128)(2,1)} %fusion) | data formatting | bytes 4194304 | tf_op jit(solution)/shard_map/convert_element_type | solution.py:354
  140.7 46.1 %shard_map.89 = f32[64,256]{1,0:T(8,128)} custom-call(bf16[64,64,256]{2,1,0:T(8,128)(2,1)} %bitcast.27), custom_call_target="tpu_custom_call" | custom-call | tf_op jit(solution)/shard_map/pallas_call | solution.py:221
  186.8 1.4 fusion.11
  (2 shorter events, 0.0 us)
Async XLA Ops:
  0.6 42.5 %copy-start = (bf16[1,192,4096]{2,1,0:T(8,128)(2,1)S(1)}, bf16[1,192,4096]{2,1,0:T(8,128)(2,1)}, u32[]{:S(2)}) copy-start(bf16[1,192,4096]{2,1,0:T(8,128)(2,1)} %param.6) | copy-start | bytes 4718596

commit v15 on v13

--- a/solution.py
+++ b/solution.py
@@ -165,6 +165,9 @@
 def _scatter_kernel(steps, canonical, x_in, o_ref, acc, rbuf, sbuf, staged, rel, send_sems, recv_sems, local_sem):
     mesh = pl.DeviceIdType.MESH
     partners = [{axis: lax.bitwise_xor(lax.axis_index(axis), 1 << bit)} for axis, _, bit in steps]
+    barrier = pltpu.get_barrier_semaphore()
+    for p in partners:
+        pl.semaphore_signal(barrier, inc=1, device_id=p, device_id_type=mesh)
     x_ref = x_in
     if canonical is not None:
         weights = []
@@ -182,9 +185,6 @@
             pltpu.make_async_copy(x_in.at[pl.ds(at, 1)], rel.at[r:r + 1], local_sem).start()
         pltpu.make_async_copy(x_in, rel, local_sem).wait()
         x_ref = rel
-    barrier = pltpu.get_barrier_semaphore()
-    for p in partners:
-        pl.semaphore_signal(barrier, inc=1, device_id=p, device_id_type=mesh)
     pl.semaphore_wait(barrier, len(partners))
     for k in reversed(range(len(steps))):
         half = 1 << k

time: 189 us -> 186 us (0.984)
  Pallas kernels: 171 us -> 169 us
    pallas_call x2, Pallas kernels: 86.9 us -> 84.1 us  [pair_scatter(): pl.pallas_call(functools.partial(_scatter_kernel, steps, canonical), out_...]
where the time goes in v15:
time: 186 us
  Pallas kernels  169 us (91%)
  local copies, waits for them, and re-layouts  6.95 us (4%)
  matrix products  5.18 us (3%)
  other arithmetic  4.39 us (2%)
    pallas_call x2, Pallas kernels, pair_scatter(): pl.pallas_call(functools.partial(_scatter_kernel, steps, canonical), out_...  84.1 us
    pallas_call x2, Pallas kernels, pair_gather(): pl.pallas_call(functools.partial(_gather_kernel, steps, canonical), out_s...  68.7 us
    pallas_call x1, Pallas kernels, attention_block(): pl.pallas_call(_attention_kernel, out_shape=(jax.ShapeDtypeStruct((rows,...  15.7 us
    convert_element_type x1, local copies, waits for them, and re-layouts, body(): parts = parts.astype(jnp.bfloat16)  4.08 us

profile of v15, /device:TPU:24, one launch (start us, length us, event | category | flops | bytes accessed | tf_op | source)
XLA Modules:
  0.0 185.8 jit_solution(6933915313728113826)
XLA Ops:
  0.6 0.0 copy-start
  0.6 0.8 convert_reduce_fusion.1
  1.5 0.7 bitcast_convert_fusion
  2.2 1.4 maximum_bitcast_fusion.1.x_ref
  3.5 0.8 copy.10.mq_ref
  4.3 38.9 %shard_map.85 = bf16[64,64,256]{2,1,0:T(8,128)(2,1)} custom-call(bf16[1,64,256]{2,1,0:T(8,128)(2,1)} %maximum_bitcast_fusion.1.x_ref), custom_call_target="tpu_custom_call" | custom-call | tf_op jit(solution)/shard_map/pallas_call | solution.py:150
  43.2 0.0 copy-done
  43.2 2.2 %fusion.7 = bf16[192,256]{1,0:T(8,128)(2,1)S(1)} fusion(bf16[4096,256]{1,0:T(8,128)(2,1)} %bitcast.28, bf16[1,192,4096]{2,1,0:T(8,128)(2,1)S(1)} %copy-done), kind=kOutput, calls=%fused_computation.6 | convolution fusion | flops 402702336 | bytes 3768320 | tf_op jit(solution)/shard_map/dot_general | solution.py:338
  45.3 0.7 maximum_bitcast_fusion.x_ref
  46.0 29.9 %shard_map.86.kvm_ref = bf16[16,193,256]{2,1,0:T(8,128)(2,1)} custom-call(bf16[1,193,256]{2,1,0:T(8,128)(2,1)} %maximum_bitcast_fusion.x_ref), custom_call_target="tpu_custom_call" | custom-call | tf_op jit(solution)/shard_map/pallas_call | solution.py:150
  75.8 0.9 convert_reduce_fusion
  76.7 0.7 reshape.48.mk_ref
  77.4 15.7 %shard_map.87 = (bf16[192,512]{1,0:T(8,128)(2,1)}, bf16[3072,256]{1,0:T(8,128)(2,1)}) custom-call(bf16[192,512]{1,0:T(8,128)(2,1)} %bitcast.30, bf16[192,512]{1,0:T(8,128)(2,1)} %bitcast.31, bf16[16,193,256]{2,1,0:T(8,128)(2,1)} %shard_map.86.kvm_ref, f32[192,1]{1,0:T(8,128)} %copy.10.mq_ref, f32[1,3072]{1,0:T(1,128)} %reshape.48.mk_ref), custom_call_target="tpu_custom_call" | custom-call | flops 3623878656 | bytes 3932160 | tf_op jit(solution)/shard_map/pallas_call | solution.py:283
  93.1 40.9 %shard_map.88 = f32[192,256]{1,0:T(8,128)} custom-call(bf16[16,192,256]{2,1,0:T(8,128)(2,1)} %bitcast.29), custom_call_target="tpu_custom_call" | custom-call | tf_op jit(solution)/shard_map/pallas_call | solution.py:221
  134.0 3.0 %fusion = bf16[4096,256]{0,1:T(8,128)(2,1)} fusion(bf16[1,192,4096]{2,1,0:T(8,128)(2,1)S(1)} %copy-done, f32[192,256]{1,0:T(8,128)} %shard_map.88), kind=kOutput, calls=%fused_computation.1 | convolution fusion | flops 403750912 | bytes 3866624 | tf_op jit(solution)/shard_map/dot_general | solution.py:352
  137.0 4.1 %copy.11 = bf16[4096,256]{1,0:T(8,128)(2,1)} copy(bf16[4096,256]{0,1:T(8,128)(2,1)} %fusion) | data formatting | bytes 4194304 | tf_op jit(solution)/shard_map/convert_element_type | solution.py:353
  141.1 43.3 %shard_map.89 = f32[64,256]{1,0:T(8,128)} custom-call(bf16[64,64,256]{2,1,0:T(8,128)(2,1)} %bitcast.27), custom_call_target="tpu_custom_call" | custom-call | tf_op jit(solution)/shard_map/pallas_call | solution.py:221
  184.4 1.4 fusion.11
  (2 shorter events, 0.0 us)
Async XLA Ops:
  0.6 42.5 %copy-start = (bf16[1,192,4096]{2,1,0:T(8,128)(2,1)S(1)}, bf16[1,192,4096]{2,1,0:T(8,128)(2,1)}, u32[]{:S(2)}) copy-start(bf16[1,192,4096]{2,1,0:T(8,128)(2,1)} %param.6) | copy-start | bytes 4718596
